TPU v7x, 128 devices: a whole 4x4x4 slice. The times are simulated.
128 devices in a mesh: tile: 16 (over y_hi, z, core), sub: 8 (over y_lo, x).
Axes of the slice: x: 4, y: 4 (y_hi: 2, y_lo: 2; y = y_hi * 2 + y_lo), z: 4, core: 2. Of those that a mesh axis runs over, the one named last changes fastest.
Arguments:
- adjoint_final: float32 [2, 16, 8192, 512], P(None, None, ('tile', 'sub')), may hold values from -6 to 6
- diff_scale: float32 [16, 8192, 512], P(None, ('tile', 'sub')), may hold values from 0.5 to 1
- vert_coupling: float32 [15, 8192, 512], P(None, ('tile', 'sub')), may hold values from 0.1 to 4
- column_depth: int32 [8192, 512], P(('tile', 'sub')), may hold values from 0 to 16
- seam_table: int32 [16, 4, 3], replicated, may hold values from 0 to 15, as said below
- tile_owner: int32 [16], replicated, may hold values from 0 to 15, each once
- prof_face: int32 [32768], P(('tile', 'sub')), may hold values from 0 to 15, as said below
- prof_cell: int32 [32768], P(('tile', 'sub')), may hold values from 0 to 262143
- prof_time: int32 [32768], P(('tile', 'sub')), may hold values from 1 to 2
- misfit: float32 [2, 16, 32768], P(None, None, ('tile', 'sub')), may hold values from -6 to 6
Outputs:
- adjoint_initial: float32 [2, 16, 8192, 512], P(None, None, ('tile', 'sub'))
Inputs may be any that keep to these rules, and one draw needn't show every extreme that they name: seam_table[f, e] = (g, e2, r) pairs every edge with a different edge and the pairing is mutual with the same r; r is 0 or 1. `prof_face`: among the 256 rows of one device, at most 4 name the same face tile and the same block of 64 tile rows; one such pair is named exactly 4 times by the rows of every device. `tile_owner`: a permutation.
All inputs are finite; a program needn't handle non-finite values.
Results may differ from a plain program's by a relative error of at most 0.000062.
Values sent between devices are 32-bit elements; how exact they have to be, the bound alone decides.
No kernel may reach another device: no remote copies, remote signals or barrier semaphores. Data moves between devices by JAX's collectives and lax.ppermute only.
A program may use at most 128 MiB of HBM per device.

v0:
```python
import functools

import jax
import jax.numpy as jnp
from jax import lax
from jax.experimental import pallas as pl
from jax.experimental.pallas import tpu as pltpu
from jax.sharding import PartitionSpec as P

CAP = 4
LEVELS = 16
PLANES = 2 * LEVELS
ROWS = 64
COLS = 512
CELLS = ROWS * COLS
N_TILE = 16
N_SUB = 8
DEVICES = N_TILE * N_SUB
FACES = 16
explicit_rate = 0.2
HIGHEST = lax.Precision.HIGHEST
VMEM = pl.BlockSpec(memory_space=pltpu.VMEM)
SMEM = pl.BlockSpec(memory_space=pltpu.SMEM)
META = 16


def iota(shape, axis):
    return lax.broadcasted_iota(jnp.int32, shape, axis)


def params(mib):
    return pltpu.CompilerParams(vmem_limit_bytes=mib * 1024 * 1024)


def f32(*shape):
    return jax.ShapeDtypeStruct(shape, jnp.float32)


def pack_kernel(ids, owner, seam, face, cell, time, misfit, out, meta):
    tile = ids[0]
    sub = ids[1]
    my_face = jnp.int32(0)
    for f in range(FACES):
        my_face = my_face + jnp.where(owner[f] == tile, f, 0)
    meta[12] = tile
    meta[13] = sub
    for edge in range(4):
        other = owner[seam[my_face, edge, 0]]
        away = (
            ((other & 1) ^ (tile & 1)) * 8
            + (((other >> 3) & 1) ^ ((tile >> 3) & 1)) * 4
            + ((((tile >> 1) & 3) + 4 - ((other >> 1) & 3)) & 3)
        )
        meta[3 * edge] = away
        meta[3 * edge + 1] = seam[my_face, edge, 1]
        meta[3 * edge + 2] = seam[my_face, edge, 2]

    rows = face.shape[1]
    faces = face[...]
    home = jnp.zeros_like(faces)
    for f in range(FACES):
        home = jnp.where(faces == f, owner[f], home)
    cells = cell[...]
    tile_row = cells >> 9
    target = home * N_SUB + (tile_row >> 6)
    code = (time[...] - 1) * CELLS + (tile_row & (ROWS - 1)) * COLS + (cells & (COLS - 1))
    first = iota((rows, rows), 0)
    second = iota((rows, rows), 1)
    target_row = jnp.broadcast_to(target.astype(jnp.float32), (rows, rows))
    target_col = jnp.sum(jnp.where(first == second, target_row, 0.0), axis=1, keepdims=True)
    rank = jnp.sum(
        jnp.where((target_col == target_row) & (first < second), 1.0, 0.0), axis=0, keepdims=True
    )
    rank = rank.astype(jnp.int32)
    values = misfit[...]
    tag = code.astype(jnp.float32) + 1.0
    dest = iota((DEVICES, rows), 0)
    total = jnp.zeros((DEVICES, 2 * DEVICES), jnp.float32)
    for k in range(CAP):
        hit = jnp.where((dest == target) & (rank == k), 1.0, 0.0)
        pieces = []
        if k > 0:
            pieces.append(jnp.zeros((PLANES * k, rows), jnp.float32))
        pieces.append(values)
        if k < CAP - 1:
            pieces.append(jnp.zeros((PLANES * (CAP - 1 - k), rows), jnp.float32))
        pieces.append(jnp.where(dest == k, tag, 0.0))
        stacked = jnp.concatenate(pieces, axis=0)
        total = total + lax.dot_general(
            hit, stacked, (((1,), (1,)), ((), ())), precision=HIGHEST,
            preferred_element_type=jnp.float32,
        )
    out[:, 0, :] = total[:, :DEVICES]
    out[:, 1, :] = total[:, DEVICES:] - 1.0


def pack(ids, owner, seam, face, cell, time, misfit):
    return pl.pallas_call(
        pack_kernel,
        out_shape=(f32(DEVICES, 2, DEVICES), jax.ShapeDtypeStruct((META,), jnp.int32)),
        in_specs=[SMEM, SMEM, SMEM, VMEM, VMEM, VMEM, VMEM],
        out_specs=(VMEM, SMEM),
        compiler_params=params(32),
        name="pack",
    )(ids, owner, seam, face, cell, time, misfit)


def forcing_kernel(moment, slots, out, parts, place):
    values = jnp.transpose(slots[:, 0, :])
    tags = (slots[:, 1, :] + 0.5).astype(jnp.int32)
    tags = jnp.where(slots[:, 1, :] < 0.0, -1, tags)
    tags_t = jnp.transpose(tags.astype(jnp.float32)).astype(jnp.int32)
    tag_row = jnp.concatenate([tags_t[k : k + 1, :] for k in range(CAP)], axis=1)
    valid = (tag_row >= moment * CELLS) & (tag_row < (moment + 1) * CELLS)
    row_of = jnp.where(valid, (tag_row & (CELLS - 1)) >> 9, -1)
    on_row = iota((ROWS, CAP * DEVICES), 0) == row_of
    wide = jnp.concatenate([values[PLANES * k : PLANES * (k + 1), :] for k in range(CAP)], axis=1)
    high = wide.astype(jnp.bfloat16).astype(jnp.float32)
    rest = wide - high
    middle = rest.astype(jnp.bfloat16).astype(jnp.float32)
    parts[0] = high
    parts[1] = middle
    parts[2] = rest - middle
    for k in range(CAP):
        col = tags[:, k : k + 1] & (COLS - 1)
        place[k * DEVICES : (k + 1) * DEVICES, :] = jnp.where(
            iota((DEVICES, COLS), 1) == col, 1.0, 0.0
        ).astype(jnp.bfloat16)
    group = 4

    def step(g, carry):
        total = None
        for part in range(3):
            left = []
            for q in range(group):
                row = parts[part, pl.ds(g * group + q, 1), :]
                left.append(jnp.where(on_row, row, 0.0).astype(jnp.bfloat16))
            got = jnp.dot(
                jnp.concatenate(left, axis=0), place[...], preferred_element_type=jnp.float32
            )
            total = got if total is None else total + got
        out[pl.ds(pl.multiple_of(g * group * ROWS, 8), group * ROWS), :] = total
        return carry

    lax.fori_loop(0, PLANES // group, step, 0)


def forcing(slots, moment):
    return pl.pallas_call(
        functools.partial(forcing_kernel, moment),
        out_shape=f32(PLANES * ROWS, COLS),
        in_specs=[VMEM],
        out_specs=VMEM,
        scratch_shapes=[
            pltpu.VMEM((3, PLANES, CAP * DEVICES), jnp.float32),
            pltpu.VMEM((CAP * DEVICES, COLS), jnp.bfloat16),
        ],
        compiler_params=params(32),
        cost_estimate=pl.CostEstimate(flops=3221225472, bytes_accessed=4325376, transcendentals=0),
        name=f"forcing_{moment}",
    )(slots)


QUARTER = PLANES * ROWS


def tile_rows(quarter, plane, block):
    return pl.ds(pl.multiple_of(quarter * QUARTER + plane * ROWS + block * 8, 8), 8)


def eliminate(value, coupling, depth, at):
    links = []
    for k in range(LEVELS - 1):
        links.append(jnp.where(k + 1 < depth, coupling[at(k)], 0.0))
    ratio = []
    partial = [[], []]
    for k in range(LEVELS):
        pivot = jnp.float32(1.0)
        if k > 0:
            pivot = pivot + links[k - 1]
        if k < LEVELS - 1:
            pivot = pivot + links[k]
        if k > 0:
            pivot = pivot - links[k - 1] * ratio[k - 1]
        inverse = 1.0 / pivot
        for tracer in range(2):
            right = value(tracer * LEVELS + k)
            if k > 0:
                right = right + links[k - 1] * partial[tracer][k - 1]
            partial[tracer].append(right * inverse)
        if k < LEVELS - 1:
            ratio.append(links[k] * inverse)
    for k in range(LEVELS - 2, -1, -1):
        for tracer in range(2):
            partial[tracer][k] = partial[tracer][k] + ratio[k] * partial[tracer][k + 1]
    return partial


def solve_tile(value, coupling, scale, depth_ref, solved, weighted, sides, block, quarter):
    columns = slice(quarter * 128, (quarter + 1) * 128)

    def at(plane):
        return (pl.ds(pl.multiple_of(plane * ROWS + block * 8, 8), 8), columns)

    depth = depth_ref[pl.ds(pl.multiple_of(block * 8, 8), 8), columns]
    result = eliminate(value, coupling, depth, at)
    lane = iota((8, 128), 1)
    column = jnp.zeros((8, 128), jnp.float32)
    for k in range(LEVELS):
        weight = jnp.where(k < depth, scale[at(k)], 0.0)
        for tracer in range(2):
            plane = tracer * LEVELS + k
            found = result[tracer][k]
            heavy = weight * found
            solved[tile_rows(quarter, plane, block), :] = found
            weighted[tile_rows(quarter, plane, block), :] = heavy
            if quarter == 0:
                moved = heavy if plane == 0 else pltpu.roll(heavy, plane, 1)
                column = jnp.where(lane == plane, moved, column)
            if quarter == 3:
                column = jnp.where(lane == plane, pltpu.roll(heavy, plane + 1, 1), column)
    if quarter == 0:
        sides[pl.ds(pl.multiple_of(block * 8, 8), 8), :] = column
    if quarter == 3:
        sides[pl.ds(pl.multiple_of(ROWS + block * 8, 8), 8), :] = column


def send_edges(meta, weighted, sides, payload, first_row, last_row):
    sub = meta[13]
    payload[0] = jnp.transpose(sides[...])[:PLANES, :]
    for b in range(4):
        top = weighted[pl.ds(b * PLANES * ROWS, PLANES, stride=ROWS), :]
        bottom = weighted[pl.ds(b * PLANES * ROWS + ROWS - 1, PLANES, stride=ROWS), :]
        payload[1 + b] = jnp.where(sub == N_SUB - 1, bottom, top)
        first_row[b] = top
        last_row[b] = bottom


EDGES = (f32(5, PLANES, 128), f32(4, PLANES, 128), f32(4, PLANES, 128))


def first_kernel(meta, adjoint, force, coupling, scale, depth, solved, weighted, payload,
                 first_row, last_row, sides):
    def step(block, carry):
        for quarter in range(4):
            columns = slice(quarter * 128, (quarter + 1) * 128)

            def value(plane):
                at = (pl.ds(pl.multiple_of(plane * ROWS + block * 8, 8), 8), columns)
                return adjoint[at] + force[at]

            solve_tile(value, coupling, scale, depth, solved, weighted, sides, block, quarter)
        return carry

    lax.fori_loop(0, ROWS // 8, step, 0)
    send_edges(meta, weighted, sides, payload, first_row, last_row)


def first_solve(meta, adjoint, force, coupling, scale, depth):
    big = f32(4 * QUARTER, 128)
    return pl.pallas_call(
        first_kernel,
        out_shape=(big, big) + EDGES,
        in_specs=[SMEM] + [VMEM] * 5,
        out_specs=(VMEM,) * 5,
        scratch_shapes=[pltpu.VMEM((128, 128), jnp.float32)],
        compiler_params=params(32),
        cost_estimate=pl.CostEstimate(flops=30000000, bytes_accessed=20000000, transcendentals=0),
        name="first_solve",
    )(meta, adjoint, force, coupling, scale, depth)


def route_kernel(meta, gathered, send, here, across):
    sub = meta[13]
    lane = iota((PLANES, 128), 1)

    def half(edge, dest, wanted):
        place, other_edge, turned = meta[3 * edge], meta[3 * edge + 1], meta[3 * edge + 2]
        chunk = jnp.where(turned == 1, N_SUB - 1 - dest, dest)
        block = jnp.where(other_edge < 2, 1 + (chunk >> 1), 0)
        side = jnp.where(other_edge < 2, chunk & 1, other_edge - 2)
        found = gathered[place, block]
        return jnp.where(side == wanted, found, pltpu.roll(found, 64, 1))

    for dest in range(N_SUB):
        send[dest, 0] = jnp.where(lane < 64, half(2, dest, 0), half(3, dest, 1))
        send[dest, 1] = jnp.zeros((PLANES, 128), jnp.float32)
    for edge, dest in ((0, 0), (1, N_SUB - 1)):
        found = gathered[meta[3 * edge], 0]
        send[dest, 1] = jnp.where(
            meta[3 * edge + 1] == 2, found, pltpu.roll(found, 64, 1)
        )
    own = jnp.where(sub == N_SUB - 1, 1, 0)
    place_here = meta[3 * own]
    place_across = meta[3 * (1 - own)]
    for b in range(4):
        here[b] = gathered[place_here, 1 + b]
        across[b] = gathered[place_across, 1 + b]


def route(meta, gathered):
    return pl.pallas_call(
        route_kernel,
        out_shape=(f32(N_SUB, 2, PLANES, 128), f32(4, PLANES, 128), f32(4, PLANES, 128)),
        in_specs=[SMEM, VMEM],
        out_specs=(VMEM,) * 3,
        compiler_params=params(16),
        cost_estimate=pl.CostEstimate(flops=1000000, bytes_accessed=1000000, transcendentals=0),
        name="route",
    )(meta, gathered)


def exchange(meta, payload, first_row, last_row):
    def turn(k):
        return [
            (y * 8 + z * 2 + c, y * 8 + ((z + k) % 4) * 2 + c)
            for y in range(2)
            for z in range(4)
            for c in range(2)
        ]

    all_parts = payload[None]
    all_parts = jnp.concatenate(
        [all_parts] + [lax.ppermute(all_parts, "tile", turn(k)) for k in (1, 2, 3)], axis=0
    )
    all_parts = jnp.concatenate(
        [all_parts, lax.ppermute(all_parts, "tile", [(i, i ^ 8) for i in range(N_TILE)])], axis=0
    )
    all_parts = jnp.concatenate(
        [all_parts, lax.ppermute(all_parts, "tile", [(i, i ^ 1) for i in range(N_TILE)])], axis=0
    )
    above = lax.ppermute(last_row, "sub", [(i, i + 1) for i in range(N_SUB - 1)])
    below = lax.ppermute(first_row, "sub", [(i + 1, i) for i in range(N_SUB - 1)])
    send, here, across = route(meta, all_parts)
    got = lax.all_to_all(send, "sub", split_axis=0, concat_axis=0, tiled=True)
    across = lax.ppermute(across, "sub", [(0, N_SUB - 1), (N_SUB - 1, 0)])
    return got, here, across, above, below


def place_halo(meta, got, here, across, above, below, halo, strips):
    sub = meta[13]
    lane = iota((PLANES, 128), 1)

    def source(edge):
        other_edge, turned = meta[3 * edge + 1], meta[3 * edge + 2]
        same = jnp.where(turned == 1, N_SUB - 1 - sub, sub)
        return jnp.where(other_edge == 0, 0, jnp.where(other_edge == 1, N_SUB - 1, same))

    sides = jnp.where(lane < 64, got[source(2), 0], got[source(3), 0])
    to = iota((128, 128), 0)
    of = iota((128, 128), 1)
    turned = jnp.where(to < 64, meta[8], meta[11])
    wanted = jnp.where(turned == 1, (to & 64) + 63 - (to & 63), to)
    pick = jnp.where(of == wanted, 1.0, 0.0)
    strips[:, :PLANES] = lax.dot_general(
        pick, sides, (((1,), (1,)), ((), ())), precision=HIGHEST, preferred_element_type=jnp.float32
    )

    own = jnp.where(sub == N_SUB - 1, 1, 0)
    other_edge, turned = meta[3 * own + 1], meta[3 * own + 2]
    flip = jnp.where(of == jnp.where(turned == 1, 127 - to, to), 1.0, 0.0)
    row = []
    for b in range(4):
        joined = jnp.where(lane < 64, got[2 * b, 1], pltpu.roll(got[2 * b + 1, 1], 64, 1))
        joined = jnp.where(other_edge < 2, across[b], joined)
        row.append(jnp.where(other_edge == own, here[b], joined))
    for b in range(4):
        ordered = jnp.where(turned == 1, row[3 - b], row[b])
        strip = jnp.dot(ordered, flip, precision=HIGHEST, preferred_element_type=jnp.float32)
        at = b * PLANES * 16
        halo[pl.ds(at + 7, PLANES, stride=16), :] = jnp.where(sub == 0, strip, above[b])
        halo[pl.ds(at + 8, PLANES, stride=16), :] = jnp.where(sub == N_SUB - 1, strip, below[b])


def stepped(solved, weighted, scale, depth_ref, halo, strips, block, quarter):
    columns = slice(quarter * 128, (quarter + 1) * 128)
    lane = iota((8, 128), 1)
    row = iota((8, 128), 0)

    here = pl.ds(pl.multiple_of(block * 8, 8), 8)
    depth = depth_ref[here, columns]
    west = strips[here, :]
    east = strips[pl.ds(pl.multiple_of(ROWS + block * 8, 8), 8), :]
    before = jnp.maximum(block - 1, 0)
    after = jnp.minimum(block + 1, ROWS // 8 - 1)

    def value(plane):
        level = plane % LEVELS
        near = (quarter * PLANES + plane) * 16
        center = weighted[tile_rows(quarter, plane, block), :]
        up = jnp.where(block == 0, halo[near : near + 8, :],
                       weighted[tile_rows(quarter, plane, before), :])
        down = jnp.where(block == ROWS // 8 - 1, halo[near + 8 : near + 16, :],
                         weighted[tile_rows(quarter, plane, after), :])
        if quarter == 0:
            left = pltpu.roll(west, 127 - plane, 1)
        else:
            left = weighted[tile_rows(quarter - 1, plane, block), :]
        if quarter == 3:
            right = east if plane == 0 else pltpu.roll(east, 128 - plane, 1)
        else:
            right = weighted[tile_rows(quarter + 1, plane, block), :]
        total = pltpu.roll(jnp.where(row == 7, up, center), 1, 0)
        total = total + pltpu.roll(jnp.where(row == 0, down, center), 7, 0)
        total = total + pltpu.roll(jnp.where(lane == 127, left, center), 1, 1)
        total = total + pltpu.roll(jnp.where(lane == 0, right, center), 127, 1)
        at = pl.ds(pl.multiple_of(level * ROWS + block * 8, 8), 8)
        weight = jnp.where(level < depth, scale[at, columns], 0.0)
        return solved[tile_rows(quarter, plane, block), :] + explicit_rate * weight * (
            total - 4.0 * center
        )

    return value


def second_kernel(meta, got, here, across, above, below, solved_in, weighted_in, force, coupling,
                  scale, depth, solved, weighted, payload, first_row, last_row, sides, halo,
                  strips):
    place_halo(meta, got, here, across, above, below, halo, strips)

    def step(block, carry):
        for quarter in range(4):
            columns = slice(quarter * 128, (quarter + 1) * 128)
            late = stepped(solved_in, weighted_in, scale, depth, halo, strips, block, quarter)

            def value(plane):
                at = (pl.ds(pl.multiple_of(plane * ROWS + block * 8, 8), 8), columns)
                return late(plane) + force[at]

            solve_tile(value, coupling, scale, depth, solved, weighted, sides, block, quarter)
        return carry

    lax.fori_loop(0, ROWS // 8, step, 0)
    send_edges(meta, weighted, sides, payload, first_row, last_row)


HALO = [
    pltpu.VMEM((4 * PLANES * 16, 128), jnp.float32),
    pltpu.VMEM((128, 128), jnp.float32),
]


def second_solve(meta, halos, solved, weighted, force, coupling, scale, depth):
    big = f32(4 * QUARTER, 128)
    return pl.pallas_call(
        second_kernel,
        out_shape=(big, big) + EDGES,
        in_specs=[SMEM] + [VMEM] * 11,
        out_specs=(VMEM,) * 5,
        scratch_shapes=[pltpu.VMEM((128, 128), jnp.float32)] + HALO,
        compiler_params=params(32),
        cost_estimate=pl.CostEstimate(flops=50000000, bytes_accessed=30000000, transcendentals=0),
        name="second_solve",
    )(meta, *halos, solved, weighted, force, coupling, scale, depth)


def last_kernel(meta, got, here, across, above, below, solved, weighted, scale, depth, out, halo,
                strips):
    place_halo(meta, got, here, across, above, below, halo, strips)

    def step(block, carry):
        for quarter in range(4):
            columns = slice(quarter * 128, (quarter + 1) * 128)
            value = stepped(solved, weighted, scale, depth, halo, strips, block, quarter)
            for plane in range(PLANES):
                at = (pl.ds(pl.multiple_of(plane * ROWS + block * 8, 8), 8), columns)
                out[at] = value(plane)
        return carry

    lax.fori_loop(0, ROWS // 8, step, 0)


def last_step(meta, halos, solved, weighted, scale, depth):
    return pl.pallas_call(
        last_kernel,
        out_shape=f32(PLANES * ROWS, COLS),
        in_specs=[SMEM] + [VMEM] * 9,
        out_specs=VMEM,
        scratch_shapes=HALO,
        compiler_params=params(32),
        cost_estimate=pl.CostEstimate(flops=20000000, bytes_accessed=20000000, transcendentals=0),
        name="last_step",
    )(meta, *halos, solved, weighted, scale, depth)


def body(
    adjoint_final,
    diff_scale,
    vert_coupling,
    column_depth,
    seam_table,
    tile_owner,
    prof_face,
    prof_cell,
    prof_time,
    misfit,
):
    ids = jnp.stack([lax.axis_index("tile"), lax.axis_index("sub")]).astype(jnp.int32)
    rows = prof_face.shape[0]
    slots, meta = pack(
        ids,
        tile_owner,
        seam_table,
        prof_face.reshape(1, rows),
        prof_cell.reshape(1, rows),
        prof_time.reshape(1, rows),
        misfit.reshape(PLANES, rows),
    )
    slots = lax.all_to_all(slots, ("tile", "sub"), split_axis=0, concat_axis=0, tiled=True)
    adjoint = adjoint_final.reshape(PLANES * ROWS, COLS)
    scale = diff_scale.reshape(LEVELS * ROWS, COLS)
    coupling = vert_coupling.reshape((LEVELS - 1) * ROWS, COLS)
    late = forcing(slots, 1)
    solved, weighted, *edges = first_solve(meta, adjoint, late, coupling, scale, column_depth)
    early = forcing(slots, 0)
    halos = exchange(meta, *edges)
    solved, weighted, *edges = second_solve(
        meta, halos, solved, weighted, early, coupling, scale, column_depth
    )
    halos = exchange(meta, *edges)
    out = last_step(meta, halos, solved, weighted, scale, column_depth)
    return out.reshape(adjoint_final.shape)


def solution(mesh):
    return jax.shard_map(
        body,
        mesh=mesh,
        in_specs=(
            P(None, None, ("tile", "sub"), None),
            P(None, ("tile", "sub"), None),
            P(None, ("tile", "sub"), None),
            P(("tile", "sub"), None),
            P(),
            P(),
            P(("tile", "sub")),
            P(("tile", "sub")),
            P(("tile", "sub")),
            P(None, None, ("tile", "sub")),
        ),
        out_specs=P(None, None, ("tile", "sub"), None),
        check_vma=False,
    )
```

profile of v0, /device:TPU:0, one launch (start us, length us, event | category | flops | bytes accessed | tf_op | source)
XLA Modules:
  0.0 162.8 jit_solution(16219200063818305232)
XLA Ops:
  0.0 0.8 copy.11.seam
  0.9 0.8 copy-done.14
  1.6 0.7 copy-done.15
  2.3 0.7 copy-done.16
  3.0 0.7 copy-done.17
  4.3 1.9 %pack.1 = (f32[128,2,128]{2,1,0:T(2,128)S(1)}, s32[16]{0:T(128)S(1)}) custom-call(s32[2]{0:T(128)S(1)} %pad_add_fusion.ids, s32[16]{0:T(128)S(1)} %copy-done.18, s32[16,4,3]{2,1,0:T(4,128)S(1)} %copy.11.seam, s32[1,256]{1,0:T(1,128)S(1)} %bitcast.31, s32[1,256]{1,0:T(1,128)S(1)} %bitcast.32, s32[1,256]{1,0:T(1,128)S(1)} %bitcast.33, f32[32,256]{1,0:T(8,128)S(1)} %bitcast.30), custom_call_target="tpu_custom_call" | custom-call | tf_op jit(solution)/shard_map/pack/pallas_call | solution.py:98
  6.2 20.6 %all_to_all.15.slots = f32[128,2,128]{2,1,0:T(2,128)S(1)} all-to-all(f32[128,2,128]{2,1,0:T(2,128)S(1)} %get-tuple-element.24), channel_id=1, replica_groups=mesh['tile'=16,'sub'=8] {'tile','sub'}, dimensions={0} | all-to-all | bytes 262144 | tf_op jit(solution)/shard_map/all_to_all | solution.py:509
  26.8 5.4 %forcing_1.1.force = f32[2048,512]{1,0:T(8,128)S(1)} custom-call(f32[128,2,128]{2,1,0:T(2,128)S(1)} %all_to_all.15.slots), custom_call_target="tpu_custom_call" | custom-call | flops 3221225472 | bytes 4325376 | tf_op jit(solution)/shard_map/forcing_1/pallas_call | solution.py:149
  32.2 3.9 %first_solve.1 = (f32[8192,128]{1,0:T(8,128)S(1)}, f32[8192,128]{1,0:T(8,128)S(1)}, f32[5,32,128]{2,1,0:T(8,128)S(1)}, f32[4,32,128]{2,1,0:T(8,128)S(1)}, f32[4,32,128]{2,1,0:T(8,128)S(1)}) custom-call(s32[16]{0:T(128)S(1)} %get-tuple-element.23.meta, f32[2048,512]{1,0:T(8,128)S(1)} %bitcast.21, f32[2048,512]{1,0:T(8,128)S(1)} %forcing_1.1.force, ...), custom_call_target="tpu_custom_call" | custom-call | flops 30000000 | bytes 20000000 | tf_op jit(solution)/shard_map/first_solve/pallas_call | solution.py:261
  36.1 2.0 %copy-done.7 = f32[8192,128]{1,0:T(8,128)} copy-done((f32[8192,128]{1,0:T(8,128)}, f32[8192,128]{1,0:T(8,128)S(1)}, u32[]{:S(2)}) %copy-start.7) | copy-done | bytes 4194328
  38.1 2.0 %copy-done.9 = f32[8192,128]{1,0:T(8,128)} copy-done((f32[8192,128]{1,0:T(8,128)}, f32[8192,128]{1,0:T(8,128)S(1)}, u32[]{:S(2)}) %copy-start.9) | copy-done | bytes 4194328
  40.7 2.2 %collective-permute-start.1 = (f32[1,5,32,128]{3,2,1,0:T(8,128)S(1)}, f32[1,5,32,128]{3,2,1,0:T(8,128)S(1)}, u32[]{:S(2)}, u32[]{:S(2)}) collective-permute-start(f32[1,5,32,128]{3,2,1,0:T(8,128)S(1)} %bitcast.27), channel_id=1, source_target_pairs={{0,32},{8,40},{16,48},{24,56},{32,0},{40,8},{48,16},{56,24},{64,96... | collective-permute-start | bytes 245768 | tf_op jit(solution)/shard_map/ppermute | solution.py:324
  43.0 2.0 %collective-permute-done.2 = f32[1,5,32,128]{3,2,1,0:T(8,128)S(1)} collective-permute-done((f32[1,5,32,128]{3,2,1,0:T(8,128)S(1)}, f32[1,5,32,128]{3,2,1,0:T(8,128)S(1)}, u32[]{:S(2)}, u32[]{:S(2)}) %collective-permute-start.2) | collective-permute-done | bytes 81952 | tf_op jit(solution)/shard_map/ppermute | solution.py:324
  45.0 2.3 %collective-permute-done.1 = f32[1,5,32,128]{3,2,1,0:T(8,128)S(1)} collective-permute-done((f32[1,5,32,128]{3,2,1,0:T(8,128)S(1)}, f32[1,5,32,128]{3,2,1,0:T(8,128)S(1)}, u32[]{:S(2)}, u32[]{:S(2)}) %collective-permute-start.1) | collective-permute-done | bytes 81952 | tf_op jit(solution)/shard_map/ppermute | solution.py:324
  47.4 1.2 collective-permute-done
  48.6 1.3 collective-permute-start.3
  50.0 8.7 %collective-permute-done.3 = f32[4,5,32,128]{3,2,1,0:T(8,128)S(1)} collective-permute-done((f32[4,5,32,128]{3,2,1,0:T(8,128)S(1)}, f32[4,5,32,128]{3,2,1,0:T(8,128)S(1)}, u32[]{:S(2)}, u32[]{:S(2)}) %collective-permute-start.3) | collective-permute-done | bytes 327712 | tf_op jit(solution)/shard_map/ppermute | solution.py:327
  58.9 2.7 %collective-permute-start.6 = (f32[4,32,128]{2,1,0:T(8,128)S(1)}, f32[4,32,128]{2,1,0:T(8,128)S(1)}, u32[]{:S(2)}, u32[]{:S(2)}) collective-permute-start(f32[4,32,128]{2,1,0:T(8,128)S(1)} %get-tuple-element.29), channel_id=1, source_target_pairs={{0,1},{1,2},{2,3},{3,4},{4,5},{5,6},{6,7},{8,9},{9,10},{10,11},{11... | collective-permute-start | bytes 196616 | tf_op jit(solution)/shard_map/ppermute | solution.py:332
  61.6 1.3 collective-permute-start.7
  62.9 1.4 route.2
  64.4 5.8 %all-to-all-start.1 = ((f32[8,2,32,128]{3,2,1,0:T(8,128)}), f32[8,2,32,128]{3,2,1,0:T(8,128)S(1)}, u32[]{:S(2)}, u32[]{:S(2)}) async-start(f32[8,2,32,128]{3,2,1,0:T(8,128)} %get-tuple-element.26), calls=%async_computation.1 | async-start | bytes 524288 | tf_op jit(solution)/shard_map/all_to_all | solution.py:335
  70.2 6.0 %collective-permute-start.5 = (f32[4,32,128]{2,1,0:T(8,128)S(1)}, f32[4,32,128]{2,1,0:T(8,128)S(1)}, u32[]{:S(2)}, u32[]{:S(2)}) collective-permute-start(f32[4,32,128]{2,1,0:T(8,128)S(1)} %get-tuple-element.28), channel_id=1, source_target_pairs={{0,7},{7,0},{8,15},{15,8},{16,23},{23,16},{24,31},{31,24},{32,39},... | collective-permute-start | bytes 196616 | tf_op jit(solution)/shard_map/ppermute | solution.py:336
  76.2 5.4 %forcing_0.1.force = f32[2048,512]{1,0:T(8,128)S(1)} custom-call(f32[128,2,128]{2,1,0:T(2,128)S(1)} %all_to_all.15.slots), custom_call_target="tpu_custom_call" | custom-call | flops 3221225472 | bytes 4325376 | tf_op jit(solution)/shard_map/forcing_0/pallas_call | solution.py:149
  81.6 2.0 %copy-done.11 = f32[2048,512]{1,0:T(8,128)} copy-done((f32[2048,512]{1,0:T(8,128)}, f32[2048,512]{1,0:T(8,128)S(1)}, u32[]{:S(2)}) %copy-start.11) | copy-done | bytes 4194328
  83.6 1.5 copy-done.2
  85.2 2.2 %copy-done.8 = f32[8192,128]{1,0:T(8,128)S(1)} copy-done((f32[8192,128]{1,0:T(8,128)S(1)}, f32[8192,128]{1,0:T(8,128)}, u32[]{:S(2)}) %copy-start.8) | copy-done | bytes 4194328
  87.4 2.2 %copy-done.10 = f32[8192,128]{1,0:T(8,128)S(1)} copy-done((f32[8192,128]{1,0:T(8,128)S(1)}, f32[8192,128]{1,0:T(8,128)}, u32[]{:S(2)}) %copy-start.10) | copy-done | bytes 4194328
  89.6 13.9 %second_solve.1 = (f32[8192,128]{1,0:T(8,128)S(1)}, f32[8192,128]{1,0:T(8,128)S(1)}, f32[5,32,128]{2,1,0:T(8,128)S(1)}, f32[4,32,128]{2,1,0:T(8,128)S(1)}, f32[4,32,128]{2,1,0:T(8,128)S(1)}) custom-call(s32[16]{0:T(128)S(1)} %get-tuple-element.23.meta, f32[8,2,32,128]{3,2,1,0:T(8,128)S(1)} %all-to-all-done.1.got, f32[4,32,128]{2,1,0:T(8,128)S(1)} %get-tuple-element.27.here, ...), custom_call_target="tpu_custom_call" | custom-call | flops 50000000 | bytes 30000000 | tf_op jit(solution)/shard_map/second_solve/pallas_call | solution.py:445
  103.4 2.0 %copy-done.3 = f32[8192,128]{1,0:T(8,128)} copy-done((f32[8192,128]{1,0:T(8,128)}, f32[8192,128]{1,0:T(8,128)S(1)}, u32[]{:S(2)}) %copy-start.3) | copy-done | bytes 4194328
  105.5 2.0 %copy-done.5 = f32[8192,128]{1,0:T(8,128)} copy-done((f32[8192,128]{1,0:T(8,128)}, f32[8192,128]{1,0:T(8,128)S(1)}, u32[]{:S(2)}) %copy-start.5) | copy-done | bytes 4194328
  107.4 0.8 collective-permute-start.10
  108.2 0.8 collective-permute-start.9
  109.0 0.9 collective-permute-start.8
  109.9 1.9 %collective-permute-done.10 = f32[1,5,32,128]{3,2,1,0:T(8,128)S(1)} collective-permute-done((f32[1,5,32,128]{3,2,1,0:T(8,128)S(1)}, f32[1,5,32,128]{3,2,1,0:T(8,128)S(1)}, u32[]{:S(2)}, u32[]{:S(2)}) %collective-permute-start.10) | collective-permute-done | bytes 81952 | tf_op jit(solution)/shard_map/ppermute | solution.py:324
  111.9 2.7 %collective-permute-done.9 = f32[1,5,32,128]{3,2,1,0:T(8,128)S(1)} collective-permute-done((f32[1,5,32,128]{3,2,1,0:T(8,128)S(1)}, f32[1,5,32,128]{3,2,1,0:T(8,128)S(1)}, u32[]{:S(2)}, u32[]{:S(2)}) %collective-permute-start.9) | collective-permute-done | bytes 81952 | tf_op jit(solution)/shard_map/ppermute | solution.py:324
  114.5 0.7 collective-permute-done.8
  115.3 2.1 %collective-permute-start.11 = (f32[4,5,32,128]{3,2,1,0:T(8,128)S(1)}, f32[4,5,32,128]{3,2,1,0:T(8,128)S(1)}, u32[]{:S(2)}, u32[]{:S(2)}) collective-permute-start(f32[4,5,32,128]{3,2,1,0:T(8,128)S(1)} %pad_maximum_fusion.1), channel_id=1, source_target_pairs={{0,64},{8,72},{16,80},{24,88},{32,96},{40,104},{48,112},{56,120},{... | collective-permute-start | bytes 983048 | tf_op jit(solution)/shard_map/ppermute | solution.py:327
  117.4 6.5 %collective-permute-done.11 = f32[4,5,32,128]{3,2,1,0:T(8,128)S(1)} collective-permute-done((f32[4,5,32,128]{3,2,1,0:T(8,128)S(1)}, f32[4,5,32,128]{3,2,1,0:T(8,128)S(1)}, u32[]{:S(2)}, u32[]{:S(2)}) %collective-permute-start.11) | collective-permute-done | bytes 327712 | tf_op jit(solution)/shard_map/ppermute | solution.py:327
  124.1 2.1 %collective-permute-done.12 = f32[8,5,32,128]{3,2,1,0:T(8,128)S(1)} collective-permute-done((f32[8,5,32,128]{3,2,1,0:T(8,128)S(1)}, f32[8,5,32,128]{3,2,1,0:T(8,128)S(1)}, u32[]{:S(2)}, u32[]{:S(2)}) %collective-permute-start.12) | collective-permute-done | bytes 655392 | tf_op jit(solution)/shard_map/ppermute | solution.py:330
  126.2 1.4 route.3
  127.6 3.4 %all-to-all-start.2 = ((f32[8,2,32,128]{3,2,1,0:T(8,128)}), f32[8,2,32,128]{3,2,1,0:T(8,128)S(1)}, u32[]{:S(2)}, u32[]{:S(2)}) async-start(f32[8,2,32,128]{3,2,1,0:T(8,128)} %get-tuple-element.34), calls=%async_computation.2 | async-start | bytes 524288 | tf_op jit(solution)/shard_map/all_to_all | solution.py:335
  131.0 3.8 %collective-permute-start.14 = (f32[4,32,128]{2,1,0:T(8,128)S(1)}, f32[4,32,128]{2,1,0:T(8,128)S(1)}, u32[]{:S(2)}, u32[]{:S(2)}) collective-permute-start(f32[4,32,128]{2,1,0:T(8,128)S(1)} %get-tuple-element.37), channel_id=1, source_target_pairs={{0,1},{1,2},{2,3},{3,4},{4,5},{5,6},{6,7},{8,9},{9,10},{10,11},{11... | collective-permute-start | bytes 196616 | tf_op jit(solution)/shard_map/ppermute | solution.py:332
  134.9 1.3 collective-permute-start.15
  136.2 6.7 %collective-permute-start.13 = (f32[4,32,128]{2,1,0:T(8,128)S(1)}, f32[4,32,128]{2,1,0:T(8,128)S(1)}, u32[]{:S(2)}, u32[]{:S(2)}) collective-permute-start(f32[4,32,128]{2,1,0:T(8,128)S(1)} %get-tuple-element.36), channel_id=1, source_target_pairs={{0,7},{7,0},{8,15},{15,8},{16,23},{23,16},{24,31},{31,24},{32,39},... | collective-permute-start | bytes 196616 | tf_op jit(solution)/shard_map/ppermute | solution.py:336
  142.9 2.2 %collective-permute-done.13.across = f32[4,32,128]{2,1,0:T(8,128)S(1)} collective-permute-done((f32[4,32,128]{2,1,0:T(8,128)S(1)}, f32[4,32,128]{2,1,0:T(8,128)S(1)}, u32[]{:S(2)}, u32[]{:S(2)}) %collective-permute-start.13) | collective-permute-done | bytes 65568 | tf_op jit(solution)/shard_map/ppermute | solution.py:336
  145.1 2.2 %copy-done.4 = f32[8192,128]{1,0:T(8,128)S(1)} copy-done((f32[8192,128]{1,0:T(8,128)S(1)}, f32[8192,128]{1,0:T(8,128)}, u32[]{:S(2)}) %copy-start.4) | copy-done | bytes 4194328
  147.3 2.2 %copy-done.6 = f32[8192,128]{1,0:T(8,128)S(1)} copy-done((f32[8192,128]{1,0:T(8,128)S(1)}, f32[8192,128]{1,0:T(8,128)}, u32[]{:S(2)}) %copy-start.6) | copy-done | bytes 4194328
  149.5 13.3 %last_step.1 = f32[2048,512]{1,0:T(8,128)} custom-call(s32[16]{0:T(128)S(1)} %get-tuple-element.23.meta, f32[8,2,32,128]{3,2,1,0:T(8,128)S(1)} %all-to-all-done.2.got, f32[4,32,128]{2,1,0:T(8,128)S(1)} %get-tuple-element.35.here, f32[4,32,128]{2,1,0:T(8,128)S(1)} %collective-permute-done.13.across, f32[4,32,128]{2,1,0:T(8,128)S(1)} %collective-permute-done.14.above, ...), custom_call_target="tpu_custom_call" | custom-call | flops 20000000 | bytes 20000000 | tf_op jit(solution)/shard_map/last_step/pallas_call | solution.py:474
  (51 shorter events, 2.0 us)
Async XLA Ops:
  0.9 0.8 copy-start.14
  1.6 0.7 copy-start.15
  2.3 0.7 copy-start.16
  3.0 0.7 copy-start.17
  3.7 0.7 copy-start.18
  26.8 5.4 %copy-start = (f32[16,64,512]{2,1,0:T(8,128)S(1)}, f32[16,64,512]{2,1,0:T(8,128)}, u32[]{:S(2)}) copy-start(f32[16,64,512]{2,1,0:T(8,128)} %param.11) | copy-start | bytes 6291460
  26.8 5.4 %copy-start.1 = (f32[15,64,512]{2,1,0:T(8,128)S(1)}, f32[15,64,512]{2,1,0:T(8,128)}, u32[]{:S(2)}) copy-start(f32[15,64,512]{2,1,0:T(8,128)} %param.12) | copy-start | bytes 5898244
  26.8 5.4 %copy-start.12 = (f32[2,16,64,512]{3,2,1,0:T(8,128)S(1)}, f32[2,16,64,512]{3,2,1,0:T(8,128)}, u32[]{:S(2)}) copy-start(f32[2,16,64,512]{3,2,1,0:T(8,128)} %param.10) | copy-start | bytes 12582916
  26.8 5.4 %copy-start.13 = (s32[64,512]{1,0:T(8,128)S(1)}, s32[64,512]{1,0:T(8,128)}, u32[]{:S(2)}) copy-start(s32[64,512]{1,0:T(8,128)} %depth.5) | copy-start | bytes 393220
  36.1 2.0 %copy-start.7 = (f32[8192,128]{1,0:T(8,128)}, f32[8192,128]{1,0:T(8,128)S(1)}, u32[]{:S(2)}) copy-start(f32[8192,128]{1,0:T(8,128)S(1)} %get-tuple-element.31.solved_in) | copy-start | bytes 12582916
  38.1 2.0 %copy-start.9 = (f32[8192,128]{1,0:T(8,128)}, f32[8192,128]{1,0:T(8,128)S(1)}, u32[]{:S(2)}) copy-start(f32[8192,128]{1,0:T(8,128)S(1)} %get-tuple-element.32.weighted_in) | copy-start | bytes 12582916
  40.0 5.0 %collective-permute-start.2 = (f32[1,5,32,128]{3,2,1,0:T(8,128)S(1)}, f32[1,5,32,128]{3,2,1,0:T(8,128)S(1)}, u32[]{:S(2)}, u32[]{:S(2)}) collective-permute-start(f32[1,5,32,128]{3,2,1,0:T(8,128)S(1)} %bitcast.26), channel_id=1, source_target_pairs={{0,48},{8,56},{16,0},{24,8},{32,16},{40,24},{48,32},{56,40},{64,11... | collective-permute-start | bytes 245768 | tf_op jit(solution)/shard_map/ppermute | solution.py:324
  40.7 6.6 %collective-permute-start.1 = (f32[1,5,32,128]{3,2,1,0:T(8,128)S(1)}, f32[1,5,32,128]{3,2,1,0:T(8,128)S(1)}, u32[]{:S(2)}, u32[]{:S(2)}) collective-permute-start(f32[1,5,32,128]{3,2,1,0:T(8,128)S(1)} %bitcast.27), channel_id=1, source_target_pairs={{0,32},{8,40},{16,48},{24,56},{32,0},{40,8},{48,16},{56,24},{64,96... | collective-permute-start | bytes 245768 | tf_op jit(solution)/shard_map/ppermute | solution.py:324
  42.9 5.7 %collective-permute-start = (f32[1,5,32,128]{3,2,1,0:T(8,128)S(1)}, f32[1,5,32,128]{3,2,1,0:T(8,128)S(1)}, u32[]{:S(2)}, u32[]{:S(2)}) collective-permute-start(f32[1,5,32,128]{3,2,1,0:T(8,128)S(1)} %bitcast.28), channel_id=1, source_target_pairs={{0,16},{8,24},{16,32},{24,40},{32,48},{40,56},{48,0},{56,8},{64,80... | collective-permute-start | bytes 245768 | tf_op jit(solution)/shard_map/ppermute | solution.py:324
  48.6 10.1 %collective-permute-start.3 = (f32[4,5,32,128]{3,2,1,0:T(8,128)S(1)}, f32[4,5,32,128]{3,2,1,0:T(8,128)S(1)}, u32[]{:S(2)}, u32[]{:S(2)}) collective-permute-start(f32[4,5,32,128]{3,2,1,0:T(8,128)S(1)} %pad_maximum_fusion), channel_id=1, source_target_pairs={{0,64},{8,72},{16,80},{24,88},{32,96},{40,104},{48,112},{56,120},{... | collective-permute-start | bytes 983048 | tf_op jit(solution)/shard_map/ppermute | solution.py:327
  58.8 4.1 %collective-permute-start.4 = (f32[8,5,32,128]{3,2,1,0:T(8,128)S(1)}, f32[8,5,32,128]{3,2,1,0:T(8,128)S(1)}, u32[]{:S(2)}, u32[]{:S(2)}) collective-permute-start(f32[8,5,32,128]{3,2,1,0:T(8,128)S(1)} %get-tuple-element.43), channel_id=1, source_target_pairs={{0,8},{8,0},{16,24},{24,16},{32,40},{40,32},{48,56},{56,48},{64,72... | collective-permute-start | bytes 1966088 | tf_op jit(solution)/shard_map/ppermute | solution.py:330
  58.9 24.7 %collective-permute-start.6 = (f32[4,32,128]{2,1,0:T(8,128)S(1)}, f32[4,32,128]{2,1,0:T(8,128)S(1)}, u32[]{:S(2)}, u32[]{:S(2)}) collective-permute-start(f32[4,32,128]{2,1,0:T(8,128)S(1)} %get-tuple-element.29), channel_id=1, source_target_pairs={{0,1},{1,2},{2,3},{3,4},{4,5},{5,6},{6,7},{8,9},{9,10},{10,11},{11... | collective-permute-start | bytes 196616 | tf_op jit(solution)/shard_map/ppermute | solution.py:332
  61.6 22.0 %collective-permute-start.7 = (f32[4,32,128]{2,1,0:T(8,128)S(1)}, f32[4,32,128]{2,1,0:T(8,128)S(1)}, u32[]{:S(2)}, u32[]{:S(2)}) collective-permute-start(f32[4,32,128]{2,1,0:T(8,128)S(1)} %get-tuple-element.30), channel_id=1, source_target_pairs={{1,0},{2,1},{3,2},{4,3},{5,4},{6,5},{7,6},{9,8},{10,9},{11,10},{12... | collective-permute-start | bytes 196616 | tf_op jit(solution)/shard_map/ppermute | solution.py:333
  64.4 19.3 %all-to-all-start.1 = ((f32[8,2,32,128]{3,2,1,0:T(8,128)}), f32[8,2,32,128]{3,2,1,0:T(8,128)S(1)}, u32[]{:S(2)}, u32[]{:S(2)}) async-start(f32[8,2,32,128]{3,2,1,0:T(8,128)} %get-tuple-element.26), calls=%async_computation.1 | async-start | bytes 524288 | tf_op jit(solution)/shard_map/all_to_all | solution.py:335
  70.2 13.5 %collective-permute-start.5 = (f32[4,32,128]{2,1,0:T(8,128)S(1)}, f32[4,32,128]{2,1,0:T(8,128)S(1)}, u32[]{:S(2)}, u32[]{:S(2)}) collective-permute-start(f32[4,32,128]{2,1,0:T(8,128)S(1)} %get-tuple-element.28), channel_id=1, source_target_pairs={{0,7},{7,0},{8,15},{15,8},{16,23},{23,16},{24,31},{31,24},{32,39},... | collective-permute-start | bytes 196616 | tf_op jit(solution)/shard_map/ppermute | solution.py:336
  81.6 2.0 %copy-start.11 = (f32[2048,512]{1,0:T(8,128)}, f32[2048,512]{1,0:T(8,128)S(1)}, u32[]{:S(2)}) copy-start(f32[2048,512]{1,0:T(8,128)S(1)} %forcing_0.1.force) | copy-start | bytes 12582916
  83.6 1.5 copy-start.2
  85.2 2.2 %copy-start.8 = (f32[8192,128]{1,0:T(8,128)S(1)}, f32[8192,128]{1,0:T(8,128)}, u32[]{:S(2)}) copy-start(f32[8192,128]{1,0:T(8,128)} %copy-done.7) | copy-start | bytes 12582916
  87.4 2.2 %copy-start.10 = (f32[8192,128]{1,0:T(8,128)S(1)}, f32[8192,128]{1,0:T(8,128)}, u32[]{:S(2)}) copy-start(f32[8192,128]{1,0:T(8,128)} %copy-done.9) | copy-start | bytes 12582916
  103.4 2.0 %copy-start.3 = (f32[8192,128]{1,0:T(8,128)}, f32[8192,128]{1,0:T(8,128)S(1)}, u32[]{:S(2)}) copy-start(f32[8192,128]{1,0:T(8,128)S(1)} %get-tuple-element.39.solved) | copy-start | bytes 12582916
  105.5 2.0 %copy-start.5 = (f32[8192,128]{1,0:T(8,128)}, f32[8192,128]{1,0:T(8,128)S(1)}, u32[]{:S(2)}) copy-start(f32[8192,128]{1,0:T(8,128)S(1)} %get-tuple-element.40.weighted) | copy-start | bytes 12582916
  107.4 4.4 %collective-permute-start.10 = (f32[1,5,32,128]{3,2,1,0:T(8,128)S(1)}, f32[1,5,32,128]{3,2,1,0:T(8,128)S(1)}, u32[]{:S(2)}, u32[]{:S(2)}) collective-permute-start(f32[1,5,32,128]{3,2,1,0:T(8,128)S(1)} %bitcast.22), channel_id=1, source_target_pairs={{0,48},{8,56},{16,0},{24,8},{32,16},{40,24},{48,32},{56,40},{64,11... | collective-permute-start | bytes 245768 | tf_op jit(solution)/shard_map/ppermute | solution.py:324
  108.2 6.3 %collective-permute-start.9 = (f32[1,5,32,128]{3,2,1,0:T(8,128)S(1)}, f32[1,5,32,128]{3,2,1,0:T(8,128)S(1)}, u32[]{:S(2)}, u32[]{:S(2)}) collective-permute-start(f32[1,5,32,128]{3,2,1,0:T(8,128)S(1)} %bitcast.23), channel_id=1, source_target_pairs={{0,32},{8,40},{16,48},{24,56},{32,0},{40,8},{48,16},{56,24},{64,96... | collective-permute-start | bytes 245768 | tf_op jit(solution)/shard_map/ppermute | solution.py:324
  109.0 6.3 %collective-permute-start.8 = (f32[1,5,32,128]{3,2,1,0:T(8,128)S(1)}, f32[1,5,32,128]{3,2,1,0:T(8,128)S(1)}, u32[]{:S(2)}, u32[]{:S(2)}) collective-permute-start(f32[1,5,32,128]{3,2,1,0:T(8,128)S(1)} %bitcast.24), channel_id=1, source_target_pairs={{0,16},{8,24},{16,32},{24,40},{32,48},{40,56},{48,0},{56,8},{64,80... | collective-permute-start | bytes 245768 | tf_op jit(solution)/shard_map/ppermute | solution.py:324
  115.3 8.7 %collective-permute-start.11 = (f32[4,5,32,128]{3,2,1,0:T(8,128)S(1)}, f32[4,5,32,128]{3,2,1,0:T(8,128)S(1)}, u32[]{:S(2)}, u32[]{:S(2)}) collective-permute-start(f32[4,5,32,128]{3,2,1,0:T(8,128)S(1)} %pad_maximum_fusion.1), channel_id=1, source_target_pairs={{0,64},{8,72},{16,80},{24,88},{32,96},{40,104},{48,112},{56,120},{... | collective-permute-start | bytes 983048 | tf_op jit(solution)/shard_map/ppermute | solution.py:327
  124.0 2.2 %collective-permute-start.12 = (f32[8,5,32,128]{3,2,1,0:T(8,128)S(1)}, f32[8,5,32,128]{3,2,1,0:T(8,128)S(1)}, u32[]{:S(2)}, u32[]{:S(2)}) collective-permute-start(f32[8,5,32,128]{3,2,1,0:T(8,128)S(1)} %get-tuple-element.41), channel_id=1, source_target_pairs={{0,8},{8,0},{16,24},{24,16},{32,40},{40,32},{48,56},{56,48},{64,72... | collective-permute-start | bytes 1966088 | tf_op jit(solution)/shard_map/ppermute | solution.py:330
  127.6 17.5 %all-to-all-start.2 = ((f32[8,2,32,128]{3,2,1,0:T(8,128)}), f32[8,2,32,128]{3,2,1,0:T(8,128)S(1)}, u32[]{:S(2)}, u32[]{:S(2)}) async-start(f32[8,2,32,128]{3,2,1,0:T(8,128)} %get-tuple-element.34), calls=%async_computation.2 | async-start | bytes 524288 | tf_op jit(solution)/shard_map/all_to_all | solution.py:335
  131.0 11.8 %collective-permute-start.14 = (f32[4,32,128]{2,1,0:T(8,128)S(1)}, f32[4,32,128]{2,1,0:T(8,128)S(1)}, u32[]{:S(2)}, u32[]{:S(2)}) collective-permute-start(f32[4,32,128]{2,1,0:T(8,128)S(1)} %get-tuple-element.37), channel_id=1, source_target_pairs={{0,1},{1,2},{2,3},{3,4},{4,5},{5,6},{6,7},{8,9},{9,10},{10,11},{11... | collective-permute-start | bytes 196616 | tf_op jit(solution)/shard_map/ppermute | solution.py:332
  134.9 8.0 %collective-permute-start.15 = (f32[4,32,128]{2,1,0:T(8,128)S(1)}, f32[4,32,128]{2,1,0:T(8,128)S(1)}, u32[]{:S(2)}, u32[]{:S(2)}) collective-permute-start(f32[4,32,128]{2,1,0:T(8,128)S(1)} %get-tuple-element.38), channel_id=1, source_target_pairs={{1,0},{2,1},{3,2},{4,3},{5,4},{6,5},{7,6},{9,8},{10,9},{11,10},{12... | collective-permute-start | bytes 196616 | tf_op jit(solution)/shard_map/ppermute | solution.py:333
  136.2 8.9 %collective-permute-start.13 = (f32[4,32,128]{2,1,0:T(8,128)S(1)}, f32[4,32,128]{2,1,0:T(8,128)S(1)}, u32[]{:S(2)}, u32[]{:S(2)}) collective-permute-start(f32[4,32,128]{2,1,0:T(8,128)S(1)} %get-tuple-element.36), channel_id=1, source_target_pairs={{0,7},{7,0},{8,15},{15,8},{16,23},{23,16},{24,31},{31,24},{32,39},... | collective-permute-start | bytes 196616 | tf_op jit(solution)/shard_map/ppermute | solution.py:336
  145.1 2.2 %copy-start.4 = (f32[8192,128]{1,0:T(8,128)S(1)}, f32[8192,128]{1,0:T(8,128)}, u32[]{:S(2)}) copy-start(f32[8192,128]{1,0:T(8,128)} %copy-done.3) | copy-start | bytes 12582916
  147.3 2.2 %copy-start.6 = (f32[8192,128]{1,0:T(8,128)S(1)}, f32[8192,128]{1,0:T(8,128)}, u32[]{:S(2)}) copy-start(f32[8192,128]{1,0:T(8,128)} %copy-done.5) | copy-start | bytes 12582916
where the time goes:
time: 164 us; the launch traced here: 163 us
  Pallas kernels  46.5 us (28%)
  starting transfers between devices  40 us (24%)
  waiting for transfers between devices  30.4 us (19%)
  local copies, waits for them, and re-layouts  24.8 us (15%)
  blocking collectives  20.6 us (13%)
    unnamed x47, local copies, waits for them, and re-layouts  24.6 us
    all_to_all x1, blocking collectives, body(): lax.all_to_all(slots, ('tile', 'sub'), split_axis=0, concat_axis=0, tiled...  20.6 us
    ppermute x2, waiting for transfers between devices, exchange(): lax.ppermute(all_parts, 'tile', [(i, i ^ 8) for i in range(N_TILE)])  15.2 us
    pallas_call x1, Pallas kernels, second_solve(): pl.pallas_call(second_kernel, out_shape=(big, big) + EDGES, in_specs=[SME...  13.9 us
    pallas_call x1, Pallas kernels, last_step(): pl.pallas_call(last_kernel, out_shape=f32(PLANES * ROWS, COLS), in_specs=...  13.3 us
    ppermute x2, starting transfers between devices, exchange(): across = lax.ppermute(across, 'sub', [(0, N_SUB - 1), (N_SUB - 1, 0)])  12.7 us
    ppermute x6, waiting for transfers between devices, exchange(): lax.ppermute(all_parts, 'tile', turn(k))  10.9 us
    pallas_call x2, Pallas kernels, forcing(): pl.pallas_call(functools.partial(forcing_kernel, moment), out_shape=f32(P...  10.8 us
  transfers between devices with their start and end apart: 18, of which 10 were waited for; matrix products, arithmetic and copies ran while one was open for 0% of the time, Pallas kernels for 4%

commit v1 on v0

--- a/solution.py
+++ b/solution.py
@@ -36,24 +36,42 @@
     return jax.ShapeDtypeStruct(shape, jnp.float32)
 
 
-def pack_kernel(ids, owner, seam, face, cell, time, misfit, out, meta):
-    tile = ids[0]
-    sub = ids[1]
+def pack_kernel(owner_in, seam_in, face_in, cell_in, time_in, misfit_in, out, meta, owner, seam,
+                face, cell, time, misfit, sems):
+    copies = [
+        pltpu.make_async_copy(source, target, sems.at[i])
+        for i, (source, target) in enumerate(
+            (
+                (owner_in, owner),
+                (seam_in, seam),
+                (face_in, face),
+                (cell_in, cell),
+                (time_in, time),
+                (misfit_in, misfit),
+            )
+        )
+    ]
+    for copy in copies:
+        copy.start()
+    for copy in copies:
+        copy.wait()
+    tile = lax.axis_index("tile")
+    sub = lax.axis_index("sub")
     my_face = jnp.int32(0)
     for f in range(FACES):
         my_face = my_face + jnp.where(owner[f] == tile, f, 0)
     meta[12] = tile
     meta[13] = sub
     for edge in range(4):
-        other = owner[seam[my_face, edge, 0]]
+        other = owner[seam[0, edge, my_face]]
         away = (
             ((other & 1) ^ (tile & 1)) * 8
             + (((other >> 3) & 1) ^ ((tile >> 3) & 1)) * 4
             + ((((tile >> 1) & 3) + 4 - ((other >> 1) & 3)) & 3)
         )
         meta[3 * edge] = away
-        meta[3 * edge + 1] = seam[my_face, edge, 1]
-        meta[3 * edge + 2] = seam[my_face, edge, 2]
+        meta[3 * edge + 1] = seam[1, edge, my_face]
+        meta[3 * edge + 2] = seam[2, edge, my_face]
 
     rows = face.shape[1]
     faces = face[...]
@@ -94,15 +112,26 @@
     out[:, 1, :] = total[:, DEVICES:] - 1.0
 
 
-def pack(ids, owner, seam, face, cell, time, misfit):
+def pack(owner, seam, face, cell, time, misfit):
+    rows = face.shape[1]
+    line = pltpu.VMEM((1, rows), jnp.int32)
     return pl.pallas_call(
         pack_kernel,
         out_shape=(f32(DEVICES, 2, DEVICES), jax.ShapeDtypeStruct((META,), jnp.int32)),
-        in_specs=[SMEM, SMEM, SMEM, VMEM, VMEM, VMEM, VMEM],
+        in_specs=[pl.BlockSpec(memory_space=pltpu.HBM)] * 6,
         out_specs=(VMEM, SMEM),
-        compiler_params=params(32),
+        scratch_shapes=[
+            pltpu.SMEM(owner.shape, jnp.int32),
+            pltpu.SMEM(seam.shape, jnp.int32),
+            line,
+            line,
+            line,
+            pltpu.VMEM(misfit.shape, jnp.float32),
+            pltpu.SemaphoreType.DMA((6,)),
+        ],
+        compiler_params=params(8),
         name="pack",
-    )(ids, owner, seam, face, cell, time, misfit)
+    )(owner, seam, face, cell, time, misfit)
 
 
 def forcing_kernel(moment, slots, out, parts, place):
@@ -155,7 +184,7 @@
             pltpu.VMEM((3, PLANES, CAP * DEVICES), jnp.float32),
             pltpu.VMEM((CAP * DEVICES, COLS), jnp.bfloat16),
         ],
-        compiler_params=params(32),
+        compiler_params=params(8),
         cost_estimate=pl.CostEstimate(flops=3221225472, bytes_accessed=4325376, transcendentals=0),
         name=f"forcing_{moment}",
     )(slots)
@@ -166,6 +195,16 @@
 
 def tile_rows(quarter, plane, block):
     return pl.ds(pl.multiple_of(quarter * QUARTER + plane * ROWS + block * 8, 8), 8)
+
+
+PITCH = ROWS + 16
+
+
+def wide_rows(quarter, plane, block, shift=0):
+    start = (quarter * PLANES + plane) * PITCH + 8
+    if shift:
+        return pl.ds(start + shift + block * 8, 8)
+    return pl.ds(pl.multiple_of(start + block * 8, 8), 8)
 
 
 def eliminate(value, coupling, depth, at):
@@ -213,7 +252,7 @@
             found = result[tracer][k]
             heavy = weight * found
             solved[tile_rows(quarter, plane, block), :] = found
-            weighted[tile_rows(quarter, plane, block), :] = heavy
+            weighted[wide_rows(quarter, plane, block), :] = heavy
             if quarter == 0:
                 moved = heavy if plane == 0 else pltpu.roll(heavy, plane, 1)
                 column = jnp.where(lane == plane, moved, column)
@@ -229,13 +268,14 @@
     sub = meta[13]
     payload[0] = jnp.transpose(sides[...])[:PLANES, :]
     for b in range(4):
-        top = weighted[pl.ds(b * PLANES * ROWS, PLANES, stride=ROWS), :]
-        bottom = weighted[pl.ds(b * PLANES * ROWS + ROWS - 1, PLANES, stride=ROWS), :]
+        top = weighted[pl.ds(b * PLANES * PITCH + 8, PLANES, stride=PITCH), :]
+        bottom = weighted[pl.ds(b * PLANES * PITCH + ROWS + 7, PLANES, stride=PITCH), :]
         payload[1 + b] = jnp.where(sub == N_SUB - 1, bottom, top)
         first_row[b] = top
         last_row[b] = bottom
 
 
+BIG = (f32(4 * QUARTER, 128), f32(4 * PLANES * PITCH, 128))
 EDGES = (f32(5, PLANES, 128), f32(4, PLANES, 128), f32(4, PLANES, 128))
 
 
@@ -257,14 +297,13 @@
 
 
 def first_solve(meta, adjoint, force, coupling, scale, depth):
-    big = f32(4 * QUARTER, 128)
     return pl.pallas_call(
         first_kernel,
-        out_shape=(big, big) + EDGES,
+        out_shape=BIG + EDGES,
         in_specs=[SMEM] + [VMEM] * 5,
         out_specs=(VMEM,) * 5,
         scratch_shapes=[pltpu.VMEM((128, 128), jnp.float32)],
-        compiler_params=params(32),
+        compiler_params=params(8),
         cost_estimate=pl.CostEstimate(flops=30000000, bytes_accessed=20000000, transcendentals=0),
         name="first_solve",
     )(meta, adjoint, force, coupling, scale, depth)
@@ -304,13 +343,13 @@
         out_shape=(f32(N_SUB, 2, PLANES, 128), f32(4, PLANES, 128), f32(4, PLANES, 128)),
         in_specs=[SMEM, VMEM],
         out_specs=(VMEM,) * 3,
-        compiler_params=params(16),
+        compiler_params=params(8),
         cost_estimate=pl.CostEstimate(flops=1000000, bytes_accessed=1000000, transcendentals=0),
         name="route",
     )(meta, gathered)
 
 
-def exchange(meta, payload, first_row, last_row):
+def exchange(meta, payload, first_row, last_row, beside=None):
     def turn(k):
         return [
             (y * 8 + z * 2 + c, y * 8 + ((z + k) % 4) * 2 + c)
@@ -323,21 +362,25 @@
     all_parts = jnp.concatenate(
         [all_parts] + [lax.ppermute(all_parts, "tile", turn(k)) for k in (1, 2, 3)], axis=0
     )
+    all_parts, first_row, last_row = lax.optimization_barrier((all_parts, first_row, last_row))
+    extra = () if beside is None else (beside(),)
+    above = lax.ppermute(last_row, "sub", [(i, i + 1) for i in range(N_SUB - 1)])
+    below = lax.ppermute(first_row, "sub", [(i + 1, i) for i in range(N_SUB - 1)])
     all_parts = jnp.concatenate(
         [all_parts, lax.ppermute(all_parts, "tile", [(i, i ^ 8) for i in range(N_TILE)])], axis=0
     )
+    all_parts, above, below, *extra = lax.optimization_barrier((all_parts, above, below, *extra))
     all_parts = jnp.concatenate(
         [all_parts, lax.ppermute(all_parts, "tile", [(i, i ^ 1) for i in range(N_TILE)])], axis=0
     )
-    above = lax.ppermute(last_row, "sub", [(i, i + 1) for i in range(N_SUB - 1)])
-    below = lax.ppermute(first_row, "sub", [(i + 1, i) for i in range(N_SUB - 1)])
     send, here, across = route(meta, all_parts)
+    across = lax.ppermute(across, "sub", [(0, N_SUB - 1), (N_SUB - 1, 0)])
+    send, across = lax.optimization_barrier((send, across))
     got = lax.all_to_all(send, "sub", split_axis=0, concat_axis=0, tiled=True)
-    across = lax.ppermute(across, "sub", [(0, N_SUB - 1), (N_SUB - 1, 0)])
-    return got, here, across, above, below
-
-
-def place_halo(meta, got, here, across, above, below, halo, strips):
+    return (got, here, across, above, below), extra
+
+
+def place_halo(meta, got, here, across, above, below, weighted, strips):
     sub = meta[13]
     lane = iota((PLANES, 128), 1)
 
@@ -367,46 +410,41 @@
     for b in range(4):
         ordered = jnp.where(turned == 1, row[3 - b], row[b])
         strip = jnp.dot(ordered, flip, precision=HIGHEST, preferred_element_type=jnp.float32)
-        at = b * PLANES * 16
-        halo[pl.ds(at + 7, PLANES, stride=16), :] = jnp.where(sub == 0, strip, above[b])
-        halo[pl.ds(at + 8, PLANES, stride=16), :] = jnp.where(sub == N_SUB - 1, strip, below[b])
-
-
-def stepped(solved, weighted, scale, depth_ref, halo, strips, block, quarter):
+        at = b * PLANES * PITCH
+        above_row = jnp.where(sub == 0, strip, above[b])
+        below_row = jnp.where(sub == N_SUB - 1, strip, below[b])
+        weighted[pl.ds(at + 7, PLANES, stride=PITCH), :] = above_row
+        weighted[pl.ds(at + ROWS + 8, PLANES, stride=PITCH), :] = below_row
+
+
+def stepped(solved, weighted, scale, depth_ref, strips, block, quarter):
     columns = slice(quarter * 128, (quarter + 1) * 128)
     lane = iota((8, 128), 1)
-    row = iota((8, 128), 0)
-
     here = pl.ds(pl.multiple_of(block * 8, 8), 8)
     depth = depth_ref[here, columns]
     west = strips[here, :]
     east = strips[pl.ds(pl.multiple_of(ROWS + block * 8, 8), 8), :]
-    before = jnp.maximum(block - 1, 0)
-    after = jnp.minimum(block + 1, ROWS // 8 - 1)
+    weights = {}
 
     def value(plane):
         level = plane % LEVELS
-        near = (quarter * PLANES + plane) * 16
-        center = weighted[tile_rows(quarter, plane, block), :]
-        up = jnp.where(block == 0, halo[near : near + 8, :],
-                       weighted[tile_rows(quarter, plane, before), :])
-        down = jnp.where(block == ROWS // 8 - 1, halo[near + 8 : near + 16, :],
-                         weighted[tile_rows(quarter, plane, after), :])
+        if level not in weights:
+            at = pl.ds(pl.multiple_of(level * ROWS + block * 8, 8), 8)
+            weights[level] = jnp.where(level < depth, scale[at, columns], 0.0) * explicit_rate
+        center = weighted[wide_rows(quarter, plane, block), :]
         if quarter == 0:
             left = pltpu.roll(west, 127 - plane, 1)
         else:
-            left = weighted[tile_rows(quarter - 1, plane, block), :]
+            left = weighted[wide_rows(quarter - 1, plane, block), :]
         if quarter == 3:
             right = east if plane == 0 else pltpu.roll(east, 128 - plane, 1)
         else:
-            right = weighted[tile_rows(quarter + 1, plane, block), :]
-        total = pltpu.roll(jnp.where(row == 7, up, center), 1, 0)
-        total = total + pltpu.roll(jnp.where(row == 0, down, center), 7, 0)
+            right = weighted[wide_rows(quarter + 1, plane, block), :]
+        total = weighted[wide_rows(quarter, plane, block, -1), :]
+        total = total + weighted[wide_rows(quarter, plane, block, 1), :]
         total = total + pltpu.roll(jnp.where(lane == 127, left, center), 1, 1)
         total = total + pltpu.roll(jnp.where(lane == 0, right, center), 127, 1)
-        at = pl.ds(pl.multiple_of(level * ROWS + block * 8, 8), 8)
-        weight = jnp.where(level < depth, scale[at, columns], 0.0)
-        return solved[tile_rows(quarter, plane, block), :] + explicit_rate * weight * (
+        return solved[tile_rows(quarter, plane, block), :] + weights[level] * (
             total - 4.0 * center
         )
 
@@ -414,14 +452,14 @@
 
 
 def second_kernel(meta, got, here, across, above, below, solved_in, weighted_in, force, coupling,
-                  scale, depth, solved, weighted, payload, first_row, last_row, sides, halo,
-                  strips):
-    place_halo(meta, got, here, across, above, below, halo, strips)
+                  scale, depth, solved, weighted, payload, first_row, last_row, weighted_late,
+                  sides, strips):
+    place_halo(meta, got, here, across, above, below, weighted_late, strips)
 
     def step(block, carry):
         for quarter in range(4):
             columns = slice(quarter * 128, (quarter + 1) * 128)
-            late = stepped(solved_in, weighted_in, scale, depth, halo, strips, block, quarter)
+            late = stepped(solved_in, weighted_late, scale, depth, strips, block, quarter)
 
             def value(plane):
                 at = (pl.ds(pl.multiple_of(plane * ROWS + block * 8, 8), 8), columns)
@@ -434,53 +472,62 @@
     send_edges(meta, weighted, sides, payload, first_row, last_row)
 
 
-HALO = [
-    pltpu.VMEM((4 * PLANES * 16, 128), jnp.float32),
-    pltpu.VMEM((128, 128), jnp.float32),
-]
-
-
 def second_solve(meta, halos, solved, weighted, force, coupling, scale, depth):
-    big = f32(4 * QUARTER, 128)
     return pl.pallas_call(
         second_kernel,
-        out_shape=(big, big) + EDGES,
+        out_shape=BIG + EDGES + BIG[1:],
         in_specs=[SMEM] + [VMEM] * 11,
-        out_specs=(VMEM,) * 5,
-        scratch_shapes=[pltpu.VMEM((128, 128), jnp.float32)] + HALO,
-        compiler_params=params(32),
+        out_specs=(VMEM,) * 6,
+        input_output_aliases={7: 5},
+        scratch_shapes=[pltpu.VMEM((128, 128), jnp.float32)] * 2,
+        compiler_params=params(8),
         cost_estimate=pl.CostEstimate(flops=50000000, bytes_accessed=30000000, transcendentals=0),
         name="second_solve",
     )(meta, *halos, solved, weighted, force, coupling, scale, depth)
 
 
-def last_kernel(meta, got, here, across, above, below, solved, weighted, scale, depth, out, halo,
-                strips):
-    place_halo(meta, got, here, across, above, below, halo, strips)
+def last_kernel(meta, got, here, across, above, below, solved, weighted_in, scale, depth, out,
+                weighted, strips, ready, sems):
+    place_halo(meta, got, here, across, above, below, weighted, strips)
+
+    def copy(block):
+        return pltpu.make_async_copy(
+            ready.at[block],
+            out.at[:, pl.ds(pl.multiple_of(block * 8, 8), 8), :],
+            sems.at[block],
+        )
 
     def step(block, carry):
         for quarter in range(4):
             columns = slice(quarter * 128, (quarter + 1) * 128)
-            value = stepped(solved, weighted, scale, depth, halo, strips, block, quarter)
-            for plane in range(PLANES):
-                at = (pl.ds(pl.multiple_of(plane * ROWS + block * 8, 8), 8), columns)
-                out[at] = value(plane)
+            value = stepped(solved, weighted, scale, depth, strips, block, quarter)
+            for level in range(LEVELS):
+                for plane in (level, LEVELS + level):
+                    ready[block, plane, :, columns] = value(plane)
+        copy(block).start()
         return carry
 
     lax.fori_loop(0, ROWS // 8, step, 0)
+    for block in range(ROWS // 8):
+        copy(block).wait()
 
 
 def last_step(meta, halos, solved, weighted, scale, depth):
     return pl.pallas_call(
         last_kernel,
-        out_shape=f32(PLANES * ROWS, COLS),
+        out_shape=(f32(PLANES, ROWS, COLS), BIG[1]),
         in_specs=[SMEM] + [VMEM] * 9,
-        out_specs=VMEM,
-        scratch_shapes=HALO,
-        compiler_params=params(32),
+        out_specs=(pl.BlockSpec(memory_space=pl.ANY), VMEM),
+        input_output_aliases={7: 1},
+        scratch_shapes=[
+            pltpu.VMEM((128, 128), jnp.float32),
+            pltpu.VMEM((ROWS // 8, PLANES, 8, COLS), jnp.float32),
+            pltpu.SemaphoreType.DMA((ROWS // 8,)),
+        ],
+        compiler_params=params(8),
         cost_estimate=pl.CostEstimate(flops=20000000, bytes_accessed=20000000, transcendentals=0),
         name="last_step",
-    )(meta, *halos, solved, weighted, scale, depth)
+    )(meta, *halos, solved, weighted, scale, depth)[0]
 
 
 def body(
@@ -495,12 +542,10 @@
     prof_time,
     misfit,
 ):
-    ids = jnp.stack([lax.axis_index("tile"), lax.axis_index("sub")]).astype(jnp.int32)
     rows = prof_face.shape[0]
     slots, meta = pack(
-        ids,
         tile_owner,
-        seam_table,
+        jnp.transpose(seam_table, (2, 1, 0)),
         prof_face.reshape(1, rows),
         prof_cell.reshape(1, rows),
         prof_time.reshape(1, rows),
@@ -512,12 +557,11 @@
     coupling = vert_coupling.reshape((LEVELS - 1) * ROWS, COLS)
     late = forcing(slots, 1)
     solved, weighted, *edges = first_solve(meta, adjoint, late, coupling, scale, column_depth)
-    early = forcing(slots, 0)
-    halos = exchange(meta, *edges)
-    solved, weighted, *edges = second_solve(
+    halos, (early,) = exchange(meta, *edges, lambda: forcing(slots, 0))
+    solved, weighted, *edges, _ = second_solve(
         meta, halos, solved, weighted, early, coupling, scale, column_depth
     )
-    halos = exchange(meta, *edges)
+    halos, _ = exchange(meta, *edges)
     out = last_step(meta, halos, solved, weighted, scale, column_depth)
     return out.reshape(adjoint_final.shape)
 

time: 164 us -> 144 us (0.88)
  local copies, waits for them, and re-layouts: 24.8 us -> 4.15 us
  blocking collectives: 20.6 us -> 39.9 us
  starting transfers between devices: 40 us -> 21.4 us
  waiting for transfers between devices: 30.4 us -> 36.7 us
  Pallas kernels: 46.5 us -> 40.9 us
    unnamed x47 -> x20, local copies, waits for them, and re-layouts: 24.6 us -> 4.15 us
    all_to_all x0 -> x2, blocking collectives: none -> 19.4 us  [exchange(): got = lax.all_to_all(send, 'sub', split_axis=0, concat_axis=0, tiled=True)]
    ppermute x2, waiting for transfers between devices: 15.2 us -> 2.7 us  [exchange(): lax.ppermute(all_parts, 'tile', [(i, i ^ 8) for i in range(N_TILE)])]
    ppermute x2, waiting for transfers between devices: 2.21 us -> 12.5 us  [exchange(): across = lax.ppermute(across, 'sub', [(0, N_SUB - 1), (N_SUB - 1, 0)])]
    all_to_all x2 -> x0, starting transfers between devices: 9.22 us -> none  [exchange(): got = lax.all_to_all(send, 'sub', split_axis=0, concat_axis=0, tiled=True)]
    ppermute x2, starting transfers between devices: 12.7 us -> 4.07 us  [exchange(): across = lax.ppermute(across, 'sub', [(0, N_SUB - 1), (N_SUB - 1, 0)])]
    ppermute x2, waiting for transfers between devices: 0.01 us -> 6.38 us  [exchange(): lax.ppermute(first_row, 'sub', [(i + 1, i) for i in range(N_SUB - 1)])]
    pallas_call x3, Pallas kernels: 31 us -> 27.3 us  [the longest x1 12.8 us: last_step(): pl.pallas_call(last_kernel, out_shape=(f32(PLANES, ROWS, COLS), BIG[1]),...]
  transfers between devices with their start and end apart: 18 -> 16, of which waited for: 10 -> 14; matrix products, arithmetic and copies ran while one was open for 0% -> 0% of each run, Pallas kernels for 4% -> 4%
where the time goes in v1:
time: 144 us
  Pallas kernels  40.9 us (28%)
  blocking collectives  39.9 us (28%)
  waiting for transfers between devices  36.7 us (25%)
  starting transfers between devices  21.4 us (15%)
  local copies, waits for them, and re-layouts  4.15 us (3%)
    all_to_all x1, blocking collectives, body(): lax.all_to_all(slots, ('tile', 'sub'), split_axis=0, concat_axis=0, tiled...  20.6 us
    all_to_all x2, blocking collectives, exchange(): got = lax.all_to_all(send, 'sub', split_axis=0, concat_axis=0, tiled=True)  19.4 us
    pallas_call x1, Pallas kernels, last_step(): pl.pallas_call(last_kernel, out_shape=(f32(PLANES, ROWS, COLS), BIG[1]),...  12.8 us
    ppermute x2, waiting for transfers between devices, exchange(): across = lax.ppermute(across, 'sub', [(0, N_SUB - 1), (N_SUB - 1, 0)])  12.5 us
    pallas_call x1, Pallas kernels, second_solve(): pl.pallas_call(second_kernel, out_shape=BIG + EDGES + BIG[1:], in_specs=[...  11.1 us
    pallas_call x2, Pallas kernels, forcing(): pl.pallas_call(functools.partial(forcing_kernel, moment), out_shape=f32(P...  10.7 us
    ppermute x6, waiting for transfers between devices, exchange(): lax.ppermute(all_parts, 'tile', turn(k))  10.5 us
    ppermute x2, waiting for transfers between devices, exchange(): lax.ppermute(first_row, 'sub', [(i + 1, i) for i in range(N_SUB - 1)])  6.38 us
  transfers between devices with their start and end apart: 16, of which 14 were waited for; matrix products, arithmetic and copies ran while one was open for 0% of the time, Pallas kernels for 4%

profile of v1, /device:TPU:0, one launch (start us, length us, event | category | flops | bytes accessed | tf_op | source)
XLA Modules:
  0.0 143.6 jit_solution(13848421923112592049)
XLA Ops:
  0.0 0.8 copy-done.4
  0.8 0.7 copy-done.5
  1.5 0.7 copy-done.6
  2.1 0.7 copy-done.7
  2.8 0.7 copy-done.8
  3.5 0.7 copy-done.9
  4.1 1.5 %pack.1 = (f32[128,2,128]{2,1,0:T(2,128)S(1)}, s32[16]{0:T(128)S(1)}) custom-call(s32[16]{0:T(128)S(1)} %copy-done.9, s32[3,4,16]{2,1,0:T(4,128)S(1)} %bitcast.26, s32[1,256]{1,0:T(1,128)S(1)} %bitcast.27, s32[1,256]{1,0:T(1,128)S(1)} %bitcast.28, s32[1,256]{1,0:T(1,128)S(1)} %bitcast.29, f32[32,256]{1,0:T(8,128)S(1)} %bitcast.25), custom_call_target="tpu_custom_call" | custom-call | tf_op jit(solution)/shard_map/pack/pallas_call | solution.py:118
  5.6 20.6 %all_to_all.15.slots = f32[128,2,128]{2,1,0:T(2,128)S(1)} all-to-all(f32[128,2,128]{2,1,0:T(2,128)S(1)} %get-tuple-element.42), channel_id=1, replica_groups=mesh['tile'=16,'sub'=8] {'tile','sub'}, dimensions={0} | all-to-all | bytes 262144 | tf_op jit(solution)/shard_map/all_to_all | solution.py:554
  26.2 5.4 %forcing_1.1.force = f32[2048,512]{1,0:T(8,128)S(1)} custom-call(f32[128,2,128]{2,1,0:T(2,128)S(1)} %all_to_all.15.slots), custom_call_target="tpu_custom_call" | custom-call | flops 3221225472 | bytes 4325376 | tf_op jit(solution)/shard_map/forcing_1/pallas_call | solution.py:178
  31.6 3.4 %first_solve.1 = (f32[8192,128]{1,0:T(8,128)S(1)}, f32[10240,128]{1,0:T(8,128)S(1)}, f32[5,32,128]{2,1,0:T(8,128)S(1)}, f32[4,32,128]{2,1,0:T(8,128)S(1)}, f32[4,32,128]{2,1,0:T(8,128)S(1)}) custom-call(s32[16]{0:T(128)S(1)} %get-tuple-element.41.meta, f32[2048,512]{1,0:T(8,128)S(1)} %bitcast.16, f32[2048,512]{1,0:T(8,128)S(1)} %forcing_1.1.force, ...), custom_call_target="tpu_custom_call" | custom-call | flops 30000000 | bytes 20000000 | tf_op jit(solution)/shard_map/first_solve/pallas_call | solution.py:300
  35.0 0.7 collective-permute-start.2
  35.7 2.2 %collective-permute-start.1 = (f32[1,5,32,128]{3,2,1,0:T(8,128)S(1)}, f32[1,5,32,128]{3,2,1,0:T(8,128)S(1)}, u32[]{:S(2)}, u32[]{:S(2)}) collective-permute-start(f32[1,5,32,128]{3,2,1,0:T(8,128)S(1)} %bitcast.22), channel_id=1, source_target_pairs={{0,32},{8,40},{16,48},{24,56},{32,0},{40,8},{48,16},{56,24},{64,96... | collective-permute-start | bytes 245768 | tf_op jit(solution)/shard_map/ppermute | solution.py:363
  38.0 0.0 collective-permute-start
  38.0 2.0 %collective-permute-done.2 = f32[1,5,32,128]{3,2,1,0:T(8,128)S(1)} collective-permute-done((f32[1,5,32,128]{3,2,1,0:T(8,128)S(1)}, f32[1,5,32,128]{3,2,1,0:T(8,128)S(1)}, u32[]{:S(2)}, u32[]{:S(2)}) %collective-permute-start.2) | collective-permute-done | bytes 81952 | tf_op jit(solution)/shard_map/ppermute | solution.py:363
  40.0 2.3 %collective-permute-done.1 = f32[1,5,32,128]{3,2,1,0:T(8,128)S(1)} collective-permute-done((f32[1,5,32,128]{3,2,1,0:T(8,128)S(1)}, f32[1,5,32,128]{3,2,1,0:T(8,128)S(1)}, u32[]{:S(2)}, u32[]{:S(2)}) %collective-permute-start.1) | collective-permute-done | bytes 81952 | tf_op jit(solution)/shard_map/ppermute | solution.py:363
  42.4 1.2 collective-permute-done
  43.6 1.3 collective-permute-start.3
  45.0 5.4 %forcing_0.1.force = f32[2048,512]{1,0:T(8,128)S(1)} custom-call(f32[128,2,128]{2,1,0:T(2,128)S(1)} %all_to_all.15.slots), custom_call_target="tpu_custom_call" | custom-call | flops 3221225472 | bytes 4325376 | tf_op jit(solution)/shard_map/forcing_0/pallas_call | solution.py:178
  50.3 2.5 %collective-permute-start.4 = (f32[4,32,128]{2,1,0:T(8,128)S(1)}, f32[4,32,128]{2,1,0:T(8,128)S(1)}, u32[]{:S(2)}, u32[]{:S(2)}) collective-permute-start(f32[4,32,128]{2,1,0:T(8,128)S(1)} %get-tuple-element.47), channel_id=1, source_target_pairs={{0,1},{1,2},{2,3},{3,4},{4,5},{5,6},{6,7},{8,9},{9,10},{10,11},{11... | collective-permute-start | bytes 196616 | tf_op jit(solution)/shard_map/ppermute | solution.py:367
  52.8 1.3 collective-permute-start.5
  54.1 0.0 collective-permute-done.3
  54.2 0.5 collective-permute-done.4.above
  54.7 4.3 %collective-permute-done.5.below = f32[4,32,128]{2,1,0:T(8,128)S(1)} collective-permute-done((f32[4,32,128]{2,1,0:T(8,128)S(1)}, f32[4,32,128]{2,1,0:T(8,128)S(1)}, u32[]{:S(2)}, u32[]{:S(2)}) %collective-permute-start.5) | collective-permute-done | bytes 65568 | tf_op jit(solution)/shard_map/ppermute | solution.py:368
  59.0 2.1 %collective-permute-done.6 = f32[8,5,32,128]{3,2,1,0:T(8,128)S(1)} collective-permute-done((f32[8,5,32,128]{3,2,1,0:T(8,128)S(1)}, f32[8,5,32,128]{3,2,1,0:T(8,128)S(1)}, u32[]{:S(2)}, u32[]{:S(2)}) %collective-permute-start.6) | collective-permute-done | bytes 655392 | tf_op jit(solution)/shard_map/ppermute | solution.py:374
  61.1 0.1 pad_maximum_fusion.gathered
  61.2 0.7 route.2
  61.9 2.1 %collective-permute-start.7 = (f32[4,32,128]{2,1,0:T(8,128)S(1)}, f32[4,32,128]{2,1,0:T(8,128)S(1)}, u32[]{:S(2)}, u32[]{:S(2)}) collective-permute-start(f32[4,32,128]{2,1,0:T(8,128)S(1)} %get-tuple-element.51), channel_id=1, source_target_pairs={{0,7},{7,0},{8,15},{15,8},{16,23},{23,16},{24,31},{31,24},{32,39},... | collective-permute-start | bytes 196616 | tf_op jit(solution)/shard_map/ppermute | solution.py:377
  64.0 6.1 %collective-permute-done.7.across = f32[4,32,128]{2,1,0:T(8,128)S(1)} collective-permute-done((f32[4,32,128]{2,1,0:T(8,128)S(1)}, f32[4,32,128]{2,1,0:T(8,128)S(1)}, u32[]{:S(2)}, u32[]{:S(2)}) %collective-permute-start.7) | collective-permute-done | bytes 65568 | tf_op jit(solution)/shard_map/ppermute | solution.py:377
  70.2 9.7 %all_to_all.16.got = f32[8,2,32,128]{3,2,1,0:T(8,128)S(1)} all-to-all(f32[8,2,32,128]{3,2,1,0:T(8,128)S(1)} %get-tuple-element.52), channel_id=1, replica_groups=mesh['tile'=16,'sub'=8] {'sub'}, dimensions={0} | all-to-all | bytes 524288 | tf_op jit(solution)/shard_map/all_to_all | solution.py:379
  79.8 11.1 %second_solve.1 = (f32[8192,128]{1,0:T(8,128)S(1)}, f32[10240,128]{1,0:T(8,128)S(1)}, f32[5,32,128]{2,1,0:T(8,128)S(1)}, f32[4,32,128]{2,1,0:T(8,128)S(1)}, f32[...) custom-call(s32[16]{0:T(128)S(1)} %get-tuple-element.41.meta, ...), custom_call_target="tpu_custom_call", output_to_operand_aliasing={{5}: (7, {})} | custom-call | flops 50000000 | bytes 30000000 | tf_op jit(solution)/shard_map/second_solve/pallas_call | solution.py:476
  91.0 0.6 collective-permute-start.10
  91.6 1.1 collective-permute-start.9
  92.8 0.8 collective-permute-start.8
  93.6 1.9 %collective-permute-done.10 = f32[1,5,32,128]{3,2,1,0:T(8,128)S(1)} collective-permute-done((f32[1,5,32,128]{3,2,1,0:T(8,128)S(1)}, f32[1,5,32,128]{3,2,1,0:T(8,128)S(1)}, u32[]{:S(2)}, u32[]{:S(2)}) %collective-permute-start.10) | collective-permute-done | bytes 81952 | tf_op jit(solution)/shard_map/ppermute | solution.py:363
  95.5 2.1 %collective-permute-done.9 = f32[1,5,32,128]{3,2,1,0:T(8,128)S(1)} collective-permute-done((f32[1,5,32,128]{3,2,1,0:T(8,128)S(1)}, f32[1,5,32,128]{3,2,1,0:T(8,128)S(1)}, u32[]{:S(2)}, u32[]{:S(2)}) %collective-permute-start.9) | collective-permute-done | bytes 81952 | tf_op jit(solution)/shard_map/ppermute | solution.py:363
  97.6 0.9 collective-permute-done.8
  98.5 2.6 %collective-permute-start.11 = (f32[4,5,32,128]{3,2,1,0:T(8,128)S(1)}, f32[4,5,32,128]{3,2,1,0:T(8,128)S(1)}, u32[]{:S(2)}, u32[]{:S(2)}) collective-permute-start(f32[4,5,32,128]{3,2,1,0:T(8,128)S(1)} %pad_maximum_fusion.5), channel_id=1, source_target_pairs={{0,64},{8,72},{16,80},{24,88},{32,96},{40,104},{48,112},{56,120},{... | collective-permute-start | bytes 983048 | tf_op jit(solution)/shard_map/ppermute | solution.py:370
  101.1 2.8 %collective-permute-start.12 = (f32[4,32,128]{2,1,0:T(8,128)S(1)}, f32[4,32,128]{2,1,0:T(8,128)S(1)}, u32[]{:S(2)}, u32[]{:S(2)}) collective-permute-start(f32[4,32,128]{2,1,0:T(8,128)S(1)} %get-tuple-element.64), channel_id=1, source_target_pairs={{0,1},{1,2},{2,3},{3,4},{4,5},{5,6},{6,7},{8,9},{9,10},{10,11},{11... | collective-permute-start | bytes 196616 | tf_op jit(solution)/shard_map/ppermute | solution.py:367
  103.8 1.3 collective-permute-start.13
  105.1 2.7 %collective-permute-done.11 = f32[4,5,32,128]{3,2,1,0:T(8,128)S(1)} collective-permute-done((f32[4,5,32,128]{3,2,1,0:T(8,128)S(1)}, f32[4,5,32,128]{3,2,1,0:T(8,128)S(1)}, u32[]{:S(2)}, u32[]{:S(2)}) %collective-permute-start.11) | collective-permute-done | bytes 327712 | tf_op jit(solution)/shard_map/ppermute | solution.py:370
  107.9 2.1 %collective-permute-done.13.below = f32[4,32,128]{2,1,0:T(8,128)S(1)} collective-permute-done((f32[4,32,128]{2,1,0:T(8,128)S(1)}, f32[4,32,128]{2,1,0:T(8,128)S(1)}, u32[]{:S(2)}, u32[]{:S(2)}) %collective-permute-start.13) | collective-permute-done | bytes 65568 | tf_op jit(solution)/shard_map/ppermute | solution.py:368
  110.0 2.1 %collective-permute-done.14 = f32[8,5,32,128]{3,2,1,0:T(8,128)S(1)} collective-permute-done((f32[8,5,32,128]{3,2,1,0:T(8,128)S(1)}, f32[8,5,32,128]{3,2,1,0:T(8,128)S(1)}, u32[]{:S(2)}, u32[]{:S(2)}) %collective-permute-start.14) | collective-permute-done | bytes 655392 | tf_op jit(solution)/shard_map/ppermute | solution.py:374
  112.1 0.1 pad_maximum_fusion.1.gathered
  112.2 0.7 route.3
  112.9 1.9 %collective-permute-start.15 = (f32[4,32,128]{2,1,0:T(8,128)S(1)}, f32[4,32,128]{2,1,0:T(8,128)S(1)}, u32[]{:S(2)}, u32[]{:S(2)}) collective-permute-start(f32[4,32,128]{2,1,0:T(8,128)S(1)} %get-tuple-element.68), channel_id=1, source_target_pairs={{0,7},{7,0},{8,15},{15,8},{16,23},{23,16},{24,31},{31,24},{32,39},... | collective-permute-start | bytes 196616 | tf_op jit(solution)/shard_map/ppermute | solution.py:377
  114.8 6.3 %collective-permute-done.15.across = f32[4,32,128]{2,1,0:T(8,128)S(1)} collective-permute-done((f32[4,32,128]{2,1,0:T(8,128)S(1)}, f32[4,32,128]{2,1,0:T(8,128)S(1)}, u32[]{:S(2)}, u32[]{:S(2)}) %collective-permute-start.15) | collective-permute-done | bytes 65568 | tf_op jit(solution)/shard_map/ppermute | solution.py:377
  121.1 9.7 %all_to_all.17.got = f32[8,2,32,128]{3,2,1,0:T(8,128)S(1)} all-to-all(f32[8,2,32,128]{3,2,1,0:T(8,128)S(1)} %get-tuple-element.69), channel_id=1, replica_groups=mesh['tile'=16,'sub'=8] {'sub'}, dimensions={0} | all-to-all | bytes 524288 | tf_op jit(solution)/shard_map/all_to_all | solution.py:379
  130.8 12.8 %last_step.1 = (f32[32,64,512]{2,1,0:T(8,128)}, f32[10240,128]{1,0:T(8,128)S(1)}) custom-call(s32[16]{0:T(128)S(1)} %get-tuple-element.41.meta, f32[8,2,32,128]{3,2,1,0:T(8,128)S(1)} %all_to_all.17.got, f32[4,32,128]{2,1,0:T(8,128)S(1)} %get-tuple-element.70.here, f32[4,32,128]{2,1,0:T(8,128)S(1)} %collective-permute-done.15.across, ...), custom_call_target="tpu_custom_call", output_to_operand_aliasing={{1}: (7, {})} | custom-call | flops 20000000 | bytes 20000000 | tf_op jit(solution)/shard_map/last_step/pallas_call | solution.py:516
  (21 shorter events, 0.2 us)
Async XLA Ops:
  0.0 0.8 copy-start.4
  0.8 0.7 copy-start.5
  1.5 0.7 copy-start.6
  2.1 0.7 copy-start.7
  2.8 0.7 copy-start.8
  3.5 0.7 copy-start.9
  26.2 5.4 %copy-start = (f32[16,64,512]{2,1,0:T(8,128)S(1)}, f32[16,64,512]{2,1,0:T(8,128)}, u32[]{:S(2)}) copy-start(f32[16,64,512]{2,1,0:T(8,128)} %param.11) | copy-start | bytes 6291460
  26.2 5.4 %copy-start.1 = (f32[15,64,512]{2,1,0:T(8,128)S(1)}, f32[15,64,512]{2,1,0:T(8,128)}, u32[]{:S(2)}) copy-start(f32[15,64,512]{2,1,0:T(8,128)} %param.12) | copy-start | bytes 5898244
  26.2 5.4 %copy-start.2 = (f32[2,16,64,512]{3,2,1,0:T(8,128)S(1)}, f32[2,16,64,512]{3,2,1,0:T(8,128)}, u32[]{:S(2)}) copy-start(f32[2,16,64,512]{3,2,1,0:T(8,128)} %param.10) | copy-start | bytes 12582916
  26.2 5.4 %copy-start.3 = (s32[64,512]{1,0:T(8,128)S(1)}, s32[64,512]{1,0:T(8,128)}, u32[]{:S(2)}) copy-start(s32[64,512]{1,0:T(8,128)} %depth.5) | copy-start | bytes 393220
  35.0 5.0 %collective-permute-start.2 = (f32[1,5,32,128]{3,2,1,0:T(8,128)S(1)}, f32[1,5,32,128]{3,2,1,0:T(8,128)S(1)}, u32[]{:S(2)}, u32[]{:S(2)}) collective-permute-start(f32[1,5,32,128]{3,2,1,0:T(8,128)S(1)} %bitcast.21), channel_id=1, source_target_pairs={{0,48},{8,56},{16,0},{24,8},{32,16},{40,24},{48,32},{56,40},{64,11... | collective-permute-start | bytes 245768 | tf_op jit(solution)/shard_map/ppermute | solution.py:363
  35.7 6.6 %collective-permute-start.1 = (f32[1,5,32,128]{3,2,1,0:T(8,128)S(1)}, f32[1,5,32,128]{3,2,1,0:T(8,128)S(1)}, u32[]{:S(2)}, u32[]{:S(2)}) collective-permute-start(f32[1,5,32,128]{3,2,1,0:T(8,128)S(1)} %bitcast.22), channel_id=1, source_target_pairs={{0,32},{8,40},{16,48},{24,56},{32,0},{40,8},{48,16},{56,24},{64,96... | collective-permute-start | bytes 245768 | tf_op jit(solution)/shard_map/ppermute | solution.py:363
  38.0 5.7 %collective-permute-start = (f32[1,5,32,128]{3,2,1,0:T(8,128)S(1)}, f32[1,5,32,128]{3,2,1,0:T(8,128)S(1)}, u32[]{:S(2)}, u32[]{:S(2)}) collective-permute-start(f32[1,5,32,128]{3,2,1,0:T(8,128)S(1)} %bitcast.23), channel_id=1, source_target_pairs={{0,16},{8,24},{16,32},{24,40},{32,48},{40,56},{48,0},{56,8},{64,80... | collective-permute-start | bytes 245768 | tf_op jit(solution)/shard_map/ppermute | solution.py:363
  43.6 10.5 %collective-permute-start.3 = (f32[4,5,32,128]{3,2,1,0:T(8,128)S(1)}, f32[4,5,32,128]{3,2,1,0:T(8,128)S(1)}, u32[]{:S(2)}, u32[]{:S(2)}) collective-permute-start(f32[4,5,32,128]{3,2,1,0:T(8,128)S(1)} %pad_maximum_fusion.4), channel_id=1, source_target_pairs={{0,64},{8,72},{16,80},{24,88},{32,96},{40,104},{48,112},{56,120},{... | collective-permute-start | bytes 983048 | tf_op jit(solution)/shard_map/ppermute | solution.py:370
  50.3 4.4 %collective-permute-start.4 = (f32[4,32,128]{2,1,0:T(8,128)S(1)}, f32[4,32,128]{2,1,0:T(8,128)S(1)}, u32[]{:S(2)}, u32[]{:S(2)}) collective-permute-start(f32[4,32,128]{2,1,0:T(8,128)S(1)} %get-tuple-element.47), channel_id=1, source_target_pairs={{0,1},{1,2},{2,3},{3,4},{4,5},{5,6},{6,7},{8,9},{9,10},{10,11},{11... | collective-permute-start | bytes 196616 | tf_op jit(solution)/shard_map/ppermute | solution.py:367
  52.8 6.2 %collective-permute-start.5 = (f32[4,32,128]{2,1,0:T(8,128)S(1)}, f32[4,32,128]{2,1,0:T(8,128)S(1)}, u32[]{:S(2)}, u32[]{:S(2)}) collective-permute-start(f32[4,32,128]{2,1,0:T(8,128)S(1)} %get-tuple-element.48), channel_id=1, source_target_pairs={{1,0},{2,1},{3,2},{4,3},{5,4},{6,5},{7,6},{9,8},{10,9},{11,10},{12... | collective-permute-start | bytes 196616 | tf_op jit(solution)/shard_map/ppermute | solution.py:368
  59.0 2.1 %collective-permute-start.6 = (f32[8,5,32,128]{3,2,1,0:T(8,128)S(1)}, f32[8,5,32,128]{3,2,1,0:T(8,128)S(1)}, u32[]{:S(2)}, u32[]{:S(2)}) collective-permute-start(f32[8,5,32,128]{3,2,1,0:T(8,128)S(1)} %pad_maximum_fusion.2), channel_id=1, source_target_pairs={{0,8},{8,0},{16,24},{24,16},{32,40},{40,32},{48,56},{56,48},{64,72... | collective-permute-start | bytes 1966088 | tf_op jit(solution)/shard_map/ppermute | solution.py:374
  61.9 8.3 %collective-permute-start.7 = (f32[4,32,128]{2,1,0:T(8,128)S(1)}, f32[4,32,128]{2,1,0:T(8,128)S(1)}, u32[]{:S(2)}, u32[]{:S(2)}) collective-permute-start(f32[4,32,128]{2,1,0:T(8,128)S(1)} %get-tuple-element.51), channel_id=1, source_target_pairs={{0,7},{7,0},{8,15},{15,8},{16,23},{23,16},{24,31},{31,24},{32,39},... | collective-permute-start | bytes 196616 | tf_op jit(solution)/shard_map/ppermute | solution.py:377
  91.0 4.5 %collective-permute-start.10 = (f32[1,5,32,128]{3,2,1,0:T(8,128)S(1)}, f32[1,5,32,128]{3,2,1,0:T(8,128)S(1)}, u32[]{:S(2)}, u32[]{:S(2)}) collective-permute-start(f32[1,5,32,128]{3,2,1,0:T(8,128)S(1)} %bitcast.17), channel_id=1, source_target_pairs={{0,48},{8,56},{16,0},{24,8},{32,16},{40,24},{48,32},{56,40},{64,11... | collective-permute-start | bytes 245768 | tf_op jit(solution)/shard_map/ppermute | solution.py:363
  91.6 5.9 %collective-permute-start.9 = (f32[1,5,32,128]{3,2,1,0:T(8,128)S(1)}, f32[1,5,32,128]{3,2,1,0:T(8,128)S(1)}, u32[]{:S(2)}, u32[]{:S(2)}) collective-permute-start(f32[1,5,32,128]{3,2,1,0:T(8,128)S(1)} %bitcast.18), channel_id=1, source_target_pairs={{0,32},{8,40},{16,48},{24,56},{32,0},{40,8},{48,16},{56,24},{64,96... | collective-permute-start | bytes 245768 | tf_op jit(solution)/shard_map/ppermute | solution.py:363
  92.8 5.7 %collective-permute-start.8 = (f32[1,5,32,128]{3,2,1,0:T(8,128)S(1)}, f32[1,5,32,128]{3,2,1,0:T(8,128)S(1)}, u32[]{:S(2)}, u32[]{:S(2)}) collective-permute-start(f32[1,5,32,128]{3,2,1,0:T(8,128)S(1)} %bitcast.19), channel_id=1, source_target_pairs={{0,16},{8,24},{16,32},{24,40},{32,48},{40,56},{48,0},{56,8},{64,80... | collective-permute-start | bytes 245768 | tf_op jit(solution)/shard_map/ppermute | solution.py:363
  98.5 9.4 %collective-permute-start.11 = (f32[4,5,32,128]{3,2,1,0:T(8,128)S(1)}, f32[4,5,32,128]{3,2,1,0:T(8,128)S(1)}, u32[]{:S(2)}, u32[]{:S(2)}) collective-permute-start(f32[4,5,32,128]{3,2,1,0:T(8,128)S(1)} %pad_maximum_fusion.5), channel_id=1, source_target_pairs={{0,64},{8,72},{16,80},{24,88},{32,96},{40,104},{48,112},{56,120},{... | collective-permute-start | bytes 983048 | tf_op jit(solution)/shard_map/ppermute | solution.py:370
  101.1 6.8 %collective-permute-start.12 = (f32[4,32,128]{2,1,0:T(8,128)S(1)}, f32[4,32,128]{2,1,0:T(8,128)S(1)}, u32[]{:S(2)}, u32[]{:S(2)}) collective-permute-start(f32[4,32,128]{2,1,0:T(8,128)S(1)} %get-tuple-element.64), channel_id=1, source_target_pairs={{0,1},{1,2},{2,3},{3,4},{4,5},{5,6},{6,7},{8,9},{9,10},{10,11},{11... | collective-permute-start | bytes 196616 | tf_op jit(solution)/shard_map/ppermute | solution.py:367
  103.8 6.2 %collective-permute-start.13 = (f32[4,32,128]{2,1,0:T(8,128)S(1)}, f32[4,32,128]{2,1,0:T(8,128)S(1)}, u32[]{:S(2)}, u32[]{:S(2)}) collective-permute-start(f32[4,32,128]{2,1,0:T(8,128)S(1)} %get-tuple-element.65), channel_id=1, source_target_pairs={{1,0},{2,1},{3,2},{4,3},{5,4},{6,5},{7,6},{9,8},{10,9},{11,10},{12... | collective-permute-start | bytes 196616 | tf_op jit(solution)/shard_map/ppermute | solution.py:368
  110.0 2.1 %collective-permute-start.14 = (f32[8,5,32,128]{3,2,1,0:T(8,128)S(1)}, f32[8,5,32,128]{3,2,1,0:T(8,128)S(1)}, u32[]{:S(2)}, u32[]{:S(2)}) collective-permute-start(f32[8,5,32,128]{3,2,1,0:T(8,128)S(1)} %pad_maximum_fusion.3), channel_id=1, source_target_pairs={{0,8},{8,0},{16,24},{24,16},{32,40},{40,32},{48,56},{56,48},{64,72... | collective-permute-start | bytes 1966088 | tf_op jit(solution)/shard_map/ppermute | solution.py:374
  112.9 8.3 %collective-permute-start.15 = (f32[4,32,128]{2,1,0:T(8,128)S(1)}, f32[4,32,128]{2,1,0:T(8,128)S(1)}, u32[]{:S(2)}, u32[]{:S(2)}) collective-permute-start(f32[4,32,128]{2,1,0:T(8,128)S(1)} %get-tuple-element.68), channel_id=1, source_target_pairs={{0,7},{7,0},{8,15},{15,8},{16,23},{23,16},{24,31},{31,24},{32,39},... | collective-permute-start | bytes 196616 | tf_op jit(solution)/shard_map/ppermute | solution.py:377

commit v2 on v1

--- a/solution.py
+++ b/solution.py
@@ -22,6 +22,7 @@
 VMEM = pl.BlockSpec(memory_space=pltpu.VMEM)
 SMEM = pl.BlockSpec(memory_space=pltpu.SMEM)
 META = 16
+PARTS = 2
 
 
 def iota(shape, axis):
@@ -36,52 +37,42 @@
     return jax.ShapeDtypeStruct(shape, jnp.float32)
 
 
-def pack_kernel(owner_in, seam_in, face_in, cell_in, time_in, misfit_in, out, meta, owner, seam,
-                face, cell, time, misfit, sems):
-    copies = [
-        pltpu.make_async_copy(source, target, sems.at[i])
-        for i, (source, target) in enumerate(
-            (
-                (owner_in, owner),
-                (seam_in, seam),
-                (face_in, face),
-                (cell_in, cell),
-                (time_in, time),
-                (misfit_in, misfit),
-            )
-        )
-    ]
-    for copy in copies:
-        copy.start()
-    for copy in copies:
-        copy.wait()
+def pack_kernel(seam_table, numbers, misfit, out, meta, small):
+    def owner(f):
+        return small[0, f]
+
+    def seam(part, edge, f):
+        return seam_table[part, edge, f]
+
+    pltpu.sync_copy(numbers.at[pl.ds(3, 1), :], small)
+
     tile = lax.axis_index("tile")
     sub = lax.axis_index("sub")
     my_face = jnp.int32(0)
     for f in range(FACES):
-        my_face = my_face + jnp.where(owner[f] == tile, f, 0)
+        my_face = my_face + jnp.where(owner(f) == tile, f, 0)
     meta[12] = tile
     meta[13] = sub
     for edge in range(4):
-        other = owner[seam[0, edge, my_face]]
+        other = owner(seam(0, edge, my_face))
         away = (
             ((other & 1) ^ (tile & 1)) * 8
             + (((other >> 3) & 1) ^ ((tile >> 3) & 1)) * 4
             + ((((tile >> 1) & 3) + 4 - ((other >> 1) & 3)) & 3)
         )
         meta[3 * edge] = away
-        meta[3 * edge + 1] = seam[1, edge, my_face]
-        meta[3 * edge + 2] = seam[2, edge, my_face]
-
-    rows = face.shape[1]
-    faces = face[...]
+        meta[3 * edge + 1] = seam(1, edge, my_face)
+        meta[3 * edge + 2] = seam(2, edge, my_face)
+
+    rows = numbers.shape[1]
+    faces = numbers[0:1, :]
     home = jnp.zeros_like(faces)
     for f in range(FACES):
-        home = jnp.where(faces == f, owner[f], home)
-    cells = cell[...]
+        home = jnp.where(faces == f, owner(f), home)
+    cells = numbers[1:2, :]
     tile_row = cells >> 9
     target = home * N_SUB + (tile_row >> 6)
-    code = (time[...] - 1) * CELLS + (tile_row & (ROWS - 1)) * COLS + (cells & (COLS - 1))
+    code = (numbers[2:3, :] - 1) * CELLS + (tile_row & (ROWS - 1)) * COLS + (cells & (COLS - 1))
     first = iota((rows, rows), 0)
     second = iota((rows, rows), 1)
     target_row = jnp.broadcast_to(target.astype(jnp.float32), (rows, rows))
@@ -112,26 +103,16 @@
     out[:, 1, :] = total[:, DEVICES:] - 1.0
 
 
-def pack(owner, seam, face, cell, time, misfit):
-    rows = face.shape[1]
-    line = pltpu.VMEM((1, rows), jnp.int32)
+def pack(seams, numbers, misfit):
     return pl.pallas_call(
         pack_kernel,
         out_shape=(f32(DEVICES, 2, DEVICES), jax.ShapeDtypeStruct((META,), jnp.int32)),
-        in_specs=[pl.BlockSpec(memory_space=pltpu.HBM)] * 6,
+        in_specs=[SMEM, VMEM, VMEM],
         out_specs=(VMEM, SMEM),
-        scratch_shapes=[
-            pltpu.SMEM(owner.shape, jnp.int32),
-            pltpu.SMEM(seam.shape, jnp.int32),
-            line,
-            line,
-            line,
-            pltpu.VMEM(misfit.shape, jnp.float32),
-            pltpu.SemaphoreType.DMA((6,)),
-        ],
+        scratch_shapes=[pltpu.SMEM((1, numbers.shape[1]), jnp.int32)],
         compiler_params=params(8),
         name="pack",
-    )(owner, seam, face, cell, time, misfit)
+    )(seams, numbers, misfit)
 
 
 def forcing_kernel(moment, slots, out, parts, place):
@@ -145,11 +126,8 @@
     on_row = iota((ROWS, CAP * DEVICES), 0) == row_of
     wide = jnp.concatenate([values[PLANES * k : PLANES * (k + 1), :] for k in range(CAP)], axis=1)
     high = wide.astype(jnp.bfloat16).astype(jnp.float32)
-    rest = wide - high
-    middle = rest.astype(jnp.bfloat16).astype(jnp.float32)
     parts[0] = high
-    parts[1] = middle
-    parts[2] = rest - middle
+    parts[1] = wide - high
     for k in range(CAP):
         col = tags[:, k : k + 1] & (COLS - 1)
         place[k * DEVICES : (k + 1) * DEVICES, :] = jnp.where(
@@ -159,7 +137,7 @@
 
     def step(g, carry):
         total = None
-        for part in range(3):
+        for part in range(PARTS):
             left = []
             for q in range(group):
                 row = parts[part, pl.ds(g * group + q, 1), :]
@@ -181,11 +159,11 @@
         in_specs=[VMEM],
         out_specs=VMEM,
         scratch_shapes=[
-            pltpu.VMEM((3, PLANES, CAP * DEVICES), jnp.float32),
+            pltpu.VMEM((PARTS, PLANES, CAP * DEVICES), jnp.float32),
             pltpu.VMEM((CAP * DEVICES, COLS), jnp.bfloat16),
         ],
         compiler_params=params(8),
-        cost_estimate=pl.CostEstimate(flops=3221225472, bytes_accessed=4325376, transcendentals=0),
+        cost_estimate=pl.CostEstimate(flops=2147483648, bytes_accessed=4325376, transcendentals=0),
         name=f"forcing_{moment}",
     )(slots)
 
@@ -432,18 +410,20 @@
             at = pl.ds(pl.multiple_of(level * ROWS + block * 8, 8), 8)
             weights[level] = jnp.where(level < depth, scale[at, columns], 0.0) * explicit_rate
         center = weighted[wide_rows(quarter, plane, block), :]
+        total = weighted[wide_rows(quarter, plane, block, -1), :]
+        total = total + weighted[wide_rows(quarter, plane, block, 1), :]
         if quarter == 0:
-            left = pltpu.roll(west, 127 - plane, 1)
+            edge = west if plane == 0 else pltpu.roll(west, 128 - plane, 1)
+            total = total + jnp.where(lane == 0, edge, pltpu.roll(center, 1, 1))
         else:
             left = weighted[wide_rows(quarter - 1, plane, block), :]
+            total = total + pltpu.roll(jnp.where(lane == 127, left, center), 1, 1)
         if quarter == 3:
-            right = east if plane == 0 else pltpu.roll(east, 128 - plane, 1)
+            edge = pltpu.roll(east, 127 - plane, 1)
+            total = total + jnp.where(lane == 127, edge, pltpu.roll(center, 127, 1))
         else:
             right = weighted[wide_rows(quarter + 1, plane, block), :]
-        total = weighted[wide_rows(quarter, plane, block, -1), :]
-        total = total + weighted[wide_rows(quarter, plane, block, 1), :]
-        total = total + pltpu.roll(jnp.where(lane == 127, left, center), 1, 1)
-        total = total + pltpu.roll(jnp.where(lane == 0, right, center), 127, 1)
+            total = total + pltpu.roll(jnp.where(lane == 0, right, center), 127, 1)
         return solved[tile_rows(quarter, plane, block), :] + weights[level] * (
             total - 4.0 * center
         )
@@ -543,14 +523,10 @@
     misfit,
 ):
     rows = prof_face.shape[0]
-    slots, meta = pack(
-        tile_owner,
-        jnp.transpose(seam_table, (2, 1, 0)),
-        prof_face.reshape(1, rows),
-        prof_cell.reshape(1, rows),
-        prof_time.reshape(1, rows),
-        misfit.reshape(PLANES, rows),
-    )
+    seams = jnp.transpose(seam_table, (2, 1, 0))
+    owners = jnp.pad(tile_owner, (0, rows - tile_owner.shape[0]))
+    numbers = jnp.stack([prof_face, prof_cell, prof_time, owners])
+    slots, meta = pack(seams, numbers, misfit.reshape(PLANES, rows))
     slots = lax.all_to_all(slots, ("tile", "sub"), split_axis=0, concat_axis=0, tiled=True)
     adjoint = adjoint_final.reshape(PLANES * ROWS, COLS)
     scale = diff_scale.reshape(LEVELS * ROWS, COLS)

time: 144 us -> 131 us (0.910)
  Pallas kernels: 40.9 us -> 26.9 us
    pallas_call x1, Pallas kernels: 12.8 us -> 5.2 us  [last_step(): pl.pallas_call(last_kernel, out_shape=(f32(PLANES, ROWS, COLS), BIG[1]),...]
    pallas_call x1, Pallas kernels: 11.1 us -> 6.34 us  [second_solve(): pl.pallas_call(second_kernel, out_shape=BIG + EDGES + BIG[1:], in_specs=[...]
    pallas_call x2, Pallas kernels: 10.7 us -> 8.58 us  [forcing(): pl.pallas_call(functools.partial(forcing_kernel, moment), out_shape=f32(P...]
    unnamed x20 -> x14, local copies, waits for them, and re-layouts: 4.15 us -> 2.88 us
  transfers between devices with their start and end apart: 16 -> 16, of which waited for: 14 -> 14; matrix products, arithmetic and copies ran while one was open for 0% -> 0% of each run, Pallas kernels for 4% -> 3%
where the time goes in v2:
time: 131 us; the launch traced here: 130 us
  blocking collectives  39.9 us (30%)
  waiting for transfers between devices  36.7 us (28%)
  Pallas kernels  26.9 us (21%)
  starting transfers between devices  21.5 us (16%)
  local copies, waits for them, and re-layouts  3.69 us (3%)
  other arithmetic  1.46 us (1%)
    all_to_all x1, blocking collectives, body(): lax.all_to_all(slots, ('tile', 'sub'), split_axis=0, concat_axis=0, tiled...  20.6 us
    all_to_all x2, blocking collectives, exchange(): got = lax.all_to_all(send, 'sub', split_axis=0, concat_axis=0, tiled=True)  19.4 us
    ppermute x2, waiting for transfers between devices, exchange(): across = lax.ppermute(across, 'sub', [(0, N_SUB - 1), (N_SUB - 1, 0)])  12.5 us
    ppermute x6, waiting for transfers between devices, exchange(): lax.ppermute(all_parts, 'tile', turn(k))  10.5 us
    pallas_call x2, Pallas kernels, forcing(): pl.pallas_call(functools.partial(forcing_kernel, moment), out_shape=f32(P...  8.58 us
    ppermute x2, waiting for transfers between devices, exchange(): lax.ppermute(first_row, 'sub', [(i + 1, i) for i in range(N_SUB - 1)])  6.37 us
    pallas_call x1, Pallas kernels, second_solve(): pl.pallas_call(second_kernel, out_shape=BIG + EDGES + BIG[1:], in_specs=[...  6.34 us
    ppermute x6, starting transfers between devices, exchange(): lax.ppermute(all_parts, 'tile', turn(k))  5.57 us
  transfers between devices with their start and end apart: 16, of which 14 were waited for; matrix products, arithmetic and copies ran while one was open for 0% of the time, Pallas kernels for 3%

profile of v2, /device:TPU:0, one launch (start us, length us, event | category | flops | bytes accessed | tf_op | source)
XLA Modules:
  0.0 130.4 jit_solution(5219910136728444815)
XLA Ops:
  0.0 0.8 pad.4
  0.8 1.1 pad_add_fusion.numbers
  2.0 0.0 copy-start.5
  2.0 1.3 copy-done.5
  3.2 0.7 copy-done.6
  3.9 2.0 %pack.1 = (f32[128,2,128]{2,1,0:T(2,128)S(1)}, s32[16]{0:T(128)S(1)}) custom-call(s32[3,4,16]{2,1,0:T(4,128)S(1)} %bitcast.27, s32[4,256]{1,0:T(4,128)S(1)} %pad_add_fusion.numbers, f32[32,256]{1,0:T(8,128)S(1)} %bitcast.26), custom_call_target="tpu_custom_call" | custom-call | tf_op jit(solution)/shard_map/pack/pallas_call | solution.py:107
  5.9 20.6 %all_to_all.15.slots = f32[128,2,128]{2,1,0:T(2,128)S(1)} all-to-all(f32[128,2,128]{2,1,0:T(2,128)S(1)} %get-tuple-element.42), channel_id=1, replica_groups=mesh['tile'=16,'sub'=8] {'tile','sub'}, dimensions={0} | all-to-all | bytes 262144 | tf_op jit(solution)/shard_map/all_to_all | solution.py:530
  26.5 4.3 %forcing_1.1.force = f32[2048,512]{1,0:T(8,128)S(1)} custom-call(f32[128,2,128]{2,1,0:T(2,128)S(1)} %all_to_all.15.slots), custom_call_target="tpu_custom_call" | custom-call | flops 2147483648 | bytes 4325376 | tf_op jit(solution)/shard_map/forcing_1/pallas_call | solution.py:156
  30.8 0.0 copy-start.3
  30.8 0.9 copy-done.3
  31.7 3.4 %first_solve.1 = (f32[8192,128]{1,0:T(8,128)S(1)}, f32[10240,128]{1,0:T(8,128)S(1)}, f32[5,32,128]{2,1,0:T(8,128)S(1)}, f32[4,32,128]{2,1,0:T(8,128)S(1)}, f32[4,32,128]{2,1,0:T(8,128)S(1)}) custom-call(s32[16]{0:T(128)S(1)} %get-tuple-element.41.meta, f32[2048,512]{1,0:T(8,128)S(1)} %bitcast.17, f32[2048,512]{1,0:T(8,128)S(1)} %forcing_1.1.force, ...), custom_call_target="tpu_custom_call" | custom-call | flops 30000000 | bytes 20000000 | tf_op jit(solution)/shard_map/first_solve/pallas_call | solution.py:278
  35.1 0.7 collective-permute-start.2
  35.8 2.2 %collective-permute-start.1 = (f32[1,5,32,128]{3,2,1,0:T(8,128)S(1)}, f32[1,5,32,128]{3,2,1,0:T(8,128)S(1)}, u32[]{:S(2)}, u32[]{:S(2)}) collective-permute-start(f32[1,5,32,128]{3,2,1,0:T(8,128)S(1)} %bitcast.23), channel_id=1, source_target_pairs={{0,32},{8,40},{16,48},{24,56},{32,0},{40,8},{48,16},{56,24},{64,96... | collective-permute-start | bytes 245768 | tf_op jit(solution)/shard_map/ppermute | solution.py:341
  38.0 0.0 collective-permute-start
  38.1 2.0 %collective-permute-done.2 = f32[1,5,32,128]{3,2,1,0:T(8,128)S(1)} collective-permute-done((f32[1,5,32,128]{3,2,1,0:T(8,128)S(1)}, f32[1,5,32,128]{3,2,1,0:T(8,128)S(1)}, u32[]{:S(2)}, u32[]{:S(2)}) %collective-permute-start.2) | collective-permute-done | bytes 81952 | tf_op jit(solution)/shard_map/ppermute | solution.py:341
  40.1 2.3 %collective-permute-done.1 = f32[1,5,32,128]{3,2,1,0:T(8,128)S(1)} collective-permute-done((f32[1,5,32,128]{3,2,1,0:T(8,128)S(1)}, f32[1,5,32,128]{3,2,1,0:T(8,128)S(1)}, u32[]{:S(2)}, u32[]{:S(2)}) %collective-permute-start.1) | collective-permute-done | bytes 81952 | tf_op jit(solution)/shard_map/ppermute | solution.py:341
  42.4 1.2 collective-permute-done
  43.7 1.3 %collective-permute-start.3 = (f32[4,5,32,128]{3,2,1,0:T(8,128)S(1)}, f32[4,5,32,128]{3,2,1,0:T(8,128)S(1)}, u32[]{:S(2)}, u32[]{:S(2)}) collective-permute-start(f32[4,5,32,128]{3,2,1,0:T(8,128)S(1)} %pad_maximum_fusion.4), channel_id=1, source_target_pairs={{0,64},{8,72},{16,80},{24,88},{32,96},{40,104},{48,112},{56,120},{... | collective-permute-start | bytes 983048 | tf_op jit(solution)/shard_map/ppermute | solution.py:348
  45.0 4.3 %forcing_0.1.force = f32[2048,512]{1,0:T(8,128)S(1)} custom-call(f32[128,2,128]{2,1,0:T(2,128)S(1)} %all_to_all.15.slots), custom_call_target="tpu_custom_call" | custom-call | flops 2147483648 | bytes 4325376 | tf_op jit(solution)/shard_map/forcing_0/pallas_call | solution.py:156
  49.3 2.6 %collective-permute-start.4 = (f32[4,32,128]{2,1,0:T(8,128)S(1)}, f32[4,32,128]{2,1,0:T(8,128)S(1)}, u32[]{:S(2)}, u32[]{:S(2)}) collective-permute-start(f32[4,32,128]{2,1,0:T(8,128)S(1)} %get-tuple-element.47), channel_id=1, source_target_pairs={{0,1},{1,2},{2,3},{3,4},{4,5},{5,6},{6,7},{8,9},{9,10},{10,11},{11... | collective-permute-start | bytes 196616 | tf_op jit(solution)/shard_map/ppermute | solution.py:345
  51.9 1.3 collective-permute-start.5
  53.2 0.5 collective-permute-done.3
  53.8 4.3 %collective-permute-done.5.below = f32[4,32,128]{2,1,0:T(8,128)S(1)} collective-permute-done((f32[4,32,128]{2,1,0:T(8,128)S(1)}, f32[4,32,128]{2,1,0:T(8,128)S(1)}, u32[]{:S(2)}, u32[]{:S(2)}) %collective-permute-start.5) | collective-permute-done | bytes 65568 | tf_op jit(solution)/shard_map/ppermute | solution.py:346
  58.1 2.1 %collective-permute-done.6 = f32[8,5,32,128]{3,2,1,0:T(8,128)S(1)} collective-permute-done((f32[8,5,32,128]{3,2,1,0:T(8,128)S(1)}, f32[8,5,32,128]{3,2,1,0:T(8,128)S(1)}, u32[]{:S(2)}, u32[]{:S(2)}) %collective-permute-start.6) | collective-permute-done | bytes 655392 | tf_op jit(solution)/shard_map/ppermute | solution.py:352
  60.2 0.1 pad_maximum_fusion.gathered
  60.3 0.7 route.2
  61.0 2.1 %collective-permute-start.7 = (f32[4,32,128]{2,1,0:T(8,128)S(1)}, f32[4,32,128]{2,1,0:T(8,128)S(1)}, u32[]{:S(2)}, u32[]{:S(2)}) collective-permute-start(f32[4,32,128]{2,1,0:T(8,128)S(1)} %get-tuple-element.51), channel_id=1, source_target_pairs={{0,7},{7,0},{8,15},{15,8},{16,23},{23,16},{24,31},{31,24},{32,39},... | collective-permute-start | bytes 196616 | tf_op jit(solution)/shard_map/ppermute | solution.py:355
  63.2 6.1 %collective-permute-done.7.across = f32[4,32,128]{2,1,0:T(8,128)S(1)} collective-permute-done((f32[4,32,128]{2,1,0:T(8,128)S(1)}, f32[4,32,128]{2,1,0:T(8,128)S(1)}, u32[]{:S(2)}, u32[]{:S(2)}) %collective-permute-start.7) | collective-permute-done | bytes 65568 | tf_op jit(solution)/shard_map/ppermute | solution.py:355
  69.3 9.7 %all_to_all.16.got = f32[8,2,32,128]{3,2,1,0:T(8,128)S(1)} all-to-all(f32[8,2,32,128]{3,2,1,0:T(8,128)S(1)} %get-tuple-element.52), channel_id=1, replica_groups=mesh['tile'=16,'sub'=8] {'sub'}, dimensions={0} | all-to-all | bytes 524288 | tf_op jit(solution)/shard_map/all_to_all | solution.py:357
  79.0 6.3 %second_solve.1 = (f32[8192,128]{1,0:T(8,128)S(1)}, f32[10240,128]{1,0:T(8,128)S(1)}, f32[5,32,128]{2,1,0:T(8,128)S(1)}, f32[4,32,128]{2,1,0:T(8,128)S(1)}, f32[...) custom-call(s32[16]{0:T(128)S(1)} %get-tuple-element.41.meta, ...), custom_call_target="tpu_custom_call", output_to_operand_aliasing={{5}: (7, {})} | custom-call | flops 50000000 | bytes 30000000 | tf_op jit(solution)/shard_map/second_solve/pallas_call | solution.py:456
  85.3 0.6 collective-permute-start.10
  85.9 1.1 collective-permute-start.9
  87.1 0.8 collective-permute-start.8
  87.9 1.9 %collective-permute-done.10 = f32[1,5,32,128]{3,2,1,0:T(8,128)S(1)} collective-permute-done((f32[1,5,32,128]{3,2,1,0:T(8,128)S(1)}, f32[1,5,32,128]{3,2,1,0:T(8,128)S(1)}, u32[]{:S(2)}, u32[]{:S(2)}) %collective-permute-start.10) | collective-permute-done | bytes 81952 | tf_op jit(solution)/shard_map/ppermute | solution.py:341
  89.8 2.1 %collective-permute-done.9 = f32[1,5,32,128]{3,2,1,0:T(8,128)S(1)} collective-permute-done((f32[1,5,32,128]{3,2,1,0:T(8,128)S(1)}, f32[1,5,32,128]{3,2,1,0:T(8,128)S(1)}, u32[]{:S(2)}, u32[]{:S(2)}) %collective-permute-start.9) | collective-permute-done | bytes 81952 | tf_op jit(solution)/shard_map/ppermute | solution.py:341
  91.9 0.9 collective-permute-done.8
  92.8 2.6 %collective-permute-start.11 = (f32[4,5,32,128]{3,2,1,0:T(8,128)S(1)}, f32[4,5,32,128]{3,2,1,0:T(8,128)S(1)}, u32[]{:S(2)}, u32[]{:S(2)}) collective-permute-start(f32[4,5,32,128]{3,2,1,0:T(8,128)S(1)} %pad_maximum_fusion.5), channel_id=1, source_target_pairs={{0,64},{8,72},{16,80},{24,88},{32,96},{40,104},{48,112},{56,120},{... | collective-permute-start | bytes 983048 | tf_op jit(solution)/shard_map/ppermute | solution.py:348
  95.4 2.8 %collective-permute-start.12 = (f32[4,32,128]{2,1,0:T(8,128)S(1)}, f32[4,32,128]{2,1,0:T(8,128)S(1)}, u32[]{:S(2)}, u32[]{:S(2)}) collective-permute-start(f32[4,32,128]{2,1,0:T(8,128)S(1)} %get-tuple-element.64), channel_id=1, source_target_pairs={{0,1},{1,2},{2,3},{3,4},{4,5},{5,6},{6,7},{8,9},{9,10},{10,11},{11... | collective-permute-start | bytes 196616 | tf_op jit(solution)/shard_map/ppermute | solution.py:345
  98.1 1.3 collective-permute-start.13
  99.4 2.7 %collective-permute-done.11 = f32[4,5,32,128]{3,2,1,0:T(8,128)S(1)} collective-permute-done((f32[4,5,32,128]{3,2,1,0:T(8,128)S(1)}, f32[4,5,32,128]{3,2,1,0:T(8,128)S(1)}, u32[]{:S(2)}, u32[]{:S(2)}) %collective-permute-start.11) | collective-permute-done | bytes 327712 | tf_op jit(solution)/shard_map/ppermute | solution.py:348
  102.2 2.1 %collective-permute-done.13.below = f32[4,32,128]{2,1,0:T(8,128)S(1)} collective-permute-done((f32[4,32,128]{2,1,0:T(8,128)S(1)}, f32[4,32,128]{2,1,0:T(8,128)S(1)}, u32[]{:S(2)}, u32[]{:S(2)}) %collective-permute-start.13) | collective-permute-done | bytes 65568 | tf_op jit(solution)/shard_map/ppermute | solution.py:346
  104.3 2.1 %collective-permute-done.14 = f32[8,5,32,128]{3,2,1,0:T(8,128)S(1)} collective-permute-done((f32[8,5,32,128]{3,2,1,0:T(8,128)S(1)}, f32[8,5,32,128]{3,2,1,0:T(8,128)S(1)}, u32[]{:S(2)}, u32[]{:S(2)}) %collective-permute-start.14) | collective-permute-done | bytes 655392 | tf_op jit(solution)/shard_map/ppermute | solution.py:352
  106.4 0.1 pad_maximum_fusion.1.gathered
  106.5 0.7 route.3
  107.2 1.9 %collective-permute-start.15 = (f32[4,32,128]{2,1,0:T(8,128)S(1)}, f32[4,32,128]{2,1,0:T(8,128)S(1)}, u32[]{:S(2)}, u32[]{:S(2)}) collective-permute-start(f32[4,32,128]{2,1,0:T(8,128)S(1)} %get-tuple-element.68), channel_id=1, source_target_pairs={{0,7},{7,0},{8,15},{15,8},{16,23},{23,16},{24,31},{31,24},{32,39},... | collective-permute-start | bytes 196616 | tf_op jit(solution)/shard_map/ppermute | solution.py:355
  109.1 6.3 %collective-permute-done.15.across = f32[4,32,128]{2,1,0:T(8,128)S(1)} collective-permute-done((f32[4,32,128]{2,1,0:T(8,128)S(1)}, f32[4,32,128]{2,1,0:T(8,128)S(1)}, u32[]{:S(2)}, u32[]{:S(2)}) %collective-permute-start.15) | collective-permute-done | bytes 65568 | tf_op jit(solution)/shard_map/ppermute | solution.py:355
  115.5 9.7 %all_to_all.17.got = f32[8,2,32,128]{3,2,1,0:T(8,128)S(1)} all-to-all(f32[8,2,32,128]{3,2,1,0:T(8,128)S(1)} %get-tuple-element.69), channel_id=1, replica_groups=mesh['tile'=16,'sub'=8] {'sub'}, dimensions={0} | all-to-all | bytes 524288 | tf_op jit(solution)/shard_map/all_to_all | solution.py:357
  125.2 5.2 %last_step.1 = (f32[32,64,512]{2,1,0:T(8,128)}, f32[10240,128]{1,0:T(8,128)S(1)}) custom-call(s32[16]{0:T(128)S(1)} %get-tuple-element.41.meta, f32[8,2,32,128]{3,2,1,0:T(8,128)S(1)} %all_to_all.17.got, f32[4,32,128]{2,1,0:T(8,128)S(1)} %get-tuple-element.70.here, f32[4,32,128]{2,1,0:T(8,128)S(1)} %collective-permute-done.15.across, ...), custom_call_target="tpu_custom_call", output_to_operand_aliasing={{1}: (7, {})} | custom-call | flops 20000000 | bytes 20000000 | tf_op jit(solution)/shard_map/last_step/pallas_call | solution.py:496
  (17 shorter events, 0.2 us)
Async XLA Ops:
  0.0 30.8 %copy-start.1 = (f32[15,64,512]{2,1,0:T(8,128)S(1)}, f32[15,64,512]{2,1,0:T(8,128)}, u32[]{:S(2)}) copy-start(f32[15,64,512]{2,1,0:T(8,128)} %param.12) | copy-start | bytes 5898244
  0.0 30.8 %copy-start = (f32[16,64,512]{2,1,0:T(8,128)S(1)}, f32[16,64,512]{2,1,0:T(8,128)}, u32[]{:S(2)}) copy-start(f32[16,64,512]{2,1,0:T(8,128)} %param.11) | copy-start | bytes 6291460
  0.0 30.8 %copy-start.2 = (f32[2,16,64,512]{3,2,1,0:T(8,128)S(1)}, f32[2,16,64,512]{3,2,1,0:T(8,128)}, u32[]{:S(2)}) copy-start(f32[2,16,64,512]{3,2,1,0:T(8,128)} %param.10) | copy-start | bytes 12582916
  2.0 1.3 copy-start.5
  3.2 0.7 copy-start.6
  30.8 0.9 copy-start.3
  35.1 5.0 %collective-permute-start.2 = (f32[1,5,32,128]{3,2,1,0:T(8,128)S(1)}, f32[1,5,32,128]{3,2,1,0:T(8,128)S(1)}, u32[]{:S(2)}, u32[]{:S(2)}) collective-permute-start(f32[1,5,32,128]{3,2,1,0:T(8,128)S(1)} %bitcast.22), channel_id=1, source_target_pairs={{0,48},{8,56},{16,0},{24,8},{32,16},{40,24},{48,32},{56,40},{64,11... | collective-permute-start | bytes 245768 | tf_op jit(solution)/shard_map/ppermute | solution.py:341
  35.8 6.6 %collective-permute-start.1 = (f32[1,5,32,128]{3,2,1,0:T(8,128)S(1)}, f32[1,5,32,128]{3,2,1,0:T(8,128)S(1)}, u32[]{:S(2)}, u32[]{:S(2)}) collective-permute-start(f32[1,5,32,128]{3,2,1,0:T(8,128)S(1)} %bitcast.23), channel_id=1, source_target_pairs={{0,32},{8,40},{16,48},{24,56},{32,0},{40,8},{48,16},{56,24},{64,96... | collective-permute-start | bytes 245768 | tf_op jit(solution)/shard_map/ppermute | solution.py:341
  38.0 5.7 %collective-permute-start = (f32[1,5,32,128]{3,2,1,0:T(8,128)S(1)}, f32[1,5,32,128]{3,2,1,0:T(8,128)S(1)}, u32[]{:S(2)}, u32[]{:S(2)}) collective-permute-start(f32[1,5,32,128]{3,2,1,0:T(8,128)S(1)} %bitcast.24), channel_id=1, source_target_pairs={{0,16},{8,24},{16,32},{24,40},{32,48},{40,56},{48,0},{56,8},{64,80... | collective-permute-start | bytes 245768 | tf_op jit(solution)/shard_map/ppermute | solution.py:341
  43.7 10.1 %collective-permute-start.3 = (f32[4,5,32,128]{3,2,1,0:T(8,128)S(1)}, f32[4,5,32,128]{3,2,1,0:T(8,128)S(1)}, u32[]{:S(2)}, u32[]{:S(2)}) collective-permute-start(f32[4,5,32,128]{3,2,1,0:T(8,128)S(1)} %pad_maximum_fusion.4), channel_id=1, source_target_pairs={{0,64},{8,72},{16,80},{24,88},{32,96},{40,104},{48,112},{56,120},{... | collective-permute-start | bytes 983048 | tf_op jit(solution)/shard_map/ppermute | solution.py:348
  49.3 29.7 %copy-start.4 = (s32[64,512]{1,0:T(8,128)S(1)}, s32[64,512]{1,0:T(8,128)}, u32[]{:S(2)}) copy-start(s32[64,512]{1,0:T(8,128)} %depth.5) | copy-start | bytes 393220
  49.3 4.5 %collective-permute-start.4 = (f32[4,32,128]{2,1,0:T(8,128)S(1)}, f32[4,32,128]{2,1,0:T(8,128)S(1)}, u32[]{:S(2)}, u32[]{:S(2)}) collective-permute-start(f32[4,32,128]{2,1,0:T(8,128)S(1)} %get-tuple-element.47), channel_id=1, source_target_pairs={{0,1},{1,2},{2,3},{3,4},{4,5},{5,6},{6,7},{8,9},{9,10},{10,11},{11... | collective-permute-start | bytes 196616 | tf_op jit(solution)/shard_map/ppermute | solution.py:345
  51.9 6.2 %collective-permute-start.5 = (f32[4,32,128]{2,1,0:T(8,128)S(1)}, f32[4,32,128]{2,1,0:T(8,128)S(1)}, u32[]{:S(2)}, u32[]{:S(2)}) collective-permute-start(f32[4,32,128]{2,1,0:T(8,128)S(1)} %get-tuple-element.48), channel_id=1, source_target_pairs={{1,0},{2,1},{3,2},{4,3},{5,4},{6,5},{7,6},{9,8},{10,9},{11,10},{12... | collective-permute-start | bytes 196616 | tf_op jit(solution)/shard_map/ppermute | solution.py:346
  58.1 2.1 %collective-permute-start.6 = (f32[8,5,32,128]{3,2,1,0:T(8,128)S(1)}, f32[8,5,32,128]{3,2,1,0:T(8,128)S(1)}, u32[]{:S(2)}, u32[]{:S(2)}) collective-permute-start(f32[8,5,32,128]{3,2,1,0:T(8,128)S(1)} %pad_maximum_fusion.2), channel_id=1, source_target_pairs={{0,8},{8,0},{16,24},{24,16},{32,40},{40,32},{48,56},{56,48},{64,72... | collective-permute-start | bytes 1966088 | tf_op jit(solution)/shard_map/ppermute | solution.py:352
  61.0 8.3 %collective-permute-start.7 = (f32[4,32,128]{2,1,0:T(8,128)S(1)}, f32[4,32,128]{2,1,0:T(8,128)S(1)}, u32[]{:S(2)}, u32[]{:S(2)}) collective-permute-start(f32[4,32,128]{2,1,0:T(8,128)S(1)} %get-tuple-element.51), channel_id=1, source_target_pairs={{0,7},{7,0},{8,15},{15,8},{16,23},{23,16},{24,31},{31,24},{32,39},... | collective-permute-start | bytes 196616 | tf_op jit(solution)/shard_map/ppermute | solution.py:355
  85.3 4.5 %collective-permute-start.10 = (f32[1,5,32,128]{3,2,1,0:T(8,128)S(1)}, f32[1,5,32,128]{3,2,1,0:T(8,128)S(1)}, u32[]{:S(2)}, u32[]{:S(2)}) collective-permute-start(f32[1,5,32,128]{3,2,1,0:T(8,128)S(1)} %bitcast.18), channel_id=1, source_target_pairs={{0,48},{8,56},{16,0},{24,8},{32,16},{40,24},{48,32},{56,40},{64,11... | collective-permute-start | bytes 245768 | tf_op jit(solution)/shard_map/ppermute | solution.py:341
  85.9 5.9 %collective-permute-start.9 = (f32[1,5,32,128]{3,2,1,0:T(8,128)S(1)}, f32[1,5,32,128]{3,2,1,0:T(8,128)S(1)}, u32[]{:S(2)}, u32[]{:S(2)}) collective-permute-start(f32[1,5,32,128]{3,2,1,0:T(8,128)S(1)} %bitcast.19), channel_id=1, source_target_pairs={{0,32},{8,40},{16,48},{24,56},{32,0},{40,8},{48,16},{56,24},{64,96... | collective-permute-start | bytes 245768 | tf_op jit(solution)/shard_map/ppermute | solution.py:341
  87.1 5.7 %collective-permute-start.8 = (f32[1,5,32,128]{3,2,1,0:T(8,128)S(1)}, f32[1,5,32,128]{3,2,1,0:T(8,128)S(1)}, u32[]{:S(2)}, u32[]{:S(2)}) collective-permute-start(f32[1,5,32,128]{3,2,1,0:T(8,128)S(1)} %bitcast.20), channel_id=1, source_target_pairs={{0,16},{8,24},{16,32},{24,40},{32,48},{40,56},{48,0},{56,8},{64,80... | collective-permute-start | bytes 245768 | tf_op jit(solution)/shard_map/ppermute | solution.py:341
  92.8 9.4 %collective-permute-start.11 = (f32[4,5,32,128]{3,2,1,0:T(8,128)S(1)}, f32[4,5,32,128]{3,2,1,0:T(8,128)S(1)}, u32[]{:S(2)}, u32[]{:S(2)}) collective-permute-start(f32[4,5,32,128]{3,2,1,0:T(8,128)S(1)} %pad_maximum_fusion.5), channel_id=1, source_target_pairs={{0,64},{8,72},{16,80},{24,88},{32,96},{40,104},{48,112},{56,120},{... | collective-permute-start | bytes 983048 | tf_op jit(solution)/shard_map/ppermute | solution.py:348
  95.4 6.8 %collective-permute-start.12 = (f32[4,32,128]{2,1,0:T(8,128)S(1)}, f32[4,32,128]{2,1,0:T(8,128)S(1)}, u32[]{:S(2)}, u32[]{:S(2)}) collective-permute-start(f32[4,32,128]{2,1,0:T(8,128)S(1)} %get-tuple-element.64), channel_id=1, source_target_pairs={{0,1},{1,2},{2,3},{3,4},{4,5},{5,6},{6,7},{8,9},{9,10},{10,11},{11... | collective-permute-start | bytes 196616 | tf_op jit(solution)/shard_map/ppermute | solution.py:345
  98.1 6.2 %collective-permute-start.13 = (f32[4,32,128]{2,1,0:T(8,128)S(1)}, f32[4,32,128]{2,1,0:T(8,128)S(1)}, u32[]{:S(2)}, u32[]{:S(2)}) collective-permute-start(f32[4,32,128]{2,1,0:T(8,128)S(1)} %get-tuple-element.65), channel_id=1, source_target_pairs={{1,0},{2,1},{3,2},{4,3},{5,4},{6,5},{7,6},{9,8},{10,9},{11,10},{12... | collective-permute-start | bytes 196616 | tf_op jit(solution)/shard_map/ppermute | solution.py:346
  104.3 2.1 %collective-permute-start.14 = (f32[8,5,32,128]{3,2,1,0:T(8,128)S(1)}, f32[8,5,32,128]{3,2,1,0:T(8,128)S(1)}, u32[]{:S(2)}, u32[]{:S(2)}) collective-permute-start(f32[8,5,32,128]{3,2,1,0:T(8,128)S(1)} %pad_maximum_fusion.3), channel_id=1, source_target_pairs={{0,8},{8,0},{16,24},{24,16},{32,40},{40,32},{48,56},{56,48},{64,72... | collective-permute-start | bytes 1966088 | tf_op jit(solution)/shard_map/ppermute | solution.py:352
  107.2 8.3 %collective-permute-start.15 = (f32[4,32,128]{2,1,0:T(8,128)S(1)}, f32[4,32,128]{2,1,0:T(8,128)S(1)}, u32[]{:S(2)}, u32[]{:S(2)}) collective-permute-start(f32[4,32,128]{2,1,0:T(8,128)S(1)} %get-tuple-element.68), channel_id=1, source_target_pairs={{0,7},{7,0},{8,15},{15,8},{16,23},{23,16},{24,31},{31,24},{32,39},... | collective-permute-start | bytes 196616 | tf_op jit(solution)/shard_map/ppermute | solution.py:355

commit v3 on v1

--- a/solution.py
+++ b/solution.py
@@ -22,6 +22,7 @@
 VMEM = pl.BlockSpec(memory_space=pltpu.VMEM)
 SMEM = pl.BlockSpec(memory_space=pltpu.SMEM)
 META = 16
+PARTS = 2
 
 
 def iota(shape, axis):
@@ -36,14 +37,14 @@
     return jax.ShapeDtypeStruct(shape, jnp.float32)
 
 
-def pack_kernel(owner_in, seam_in, face_in, cell_in, time_in, misfit_in, out, meta, owner, seam,
+def pack_kernel(owner_in, seam_in, face_in, cell_in, time_in, misfit_in, out, meta, owners, seams,
                 face, cell, time, misfit, sems):
     copies = [
         pltpu.make_async_copy(source, target, sems.at[i])
         for i, (source, target) in enumerate(
             (
-                (owner_in, owner),
-                (seam_in, seam),
+                (owner_in, owners),
+                (seam_in, seams),
                 (face_in, face),
                 (cell_in, cell),
                 (time_in, time),
@@ -55,29 +56,37 @@
         copy.start()
     for copy in copies:
         copy.wait()
+
+    def owner(f):
+        return owners[f]
+
+    def seam(part, edge, f):
+        return seams[part, edge, f]
+
+
     tile = lax.axis_index("tile")
     sub = lax.axis_index("sub")
     my_face = jnp.int32(0)
     for f in range(FACES):
-        my_face = my_face + jnp.where(owner[f] == tile, f, 0)
+        my_face = my_face + jnp.where(owner(f) == tile, f, 0)
     meta[12] = tile
     meta[13] = sub
     for edge in range(4):
-        other = owner[seam[0, edge, my_face]]
+        other = owner(seam(0, edge, my_face))
         away = (
             ((other & 1) ^ (tile & 1)) * 8
             + (((other >> 3) & 1) ^ ((tile >> 3) & 1)) * 4
             + ((((tile >> 1) & 3) + 4 - ((other >> 1) & 3)) & 3)
         )
         meta[3 * edge] = away
-        meta[3 * edge + 1] = seam[1, edge, my_face]
-        meta[3 * edge + 2] = seam[2, edge, my_face]
+        meta[3 * edge + 1] = seam(1, edge, my_face)
+        meta[3 * edge + 2] = seam(2, edge, my_face)
 
     rows = face.shape[1]
     faces = face[...]
     home = jnp.zeros_like(faces)
     for f in range(FACES):
-        home = jnp.where(faces == f, owner[f], home)
+        home = jnp.where(faces == f, owner(f), home)
     cells = cell[...]
     tile_row = cells >> 9
     target = home * N_SUB + (tile_row >> 6)
@@ -113,12 +122,11 @@
 
 
 def pack(owner, seam, face, cell, time, misfit):
-    rows = face.shape[1]
-    line = pltpu.VMEM((1, rows), jnp.int32)
+    line = pltpu.VMEM(face.shape, jnp.int32)
     return pl.pallas_call(
         pack_kernel,
         out_shape=(f32(DEVICES, 2, DEVICES), jax.ShapeDtypeStruct((META,), jnp.int32)),
-        in_specs=[pl.BlockSpec(memory_space=pltpu.HBM)] * 6,
+        in_specs=[pl.BlockSpec(memory_space=pl.ANY)] * 6,
         out_specs=(VMEM, SMEM),
         scratch_shapes=[
             pltpu.SMEM(owner.shape, jnp.int32),
@@ -129,7 +137,7 @@
             pltpu.VMEM(misfit.shape, jnp.float32),
             pltpu.SemaphoreType.DMA((6,)),
         ],
-        compiler_params=params(8),
+        compiler_params=pltpu.CompilerParams(vmem_limit_bytes=66000000),
         name="pack",
     )(owner, seam, face, cell, time, misfit)
 
@@ -145,11 +153,8 @@
     on_row = iota((ROWS, CAP * DEVICES), 0) == row_of
     wide = jnp.concatenate([values[PLANES * k : PLANES * (k + 1), :] for k in range(CAP)], axis=1)
     high = wide.astype(jnp.bfloat16).astype(jnp.float32)
-    rest = wide - high
-    middle = rest.astype(jnp.bfloat16).astype(jnp.float32)
     parts[0] = high
-    parts[1] = middle
-    parts[2] = rest - middle
+    parts[1] = wide - high
     for k in range(CAP):
         col = tags[:, k : k + 1] & (COLS - 1)
         place[k * DEVICES : (k + 1) * DEVICES, :] = jnp.where(
@@ -159,7 +164,7 @@
 
     def step(g, carry):
         total = None
-        for part in range(3):
+        for part in range(PARTS):
             left = []
             for q in range(group):
                 row = parts[part, pl.ds(g * group + q, 1), :]
@@ -181,11 +186,11 @@
         in_specs=[VMEM],
         out_specs=VMEM,
         scratch_shapes=[
-            pltpu.VMEM((3, PLANES, CAP * DEVICES), jnp.float32),
+            pltpu.VMEM((PARTS, PLANES, CAP * DEVICES), jnp.float32),
             pltpu.VMEM((CAP * DEVICES, COLS), jnp.bfloat16),
         ],
         compiler_params=params(8),
-        cost_estimate=pl.CostEstimate(flops=3221225472, bytes_accessed=4325376, transcendentals=0),
+        cost_estimate=pl.CostEstimate(flops=2147483648, bytes_accessed=4325376, transcendentals=0),
         name=f"forcing_{moment}",
     )(slots)
 
@@ -309,7 +314,7 @@
     )(meta, adjoint, force, coupling, scale, depth)
 
 
-def route_kernel(meta, gathered, send, here, across):
+def route_kernel(meta, gathered, first_row, last_row, send, here):
     sub = meta[13]
     lane = iota((PLANES, 128), 1)
 
@@ -334,19 +339,29 @@
     place_across = meta[3 * (1 - own)]
     for b in range(4):
         here[b] = gathered[place_here, 1 + b]
-        across[b] = gathered[place_across, 1 + b]
-
-
-def route(meta, gathered):
+        across = gathered[place_across, 1 + b]
+        first = first_row[b]
+        last = last_row[b]
+        for dest in range(N_SUB):
+            if dest == 0:
+                row = jnp.where(sub == N_SUB - 1, across, first)
+            elif dest == N_SUB - 1:
+                row = jnp.where(sub == 0, across, last)
+            else:
+                row = jnp.where(sub == dest - 1, last, first)
+            send[dest, 2 + b] = row
+
+
+def route(meta, gathered, first_row, last_row):
     return pl.pallas_call(
         route_kernel,
-        out_shape=(f32(N_SUB, 2, PLANES, 128), f32(4, PLANES, 128), f32(4, PLANES, 128)),
-        in_specs=[SMEM, VMEM],
-        out_specs=(VMEM,) * 3,
+        out_shape=(f32(N_SUB, 6, PLANES, 128), f32(4, PLANES, 128)),
+        in_specs=[SMEM] + [VMEM] * 3,
+        out_specs=(VMEM,) * 2,
         compiler_params=params(8),
         cost_estimate=pl.CostEstimate(flops=1000000, bytes_accessed=1000000, transcendentals=0),
         name="route",
-    )(meta, gathered)
+    )(meta, gathered, first_row, last_row)
 
 
 def exchange(meta, payload, first_row, last_row, beside=None):
@@ -362,26 +377,24 @@
     all_parts = jnp.concatenate(
         [all_parts] + [lax.ppermute(all_parts, "tile", turn(k)) for k in (1, 2, 3)], axis=0
     )
-    all_parts, first_row, last_row = lax.optimization_barrier((all_parts, first_row, last_row))
-    extra = () if beside is None else (beside(),)
-    above = lax.ppermute(last_row, "sub", [(i, i + 1) for i in range(N_SUB - 1)])
-    below = lax.ppermute(first_row, "sub", [(i + 1, i) for i in range(N_SUB - 1)])
     all_parts = jnp.concatenate(
         [all_parts, lax.ppermute(all_parts, "tile", [(i, i ^ 8) for i in range(N_TILE)])], axis=0
     )
-    all_parts, above, below, *extra = lax.optimization_barrier((all_parts, above, below, *extra))
+    extra = () if beside is None else (beside(),)
+    all_parts, *extra = lax.optimization_barrier((all_parts, *extra))
     all_parts = jnp.concatenate(
         [all_parts, lax.ppermute(all_parts, "tile", [(i, i ^ 1) for i in range(N_TILE)])], axis=0
     )
-    send, here, across = route(meta, all_parts)
-    across = lax.ppermute(across, "sub", [(0, N_SUB - 1), (N_SUB - 1, 0)])
-    send, across = lax.optimization_barrier((send, across))
+    send, here = route(meta, all_parts, first_row, last_row)
     got = lax.all_to_all(send, "sub", split_axis=0, concat_axis=0, tiled=True)
-    return (got, here, across, above, below), extra
-
-
-def place_halo(meta, got, here, across, above, below, weighted, strips):
+    return (got, here), extra
+
+
+def place_halo(meta, got, here, weighted, strips):
     sub = meta[13]
+    before = jnp.maximum(sub - 1, 0)
+    after = jnp.minimum(sub + 1, N_SUB - 1)
+    opposite = jnp.where(sub == 0, N_SUB - 1, 0)
     lane = iota((PLANES, 128), 1)
 
     def source(edge):
@@ -405,14 +418,14 @@
     row = []
     for b in range(4):
         joined = jnp.where(lane < 64, got[2 * b, 1], pltpu.roll(got[2 * b + 1, 1], 64, 1))
-        joined = jnp.where(other_edge < 2, across[b], joined)
+        joined = jnp.where(other_edge < 2, got[opposite, 2 + b], joined)
         row.append(jnp.where(other_edge == own, here[b], joined))
     for b in range(4):
         ordered = jnp.where(turned == 1, row[3 - b], row[b])
         strip = jnp.dot(ordered, flip, precision=HIGHEST, preferred_element_type=jnp.float32)
         at = b * PLANES * PITCH
-        above_row = jnp.where(sub == 0, strip, above[b])
-        below_row = jnp.where(sub == N_SUB - 1, strip, below[b])
+        above_row = jnp.where(sub == 0, strip, got[before, 2 + b])
+        below_row = jnp.where(sub == N_SUB - 1, strip, got[after, 2 + b])
         weighted[pl.ds(at + 7, PLANES, stride=PITCH), :] = above_row
         weighted[pl.ds(at + ROWS + 8, PLANES, stride=PITCH), :] = below_row
 
@@ -432,18 +445,20 @@
             at = pl.ds(pl.multiple_of(level * ROWS + block * 8, 8), 8)
             weights[level] = jnp.where(level < depth, scale[at, columns], 0.0) * explicit_rate
         center = weighted[wide_rows(quarter, plane, block), :]
+        total = weighted[wide_rows(quarter, plane, block, -1), :]
+        total = total + weighted[wide_rows(quarter, plane, block, 1), :]
         if quarter == 0:
-            left = pltpu.roll(west, 127 - plane, 1)
+            edge = west if plane == 0 else pltpu.roll(west, 128 - plane, 1)
+            total = total + jnp.where(lane == 0, edge, pltpu.roll(center, 1, 1))
         else:
             left = weighted[wide_rows(quarter - 1, plane, block), :]
+            total = total + pltpu.roll(jnp.where(lane == 127, left, center), 1, 1)
         if quarter == 3:
-            right = east if plane == 0 else pltpu.roll(east, 128 - plane, 1)
+            edge = pltpu.roll(east, 127 - plane, 1)
+            total = total + jnp.where(lane == 127, edge, pltpu.roll(center, 127, 1))
         else:
             right = weighted[wide_rows(quarter + 1, plane, block), :]
-        total = weighted[wide_rows(quarter, plane, block, -1), :]
-        total = total + weighted[wide_rows(quarter, plane, block, 1), :]
-        total = total + pltpu.roll(jnp.where(lane == 127, left, center), 1, 1)
-        total = total + pltpu.roll(jnp.where(lane == 0, right, center), 127, 1)
+            total = total + pltpu.roll(jnp.where(lane == 0, right, center), 127, 1)
         return solved[tile_rows(quarter, plane, block), :] + weights[level] * (
             total - 4.0 * center
         )
@@ -451,10 +466,10 @@
     return value
 
 
-def second_kernel(meta, got, here, across, above, below, solved_in, weighted_in, force, coupling,
+def second_kernel(meta, got, here, solved_in, weighted_in, force, coupling,
                   scale, depth, solved, weighted, payload, first_row, last_row, weighted_late,
                   sides, strips):
-    place_halo(meta, got, here, across, above, below, weighted_late, strips)
+    place_halo(meta, got, here, weighted_late, strips)
 
     def step(block, carry):
         for quarter in range(4):
@@ -476,9 +491,9 @@
     return pl.pallas_call(
         second_kernel,
         out_shape=BIG + EDGES + BIG[1:],
-        in_specs=[SMEM] + [VMEM] * 11,
+        in_specs=[SMEM] + [VMEM] * 8,
         out_specs=(VMEM,) * 6,
-        input_output_aliases={7: 5},
+        input_output_aliases={4: 5},
         scratch_shapes=[pltpu.VMEM((128, 128), jnp.float32)] * 2,
         compiler_params=params(8),
         cost_estimate=pl.CostEstimate(flops=50000000, bytes_accessed=30000000, transcendentals=0),
@@ -486,9 +501,9 @@
     )(meta, *halos, solved, weighted, force, coupling, scale, depth)
 
 
-def last_kernel(meta, got, here, across, above, below, solved, weighted_in, scale, depth, out,
+def last_kernel(meta, got, here, solved, weighted_in, scale, depth, out,
                 weighted, strips, ready, sems):
-    place_halo(meta, got, here, across, above, below, weighted, strips)
+    place_halo(meta, got, here, weighted, strips)
 
     def copy(block):
         return pltpu.make_async_copy(
@@ -516,9 +531,9 @@
     return pl.pallas_call(
         last_kernel,
         out_shape=(f32(PLANES, ROWS, COLS), BIG[1]),
-        in_specs=[SMEM] + [VMEM] * 9,
+        in_specs=[SMEM] + [VMEM] * 6,
         out_specs=(pl.BlockSpec(memory_space=pl.ANY), VMEM),
-        input_output_aliases={7: 1},
+        input_output_aliases={4: 1},
         scratch_shapes=[
             pltpu.VMEM((128, 128), jnp.float32),
             pltpu.VMEM((ROWS // 8, PLANES, 8, COLS), jnp.float32),

time: 144 us -> 120 us (0.83)
  Pallas kernels: 40.9 us -> 27.3 us
  blocking collectives: 39.9 us -> 52.6 us
  starting transfers between devices: 21.4 us -> 9.6 us
  waiting for transfers between devices: 36.7 us -> 27.1 us
  local copies, waits for them, and re-layouts: 4.15 us -> 2.31 us
    ppermute x6 -> x0, waiting for transfers between devices: 19.4 us -> none  [the longest x2 12.5 us: exchange(): across = lax.ppermute(across, 'sub', [(0, N_SUB - 1), (N_SUB - 1, 0)])]
    ppermute x2, waiting for transfers between devices: 2.7 us -> 16.2 us  [exchange(): lax.ppermute(all_parts, 'tile', [(i, i ^ 8) for i in range(N_TILE)])]
    all_to_all x2, blocking collectives: 19.4 us -> 32 us  [exchange(): got = lax.all_to_all(send, 'sub', split_axis=0, concat_axis=0, tiled=True)]
    ppermute x6 -> x0, starting transfers between devices: 11.9 us -> none  [the longest x2 5.23 us: exchange(): lax.ppermute(last_row, 'sub', [(i, i + 1) for i in range(N_SUB - 1)])]
    pallas_call x1, Pallas kernels: 12.8 us -> 5.21 us  [last_step(): pl.pallas_call(last_kernel, out_shape=(f32(PLANES, ROWS, COLS), BIG[1]),...]
    pallas_call x1, Pallas kernels: 11.1 us -> 6.34 us  [second_solve(): pl.pallas_call(second_kernel, out_shape=BIG + EDGES + BIG[1:], in_specs=[...]
    ppermute x6, waiting for transfers between devices: 10.5 us -> 6.71 us  [exchange(): lax.ppermute(all_parts, 'tile', turn(k))]
    pallas_call x2, Pallas kernels: 10.7 us -> 8.58 us  [forcing(): pl.pallas_call(functools.partial(forcing_kernel, moment), out_shape=f32(P...]
  transfers between devices with their start and end apart: 16 -> 10, of which waited for: 14 -> 9; matrix products, arithmetic and copies ran while one was open for 0% -> 0% of each run, Pallas kernels for 4% -> 4%
where the time goes in v3:
time: 120 us; the launch traced here: 119 us
  blocking collectives  52.6 us (44%)
  Pallas kernels  27.3 us (23%)
  waiting for transfers between devices  27.1 us (23%)
  starting transfers between devices  9.6 us (8%)
  local copies, waits for them, and re-layouts  2.31 us (2%)
    all_to_all x2, blocking collectives, exchange(): got = lax.all_to_all(send, 'sub', split_axis=0, concat_axis=0, tiled=True)  32 us
    all_to_all x1, blocking collectives, body(): lax.all_to_all(slots, ('tile', 'sub'), split_axis=0, concat_axis=0, tiled...  20.6 us
    ppermute x2, waiting for transfers between devices, exchange(): lax.ppermute(all_parts, 'tile', [(i, i ^ 8) for i in range(N_TILE)])  16.2 us
    pallas_call x2, Pallas kernels, forcing(): pl.pallas_call(functools.partial(forcing_kernel, moment), out_shape=f32(P...  8.58 us
    ppermute x6, waiting for transfers between devices, exchange(): lax.ppermute(all_parts, 'tile', turn(k))  6.71 us
    pallas_call x1, Pallas kernels, second_solve(): pl.pallas_call(second_kernel, out_shape=BIG + EDGES + BIG[1:], in_specs=[...  6.34 us
    ppermute x6, starting transfers between devices, exchange(): lax.ppermute(all_parts, 'tile', turn(k))  6.19 us
    pallas_call x1, Pallas kernels, last_step(): pl.pallas_call(last_kernel, out_shape=(f32(PLANES, ROWS, COLS), BIG[1]),...  5.21 us
  transfers between devices with their start and end apart: 10, of which 9 were waited for; matrix products, arithmetic and copies ran while one was open for 0% of the time, Pallas kernels for 4%

profile of v3, /device:TPU:0, one launch (start us, length us, event | category | flops | bytes accessed | tf_op | source)
XLA Modules:
  0.0 119.3 jit_solution(4973404773275359825)
XLA Ops:
  0.0 0.0 copy-start.3
  0.0 2.4 %pack.1 = (f32[128,2,128]{2,1,0:T(2,128)}, s32[16]{0:T(128)}) custom-call(s32[16]{0:T(128)} %owner_in.1, s32[3,4,16]{2,1,0:T(4,128)} %bitcast.28, s32[1,256]{1,0:T(1,128)} %bitcast.29, s32[1,256]{1,0:T(1,128)} %bitcast.30, s32[1,256]{1,0:T(1,128)} %bitcast.31, f32[32,256]{1,0:T(8,128)} %bitcast.27), custom_call_target="tpu_custom_call" | custom-call | tf_op jit(solution)/shard_map/pack/pallas_call | solution.py:126
  2.4 0.0 copy-start
  2.4 0.0 copy-start.1
  2.4 0.0 copy-start.4
  2.4 20.6 %all_to_all.15.slots = f32[128,2,128]{2,1,0:T(2,128)S(1)} all-to-all(f32[128,2,128]{2,1,0:T(2,128)} %get-tuple-element.25), channel_id=1, replica_groups=mesh['tile'=16,'sub'=8] {'tile','sub'}, dimensions={0} | all-to-all | bytes 262144 | tf_op jit(solution)/shard_map/all_to_all | solution.py:569
  23.1 4.3 %forcing_1.1.force = f32[2048,512]{1,0:T(8,128)S(1)} custom-call(f32[128,2,128]{2,1,0:T(2,128)S(1)} %all_to_all.15.slots), custom_call_target="tpu_custom_call" | custom-call | flops 2147483648 | bytes 4325376 | tf_op jit(solution)/shard_map/forcing_1/pallas_call | solution.py:183
  27.4 0.0 copy-done.3
  27.4 0.0 copy-done
  27.4 0.0 copy-done.1
  27.4 0.0 copy-done.4
  27.4 0.0 copy-start.2
  27.4 2.2 %copy-done.2 = f32[2,16,64,512]{3,2,1,0:T(8,128)S(1)} copy-done((f32[2,16,64,512]{3,2,1,0:T(8,128)S(1)}, f32[2,16,64,512]{3,2,1,0:T(8,128)}, u32[]{:S(2)}) %copy-start.2) | copy-done | bytes 4194328
  29.6 3.4 %first_solve.1 = (f32[8192,128]{1,0:T(8,128)S(1)}, f32[10240,128]{1,0:T(8,128)S(1)}, f32[5,32,128]{2,1,0:T(8,128)S(1)}, f32[4,32,128]{2,1,0:T(8,128)S(1)}, f32[4,32,128]{2,1,0:T(8,128)S(1)}) custom-call(s32[16]{0:T(128)S(1)} %copy-done.4, f32[2048,512]{1,0:T(8,128)S(1)} %bitcast.18, f32[2048,512]{1,0:T(8,128)S(1)} %forcing_1.1.force, ...), custom_call_target="tpu_custom_call" | custom-call | flops 30000000 | bytes 20000000 | tf_op jit(solution)/shard_map/first_solve/pallas_call | solution.py:305
  33.0 0.7 collective-permute-start.2
  33.7 2.0 %collective-permute-start.1 = (f32[1,5,32,128]{3,2,1,0:T(8,128)S(1)}, f32[1,5,32,128]{3,2,1,0:T(8,128)S(1)}, u32[]{:S(2)}, u32[]{:S(2)}) collective-permute-start(f32[1,5,32,128]{3,2,1,0:T(8,128)S(1)} %bitcast.24), channel_id=1, source_target_pairs={{0,32},{8,40},{16,48},{24,56},{32,0},{40,8},{48,16},{56,24},{64,96... | collective-permute-start | bytes 245768 | tf_op jit(solution)/shard_map/ppermute | solution.py:378
  35.7 0.1 collective-permute-start
  35.8 4.3 %forcing_0.1.force = f32[2048,512]{1,0:T(8,128)S(1)} custom-call(f32[128,2,128]{2,1,0:T(2,128)S(1)} %all_to_all.15.slots), custom_call_target="tpu_custom_call" | custom-call | flops 2147483648 | bytes 4325376 | tf_op jit(solution)/shard_map/forcing_0/pallas_call | solution.py:183
  40.1 0.0 collective-permute-done.2
  40.1 0.2 collective-permute-done.1
  40.4 1.0 collective-permute-done
  41.4 1.5 %collective-permute-start.3 = (f32[4,5,32,128]{3,2,1,0:T(8,128)S(1)}, f32[4,5,32,128]{3,2,1,0:T(8,128)S(1)}, u32[]{:S(2)}, u32[]{:S(2)}) collective-permute-start(f32[4,5,32,128]{3,2,1,0:T(8,128)S(1)} %pad_maximum_fusion.2), channel_id=1, source_target_pairs={{0,64},{8,72},{16,80},{24,88},{32,96},{40,104},{48,112},{56,120},{... | collective-permute-start | bytes 983048 | tf_op jit(solution)/shard_map/ppermute | solution.py:381
  43.0 8.7 %collective-permute-done.3 = f32[4,5,32,128]{3,2,1,0:T(8,128)S(1)} collective-permute-done((f32[4,5,32,128]{3,2,1,0:T(8,128)S(1)}, f32[4,5,32,128]{3,2,1,0:T(8,128)S(1)}, u32[]{:S(2)}, u32[]{:S(2)}) %collective-permute-start.3) | collective-permute-done | bytes 327712 | tf_op jit(solution)/shard_map/ppermute | solution.py:381
  51.7 0.1 collective-permute-start.4
  51.8 2.1 %collective-permute-done.4 = f32[8,5,32,128]{3,2,1,0:T(8,128)S(1)} collective-permute-done((f32[8,5,32,128]{3,2,1,0:T(8,128)S(1)}, f32[8,5,32,128]{3,2,1,0:T(8,128)S(1)}, u32[]{:S(2)}, u32[]{:S(2)}) %collective-permute-start.4) | collective-permute-done | bytes 655392 | tf_op jit(solution)/shard_map/ppermute | solution.py:386
  53.9 0.1 pad_maximum_fusion.gathered
  54.0 0.7 route.2
  54.7 16.0 %all_to_all.16.got = f32[8,6,32,128]{3,2,1,0:T(8,128)S(1)} all-to-all(f32[8,6,32,128]{3,2,1,0:T(8,128)S(1)} %get-tuple-element.30), channel_id=1, replica_groups=mesh['tile'=16,'sub'=8] {'sub'}, dimensions={0} | all-to-all | bytes 1572864 | tf_op jit(solution)/shard_map/all_to_all | solution.py:389
  70.7 6.3 %second_solve.1 = (f32[8192,128]{1,0:T(8,128)S(1)}, f32[10240,128]{1,0:T(8,128)S(1)}, f32[5,32,128]{2,1,0:T(8,128)S(1)}, f32[4,32,128]{2,1,0:T(8,128)S(1)}, f32[...) custom-call(s32[16]{0:T(128)S(1)} %copy-done.4, ...), custom_call_target="tpu_custom_call", output_to_operand_aliasing={{5}: (4, {})} | custom-call | flops 50000000 | bytes 30000000 | tf_op jit(solution)/shard_map/second_solve/pallas_call | solution.py:491
  77.0 1.9 %collective-permute-start.7 = (f32[1,5,32,128]{3,2,1,0:T(8,128)S(1)}, f32[1,5,32,128]{3,2,1,0:T(8,128)S(1)}, u32[]{:S(2)}, u32[]{:S(2)}) collective-permute-start(f32[1,5,32,128]{3,2,1,0:T(8,128)S(1)} %bitcast.19), channel_id=1, source_target_pairs={{0,48},{8,56},{16,0},{24,8},{32,16},{40,24},{48,32},{56,40},{64,11... | collective-permute-start | bytes 245768 | tf_op jit(solution)/shard_map/ppermute | solution.py:378
  78.9 0.3 collective-permute-start.6
  79.3 1.1 collective-permute-start.5
  80.4 1.9 %collective-permute-done.7 = f32[1,5,32,128]{3,2,1,0:T(8,128)S(1)} collective-permute-done((f32[1,5,32,128]{3,2,1,0:T(8,128)S(1)}, f32[1,5,32,128]{3,2,1,0:T(8,128)S(1)}, u32[]{:S(2)}, u32[]{:S(2)}) %collective-permute-start.7) | collective-permute-done | bytes 81952 | tf_op jit(solution)/shard_map/ppermute | solution.py:378
  82.3 2.9 %collective-permute-done.6 = f32[1,5,32,128]{3,2,1,0:T(8,128)S(1)} collective-permute-done((f32[1,5,32,128]{3,2,1,0:T(8,128)S(1)}, f32[1,5,32,128]{3,2,1,0:T(8,128)S(1)}, u32[]{:S(2)}, u32[]{:S(2)}) %collective-permute-start.6) | collective-permute-done | bytes 81952 | tf_op jit(solution)/shard_map/ppermute | solution.py:378
  85.1 0.7 collective-permute-done.5
  85.8 1.7 %collective-permute-start.8 = (f32[4,5,32,128]{3,2,1,0:T(8,128)S(1)}, f32[4,5,32,128]{3,2,1,0:T(8,128)S(1)}, u32[]{:S(2)}, u32[]{:S(2)}) collective-permute-start(f32[4,5,32,128]{3,2,1,0:T(8,128)S(1)} %pad_maximum_fusion.3), channel_id=1, source_target_pairs={{0,64},{8,72},{16,80},{24,88},{32,96},{40,104},{48,112},{56,120},{... | collective-permute-start | bytes 983048 | tf_op jit(solution)/shard_map/ppermute | solution.py:381
  87.6 7.5 %collective-permute-done.8 = f32[4,5,32,128]{3,2,1,0:T(8,128)S(1)} collective-permute-done((f32[4,5,32,128]{3,2,1,0:T(8,128)S(1)}, f32[4,5,32,128]{3,2,1,0:T(8,128)S(1)}, u32[]{:S(2)}, u32[]{:S(2)}) %collective-permute-start.8) | collective-permute-done | bytes 327712 | tf_op jit(solution)/shard_map/ppermute | solution.py:381
  95.1 0.1 collective-permute-start.9
  95.2 2.1 %collective-permute-done.9 = f32[8,5,32,128]{3,2,1,0:T(8,128)S(1)} collective-permute-done((f32[8,5,32,128]{3,2,1,0:T(8,128)S(1)}, f32[8,5,32,128]{3,2,1,0:T(8,128)S(1)}, u32[]{:S(2)}, u32[]{:S(2)}) %collective-permute-start.9) | collective-permute-done | bytes 655392 | tf_op jit(solution)/shard_map/ppermute | solution.py:386
  97.3 0.1 pad_maximum_fusion.1.gathered
  97.4 0.7 route.3
  98.1 16.0 %all_to_all.17.got = f32[8,6,32,128]{3,2,1,0:T(8,128)S(1)} all-to-all(f32[8,6,32,128]{3,2,1,0:T(8,128)S(1)} %get-tuple-element.38), channel_id=1, replica_groups=mesh['tile'=16,'sub'=8] {'sub'}, dimensions={0} | all-to-all | bytes 1572864 | tf_op jit(solution)/shard_map/all_to_all | solution.py:389
  114.1 5.2 %last_step.1 = (f32[32,64,512]{2,1,0:T(8,128)}, f32[10240,128]{1,0:T(8,128)S(1)}) custom-call(s32[16]{0:T(128)S(1)} %copy-done.4, f32[8,6,32,128]{3,2,1,0:T(8,128)S(1)} %all_to_all.17.got, f32[4,32,128]{2,1,0:T(8,128)S(1)} %get-tuple-element.39.here, f32[8192,128]{1,0:T(8,128)S(1)} %get-tuple-element.40.solved, ...), custom_call_target="tpu_custom_call", output_to_operand_aliasing={{1}: (4, {})} | custom-call | flops 20000000 | bytes 20000000 | tf_op jit(solution)/shard_map/last_step/pallas_call | solution.py:531
  (12 shorter events, 0.1 us)
Async XLA Ops:
  0.0 27.4 %copy-start.3 = (s32[64,512]{1,0:T(8,128)S(1)}, s32[64,512]{1,0:T(8,128)}, u32[]{:S(2)}) copy-start(s32[64,512]{1,0:T(8,128)} %depth.5) | copy-start | bytes 393220
  2.4 25.0 %copy-start = (f32[16,64,512]{2,1,0:T(8,128)S(1)}, f32[16,64,512]{2,1,0:T(8,128)}, u32[]{:S(2)}) copy-start(f32[16,64,512]{2,1,0:T(8,128)} %param.11) | copy-start | bytes 6291460
  2.4 25.0 %copy-start.1 = (f32[15,64,512]{2,1,0:T(8,128)S(1)}, f32[15,64,512]{2,1,0:T(8,128)}, u32[]{:S(2)}) copy-start(f32[15,64,512]{2,1,0:T(8,128)} %param.12) | copy-start | bytes 5898244
  2.4 25.0 %copy-start.4 = (s32[16]{0:T(128)S(1)}, s32[16]{0:T(128)}, u32[]{:S(2)}) copy-start(s32[16]{0:T(128)} %get-tuple-element.24.meta) | copy-start | bytes 196
  27.4 2.2 %copy-start.2 = (f32[2,16,64,512]{3,2,1,0:T(8,128)S(1)}, f32[2,16,64,512]{3,2,1,0:T(8,128)}, u32[]{:S(2)}) copy-start(f32[2,16,64,512]{3,2,1,0:T(8,128)} %param.10) | copy-start | bytes 12582916
  33.0 7.1 %collective-permute-start.2 = (f32[1,5,32,128]{3,2,1,0:T(8,128)S(1)}, f32[1,5,32,128]{3,2,1,0:T(8,128)S(1)}, u32[]{:S(2)}, u32[]{:S(2)}) collective-permute-start(f32[1,5,32,128]{3,2,1,0:T(8,128)S(1)} %bitcast.23), channel_id=1, source_target_pairs={{0,48},{8,56},{16,0},{24,8},{32,16},{40,24},{48,32},{56,40},{64,11... | collective-permute-start | bytes 245768 | tf_op jit(solution)/shard_map/ppermute | solution.py:378
  33.7 6.7 %collective-permute-start.1 = (f32[1,5,32,128]{3,2,1,0:T(8,128)S(1)}, f32[1,5,32,128]{3,2,1,0:T(8,128)S(1)}, u32[]{:S(2)}, u32[]{:S(2)}) collective-permute-start(f32[1,5,32,128]{3,2,1,0:T(8,128)S(1)} %bitcast.24), channel_id=1, source_target_pairs={{0,32},{8,40},{16,48},{24,56},{32,0},{40,8},{48,16},{56,24},{64,96... | collective-permute-start | bytes 245768 | tf_op jit(solution)/shard_map/ppermute | solution.py:378
  35.7 5.7 %collective-permute-start = (f32[1,5,32,128]{3,2,1,0:T(8,128)S(1)}, f32[1,5,32,128]{3,2,1,0:T(8,128)S(1)}, u32[]{:S(2)}, u32[]{:S(2)}) collective-permute-start(f32[1,5,32,128]{3,2,1,0:T(8,128)S(1)} %bitcast.25), channel_id=1, source_target_pairs={{0,16},{8,24},{16,32},{24,40},{32,48},{40,56},{48,0},{56,8},{64,80... | collective-permute-start | bytes 245768 | tf_op jit(solution)/shard_map/ppermute | solution.py:378
  41.4 10.3 %collective-permute-start.3 = (f32[4,5,32,128]{3,2,1,0:T(8,128)S(1)}, f32[4,5,32,128]{3,2,1,0:T(8,128)S(1)}, u32[]{:S(2)}, u32[]{:S(2)}) collective-permute-start(f32[4,5,32,128]{3,2,1,0:T(8,128)S(1)} %pad_maximum_fusion.2), channel_id=1, source_target_pairs={{0,64},{8,72},{16,80},{24,88},{32,96},{40,104},{48,112},{56,120},{... | collective-permute-start | bytes 983048 | tf_op jit(solution)/shard_map/ppermute | solution.py:381
  51.7 2.2 %collective-permute-start.4 = (f32[8,5,32,128]{3,2,1,0:T(8,128)S(1)}, f32[8,5,32,128]{3,2,1,0:T(8,128)S(1)}, u32[]{:S(2)}, u32[]{:S(2)}) collective-permute-start(f32[8,5,32,128]{3,2,1,0:T(8,128)S(1)} %constant_dynamic-update-slice_fusion), channel_id=1, source_target_pairs={{0,8},{8,0},{16,24},{24,16},{32,40},{40,32},{48,56},{56,48},{64,72... | collective-permute-start | bytes 1966088 | tf_op jit(solution)/shard_map/ppermute | solution.py:386
  77.0 5.3 %collective-permute-start.7 = (f32[1,5,32,128]{3,2,1,0:T(8,128)S(1)}, f32[1,5,32,128]{3,2,1,0:T(8,128)S(1)}, u32[]{:S(2)}, u32[]{:S(2)}) collective-permute-start(f32[1,5,32,128]{3,2,1,0:T(8,128)S(1)} %bitcast.19), channel_id=1, source_target_pairs={{0,48},{8,56},{16,0},{24,8},{32,16},{40,24},{48,32},{56,40},{64,11... | collective-permute-start | bytes 245768 | tf_op jit(solution)/shard_map/ppermute | solution.py:378
  78.9 6.2 %collective-permute-start.6 = (f32[1,5,32,128]{3,2,1,0:T(8,128)S(1)}, f32[1,5,32,128]{3,2,1,0:T(8,128)S(1)}, u32[]{:S(2)}, u32[]{:S(2)}) collective-permute-start(f32[1,5,32,128]{3,2,1,0:T(8,128)S(1)} %bitcast.20), channel_id=1, source_target_pairs={{0,32},{8,40},{16,48},{24,56},{32,0},{40,8},{48,16},{56,24},{64,96... | collective-permute-start | bytes 245768 | tf_op jit(solution)/shard_map/ppermute | solution.py:378
  79.3 6.5 %collective-permute-start.5 = (f32[1,5,32,128]{3,2,1,0:T(8,128)S(1)}, f32[1,5,32,128]{3,2,1,0:T(8,128)S(1)}, u32[]{:S(2)}, u32[]{:S(2)}) collective-permute-start(f32[1,5,32,128]{3,2,1,0:T(8,128)S(1)} %bitcast.21), channel_id=1, source_target_pairs={{0,16},{8,24},{16,32},{24,40},{32,48},{40,56},{48,0},{56,8},{64,80... | collective-permute-start | bytes 245768 | tf_op jit(solution)/shard_map/ppermute | solution.py:378
  85.8 9.2 %collective-permute-start.8 = (f32[4,5,32,128]{3,2,1,0:T(8,128)S(1)}, f32[4,5,32,128]{3,2,1,0:T(8,128)S(1)}, u32[]{:S(2)}, u32[]{:S(2)}) collective-permute-start(f32[4,5,32,128]{3,2,1,0:T(8,128)S(1)} %pad_maximum_fusion.3), channel_id=1, source_target_pairs={{0,64},{8,72},{16,80},{24,88},{32,96},{40,104},{48,112},{56,120},{... | collective-permute-start | bytes 983048 | tf_op jit(solution)/shard_map/ppermute | solution.py:381
  95.1 2.2 %collective-permute-start.9 = (f32[8,5,32,128]{3,2,1,0:T(8,128)S(1)}, f32[8,5,32,128]{3,2,1,0:T(8,128)S(1)}, u32[]{:S(2)}, u32[]{:S(2)}) collective-permute-start(f32[8,5,32,128]{3,2,1,0:T(8,128)S(1)} %constant_dynamic-update-slice_fusion.5), channel_id=1, source_target_pairs={{0,8},{8,0},{16,24},{24,16},{32,40},{40,32},{48,56},{56,48},{64,72... | collective-permute-start | bytes 1966088 | tf_op jit(solution)/shard_map/ppermute | solution.py:386

commit v4 on v3

--- a/solution.py
+++ b/solution.py
@@ -142,15 +142,13 @@
     )(owner, seam, face, cell, time, misfit)
 
 
-def forcing_kernel(moment, slots, out, parts, place):
+def read_slots(moment, slots, parts, place):
     values = jnp.transpose(slots[:, 0, :])
     tags = (slots[:, 1, :] + 0.5).astype(jnp.int32)
     tags = jnp.where(slots[:, 1, :] < 0.0, -1, tags)
     tags_t = jnp.transpose(tags.astype(jnp.float32)).astype(jnp.int32)
     tag_row = jnp.concatenate([tags_t[k : k + 1, :] for k in range(CAP)], axis=1)
     valid = (tag_row >= moment * CELLS) & (tag_row < (moment + 1) * CELLS)
-    row_of = jnp.where(valid, (tag_row & (CELLS - 1)) >> 9, -1)
-    on_row = iota((ROWS, CAP * DEVICES), 0) == row_of
     wide = jnp.concatenate([values[PLANES * k : PLANES * (k + 1), :] for k in range(CAP)], axis=1)
     high = wide.astype(jnp.bfloat16).astype(jnp.float32)
     parts[0] = high
@@ -160,23 +158,40 @@
         place[k * DEVICES : (k + 1) * DEVICES, :] = jnp.where(
             iota((DEVICES, COLS), 1) == col, 1.0, 0.0
         ).astype(jnp.bfloat16)
+    return jnp.where(valid, (tag_row & (CELLS - 1)) >> 9, -1)
+
+
+def place_rows(on_row, planes, parts, place):
+    total = None
+    for part in range(PARTS):
+        left = [jnp.where(on_row, parts[part, p, :], 0.0) for p in planes]
+        got = jnp.dot(
+            jnp.concatenate(left, axis=0).astype(jnp.bfloat16),
+            place[...],
+            preferred_element_type=jnp.float32,
+        )
+        total = got if total is None else total + got
+    return total
+
+
+def forcing_kernel(moment, slots, out, parts, place):
+    row_of = read_slots(moment, slots, parts, place)
+    on_row = iota((ROWS, CAP * DEVICES), 0) == row_of
     group = 4
 
     def step(g, carry):
-        total = None
-        for part in range(PARTS):
-            left = []
-            for q in range(group):
-                row = parts[part, pl.ds(g * group + q, 1), :]
-                left.append(jnp.where(on_row, row, 0.0).astype(jnp.bfloat16))
-            got = jnp.dot(
-                jnp.concatenate(left, axis=0), place[...], preferred_element_type=jnp.float32
-            )
-            total = got if total is None else total + got
-        out[pl.ds(pl.multiple_of(g * group * ROWS, 8), group * ROWS), :] = total
+        planes = [pl.ds(g * group + q, 1) for q in range(group)]
+        rows = pl.ds(pl.multiple_of(g * group * ROWS, 8), group * ROWS)
+        out[rows, :] = place_rows(on_row, planes, parts, place)
         return carry
 
     lax.fori_loop(0, PLANES // group, step, 0)
+
+
+SLOT_SCRATCH = [
+    pltpu.VMEM((PARTS, PLANES, CAP * DEVICES), jnp.float32),
+    pltpu.VMEM((CAP * DEVICES, COLS), jnp.bfloat16),
+]
 
 
 def forcing(slots, moment):
@@ -185,10 +200,7 @@
         out_shape=f32(PLANES * ROWS, COLS),
         in_specs=[VMEM],
         out_specs=VMEM,
-        scratch_shapes=[
-            pltpu.VMEM((PARTS, PLANES, CAP * DEVICES), jnp.float32),
-            pltpu.VMEM((CAP * DEVICES, COLS), jnp.bfloat16),
-        ],
+        scratch_shapes=SLOT_SCRATCH,
         compiler_params=params(8),
         cost_estimate=pl.CostEstimate(flops=2147483648, bytes_accessed=4325376, transcendentals=0),
         name=f"forcing_{moment}",
@@ -243,8 +255,8 @@
 def solve_tile(value, coupling, scale, depth_ref, solved, weighted, sides, block, quarter):
     columns = slice(quarter * 128, (quarter + 1) * 128)
 
-    def at(plane):
-        return (pl.ds(pl.multiple_of(plane * ROWS + block * 8, 8), 8), columns)
+    def at(level):
+        return (level, pl.ds(pl.multiple_of(block * 8, 8), 8), columns)
 
     depth = depth_ref[pl.ds(pl.multiple_of(block * 8, 8), 8), columns]
     result = eliminate(value, coupling, depth, at)
@@ -269,8 +281,7 @@
         sides[pl.ds(pl.multiple_of(ROWS + block * 8, 8), 8), :] = column
 
 
-def send_edges(meta, weighted, sides, payload, first_row, last_row):
-    sub = meta[13]
+def send_edges(sub, weighted, sides, payload, first_row, last_row):
     payload[0] = jnp.transpose(sides[...])[:PLANES, :]
     for b in range(4):
         top = weighted[pl.ds(b * PLANES * PITCH + 8, PLANES, stride=PITCH), :]
@@ -284,34 +295,109 @@
 EDGES = (f32(5, PLANES, 128), f32(4, PLANES, 128), f32(4, PLANES, 128))
 
 
-def first_kernel(meta, adjoint, force, coupling, scale, depth, solved, weighted, payload,
-                 first_row, last_row, sides):
-    def step(block, carry):
+def first_kernel(slots, adjoint_in, coupling_in, scale_in, depth_in, solved_out, weighted_out,
+                 payload, first_row, last_row, solved, weighted, sides, parts, place, adjoint, coupling, scale, depth,
+                 even, odd, sems, depth_sem, out_sems):
+    blocks = ROWS // 8
+
+    def results(block):
+        rows = pl.ds(pl.multiple_of(block * 8, 8), 8)
+        wide = pl.ds(pl.multiple_of(block * 8 + 8, 8), 8)
+        whole = weighted.reshape(4 * PLANES, PITCH, 128)
+        return [
+            pltpu.make_async_copy(
+                solved.reshape(4 * PLANES, ROWS, 128).at[:, rows, :],
+                solved_out.at[:, rows, :],
+                out_sems.at[0, block],
+            ),
+            pltpu.make_async_copy(
+                whole.at[:, wide, :], weighted_out.at[:, wide, :], out_sems.at[1, block]
+            ),
+        ]
+
+    def copies(block):
+        rows = pl.ds(pl.multiple_of(block * 8, 8), 8)
+        return [
+            pltpu.make_async_copy(source.at[:, rows, :], target.at[:, rows, :], sems.at[i, block])
+            for i, (source, target) in enumerate(
+                ((adjoint_in, adjoint), (coupling_in, coupling), (scale_in, scale))
+            )
+        ]
+
+    depth_copy = pltpu.make_async_copy(depth_in, depth, depth_sem)
+    depth_copy.start()
+    for block in range(blocks):
+        for copy in copies(block):
+            copy.start()
+    row_of = read_slots(1, slots, parts, place)
+    planes = [slice(p, p + 1) for p in range(PLANES)]
+
+    def force(block, target):
+        on_row = iota((8, CAP * DEVICES), 0) + block * 8 == row_of
+        target[...] = place_rows(on_row, planes, parts, place)
+
+    def solve(block, source):
         for quarter in range(4):
             columns = slice(quarter * 128, (quarter + 1) * 128)
 
             def value(plane):
-                at = (pl.ds(pl.multiple_of(plane * ROWS + block * 8, 8), 8), columns)
-                return adjoint[at] + force[at]
+                rows = pl.ds(pl.multiple_of(block * 8, 8), 8)
+                return adjoint[plane, rows, columns] + source[plane * 8 : plane * 8 + 8, columns]
 
             solve_tile(value, coupling, scale, depth, solved, weighted, sides, block, quarter)
+        for copy in results(block):
+            copy.start()
+
+    force(0, even)
+    depth_copy.wait()
+
+    def step(pair, carry):
+        block = pair * 2
+        for copy in copies(block) + copies(block + 1):
+            copy.wait()
+        force(block + 1, odd)
+        solve(block, even)
+        force(jnp.minimum(block + 2, blocks - 1), even)
+        solve(block + 1, odd)
         return carry
 
-    lax.fori_loop(0, ROWS // 8, step, 0)
-    send_edges(meta, weighted, sides, payload, first_row, last_row)
-
-
-def first_solve(meta, adjoint, force, coupling, scale, depth):
-    return pl.pallas_call(
+    lax.fori_loop(0, blocks // 2, step, 0)
+    send_edges(lax.axis_index("sub"), weighted, sides, payload, first_row, last_row)
+    for block in range(blocks):
+        for copy in results(block):
+            copy.wait()
+
+
+def first_solve(slots, adjoint, coupling, scale, depth):
+    force = pltpu.VMEM((PLANES * 8, COLS), jnp.float32)
+    plain = pl.BlockSpec(memory_space=pl.ANY)
+    solved, weighted, *edges = pl.pallas_call(
         first_kernel,
-        out_shape=BIG + EDGES,
-        in_specs=[SMEM] + [VMEM] * 5,
-        out_specs=(VMEM,) * 5,
-        scratch_shapes=[pltpu.VMEM((128, 128), jnp.float32)],
-        compiler_params=params(8),
-        cost_estimate=pl.CostEstimate(flops=30000000, bytes_accessed=20000000, transcendentals=0),
+        out_shape=(f32(4 * PLANES, ROWS, 128), f32(4 * PLANES, PITCH, 128)) + EDGES,
+        in_specs=[VMEM] + [plain] * 4,
+        out_specs=(plain, plain, VMEM, VMEM, VMEM),
+        scratch_shapes=[
+            pltpu.VMEM(BIG[0].shape, jnp.float32),
+            pltpu.VMEM(BIG[1].shape, jnp.float32),
+            pltpu.VMEM((128, 128), jnp.float32),
+            *SLOT_SCRATCH,
+            pltpu.VMEM(adjoint.shape, jnp.float32),
+            pltpu.VMEM(coupling.shape, jnp.float32),
+            pltpu.VMEM(scale.shape, jnp.float32),
+            pltpu.VMEM(depth.shape, jnp.int32),
+            force,
+            force,
+            pltpu.SemaphoreType.DMA((3, ROWS // 8)),
+            pltpu.SemaphoreType.DMA,
+            pltpu.SemaphoreType.DMA((2, ROWS // 8)),
+        ],
+        compiler_params=params(62),
+        cost_estimate=pl.CostEstimate(
+            flops=2200000000, bytes_accessed=20000000, transcendentals=0
+        ),
         name="first_solve",
-    )(meta, adjoint, force, coupling, scale, depth)
+    )(slots, adjoint, coupling, scale, depth)
+    return solved.reshape(BIG[0].shape), weighted.reshape(BIG[1].shape), *edges
 
 
 def route_kernel(meta, gathered, first_row, last_row, send, here):
@@ -377,9 +463,16 @@
     all_parts = jnp.concatenate(
         [all_parts] + [lax.ppermute(all_parts, "tile", turn(k)) for k in (1, 2, 3)], axis=0
     )
-    all_parts = jnp.concatenate(
-        [all_parts, lax.ppermute(all_parts, "tile", [(i, i ^ 8) for i in range(N_TILE)])], axis=0
-    )
+    across_y = [(i, i ^ 8) for i in range(N_TILE)]
+    across_y_rows = [(i * N_SUB + s, j * N_SUB + s) for i, j in across_y for s in (0, N_SUB - 1)]
+    others = jnp.concatenate(
+        [
+            lax.ppermute(all_parts[:, 1:], ("tile", "sub"), across_y_rows),
+            lax.ppermute(all_parts[:, :1], "tile", across_y),
+        ][::-1],
+        axis=1,
+    )
+    all_parts = jnp.concatenate([all_parts, others], axis=0)
     extra = () if beside is None else (beside(),)
     all_parts, *extra = lax.optimization_barrier((all_parts, *extra))
     all_parts = jnp.concatenate(
@@ -442,8 +535,8 @@
     def value(plane):
         level = plane % LEVELS
         if level not in weights:
-            at = pl.ds(pl.multiple_of(level * ROWS + block * 8, 8), 8)
-            weights[level] = jnp.where(level < depth, scale[at, columns], 0.0) * explicit_rate
+            weights[level] = jnp.where(level < depth, scale[level, here, columns], 0.0)
+            weights[level] = weights[level] * explicit_rate
         center = weighted[wide_rows(quarter, plane, block), :]
         total = weighted[wide_rows(quarter, plane, block, -1), :]
         total = total + weighted[wide_rows(quarter, plane, block, 1), :]
@@ -484,7 +577,7 @@
         return carry
 
     lax.fori_loop(0, ROWS // 8, step, 0)
-    send_edges(meta, weighted, sides, payload, first_row, last_row)
+    send_edges(meta[13], weighted, sides, payload, first_row, last_row)
 
 
 def second_solve(meta, halos, solved, weighted, force, coupling, scale, depth):
@@ -567,11 +660,9 @@
         misfit.reshape(PLANES, rows),
     )
     slots = lax.all_to_all(slots, ("tile", "sub"), split_axis=0, concat_axis=0, tiled=True)
-    adjoint = adjoint_final.reshape(PLANES * ROWS, COLS)
-    scale = diff_scale.reshape(LEVELS * ROWS, COLS)
-    coupling = vert_coupling.reshape((LEVELS - 1) * ROWS, COLS)
-    late = forcing(slots, 1)
-    solved, weighted, *edges = first_solve(meta, adjoint, late, coupling, scale, column_depth)
+    adjoint = adjoint_final.reshape(PLANES, ROWS, COLS)
+    scale, coupling = diff_scale, vert_coupling
+    solved, weighted, *edges = first_solve(slots, adjoint, coupling, scale, column_depth)
     halos, (early,) = exchange(meta, *edges, lambda: forcing(slots, 0))
     solved, weighted, *edges, _ = second_solve(
         meta, halos, solved, weighted, early, coupling, scale, column_depth

time: 120 us -> 127 us (1.058)
  starting transfers between devices: 9.6 us -> 18.2 us
  waiting for transfers between devices: 27.1 us -> 22.7 us
  Pallas kernels: 27.3 us -> 30.1 us
    ppermute x2 -> x4, starting transfers between devices: 3.23 us -> 11 us  [the longest x2 7.04 us: exchange(): lax.ppermute(all_parts[:, 1:], ('tile', 'sub'), across_y_rows)]
    pallas_call x1, Pallas kernels: 3.38 us -> 10.5 us  [first_solve(): pl.pallas_call(first_kernel, out_shape=(f32(4 * PLANES, ROWS, 128), f32(4...]
    pallas_call x2 -> x1, Pallas kernels: 8.58 us -> 4.29 us  [forcing(): pl.pallas_call(functools.partial(forcing_kernel, moment), out_shape=f32(P...]
    ppermute x2 -> x4, waiting for transfers between devices: 16.2 us -> 12.8 us  [the longest x2 11.9 us: exchange(): lax.ppermute(all_parts[:, 1:], ('tile', 'sub'), across_y_rows)]
  transfers between devices with their start and end apart: 10 -> 12, of which waited for: 9 -> 10; matrix products, arithmetic and copies ran while one was open for 0% -> 1% of each run, Pallas kernels for 4% -> 3%
where the time goes in v4:
time: 127 us; the launch traced here: 126 us
  blocking collectives  53.3 us (42%)
  Pallas kernels  30.1 us (24%)
  waiting for transfers between devices  22.7 us (18%)
  starting transfers between devices  18.2 us (14%)
    all_to_all x2, blocking collectives, exchange(): got = lax.all_to_all(send, 'sub', split_axis=0, concat_axis=0, tiled=True)  32.3 us
    all_to_all x1, blocking collectives, body(): lax.all_to_all(slots, ('tile', 'sub'), split_axis=0, concat_axis=0, tiled...  21 us
    ppermute x2, waiting for transfers between devices, exchange(): lax.ppermute(all_parts[:, 1:], ('tile', 'sub'), across_y_rows)  11.9 us
    pallas_call x1, Pallas kernels, first_solve(): pl.pallas_call(first_kernel, out_shape=(f32(4 * PLANES, ROWS, 128), f32(4...  10.5 us
    ppermute x6, starting transfers between devices, exchange(): lax.ppermute(all_parts, 'tile', turn(k))  7.07 us
    ppermute x2, starting transfers between devices, exchange(): lax.ppermute(all_parts[:, 1:], ('tile', 'sub'), across_y_rows)  7.04 us
    pallas_call x1, Pallas kernels, second_solve(): pl.pallas_call(second_kernel, out_shape=BIG + EDGES + BIG[1:], in_specs=[...  6.38 us
    ppermute x6, waiting for transfers between devices, exchange(): lax.ppermute(all_parts, 'tile', turn(k))  5.8 us
  transfers between devices with their start and end apart: 12, of which 10 were waited for; matrix products, arithmetic and copies ran while one was open for 1% of the time, Pallas kernels for 3%

profile of v4, /device:TPU:0, one launch (start us, length us, event | category | flops | bytes accessed | tf_op | source)
XLA Modules:
  0.0 126.0 jit_solution(12215790212763367944)
XLA Ops:
  0.0 2.3 %pack.1 = (f32[128,2,128]{2,1,0:T(2,128)}, s32[16]{0:T(128)}) custom-call(s32[16]{0:T(128)} %owner_in.1, s32[3,4,16]{2,1,0:T(4,128)} %bitcast.29, s32[1,256]{1,0:T(1,128)} %bitcast.30, s32[1,256]{1,0:T(1,128)} %bitcast.31, s32[1,256]{1,0:T(1,128)} %bitcast.32, f32[32,256]{1,0:T(8,128)} %bitcast.28), custom_call_target="tpu_custom_call" | custom-call | tf_op jit(solution)/shard_map/pack/pallas_call | solution.py:126
  2.3 21.0 %all_to_all.15.slots = f32[128,2,128]{2,1,0:T(2,128)} all-to-all(f32[128,2,128]{2,1,0:T(2,128)} %get-tuple-element.25), channel_id=1, replica_groups=mesh['tile'=16,'sub'=8] {'tile','sub'}, dimensions={0} | all-to-all | bytes 262144 | tf_op jit(solution)/shard_map/all_to_all | solution.py:662
  23.3 10.5 %first_solve.1 = (f32[128,64,128]{2,1,0:T(8,128)}, f32[128,80,128]{2,1,0:T(8,128)}, f32[5,32,128]{2,1,0:T(8,128)}, f32[4,32,128]{2,1,0:T(8,128)}, f32[4,32,128]{2,1,0:T(8,128)}) custom-call(f32[128,2,128]{2,1,0:T(2,128)} %all_to_all.15.slots, f32[32,64,512]{2,1,0:T(8,128)} %bitcast.22, f32[15,64,512]{2,1,0:T(8,128)} %coupling.1, f32[16,64,512]{2,1,0:T(8,128)} %scale.3, ...), custom_call_target="tpu_custom_call" | custom-call | flops 2200000000 | bytes 20000000 | tf_op jit(solution)/shard_map/first_solve/pallas_call | solution.py:374
  33.8 0.7 collective-permute-start.2
  34.5 2.3 %collective-permute-start.1 = (f32[1,5,32,128]{3,2,1,0:T(8,128)}, f32[1,5,32,128]{3,2,1,0:T(8,128)S(1)}, u32[]{:S(2)}, u32[]{:S(2)}) collective-permute-start(f32[1,5,32,128]{3,2,1,0:T(8,128)} %bitcast.24), channel_id=1, source_target_pairs={{0,32},{8,40},{16,48},{24,56},{32,0},{40,8},{48,16},{56,24},{64,96... | collective-permute-start | bytes 245768 | tf_op jit(solution)/shard_map/ppermute | solution.py:464
  36.7 0.0 collective-permute-start
  36.8 1.0 constant_dynamic-update-slice_fusion.3
  37.9 0.0 copy-start.2
  37.9 4.3 %forcing_0.1.force = f32[2048,512]{1,0:T(8,128)S(1)} custom-call(f32[128,2,128]{2,1,0:T(2,128)S(1)} %copy-done.4), custom_call_target="tpu_custom_call" | custom-call | flops 2147483648 | bytes 4325376 | tf_op jit(solution)/shard_map/forcing_0/pallas_call | solution.py:198
  42.2 0.0 collective-permute-done.2
  42.2 0.0 collective-permute-done.1
  42.2 0.4 collective-permute-done
  42.6 0.0 copy-start.5
  42.6 0.0 copy-start.6
  42.6 0.0 copy-start.7
  42.7 1.3 %collective-permute-start.3 = (f32[4,1,32,128]{3,2,1,0:T(8,128)S(1)}, f32[4,1,32,128]{3,2,1,0:T(8,128)S(1)}, u32[]{:S(2)}, u32[]{:S(2)}) collective-permute-start(f32[4,1,32,128]{3,2,1,0:T(8,128)S(1)} %pad_maximum_fusion.9), channel_id=1, source_target_pairs={{0,64},{8,72},{16,80},{24,88},{32,96},{40,104},{48,112},{56,120},{... | collective-permute-start | bytes 196616 | tf_op jit(solution)/shard_map/ppermute | solution.py:471
  44.0 4.2 %collective-permute-start.4 = (f32[4,4,32,128]{3,2,1,0:T(8,128)S(1)}, f32[4,4,32,128]{3,2,1,0:T(8,128)S(1)}, u32[]{:S(2)}, u32[]{:S(2)}) collective-permute-start(f32[4,4,32,128]{3,2,1,0:T(8,128)S(1)} %pad_maximum_fusion.5), channel_id=1, source_target_pairs={{0,64},{7,71},{8,72},{15,79},{16,80},{23,87},{24,88},{31,95},{32,9... | collective-permute-start | bytes 786440 | tf_op jit(solution)/shard_map/ppermute | solution.py:470
  48.2 0.6 collective-permute-done.3
  48.9 5.2 %collective-permute-done.4 = f32[4,4,32,128]{3,2,1,0:T(8,128)S(1)} collective-permute-done((f32[4,4,32,128]{3,2,1,0:T(8,128)S(1)}, f32[4,4,32,128]{3,2,1,0:T(8,128)S(1)}, u32[]{:S(2)}, u32[]{:S(2)}) %collective-permute-start.4) | collective-permute-done | bytes 262176 | tf_op jit(solution)/shard_map/ppermute | solution.py:470
  54.1 0.1 collective-permute-start.5
  54.2 2.1 %collective-permute-done.5 = f32[8,5,32,128]{3,2,1,0:T(8,128)S(1)} collective-permute-done((f32[8,5,32,128]{3,2,1,0:T(8,128)S(1)}, f32[8,5,32,128]{3,2,1,0:T(8,128)S(1)}, u32[]{:S(2)}, u32[]{:S(2)}) %collective-permute-start.5) | collective-permute-done | bytes 655392 | tf_op jit(solution)/shard_map/ppermute | solution.py:479
  56.3 0.1 pad_maximum_fusion.gathered
  56.4 0.0 copy-start
  56.4 0.0 copy-start.3
  56.5 0.0 copy-done.5
  56.5 0.0 copy-done.6
  56.5 0.0 copy-done.7
  56.5 0.7 route.2
  57.2 16.4 %all_to_all.16.got = f32[8,6,32,128]{3,2,1,0:T(8,128)S(1)} all-to-all(f32[8,6,32,128]{3,2,1,0:T(8,128)S(1)} %get-tuple-element.30), channel_id=1, replica_groups=mesh['tile'=16,'sub'=8] {'sub'}, dimensions={0} | all-to-all | bytes 1572864 | tf_op jit(solution)/shard_map/all_to_all | solution.py:482
  73.6 0.0 slice-done
  73.6 0.0 copy-done.2
  73.7 6.4 %second_solve.1 = (f32[8192,128]{1,0:T(8,128)S(1)}, f32[10240,128]{1,0:T(8,128)S(1)}, f32[5,32,128]{2,1,0:T(8,128)S(1)}, f32[4,32,128]{2,1,0:T(8,128)S(1)}, f32[...) custom-call(s32[16]{0:T(128)S(1)} %copy-done.7, ...), custom_call_target="tpu_custom_call", output_to_operand_aliasing={{5}: (4, {})} | custom-call | flops 50000000 | bytes 30000000 | tf_op jit(solution)/shard_map/second_solve/pallas_call | solution.py:584
  80.0 2.6 %collective-permute-start.8 = (f32[1,5,32,128]{3,2,1,0:T(8,128)S(1)}, f32[1,5,32,128]{3,2,1,0:T(8,128)S(1)}, u32[]{:S(2)}, u32[]{:S(2)}) collective-permute-start(f32[1,5,32,128]{3,2,1,0:T(8,128)S(1)} %bitcast.17), channel_id=1, source_target_pairs={{0,48},{8,56},{16,0},{24,8},{32,16},{40,24},{48,32},{56,40},{64,11... | collective-permute-start | bytes 245768 | tf_op jit(solution)/shard_map/ppermute | solution.py:464
  82.6 0.3 collective-permute-start.7
  83.0 1.1 collective-permute-start.6
  84.1 1.0 collective-permute-done.8
  85.1 3.6 %collective-permute-done.7 = f32[1,5,32,128]{3,2,1,0:T(8,128)S(1)} collective-permute-done((f32[1,5,32,128]{3,2,1,0:T(8,128)S(1)}, f32[1,5,32,128]{3,2,1,0:T(8,128)S(1)}, u32[]{:S(2)}, u32[]{:S(2)}) %collective-permute-start.7) | collective-permute-done | bytes 81952 | tf_op jit(solution)/shard_map/ppermute | solution.py:464
  88.7 0.8 collective-permute-done.6
  89.5 2.6 %collective-permute-start.9 = (f32[4,1,32,128]{3,2,1,0:T(8,128)S(1)}, f32[4,1,32,128]{3,2,1,0:T(8,128)S(1)}, u32[]{:S(2)}, u32[]{:S(2)}) collective-permute-start(f32[4,1,32,128]{3,2,1,0:T(8,128)S(1)} %pad_maximum_fusion.8), channel_id=1, source_target_pairs={{0,64},{8,72},{16,80},{24,88},{32,96},{40,104},{48,112},{56,120},{... | collective-permute-start | bytes 196616 | tf_op jit(solution)/shard_map/ppermute | solution.py:471
  92.1 2.8 %collective-permute-start.10 = (f32[4,4,32,128]{3,2,1,0:T(8,128)S(1)}, f32[4,4,32,128]{3,2,1,0:T(8,128)S(1)}, u32[]{:S(2)}, u32[]{:S(2)}) collective-permute-start(f32[4,4,32,128]{3,2,1,0:T(8,128)S(1)} %pad_maximum_fusion.2), channel_id=1, source_target_pairs={{0,64},{7,71},{8,72},{15,79},{16,80},{23,87},{24,88},{31,95},{32,9... | collective-permute-start | bytes 786440 | tf_op jit(solution)/shard_map/ppermute | solution.py:470
  95.0 0.3 collective-permute-done.9
  95.2 6.7 %collective-permute-done.10 = f32[4,4,32,128]{3,2,1,0:T(8,128)S(1)} collective-permute-done((f32[4,4,32,128]{3,2,1,0:T(8,128)S(1)}, f32[4,4,32,128]{3,2,1,0:T(8,128)S(1)}, u32[]{:S(2)}, u32[]{:S(2)}) %collective-permute-start.10) | collective-permute-done | bytes 262176 | tf_op jit(solution)/shard_map/ppermute | solution.py:470
  101.9 0.1 collective-permute-start.11
  102.0 2.1 %collective-permute-done.11 = f32[8,5,32,128]{3,2,1,0:T(8,128)S(1)} collective-permute-done((f32[8,5,32,128]{3,2,1,0:T(8,128)S(1)}, f32[8,5,32,128]{3,2,1,0:T(8,128)S(1)}, u32[]{:S(2)}, u32[]{:S(2)}) %collective-permute-start.11) | collective-permute-done | bytes 655392 | tf_op jit(solution)/shard_map/ppermute | solution.py:479
  104.1 0.1 pad_maximum_fusion.1.gathered
  104.2 0.7 route.3
  104.9 15.9 %all_to_all.17.got = f32[8,6,32,128]{3,2,1,0:T(8,128)S(1)} all-to-all(f32[8,6,32,128]{3,2,1,0:T(8,128)S(1)} %get-tuple-element.38), channel_id=1, replica_groups=mesh['tile'=16,'sub'=8] {'sub'}, dimensions={0} | all-to-all | bytes 1572864 | tf_op jit(solution)/shard_map/all_to_all | solution.py:482
  120.8 5.2 %last_step.1 = (f32[32,64,512]{2,1,0:T(8,128)}, f32[10240,128]{1,0:T(8,128)S(1)}) custom-call(s32[16]{0:T(128)S(1)} %copy-done.7, f32[8,6,32,128]{3,2,1,0:T(8,128)S(1)} %all_to_all.17.got, f32[4,32,128]{2,1,0:T(8,128)S(1)} %get-tuple-element.39.here, f32[8192,128]{1,0:T(8,128)S(1)} %get-tuple-element.40.solved, ...), custom_call_target="tpu_custom_call", output_to_operand_aliasing={{1}: (4, {})} | custom-call | flops 20000000 | bytes 20000000 | tf_op jit(solution)/shard_map/last_step/pallas_call | solution.py:624
  (25 shorter events, 0.2 us)
Async XLA Ops:
  23.3 14.6 %copy-start.4 = (f32[128,2,128]{2,1,0:T(2,128)S(1)}, f32[128,2,128]{2,1,0:T(2,128)}, u32[]{:S(2)}) copy-start(f32[128,2,128]{2,1,0:T(2,128)} %all_to_all.15.slots) | copy-start | bytes 393220
  33.8 8.4 %collective-permute-start.2 = (f32[1,5,32,128]{3,2,1,0:T(8,128)}, f32[1,5,32,128]{3,2,1,0:T(8,128)S(1)}, u32[]{:S(2)}, u32[]{:S(2)}) collective-permute-start(f32[1,5,32,128]{3,2,1,0:T(8,128)} %bitcast.23), channel_id=1, source_target_pairs={{0,48},{8,56},{16,0},{24,8},{32,16},{40,24},{48,32},{56,40},{64,11... | collective-permute-start | bytes 245768 | tf_op jit(solution)/shard_map/ppermute | solution.py:464
  34.5 7.7 %collective-permute-start.1 = (f32[1,5,32,128]{3,2,1,0:T(8,128)}, f32[1,5,32,128]{3,2,1,0:T(8,128)S(1)}, u32[]{:S(2)}, u32[]{:S(2)}) collective-permute-start(f32[1,5,32,128]{3,2,1,0:T(8,128)} %bitcast.24), channel_id=1, source_target_pairs={{0,32},{8,40},{16,48},{24,56},{32,0},{40,8},{48,16},{56,24},{64,96... | collective-permute-start | bytes 245768 | tf_op jit(solution)/shard_map/ppermute | solution.py:464
  36.7 5.9 %collective-permute-start = (f32[1,5,32,128]{3,2,1,0:T(8,128)}, f32[1,5,32,128]{3,2,1,0:T(8,128)S(1)}, u32[]{:S(2)}, u32[]{:S(2)}) collective-permute-start(f32[1,5,32,128]{3,2,1,0:T(8,128)} %bitcast.25), channel_id=1, source_target_pairs={{0,16},{8,24},{16,32},{24,40},{32,48},{40,56},{48,0},{56,8},{64,80... | collective-permute-start | bytes 245768 | tf_op jit(solution)/shard_map/ppermute | solution.py:464
  36.8 5.8 %copy-start.8 = (f32[5,32,128]{2,1,0:T(8,128)S(1)}, f32[5,32,128]{2,1,0:T(8,128)}, u32[]{:S(2)}) copy-start(f32[5,32,128]{2,1,0:T(8,128)} %get-tuple-element.26) | copy-start | bytes 245764
  36.8 36.8 %slice-start = ((s8[5242880]{0:T(1024)(128)(4,1)}), s8[4194304]{0:T(1024)(128)(4,1)S(1)}, s32[]{:S(2)}) async-start(s8[5242880]{0:T(1024)(128)(4,1)} %bitcast.13), calls=%async_computation.3 | async-start | bytes 8388608
  37.8 35.8 %slice-start.1 = ((s8[5242880]{0:T(1024)(128)(4,1)}), s8[1048576]{0:T(1024)(128)(4,1)S(1)}, s32[]{:S(2)}) async-start(s8[5242880]{0:T(1024)(128)(4,1)} %bitcast.13), calls=%async_computation.4 | async-start | bytes 2097152
  37.9 35.8 %copy-start.2 = (f32[128,64,128]{2,1,0:T(8,128)S(1)}, f32[128,64,128]{2,1,0:T(8,128)}, u32[]{:S(2)}) copy-start(f32[128,64,128]{2,1,0:T(8,128)} %get-tuple-element.32) | copy-start | bytes 12582916
  42.6 13.8 %copy-start.5 = (f32[4,32,128]{2,1,0:T(8,128)S(1)}, f32[4,32,128]{2,1,0:T(8,128)}, u32[]{:S(2)}) copy-start(f32[4,32,128]{2,1,0:T(8,128)} %get-tuple-element.28.first_row) | copy-start | bytes 196612
  42.6 13.8 %copy-start.6 = (f32[4,32,128]{2,1,0:T(8,128)S(1)}, f32[4,32,128]{2,1,0:T(8,128)}, u32[]{:S(2)}) copy-start(f32[4,32,128]{2,1,0:T(8,128)} %get-tuple-element.29.last_row) | copy-start | bytes 196612
  42.6 13.8 %copy-start.7 = (s32[16]{0:T(128)S(1)}, s32[16]{0:T(128)}, u32[]{:S(2)}) copy-start(s32[16]{0:T(128)} %get-tuple-element.24.meta) | copy-start | bytes 196
  42.7 6.2 %collective-permute-start.3 = (f32[4,1,32,128]{3,2,1,0:T(8,128)S(1)}, f32[4,1,32,128]{3,2,1,0:T(8,128)S(1)}, u32[]{:S(2)}, u32[]{:S(2)}) collective-permute-start(f32[4,1,32,128]{3,2,1,0:T(8,128)S(1)} %pad_maximum_fusion.9), channel_id=1, source_target_pairs={{0,64},{8,72},{16,80},{24,88},{32,96},{40,104},{48,112},{56,120},{... | collective-permute-start | bytes 196616 | tf_op jit(solution)/shard_map/ppermute | solution.py:471
  44.0 10.2 %collective-permute-start.4 = (f32[4,4,32,128]{3,2,1,0:T(8,128)S(1)}, f32[4,4,32,128]{3,2,1,0:T(8,128)S(1)}, u32[]{:S(2)}, u32[]{:S(2)}) collective-permute-start(f32[4,4,32,128]{3,2,1,0:T(8,128)S(1)} %pad_maximum_fusion.5), channel_id=1, source_target_pairs={{0,64},{7,71},{8,72},{15,79},{16,80},{23,87},{24,88},{31,95},{32,9... | collective-permute-start | bytes 786440 | tf_op jit(solution)/shard_map/ppermute | solution.py:470
  54.1 2.2 %collective-permute-start.5 = (f32[8,5,32,128]{3,2,1,0:T(8,128)S(1)}, f32[8,5,32,128]{3,2,1,0:T(8,128)S(1)}, u32[]{:S(2)}, u32[]{:S(2)}) collective-permute-start(f32[8,5,32,128]{3,2,1,0:T(8,128)S(1)} %maximum_dynamic-update-slice_fusion), channel_id=1, source_target_pairs={{0,8},{8,0},{16,24},{24,16},{32,40},{40,32},{48,56},{56,48},{64,72... | collective-permute-start | bytes 1966088 | tf_op jit(solution)/shard_map/ppermute | solution.py:479
  56.3 17.3 %copy-start.1 = (f32[15,64,512]{2,1,0:T(8,128)S(1)}, f32[15,64,512]{2,1,0:T(8,128)}, u32[]{:S(2)}) copy-start(f32[15,64,512]{2,1,0:T(8,128)} %coupling.1) | copy-start | bytes 5898244
  56.4 17.2 %copy-start = (f32[16,64,512]{2,1,0:T(8,128)S(1)}, f32[16,64,512]{2,1,0:T(8,128)}, u32[]{:S(2)}) copy-start(f32[16,64,512]{2,1,0:T(8,128)} %scale.3) | copy-start | bytes 6291460
  56.4 17.2 %copy-start.3 = (s32[64,512]{1,0:T(8,128)S(1)}, s32[64,512]{1,0:T(8,128)}, u32[]{:S(2)}) copy-start(s32[64,512]{1,0:T(8,128)} %depth.3) | copy-start | bytes 393220
  80.0 5.0 %collective-permute-start.8 = (f32[1,5,32,128]{3,2,1,0:T(8,128)S(1)}, f32[1,5,32,128]{3,2,1,0:T(8,128)S(1)}, u32[]{:S(2)}, u32[]{:S(2)}) collective-permute-start(f32[1,5,32,128]{3,2,1,0:T(8,128)S(1)} %bitcast.17), channel_id=1, source_target_pairs={{0,48},{8,56},{16,0},{24,8},{32,16},{40,24},{48,32},{56,40},{64,11... | collective-permute-start | bytes 245768 | tf_op jit(solution)/shard_map/ppermute | solution.py:464
  82.6 6.0 %collective-permute-start.7 = (f32[1,5,32,128]{3,2,1,0:T(8,128)S(1)}, f32[1,5,32,128]{3,2,1,0:T(8,128)S(1)}, u32[]{:S(2)}, u32[]{:S(2)}) collective-permute-start(f32[1,5,32,128]{3,2,1,0:T(8,128)S(1)} %bitcast.18), channel_id=1, source_target_pairs={{0,32},{8,40},{16,48},{24,56},{32,0},{40,8},{48,16},{56,24},{64,96... | collective-permute-start | bytes 245768 | tf_op jit(solution)/shard_map/ppermute | solution.py:464
  83.0 6.5 %collective-permute-start.6 = (f32[1,5,32,128]{3,2,1,0:T(8,128)S(1)}, f32[1,5,32,128]{3,2,1,0:T(8,128)S(1)}, u32[]{:S(2)}, u32[]{:S(2)}) collective-permute-start(f32[1,5,32,128]{3,2,1,0:T(8,128)S(1)} %bitcast.19), channel_id=1, source_target_pairs={{0,16},{8,24},{16,32},{24,40},{32,48},{40,56},{48,0},{56,8},{64,80... | collective-permute-start | bytes 245768 | tf_op jit(solution)/shard_map/ppermute | solution.py:464
  89.5 5.8 %collective-permute-start.9 = (f32[4,1,32,128]{3,2,1,0:T(8,128)S(1)}, f32[4,1,32,128]{3,2,1,0:T(8,128)S(1)}, u32[]{:S(2)}, u32[]{:S(2)}) collective-permute-start(f32[4,1,32,128]{3,2,1,0:T(8,128)S(1)} %pad_maximum_fusion.8), channel_id=1, source_target_pairs={{0,64},{8,72},{16,80},{24,88},{32,96},{40,104},{48,112},{56,120},{... | collective-permute-start | bytes 196616 | tf_op jit(solution)/shard_map/ppermute | solution.py:471
  92.1 9.8 %collective-permute-start.10 = (f32[4,4,32,128]{3,2,1,0:T(8,128)S(1)}, f32[4,4,32,128]{3,2,1,0:T(8,128)S(1)}, u32[]{:S(2)}, u32[]{:S(2)}) collective-permute-start(f32[4,4,32,128]{3,2,1,0:T(8,128)S(1)} %pad_maximum_fusion.2), channel_id=1, source_target_pairs={{0,64},{7,71},{8,72},{15,79},{16,80},{23,87},{24,88},{31,95},{32,9... | collective-permute-start | bytes 786440 | tf_op jit(solution)/shard_map/ppermute | solution.py:470
  101.9 2.2 %collective-permute-start.11 = (f32[8,5,32,128]{3,2,1,0:T(8,128)S(1)}, f32[8,5,32,128]{3,2,1,0:T(8,128)S(1)}, u32[]{:S(2)}, u32[]{:S(2)}) collective-permute-start(f32[8,5,32,128]{3,2,1,0:T(8,128)S(1)} %maximum_dynamic-update-slice_fusion.1), channel_id=1, source_target_pairs={{0,8},{8,0},{16,24},{24,16},{32,40},{40,32},{48,56},{56,48},{64,72... | collective-permute-start | bytes 1966088 | tf_op jit(solution)/shard_map/ppermute | solution.py:479

commit v5 on v3

--- a/solution.py
+++ b/solution.py
@@ -190,7 +190,7 @@
             pltpu.VMEM((CAP * DEVICES, COLS), jnp.bfloat16),
         ],
         compiler_params=params(8),
-        cost_estimate=pl.CostEstimate(flops=2147483648, bytes_accessed=4325376, transcendentals=0),
+        cost_estimate=pl.CostEstimate(flops=8000000000, bytes_accessed=4325376, transcendentals=0),
         name=f"forcing_{moment}",
     )(slots)
 
@@ -210,6 +210,30 @@
     if shift:
         return pl.ds(start + shift + block * 8, 8)
     return pl.ds(pl.multiple_of(start + block * 8, 8), 8)
+
+
+def edge_tiles(tile):
+    def sides(block, carry):
+        tile(block, 0)
+        tile(block, 3)
+        return carry
+
+    def ends(end, carry):
+        tile(end * (ROWS // 8 - 1), 1)
+        tile(end * (ROWS // 8 - 1), 2)
+        return carry
+
+    lax.fori_loop(0, ROWS // 8, sides, 0)
+    lax.fori_loop(0, 2, ends, 0)
+
+
+def inner_tiles(tile):
+    def step(block, carry):
+        tile(block, 1)
+        tile(block, 2)
+        return carry
+
+    lax.fori_loop(1, ROWS // 8 - 1, step, 0)
 
 
 def eliminate(value, coupling, depth, at):
@@ -284,34 +308,60 @@
 EDGES = (f32(5, PLANES, 128), f32(4, PLANES, 128), f32(4, PLANES, 128))
 
 
-def first_kernel(meta, adjoint, force, coupling, scale, depth, solved, weighted, payload,
-                 first_row, last_row, sides):
-    def step(block, carry):
-        for quarter in range(4):
-            columns = slice(quarter * 128, (quarter + 1) * 128)
-
-            def value(plane):
-                at = (pl.ds(pl.multiple_of(plane * ROWS + block * 8, 8), 8), columns)
-                return adjoint[at] + force[at]
-
-            solve_tile(value, coupling, scale, depth, solved, weighted, sides, block, quarter)
-        return carry
-
-    lax.fori_loop(0, ROWS // 8, step, 0)
+def first_tile(adjoint, force, coupling, scale, depth, solved, weighted, sides):
+    def tile(block, quarter):
+        columns = slice(quarter * 128, (quarter + 1) * 128)
+
+        def value(plane):
+            at = (pl.ds(pl.multiple_of(plane * ROWS + block * 8, 8), 8), columns)
+            return adjoint[at] + force[at]
+
+        solve_tile(value, coupling, scale, depth, solved, weighted, sides, block, quarter)
+
+    return tile
+
+
+def first_edges_kernel(meta, adjoint, force, coupling, scale, depth, solved, weighted, payload,
+                       first_row, last_row, sides):
+    edge_tiles(first_tile(adjoint, force, coupling, scale, depth, solved, weighted, sides))
     send_edges(meta, weighted, sides, payload, first_row, last_row)
 
 
-def first_solve(meta, adjoint, force, coupling, scale, depth):
-    return pl.pallas_call(
-        first_kernel,
+def first_inner_kernel(adjoint, force, coupling, scale, depth, _, __, solved, weighted):
+    inner_tiles(first_tile(adjoint, force, coupling, scale, depth, solved, weighted, None))
+
+
+SIDES = pltpu.VMEM((128, 128), jnp.float32)
+
+
+def cost(flops):
+    return pl.CostEstimate(flops=flops, bytes_accessed=10000000, transcendentals=0)
+
+
+def first_edges(meta, *given):
+    return pl.pallas_call(
+        first_edges_kernel,
         out_shape=BIG + EDGES,
         in_specs=[SMEM] + [VMEM] * 5,
         out_specs=(VMEM,) * 5,
-        scratch_shapes=[pltpu.VMEM((128, 128), jnp.float32)],
+        scratch_shapes=[SIDES],
         compiler_params=params(8),
-        cost_estimate=pl.CostEstimate(flops=30000000, bytes_accessed=20000000, transcendentals=0),
-        name="first_solve",
-    )(meta, adjoint, force, coupling, scale, depth)
+        cost_estimate=cost(30000000),
+        name="first_edges",
+    )(meta, *given)
+
+
+def first_inner(solved, weighted, *given):
+    return pl.pallas_call(
+        first_inner_kernel,
+        out_shape=BIG,
+        in_specs=[VMEM] * 7,
+        out_specs=(VMEM,) * 2,
+        input_output_aliases={5: 0, 6: 1},
+        compiler_params=params(4),
+        cost_estimate=cost(20000000),
+        name="first_inner",
+    )(*given, solved, weighted)
 
 
 def route_kernel(meta, gathered, first_row, last_row, send, here):
@@ -364,7 +414,7 @@
     )(meta, gathered, first_row, last_row)
 
 
-def exchange(meta, payload, first_row, last_row, beside=None):
+def exchange(meta, depth, beside_z, beside_y, payload, first_row, last_row):
     def turn(k):
         return [
             (y * 8 + z * 2 + c, y * 8 + ((z + k) % 4) * 2 + c)
@@ -377,10 +427,11 @@
     all_parts = jnp.concatenate(
         [all_parts] + [lax.ppermute(all_parts, "tile", turn(k)) for k in (1, 2, 3)], axis=0
     )
+    all_parts, depth, *extra = lax.optimization_barrier((all_parts, depth, *beside_z()))
     all_parts = jnp.concatenate(
         [all_parts, lax.ppermute(all_parts, "tile", [(i, i ^ 8) for i in range(N_TILE)])], axis=0
     )
-    extra = () if beside is None else (beside(),)
+    extra = beside_y(depth, *extra)
     all_parts, *extra = lax.optimization_barrier((all_parts, *extra))
     all_parts = jnp.concatenate(
         [all_parts, lax.ppermute(all_parts, "tile", [(i, i ^ 1) for i in range(N_TILE)])], axis=0
@@ -435,8 +486,10 @@
     lane = iota((8, 128), 1)
     here = pl.ds(pl.multiple_of(block * 8, 8), 8)
     depth = depth_ref[here, columns]
-    west = strips[here, :]
-    east = strips[pl.ds(pl.multiple_of(ROWS + block * 8, 8), 8), :]
+    if quarter == 0:
+        west = strips[here, :]
+    if quarter == 3:
+        east = strips[pl.ds(pl.multiple_of(ROWS + block * 8, 8), 8), :]
     weights = {}
 
     def value(plane):
@@ -466,83 +519,156 @@
     return value
 
 
-def second_kernel(meta, got, here, solved_in, weighted_in, force, coupling,
-                  scale, depth, solved, weighted, payload, first_row, last_row, weighted_late,
-                  sides, strips):
+def second_tile(solved_in, weighted_in, force, coupling, scale, depth, solved, weighted, strips,
+                sides):
+    def tile(block, quarter):
+        columns = slice(quarter * 128, (quarter + 1) * 128)
+        late = stepped(solved_in, weighted_in, scale, depth, strips, block, quarter)
+
+        def value(plane):
+            at = (pl.ds(pl.multiple_of(plane * ROWS + block * 8, 8), 8), columns)
+            return late(plane) + force[at]
+
+        solve_tile(value, coupling, scale, depth, solved, weighted, sides, block, quarter)
+
+    return tile
+
+
+def second_inner_kernel(solved_in, weighted_in, force, coupling, scale, depth, solved, weighted):
+    inner_tiles(
+        second_tile(
+            solved_in, weighted_in, force, coupling, scale, depth, solved, weighted, None, None
+        )
+    )
+
+
+def second_edges_kernel(meta, got, here, solved_in, weighted_in, force, coupling, scale, depth, _,
+                        __, solved, weighted, payload, first_row, last_row, weighted_late, sides,
+                        strips):
     place_halo(meta, got, here, weighted_late, strips)
-
-    def step(block, carry):
-        for quarter in range(4):
-            columns = slice(quarter * 128, (quarter + 1) * 128)
-            late = stepped(solved_in, weighted_late, scale, depth, strips, block, quarter)
-
-            def value(plane):
-                at = (pl.ds(pl.multiple_of(plane * ROWS + block * 8, 8), 8), columns)
-                return late(plane) + force[at]
-
-            solve_tile(value, coupling, scale, depth, solved, weighted, sides, block, quarter)
-        return carry
-
-    lax.fori_loop(0, ROWS // 8, step, 0)
+    edge_tiles(
+        second_tile(
+            solved_in, weighted_late, force, coupling, scale, depth, solved, weighted, strips, sides
+        )
+    )
     send_edges(meta, weighted, sides, payload, first_row, last_row)
 
 
-def second_solve(meta, halos, solved, weighted, force, coupling, scale, depth):
-    return pl.pallas_call(
-        second_kernel,
+def second_inner(*given):
+    return pl.pallas_call(
+        second_inner_kernel,
+        out_shape=BIG,
+        in_specs=[VMEM] * 6,
+        out_specs=(VMEM,) * 2,
+        compiler_params=params(4),
+        cost_estimate=cost(30000000),
+        name="second_inner",
+    )(*given)
+
+
+def second_edges(meta, halos, *given):
+    return pl.pallas_call(
+        second_edges_kernel,
         out_shape=BIG + EDGES + BIG[1:],
-        in_specs=[SMEM] + [VMEM] * 8,
+        in_specs=[SMEM] + [VMEM] * 10,
         out_specs=(VMEM,) * 6,
-        input_output_aliases={4: 5},
-        scratch_shapes=[pltpu.VMEM((128, 128), jnp.float32)] * 2,
+        input_output_aliases={9: 0, 10: 1, 4: 5},
+        scratch_shapes=[SIDES] * 2,
         compiler_params=params(8),
-        cost_estimate=pl.CostEstimate(flops=50000000, bytes_accessed=30000000, transcendentals=0),
-        name="second_solve",
-    )(meta, *halos, solved, weighted, force, coupling, scale, depth)
-
-
-def last_kernel(meta, got, here, solved, weighted_in, scale, depth, out,
-                weighted, strips, ready, sems):
+        cost_estimate=cost(40000000),
+        name="second_edges",
+    )(meta, *halos, *given)
+
+
+def last_tile(solved, weighted, scale, depth, strips, ready):
+    def tile(block, quarter):
+        columns = slice(quarter * 128, (quarter + 1) * 128)
+        value = stepped(solved, weighted, scale, depth, strips, block, quarter)
+        for level in range(LEVELS):
+            for plane in (level, LEVELS + level):
+                ready[plane, pl.ds(pl.multiple_of(block * 8, 8), 8), columns] = value(plane)
+
+    return tile
+
+
+INSIDE = (slice(8, ROWS - 8), slice(128, 384))
+OUTSIDE = [
+    (slice(0, ROWS), slice(0, 128)),
+    (slice(0, ROWS), slice(384, 512)),
+    (slice(0, 8), slice(128, 384)),
+    (slice(ROWS - 8, ROWS), slice(128, 384)),
+]
+
+
+def last_inner_kernel(solved, weighted, scale, depth, out, ready, sems):
+    inner_tiles(last_tile(solved, weighted, scale, depth, None, ready))
+    rows, columns = INSIDE
+    copy = pltpu.make_async_copy(
+        ready.at[:, rows, columns], out.at[:, rows, columns], sems.at[0]
+    )
+    copy.start()
+    copy.wait()
+
+
+def last_edges_kernel(meta, got, here, solved, weighted_in, scale, depth, _, out, weighted, strips,
+                      ready, sems):
     place_halo(meta, got, here, weighted, strips)
-
-    def copy(block):
+    tile = last_tile(solved, weighted, scale, depth, strips, ready)
+
+    def copy(i):
+        rows, columns = OUTSIDE[i]
         return pltpu.make_async_copy(
-            ready.at[block],
-            out.at[:, pl.ds(pl.multiple_of(block * 8, 8), 8), :],
-            sems.at[block],
+            ready.at[:, rows, columns], out.at[:, rows, columns], sems.at[i]
         )
 
-    def step(block, carry):
-        for quarter in range(4):
-            columns = slice(quarter * 128, (quarter + 1) * 128)
-            value = stepped(solved, weighted, scale, depth, strips, block, quarter)
-            for level in range(LEVELS):
-                for plane in (level, LEVELS + level):
-                    ready[block, plane, :, columns] = value(plane)
-        copy(block).start()
-        return carry
-
-    lax.fori_loop(0, ROWS // 8, step, 0)
-    for block in range(ROWS // 8):
-        copy(block).wait()
-
-
-def last_step(meta, halos, solved, weighted, scale, depth):
-    return pl.pallas_call(
-        last_kernel,
+    def column(quarter):
+        def step(block, carry):
+            tile(block, quarter)
+            return carry
+
+        lax.fori_loop(0, ROWS // 8, step, 0)
+
+    column(0)
+    copy(0).start()
+    column(3)
+    copy(1).start()
+    for i, block in ((2, 0), (3, ROWS // 8 - 1)):
+        tile(block, 1)
+        tile(block, 2)
+        copy(i).start()
+    for i in range(4):
+        copy(i).wait()
+
+
+READY = [pltpu.VMEM((PLANES, ROWS, COLS), jnp.float32), pltpu.SemaphoreType.DMA((4,))]
+ANY = pl.BlockSpec(memory_space=pl.ANY)
+
+
+def last_inner(*given):
+    return pl.pallas_call(
+        last_inner_kernel,
+        out_shape=f32(PLANES, ROWS, COLS),
+        in_specs=[VMEM] * 4,
+        out_specs=ANY,
+        scratch_shapes=READY,
+        compiler_params=params(6),
+        cost_estimate=cost(20000000),
+        name="last_inner",
+    )(*given)
+
+
+def last_edges(meta, halos, *given):
+    return pl.pallas_call(
+        last_edges_kernel,
         out_shape=(f32(PLANES, ROWS, COLS), BIG[1]),
-        in_specs=[SMEM] + [VMEM] * 6,
-        out_specs=(pl.BlockSpec(memory_space=pl.ANY), VMEM),
-        input_output_aliases={4: 1},
-        scratch_shapes=[
-            pltpu.VMEM((128, 128), jnp.float32),
-            pltpu.VMEM((ROWS // 8, PLANES, 8, COLS), jnp.float32),
-            pltpu.SemaphoreType.DMA((ROWS // 8,)),
-        ],
+        in_specs=[SMEM] + [VMEM] * 6 + [ANY],
+        out_specs=(ANY, VMEM),
+        input_output_aliases={7: 0, 4: 1},
+        scratch_shapes=[SIDES] + READY,
         compiler_params=params(8),
-        cost_estimate=pl.CostEstimate(flops=20000000, bytes_accessed=20000000, transcendentals=0),
-        name="last_step",
-    )(meta, *halos, solved, weighted, scale, depth)[0]
+        cost_estimate=cost(20000000),
+        name="last_edges",
+    )(meta, *halos, *given)[0]
 
 
 def body(
@@ -571,13 +697,30 @@
     scale = diff_scale.reshape(LEVELS * ROWS, COLS)
     coupling = vert_coupling.reshape((LEVELS - 1) * ROWS, COLS)
     late = forcing(slots, 1)
-    solved, weighted, *edges = first_solve(meta, adjoint, late, coupling, scale, column_depth)
-    halos, (early,) = exchange(meta, *edges, lambda: forcing(slots, 0))
-    solved, weighted, *edges, _ = second_solve(
-        meta, halos, solved, weighted, early, coupling, scale, column_depth
-    )
-    halos, _ = exchange(meta, *edges)
-    out = last_step(meta, halos, solved, weighted, scale, column_depth)
+    given = (adjoint, late, coupling, scale, column_depth)
+    solved, weighted, *edges = first_edges(meta, *given)
+
+    def beside_z():
+        return (forcing(slots, 0),)
+
+    def beside_y(depth, early):
+        whole = first_inner(solved, weighted, *given[:-1], depth)
+        return *whole, early, *second_inner(*whole, early, coupling, scale, depth)
+
+    halos, (solved, weighted, early, *begun) = exchange(
+        meta, column_depth, beside_z, beside_y, *edges
+    )
+    solved, weighted, *edges, _ = second_edges(
+        meta, halos, solved, weighted, early, coupling, scale, column_depth, *begun
+    )
+    halos, begun = exchange(
+        meta,
+        column_depth,
+        lambda: (),
+        lambda depth: (last_inner(solved, weighted, scale, depth),),
+        *edges,
+    )
+    out = last_edges(meta, halos, solved, weighted, scale, column_depth, *begun)
     return out.reshape(adjoint_final.shape)
 
 

time: 120 us -> 116 us (0.967)
  waiting for transfers between devices: 27.1 us -> 21.7 us
  Pallas kernels: 27.3 us -> 31.5 us
  local copies, waits for them, and re-layouts: 2.31 us -> 0.02 us
    ppermute x2, waiting for transfers between devices: 16.2 us -> 10.8 us  [exchange(): lax.ppermute(all_parts, 'tile', [(i, i ^ 8) for i in range(N_TILE)])]
    pallas_call x3 -> x6, Pallas kernels: 14.9 us -> 19.3 us  [the longest x1 5.54 us: second_edges(): pl.pallas_call(second_edges_kernel, out_shape=BIG + EDGES + BIG[1:], in_s...]
    unnamed x18 -> x10, local copies, waits for them, and re-layouts: 2.26 us -> 0.02 us
  transfers between devices with their start and end apart: 10 -> 10, of which waited for: 9 -> 9; matrix products, arithmetic and copies ran while one was open for 0% -> 0% of each run, Pallas kernels for 4% -> 8%
where the time goes in v5:
time: 116 us
  blocking collectives  52.6 us (45%)
  Pallas kernels  31.5 us (27%)
  waiting for transfers between devices  21.7 us (19%)
  starting transfers between devices  9.63 us (8%)
    all_to_all x2, blocking collectives, exchange(): got = lax.all_to_all(send, 'sub', split_axis=0, concat_axis=0, tiled=True)  32 us
    all_to_all x1, blocking collectives, body(): lax.all_to_all(slots, ('tile', 'sub'), split_axis=0, concat_axis=0, tiled...  20.6 us
    ppermute x2, waiting for transfers between devices, exchange(): lax.ppermute(all_parts, 'tile', [(i, i ^ 8) for i in range(N_TILE)])  10.8 us
    pallas_call x2, Pallas kernels, forcing(): pl.pallas_call(functools.partial(forcing_kernel, moment), out_shape=f32(P...  8.58 us
    ppermute x6, waiting for transfers between devices, exchange(): lax.ppermute(all_parts, 'tile', turn(k))  6.73 us
    ppermute x6, starting transfers between devices, exchange(): lax.ppermute(all_parts, 'tile', turn(k))  6.22 us
    pallas_call x1, Pallas kernels, second_edges(): pl.pallas_call(second_edges_kernel, out_shape=BIG + EDGES + BIG[1:], in_s...  5.54 us
    pallas_call x1, Pallas kernels, last_edges(): pl.pallas_call(last_edges_kernel, out_shape=(f32(PLANES, ROWS, COLS), BIG...  4.95 us
  transfers between devices with their start and end apart: 10, of which 9 were waited for; matrix products, arithmetic and copies ran while one was open for 0% of the time, Pallas kernels for 8%

profile of v5, /device:TPU:0, one launch (start us, length us, event | category | flops | bytes accessed | tf_op | source)
XLA Modules:
  0.0 116.0 jit_solution(18093567016154569140)
XLA Ops:
  0.0 2.3 %pack.1 = (f32[128,2,128]{2,1,0:T(2,128)}, s32[16]{0:T(128)}) custom-call(s32[16]{0:T(128)} %owner_in.1, s32[3,4,16]{2,1,0:T(4,128)} %bitcast.32, s32[1,256]{1,0:T(1,128)} %bitcast.33, s32[1,256]{1,0:T(1,128)} %bitcast.34, s32[1,256]{1,0:T(1,128)} %bitcast.35, f32[32,256]{1,0:T(8,128)} %bitcast.31), custom_call_target="tpu_custom_call" | custom-call | tf_op jit(solution)/shard_map/pack/pallas_call | solution.py:126
  2.3 20.6 %all_to_all.15.slots = f32[128,2,128]{2,1,0:T(2,128)S(1)} all-to-all(f32[128,2,128]{2,1,0:T(2,128)} %get-tuple-element.40), channel_id=1, replica_groups=mesh['tile'=16,'sub'=8] {'tile','sub'}, dimensions={0} | all-to-all | bytes 262144 | tf_op jit(solution)/shard_map/all_to_all | solution.py:695
  22.9 0.0 copy-start
  22.9 0.0 copy-start.1
  22.9 0.0 copy-start.2
  22.9 0.0 copy-start.3
  23.0 0.0 copy-start.4
  23.0 4.3 %forcing_1.1.force = f32[2048,512]{1,0:T(8,128)S(1)} custom-call(f32[128,2,128]{2,1,0:T(2,128)S(1)} %all_to_all.15.slots), custom_call_target="tpu_custom_call" | custom-call | flops 8000000000 | bytes 4325376 | tf_op jit(solution)/shard_map/forcing_1/pallas_call | solution.py:183
  27.3 0.0 copy-done
  27.3 0.0 copy-done.1
  27.3 0.0 copy-done.2
  27.3 0.0 copy-done.3
  27.3 0.0 copy-done.4
  27.3 3.4 %first_edges.1 = (f32[8192,128]{1,0:T(8,128)S(1)}, f32[10240,128]{1,0:T(8,128)S(1)}, f32[5,32,128]{2,1,0:T(8,128)S(1)}, f32[4,32,128]{2,1,0:T(8,128)S(1)}, f32[4,32,128]{2,1,0:T(8,128)S(1)}) custom-call(s32[16]{0:T(128)S(1)} %copy-done.4, f32[2048,512]{1,0:T(8,128)S(1)} %bitcast.21, f32[2048,512]{1,0:T(8,128)S(1)} %forcing_1.1.force, ...), custom_call_target="tpu_custom_call" | custom-call | flops 30000000 | bytes 10000000 | tf_op jit(solution)/shard_map/first_edges/pallas_call | solution.py:342
  30.7 0.7 collective-permute-start.2
  31.4 2.0 %collective-permute-start.1 = (f32[1,5,32,128]{3,2,1,0:T(8,128)S(1)}, f32[1,5,32,128]{3,2,1,0:T(8,128)S(1)}, u32[]{:S(2)}, u32[]{:S(2)}) collective-permute-start(f32[1,5,32,128]{3,2,1,0:T(8,128)S(1)} %bitcast.28), channel_id=1, source_target_pairs={{0,32},{8,40},{16,48},{24,56},{32,0},{40,8},{48,16},{56,24},{64,96... | collective-permute-start | bytes 245768 | tf_op jit(solution)/shard_map/ppermute | solution.py:428
  33.5 0.1 collective-permute-start
  33.5 4.3 %forcing_0.1.force = f32[2048,512]{1,0:T(8,128)S(1)} custom-call(f32[128,2,128]{2,1,0:T(2,128)S(1)} %all_to_all.15.slots), custom_call_target="tpu_custom_call" | custom-call | flops 8000000000 | bytes 4325376 | tf_op jit(solution)/shard_map/forcing_0/pallas_call | solution.py:183
  37.8 0.0 collective-permute-done.2
  37.8 0.2 collective-permute-done.1
  38.1 1.0 collective-permute-done
  39.2 1.5 %collective-permute-start.3 = (f32[4,5,32,128]{3,2,1,0:T(8,128)S(1)}, f32[4,5,32,128]{3,2,1,0:T(8,128)S(1)}, u32[]{:S(2)}, u32[]{:S(2)}) collective-permute-start(f32[4,5,32,128]{3,2,1,0:T(8,128)S(1)} %pad_maximum_fusion.4), channel_id=1, source_target_pairs={{0,64},{8,72},{16,80},{24,88},{32,96},{40,104},{48,112},{56,120},{... | collective-permute-start | bytes 983048 | tf_op jit(solution)/shard_map/ppermute | solution.py:432
  40.6 1.1 first_inner.1
  41.8 1.8 %second_inner.1 = (f32[8192,128]{1,0:T(8,128)S(1)}, f32[10240,128]{1,0:T(8,128)S(1)}) custom-call(f32[8192,128]{1,0:T(8,128)S(1)} %get-tuple-element.56.solved_in, f32[10240,128]{1,0:T(8,128)S(1)} %get-tuple-element.57.weighted_in, f32[2048,512]{1,0:T(8,128)S(1)} %forcing_0.1.force, f32[960,512]{1,0:T(8,128)S(1)} %bitcast.19, f32[1024,512]{1,0:T(8,128)S(1)} %bitcast.13, ...), custom_call_target="tpu_custom_call" | custom-call | flops 30000000 | bytes 10000000 | tf_op jit(solution)/shard_map/second_inner/pallas_call | solution.py:558
  43.6 5.8 %collective-permute-done.3 = f32[4,5,32,128]{3,2,1,0:T(8,128)S(1)} collective-permute-done((f32[4,5,32,128]{3,2,1,0:T(8,128)S(1)}, f32[4,5,32,128]{3,2,1,0:T(8,128)S(1)}, u32[]{:S(2)}, u32[]{:S(2)}) %collective-permute-start.3) | collective-permute-done | bytes 327712 | tf_op jit(solution)/shard_map/ppermute | solution.py:432
  49.5 0.1 collective-permute-start.4
  49.6 2.1 %collective-permute-done.4 = f32[8,5,32,128]{3,2,1,0:T(8,128)S(1)} collective-permute-done((f32[8,5,32,128]{3,2,1,0:T(8,128)S(1)}, f32[8,5,32,128]{3,2,1,0:T(8,128)S(1)}, u32[]{:S(2)}, u32[]{:S(2)}) %collective-permute-start.4) | collective-permute-done | bytes 655392 | tf_op jit(solution)/shard_map/ppermute | solution.py:437
  51.7 0.1 pad_maximum_fusion.gathered
  51.8 0.7 route.2
  52.5 16.0 %all_to_all.16.got = f32[8,6,32,128]{3,2,1,0:T(8,128)S(1)} all-to-all(f32[8,6,32,128]{3,2,1,0:T(8,128)S(1)} %get-tuple-element.54), channel_id=1, replica_groups=mesh['tile'=16,'sub'=8] {'sub'}, dimensions={0} | all-to-all | bytes 1572864 | tf_op jit(solution)/shard_map/all_to_all | solution.py:440
  68.4 5.5 %second_edges.1 = (f32[8192,128]{1,0:T(8,128)S(1)}, f32[10240,128]{1,0:T(8,128)S(1)}, f32[5,32,128]{2,1,0:T(8,128)S(1)}, f32[4,32,128]{2,1,0:T(8,128)S(1)}, f32[...) custom-call(s32[16]{0:T(128)S(1)} %copy-done.4, ...), custom_call_target="tpu_custom_call", output_to_operand_aliasing={{0}: (9, {}), {1}: (10, {}), {5}: (4, {})} | custom-call | flops 40000000 | bytes 10000000 | tf_op jit(solution)/shard_map/second_edges/pallas_call | solution.py:570
  74.0 1.9 %collective-permute-start.7 = (f32[1,5,32,128]{3,2,1,0:T(8,128)S(1)}, f32[1,5,32,128]{3,2,1,0:T(8,128)S(1)}, u32[]{:S(2)}, u32[]{:S(2)}) collective-permute-start(f32[1,5,32,128]{3,2,1,0:T(8,128)S(1)} %bitcast.23), channel_id=1, source_target_pairs={{0,48},{8,56},{16,0},{24,8},{32,16},{40,24},{48,32},{56,40},{64,11... | collective-permute-start | bytes 245768 | tf_op jit(solution)/shard_map/ppermute | solution.py:428
  75.9 0.3 collective-permute-start.6
  76.2 1.1 collective-permute-start.5
  77.3 1.9 %collective-permute-done.7 = f32[1,5,32,128]{3,2,1,0:T(8,128)S(1)} collective-permute-done((f32[1,5,32,128]{3,2,1,0:T(8,128)S(1)}, f32[1,5,32,128]{3,2,1,0:T(8,128)S(1)}, u32[]{:S(2)}, u32[]{:S(2)}) %collective-permute-start.7) | collective-permute-done | bytes 81952 | tf_op jit(solution)/shard_map/ppermute | solution.py:428
  79.2 2.9 %collective-permute-done.6 = f32[1,5,32,128]{3,2,1,0:T(8,128)S(1)} collective-permute-done((f32[1,5,32,128]{3,2,1,0:T(8,128)S(1)}, f32[1,5,32,128]{3,2,1,0:T(8,128)S(1)}, u32[]{:S(2)}, u32[]{:S(2)}) %collective-permute-start.6) | collective-permute-done | bytes 81952 | tf_op jit(solution)/shard_map/ppermute | solution.py:428
  82.1 0.7 collective-permute-done.5
  82.8 1.8 %collective-permute-start.8 = (f32[4,5,32,128]{3,2,1,0:T(8,128)S(1)}, f32[4,5,32,128]{3,2,1,0:T(8,128)S(1)}, u32[]{:S(2)}, u32[]{:S(2)}) collective-permute-start(f32[4,5,32,128]{3,2,1,0:T(8,128)S(1)} %pad_maximum_fusion.5), channel_id=1, source_target_pairs={{0,64},{8,72},{16,80},{24,88},{32,96},{40,104},{48,112},{56,120},{... | collective-permute-start | bytes 983048 | tf_op jit(solution)/shard_map/ppermute | solution.py:432
  84.5 2.5 %last_inner.1._ = f32[32,64,512]{2,1,0:T(8,128)} custom-call(f32[8192,128]{1,0:T(8,128)S(1)} %get-tuple-element.63.solved, f32[10240,128]{1,0:T(8,128)S(1)} %get-tuple-element.64.weighted.weighted_in, f32[1024,512]{1,0:T(8,128)S(1)} %bitcast.15, s32[64,512]{1,0:T(8,128)S(1)} %copy-done.3), custom_call_target="tpu_custom_call" | custom-call | flops 20000000 | bytes 10000000 | tf_op jit(solution)/shard_map/last_inner/pallas_call | solution.py:648
  87.0 5.0 %collective-permute-done.8 = f32[4,5,32,128]{3,2,1,0:T(8,128)S(1)} collective-permute-done((f32[4,5,32,128]{3,2,1,0:T(8,128)S(1)}, f32[4,5,32,128]{3,2,1,0:T(8,128)S(1)}, u32[]{:S(2)}, u32[]{:S(2)}) %collective-permute-start.8) | collective-permute-done | bytes 327712 | tf_op jit(solution)/shard_map/ppermute | solution.py:432
  92.1 0.1 collective-permute-start.9
  92.2 2.1 %collective-permute-done.9 = f32[8,5,32,128]{3,2,1,0:T(8,128)S(1)} collective-permute-done((f32[8,5,32,128]{3,2,1,0:T(8,128)S(1)}, f32[8,5,32,128]{3,2,1,0:T(8,128)S(1)}, u32[]{:S(2)}, u32[]{:S(2)}) %collective-permute-start.9) | collective-permute-done | bytes 655392 | tf_op jit(solution)/shard_map/ppermute | solution.py:437
  94.3 0.1 pad_maximum_fusion.1.gathered
  94.4 0.7 route.3
  95.1 16.0 %all_to_all.17.got = f32[8,6,32,128]{3,2,1,0:T(8,128)S(1)} all-to-all(f32[8,6,32,128]{3,2,1,0:T(8,128)S(1)} %get-tuple-element.69), channel_id=1, replica_groups=mesh['tile'=16,'sub'=8] {'sub'}, dimensions={0} | all-to-all | bytes 1572864 | tf_op jit(solution)/shard_map/all_to_all | solution.py:440
  111.1 5.0 %last_edges.1 = (f32[32,64,512]{2,1,0:T(8,128)}, f32[10240,128]{1,0:T(8,128)S(1)}) custom-call(s32[16]{0:T(128)S(1)} %copy-done.4, f32[8,6,32,128]{3,2,1,0:T(8,128)S(1)} %all_to_all.17.got, f32[4,32,128]{2,1,0:T(8,128)S(1)} %get-tuple-element.70.here, f32[8192,128]{1,0:T(8,128)S(1)} %get-tuple-element.63.solved, ...), custom_call_target="tpu_custom_call", output_to_operand_aliasing={{0}: (7, {}), {1}: (4, {})} | custom-call | flops 20000000 | bytes 10000000 | tf_op jit(solution)/shard_map/last_edges/pallas_call | solution.py:661
  (4 shorter events, 0.1 us)
Async XLA Ops:
  22.9 4.3 %copy-start = (f32[16,64,512]{2,1,0:T(8,128)S(1)}, f32[16,64,512]{2,1,0:T(8,128)}, u32[]{:S(2)}) copy-start(f32[16,64,512]{2,1,0:T(8,128)} %param.11) | copy-start | bytes 6291460
  22.9 4.3 %copy-start.1 = (f32[15,64,512]{2,1,0:T(8,128)S(1)}, f32[15,64,512]{2,1,0:T(8,128)}, u32[]{:S(2)}) copy-start(f32[15,64,512]{2,1,0:T(8,128)} %param.12) | copy-start | bytes 5898244
  22.9 4.3 %copy-start.2 = (f32[2,16,64,512]{3,2,1,0:T(8,128)S(1)}, f32[2,16,64,512]{3,2,1,0:T(8,128)}, u32[]{:S(2)}) copy-start(f32[2,16,64,512]{3,2,1,0:T(8,128)} %param.10) | copy-start | bytes 12582916
  22.9 4.3 %copy-start.3 = (s32[64,512]{1,0:T(8,128)S(1)}, s32[64,512]{1,0:T(8,128)}, u32[]{:S(2)}) copy-start(s32[64,512]{1,0:T(8,128)} %depth.8) | copy-start | bytes 393220
  23.0 4.4 %copy-start.4 = (s32[16]{0:T(128)S(1)}, s32[16]{0:T(128)}, u32[]{:S(2)}) copy-start(s32[16]{0:T(128)} %get-tuple-element.39.meta) | copy-start | bytes 196
  30.7 7.1 %collective-permute-start.2 = (f32[1,5,32,128]{3,2,1,0:T(8,128)S(1)}, f32[1,5,32,128]{3,2,1,0:T(8,128)S(1)}, u32[]{:S(2)}, u32[]{:S(2)}) collective-permute-start(f32[1,5,32,128]{3,2,1,0:T(8,128)S(1)} %bitcast.27), channel_id=1, source_target_pairs={{0,48},{8,56},{16,0},{24,8},{32,16},{40,24},{48,32},{56,40},{64,11... | collective-permute-start | bytes 245768 | tf_op jit(solution)/shard_map/ppermute | solution.py:428
  31.4 6.7 %collective-permute-start.1 = (f32[1,5,32,128]{3,2,1,0:T(8,128)S(1)}, f32[1,5,32,128]{3,2,1,0:T(8,128)S(1)}, u32[]{:S(2)}, u32[]{:S(2)}) collective-permute-start(f32[1,5,32,128]{3,2,1,0:T(8,128)S(1)} %bitcast.28), channel_id=1, source_target_pairs={{0,32},{8,40},{16,48},{24,56},{32,0},{40,8},{48,16},{56,24},{64,96... | collective-permute-start | bytes 245768 | tf_op jit(solution)/shard_map/ppermute | solution.py:428
  33.5 5.7 %collective-permute-start = (f32[1,5,32,128]{3,2,1,0:T(8,128)S(1)}, f32[1,5,32,128]{3,2,1,0:T(8,128)S(1)}, u32[]{:S(2)}, u32[]{:S(2)}) collective-permute-start(f32[1,5,32,128]{3,2,1,0:T(8,128)S(1)} %bitcast.29), channel_id=1, source_target_pairs={{0,16},{8,24},{16,32},{24,40},{32,48},{40,56},{48,0},{56,8},{64,80... | collective-permute-start | bytes 245768 | tf_op jit(solution)/shard_map/ppermute | solution.py:428
  39.2 10.3 %collective-permute-start.3 = (f32[4,5,32,128]{3,2,1,0:T(8,128)S(1)}, f32[4,5,32,128]{3,2,1,0:T(8,128)S(1)}, u32[]{:S(2)}, u32[]{:S(2)}) collective-permute-start(f32[4,5,32,128]{3,2,1,0:T(8,128)S(1)} %pad_maximum_fusion.4), channel_id=1, source_target_pairs={{0,64},{8,72},{16,80},{24,88},{32,96},{40,104},{48,112},{56,120},{... | collective-permute-start | bytes 983048 | tf_op jit(solution)/shard_map/ppermute | solution.py:432
  49.5 2.2 %collective-permute-start.4 = (f32[8,5,32,128]{3,2,1,0:T(8,128)S(1)}, f32[8,5,32,128]{3,2,1,0:T(8,128)S(1)}, u32[]{:S(2)}, u32[]{:S(2)}) collective-permute-start(f32[8,5,32,128]{3,2,1,0:T(8,128)S(1)} %pad_maximum_fusion.2), channel_id=1, source_target_pairs={{0,8},{8,0},{16,24},{24,16},{32,40},{40,32},{48,56},{56,48},{64,72... | collective-permute-start | bytes 1966088 | tf_op jit(solution)/shard_map/ppermute | solution.py:437
  74.0 5.3 %collective-permute-start.7 = (f32[1,5,32,128]{3,2,1,0:T(8,128)S(1)}, f32[1,5,32,128]{3,2,1,0:T(8,128)S(1)}, u32[]{:S(2)}, u32[]{:S(2)}) collective-permute-start(f32[1,5,32,128]{3,2,1,0:T(8,128)S(1)} %bitcast.23), channel_id=1, source_target_pairs={{0,48},{8,56},{16,0},{24,8},{32,16},{40,24},{48,32},{56,40},{64,11... | collective-permute-start | bytes 245768 | tf_op jit(solution)/shard_map/ppermute | solution.py:428
  75.9 6.2 %collective-permute-start.6 = (f32[1,5,32,128]{3,2,1,0:T(8,128)S(1)}, f32[1,5,32,128]{3,2,1,0:T(8,128)S(1)}, u32[]{:S(2)}, u32[]{:S(2)}) collective-permute-start(f32[1,5,32,128]{3,2,1,0:T(8,128)S(1)} %bitcast.24), channel_id=1, source_target_pairs={{0,32},{8,40},{16,48},{24,56},{32,0},{40,8},{48,16},{56,24},{64,96... | collective-permute-start | bytes 245768 | tf_op jit(solution)/shard_map/ppermute | solution.py:428
  76.2 6.5 %collective-permute-start.5 = (f32[1,5,32,128]{3,2,1,0:T(8,128)S(1)}, f32[1,5,32,128]{3,2,1,0:T(8,128)S(1)}, u32[]{:S(2)}, u32[]{:S(2)}) collective-permute-start(f32[1,5,32,128]{3,2,1,0:T(8,128)S(1)} %bitcast.25), channel_id=1, source_target_pairs={{0,16},{8,24},{16,32},{24,40},{32,48},{40,56},{48,0},{56,8},{64,80... | collective-permute-start | bytes 245768 | tf_op jit(solution)/shard_map/ppermute | solution.py:428
  82.8 9.2 %collective-permute-start.8 = (f32[4,5,32,128]{3,2,1,0:T(8,128)S(1)}, f32[4,5,32,128]{3,2,1,0:T(8,128)S(1)}, u32[]{:S(2)}, u32[]{:S(2)}) collective-permute-start(f32[4,5,32,128]{3,2,1,0:T(8,128)S(1)} %pad_maximum_fusion.5), channel_id=1, source_target_pairs={{0,64},{8,72},{16,80},{24,88},{32,96},{40,104},{48,112},{56,120},{... | collective-permute-start | bytes 983048 | tf_op jit(solution)/shard_map/ppermute | solution.py:432
  92.1 2.2 %collective-permute-start.9 = (f32[8,5,32,128]{3,2,1,0:T(8,128)S(1)}, f32[8,5,32,128]{3,2,1,0:T(8,128)S(1)}, u32[]{:S(2)}, u32[]{:S(2)}) collective-permute-start(f32[8,5,32,128]{3,2,1,0:T(8,128)S(1)} %pad_maximum_fusion.3), channel_id=1, source_target_pairs={{0,8},{8,0},{16,24},{24,16},{32,40},{40,32},{48,56},{56,48},{64,72... | collective-permute-start | bytes 1966088 | tf_op jit(solution)/shard_map/ppermute | solution.py:437

commit v6 on v5

--- a/solution.py
+++ b/solution.py
@@ -212,19 +212,22 @@
     return pl.ds(pl.multiple_of(start + block * 8, 8), 8)
 
 
-def edge_tiles(tile):
-    def sides(block, carry):
+def side_tiles(tile):
+    def step(block, carry):
         tile(block, 0)
         tile(block, 3)
         return carry
 
-    def ends(end, carry):
-        tile(end * (ROWS // 8 - 1), 1)
-        tile(end * (ROWS // 8 - 1), 2)
+    lax.fori_loop(1, ROWS // 8 - 1, step, 0)
+
+
+def end_tiles(tile):
+    def step(end, carry):
+        for quarter in range(4):
+            tile(end * (ROWS // 8 - 1), quarter)
         return carry
 
-    lax.fori_loop(0, ROWS // 8, sides, 0)
-    lax.fori_loop(0, 2, ends, 0)
+    lax.fori_loop(0, 2, step, 0)
 
 
 def inner_tiles(tile):
@@ -323,7 +326,9 @@
 
 def first_edges_kernel(meta, adjoint, force, coupling, scale, depth, solved, weighted, payload,
                        first_row, last_row, sides):
-    edge_tiles(first_tile(adjoint, force, coupling, scale, depth, solved, weighted, sides))
+    tile = first_tile(adjoint, force, coupling, scale, depth, solved, weighted, sides)
+    side_tiles(tile)
+    end_tiles(tile)
     send_edges(meta, weighted, sides, payload, first_row, last_row)
 
 
@@ -364,7 +369,7 @@
     )(*given, solved, weighted)
 
 
-def route_kernel(meta, gathered, first_row, last_row, send, here):
+def route_kernel(meta, gathered, send, here, across):
     sub = meta[13]
     lane = iota((PLANES, 128), 1)
 
@@ -389,29 +394,19 @@
     place_across = meta[3 * (1 - own)]
     for b in range(4):
         here[b] = gathered[place_here, 1 + b]
-        across = gathered[place_across, 1 + b]
-        first = first_row[b]
-        last = last_row[b]
-        for dest in range(N_SUB):
-            if dest == 0:
-                row = jnp.where(sub == N_SUB - 1, across, first)
-            elif dest == N_SUB - 1:
-                row = jnp.where(sub == 0, across, last)
-            else:
-                row = jnp.where(sub == dest - 1, last, first)
-            send[dest, 2 + b] = row
-
-
-def route(meta, gathered, first_row, last_row):
+        across[b] = gathered[place_across, 1 + b]
+
+
+def route(meta, gathered):
     return pl.pallas_call(
         route_kernel,
-        out_shape=(f32(N_SUB, 6, PLANES, 128), f32(4, PLANES, 128)),
-        in_specs=[SMEM] + [VMEM] * 3,
-        out_specs=(VMEM,) * 2,
+        out_shape=(f32(N_SUB, 2, PLANES, 128), f32(4, PLANES, 128), f32(4, PLANES, 128)),
+        in_specs=[SMEM, VMEM],
+        out_specs=(VMEM,) * 3,
         compiler_params=params(8),
         cost_estimate=pl.CostEstimate(flops=1000000, bytes_accessed=1000000, transcendentals=0),
         name="route",
-    )(meta, gathered, first_row, last_row)
+    )(meta, gathered)
 
 
 def exchange(meta, depth, beside_z, beside_y, payload, first_row, last_row):
@@ -427,25 +422,30 @@
     all_parts = jnp.concatenate(
         [all_parts] + [lax.ppermute(all_parts, "tile", turn(k)) for k in (1, 2, 3)], axis=0
     )
-    all_parts, depth, *extra = lax.optimization_barrier((all_parts, depth, *beside_z()))
+    all_parts, depth, first_row, last_row, *extra = lax.optimization_barrier(
+        (all_parts, depth, first_row, last_row, *beside_z())
+    )
+    above = lax.ppermute(last_row, "sub", [(i, i + 1) for i in range(N_SUB - 1)])
+    below = lax.ppermute(first_row, "sub", [(i + 1, i) for i in range(N_SUB - 1)])
     all_parts = jnp.concatenate(
         [all_parts, lax.ppermute(all_parts, "tile", [(i, i ^ 8) for i in range(N_TILE)])], axis=0
     )
     extra = beside_y(depth, *extra)
-    all_parts, *extra = lax.optimization_barrier((all_parts, *extra))
+    all_parts, above, below, *extra = lax.optimization_barrier(
+        (all_parts, above, below, *extra)
+    )
     all_parts = jnp.concatenate(
         [all_parts, lax.ppermute(all_parts, "tile", [(i, i ^ 1) for i in range(N_TILE)])], axis=0
     )
-    send, here = route(meta, all_parts, first_row, last_row)
+    send, here, across = route(meta, all_parts)
     got = lax.all_to_all(send, "sub", split_axis=0, concat_axis=0, tiled=True)
-    return (got, here), extra
-
-
-def place_halo(meta, got, here, weighted, strips):
+    got, across = lax.optimization_barrier((got, across))
+    across = lax.ppermute(across, "sub", [(0, N_SUB - 1), (N_SUB - 1, 0)])
+    return got, (here, across, above, below), extra
+
+
+def place_strips(meta, got, strips):
     sub = meta[13]
-    before = jnp.maximum(sub - 1, 0)
-    after = jnp.minimum(sub + 1, N_SUB - 1)
-    opposite = jnp.where(sub == 0, N_SUB - 1, 0)
     lane = iota((PLANES, 128), 1)
 
     def source(edge):
@@ -463,20 +463,26 @@
         pick, sides, (((1,), (1,)), ((), ())), precision=HIGHEST, preferred_element_type=jnp.float32
     )
 
+
+def place_ends(meta, got, here, across, above, below, weighted):
+    sub = meta[13]
+    lane = iota((PLANES, 128), 1)
+    to = iota((128, 128), 0)
+    of = iota((128, 128), 1)
     own = jnp.where(sub == N_SUB - 1, 1, 0)
     other_edge, turned = meta[3 * own + 1], meta[3 * own + 2]
     flip = jnp.where(of == jnp.where(turned == 1, 127 - to, to), 1.0, 0.0)
     row = []
     for b in range(4):
         joined = jnp.where(lane < 64, got[2 * b, 1], pltpu.roll(got[2 * b + 1, 1], 64, 1))
-        joined = jnp.where(other_edge < 2, got[opposite, 2 + b], joined)
+        joined = jnp.where(other_edge < 2, across[b], joined)
         row.append(jnp.where(other_edge == own, here[b], joined))
     for b in range(4):
         ordered = jnp.where(turned == 1, row[3 - b], row[b])
         strip = jnp.dot(ordered, flip, precision=HIGHEST, preferred_element_type=jnp.float32)
         at = b * PLANES * PITCH
-        above_row = jnp.where(sub == 0, strip, got[before, 2 + b])
-        below_row = jnp.where(sub == N_SUB - 1, strip, got[after, 2 + b])
+        above_row = jnp.where(sub == 0, strip, above[b])
+        below_row = jnp.where(sub == N_SUB - 1, strip, below[b])
         weighted[pl.ds(at + 7, PLANES, stride=PITCH), :] = above_row
         weighted[pl.ds(at + ROWS + 8, PLANES, stride=PITCH), :] = below_row
 
@@ -542,11 +548,21 @@
     )
 
 
-def second_edges_kernel(meta, got, here, solved_in, weighted_in, force, coupling, scale, depth, _,
-                        __, solved, weighted, payload, first_row, last_row, weighted_late, sides,
-                        strips):
-    place_halo(meta, got, here, weighted_late, strips)
-    edge_tiles(
+def second_sides_kernel(meta, got, solved_in, weighted_in, force, coupling, scale, depth, _, __,
+                        solved, weighted, strips, sides):
+    place_strips(meta, got, strips)
+    side_tiles(
+        second_tile(
+            solved_in, weighted_in, force, coupling, scale, depth, solved, weighted, strips, sides
+        )
+    )
+
+
+def second_ends_kernel(meta, got, here, across, above, below, strips, sides_in, solved_in,
+                       weighted_in, force, coupling, scale, depth, _, __, solved, weighted, payload,
+                       first_row, last_row, weighted_late, sides):
+    place_ends(meta, got, here, across, above, below, weighted_late)
+    end_tiles(
         second_tile(
             solved_in, weighted_late, force, coupling, scale, depth, solved, weighted, strips, sides
         )
@@ -566,18 +582,33 @@
     )(*given)
 
 
-def second_edges(meta, halos, *given):
-    return pl.pallas_call(
-        second_edges_kernel,
-        out_shape=BIG + EDGES + BIG[1:],
-        in_specs=[SMEM] + [VMEM] * 10,
-        out_specs=(VMEM,) * 6,
-        input_output_aliases={9: 0, 10: 1, 4: 5},
-        scratch_shapes=[SIDES] * 2,
-        compiler_params=params(8),
-        cost_estimate=cost(40000000),
-        name="second_edges",
-    )(meta, *halos, *given)
+SQUARE = f32(128, 128)
+
+
+def second_sides(meta, got, *given):
+    return pl.pallas_call(
+        second_sides_kernel,
+        out_shape=BIG + (SQUARE, SQUARE),
+        in_specs=[SMEM] + [VMEM] * 9,
+        out_specs=(VMEM,) * 4,
+        input_output_aliases={8: 0, 9: 1},
+        compiler_params=params(4),
+        cost_estimate=cost(30000000),
+        name="second_sides",
+    )(meta, got, *given)
+
+
+def second_ends(meta, got, ends, *given):
+    return pl.pallas_call(
+        second_ends_kernel,
+        out_shape=BIG + EDGES + BIG[1:] + (SQUARE,),
+        in_specs=[SMEM] + [VMEM] * 15,
+        out_specs=(VMEM,) * 7,
+        input_output_aliases={14: 0, 15: 1, 9: 5, 7: 6},
+        compiler_params=params(4),
+        cost_estimate=cost(30000000),
+        name="second_ends",
+    )(meta, got, *ends, *given)
 
 
 def last_tile(solved, weighted, scale, depth, strips, ready):
@@ -592,52 +623,50 @@
 
 
 INSIDE = (slice(8, ROWS - 8), slice(128, 384))
-OUTSIDE = [
-    (slice(0, ROWS), slice(0, 128)),
-    (slice(0, ROWS), slice(384, 512)),
-    (slice(0, 8), slice(128, 384)),
-    (slice(ROWS - 8, ROWS), slice(128, 384)),
-]
+BESIDE = ((slice(8, ROWS - 8), slice(0, 128)), (slice(8, ROWS - 8), slice(384, 512)))
+ENDS = ((slice(0, 8), slice(0, COLS)), (slice(ROWS - 8, ROWS), slice(0, COLS)))
+
+
+def copies_out(ready, out, pieces, sems):
+    return [
+        pltpu.make_async_copy(ready.at[:, rows, columns], out.at[:, rows, columns], sems.at[i])
+        for i, (rows, columns) in enumerate(pieces)
+    ]
 
 
 def last_inner_kernel(solved, weighted, scale, depth, out, ready, sems):
     inner_tiles(last_tile(solved, weighted, scale, depth, None, ready))
-    rows, columns = INSIDE
-    copy = pltpu.make_async_copy(
-        ready.at[:, rows, columns], out.at[:, rows, columns], sems.at[0]
-    )
-    copy.start()
-    copy.wait()
-
-
-def last_edges_kernel(meta, got, here, solved, weighted_in, scale, depth, _, out, weighted, strips,
-                      ready, sems):
-    place_halo(meta, got, here, weighted, strips)
+    for copy in copies_out(ready, out, (INSIDE,), sems):
+        copy.start()
+        copy.wait()
+
+
+def last_sides_kernel(meta, got, solved, weighted, scale, depth, _, out, strips, ready, sems):
+    place_strips(meta, got, strips)
     tile = last_tile(solved, weighted, scale, depth, strips, ready)
-
-    def copy(i):
-        rows, columns = OUTSIDE[i]
-        return pltpu.make_async_copy(
-            ready.at[:, rows, columns], out.at[:, rows, columns], sems.at[i]
-        )
-
-    def column(quarter):
+    copies = copies_out(ready, out, BESIDE, sems)
+    for quarter, copy in zip((0, 3), copies):
         def step(block, carry):
             tile(block, quarter)
             return carry
 
-        lax.fori_loop(0, ROWS // 8, step, 0)
-
-    column(0)
-    copy(0).start()
-    column(3)
-    copy(1).start()
-    for i, block in ((2, 0), (3, ROWS // 8 - 1)):
-        tile(block, 1)
-        tile(block, 2)
-        copy(i).start()
-    for i in range(4):
-        copy(i).wait()
+        lax.fori_loop(1, ROWS // 8 - 1, step, 0)
+        copy.start()
+    for copy in copies:
+        copy.wait()
+
+
+def last_ends_kernel(meta, got, here, across, above, below, strips, solved, weighted_in, scale,
+                     depth, _, out, weighted, ready, sems):
+    place_ends(meta, got, here, across, above, below, weighted)
+    tile = last_tile(solved, weighted, scale, depth, strips, ready)
+    copies = copies_out(ready, out, ENDS, sems)
+    for block, copy in zip((0, ROWS // 8 - 1), copies):
+        for quarter in range(4):
+            tile(block, quarter)
+        copy.start()
+    for copy in copies:
+        copy.wait()
 
 
 READY = [pltpu.VMEM((PLANES, ROWS, COLS), jnp.float32), pltpu.SemaphoreType.DMA((4,))]
@@ -657,18 +686,32 @@
     )(*given)
 
 
-def last_edges(meta, halos, *given):
-    return pl.pallas_call(
-        last_edges_kernel,
+def last_sides(meta, got, *given):
+    return pl.pallas_call(
+        last_sides_kernel,
+        out_shape=(f32(PLANES, ROWS, COLS), SQUARE),
+        in_specs=[SMEM] + [VMEM] * 5 + [ANY],
+        out_specs=(ANY, VMEM),
+        input_output_aliases={6: 0},
+        scratch_shapes=READY,
+        compiler_params=params(6),
+        cost_estimate=cost(20000000),
+        name="last_sides",
+    )(meta, got, *given)
+
+
+def last_ends(meta, got, ends, *given):
+    return pl.pallas_call(
+        last_ends_kernel,
         out_shape=(f32(PLANES, ROWS, COLS), BIG[1]),
-        in_specs=[SMEM] + [VMEM] * 6 + [ANY],
+        in_specs=[SMEM] + [VMEM] * 10 + [ANY],
         out_specs=(ANY, VMEM),
-        input_output_aliases={7: 0, 4: 1},
-        scratch_shapes=[SIDES] + READY,
-        compiler_params=params(8),
+        input_output_aliases={11: 0, 8: 1},
+        scratch_shapes=READY,
+        compiler_params=params(6),
         cost_estimate=cost(20000000),
-        name="last_edges",
-    )(meta, *halos, *given)[0]
+        name="last_ends",
+    )(meta, got, *ends, *given)[0]
 
 
 def body(
@@ -707,20 +750,22 @@
         whole = first_inner(solved, weighted, *given[:-1], depth)
         return *whole, early, *second_inner(*whole, early, coupling, scale, depth)
 
-    halos, (solved, weighted, early, *begun) = exchange(
+    got, ends, (solved, weighted, early, *begun) = exchange(
         meta, column_depth, beside_z, beside_y, *edges
     )
-    solved, weighted, *edges, _ = second_edges(
-        meta, halos, solved, weighted, early, coupling, scale, column_depth, *begun
-    )
-    halos, begun = exchange(
+    given = (solved, weighted, early, coupling, scale, column_depth)
+    *begun, strips, sides = second_sides(meta, got, *given, *begun)
+    solved, weighted, *edges, _, _ = second_ends(meta, got, ends, strips, sides, *given, *begun)
+    got, ends, begun = exchange(
         meta,
         column_depth,
         lambda: (),
         lambda depth: (last_inner(solved, weighted, scale, depth),),
         *edges,
     )
-    out = last_edges(meta, halos, solved, weighted, scale, column_depth, *begun)
+    given = (solved, weighted, scale, column_depth)
+    out, strips = last_sides(meta, got, *given, *begun)
+    out = last_ends(meta, got, ends, strips, *given, out)
     return out.reshape(adjoint_final.shape)
 
 

time: 116 us -> 121 us (1.043)
  starting transfers between devices: 9.63 us -> 23.9 us
  blocking collectives: 52.6 us -> 44 us
  waiting for transfers between devices: 21.7 us -> 18.8 us
  Pallas kernels: 31.5 us -> 32.8 us
    ppermute x0 -> x6, starting transfers between devices: none -> 13.1 us  [the longest x2 6.71 us: exchange(): across = lax.ppermute(across, 'sub', [(0, N_SUB - 1), (N_SUB - 1, 0)])]
    all_to_all x2, blocking collectives: 32 us -> 23.3 us  [exchange(): got = lax.all_to_all(send, 'sub', split_axis=0, concat_axis=0, tiled=True)]
    ppermute x2, waiting for transfers between devices: 10.8 us -> 4.86 us  [exchange(): lax.ppermute(all_parts, 'tile', [(i, i ^ 8) for i in range(N_TILE)])]
    ppermute x0 -> x6, waiting for transfers between devices: none -> 3.28 us  [the longest x2 2.35 us: exchange(): across = lax.ppermute(across, 'sub', [(0, N_SUB - 1), (N_SUB - 1, 0)])]
    pallas_call x4 -> x6, Pallas kernels: 11.9 us -> 13.5 us  [the longest x1 3.74 us: last_sides(): pl.pallas_call(last_sides_kernel, out_shape=(f32(PLANES, ROWS, COLS), SQU...]
  transfers between devices with their start and end apart: 10 -> 16, of which waited for: 9 -> 12; matrix products, arithmetic and copies ran while one was open for 0% -> 0% of each run, Pallas kernels for 8% -> 14%
where the time goes in v6:
time: 121 us; the launch traced here: 120 us
  blocking collectives  44 us (36%)
  Pallas kernels  32.8 us (27%)
  starting transfers between devices  23.9 us (20%)
  waiting for transfers between devices  18.8 us (16%)
    all_to_all x2, blocking collectives, exchange(): got = lax.all_to_all(send, 'sub', split_axis=0, concat_axis=0, tiled=True)  23.3 us
    all_to_all x1, blocking collectives, body(): lax.all_to_all(slots, ('tile', 'sub'), split_axis=0, concat_axis=0, tiled...  20.6 us
    pallas_call x2, Pallas kernels, forcing(): pl.pallas_call(functools.partial(forcing_kernel, moment), out_shape=f32(P...  8.58 us
    ppermute x2, starting transfers between devices, exchange(): across = lax.ppermute(across, 'sub', [(0, N_SUB - 1), (N_SUB - 1, 0)])  6.71 us
    ppermute x6, waiting for transfers between devices, exchange(): lax.ppermute(all_parts, 'tile', turn(k))  6.5 us
    ppermute x6, starting transfers between devices, exchange(): lax.ppermute(all_parts, 'tile', turn(k))  6.41 us
    ppermute x2, waiting for transfers between devices, exchange(): lax.ppermute(all_parts, 'tile', [(i, i ^ 8) for i in range(N_TILE)])  4.86 us
    ppermute x2, starting transfers between devices, exchange(): lax.ppermute(all_parts, 'tile', [(i, i ^ 8) for i in range(N_TILE)])  4.37 us
  transfers between devices with their start and end apart: 16, of which 12 were waited for; matrix products, arithmetic and copies ran while one was open for 0% of the time, Pallas kernels for 14%

profile of v6, /device:TPU:0, one launch (start us, length us, event | category | flops | bytes accessed | tf_op | source)
XLA Modules:
  0.0 120.1 jit_solution(5637621014045068067)
XLA Ops:
  0.0 2.3 %pack.1 = (f32[128,2,128]{2,1,0:T(2,128)}, s32[16]{0:T(128)}) custom-call(s32[16]{0:T(128)} %owner_in.1, s32[3,4,16]{2,1,0:T(4,128)} %bitcast.35, s32[1,256]{1,0:T(1,128)} %bitcast.36, s32[1,256]{1,0:T(1,128)} %bitcast.37, s32[1,256]{1,0:T(1,128)} %bitcast.38, f32[32,256]{1,0:T(8,128)} %bitcast.34), custom_call_target="tpu_custom_call" | custom-call | tf_op jit(solution)/shard_map/pack/pallas_call | solution.py:126
  2.3 20.6 %all_to_all.15.slots = f32[128,2,128]{2,1,0:T(2,128)S(1)} all-to-all(f32[128,2,128]{2,1,0:T(2,128)} %get-tuple-element.60), channel_id=1, replica_groups=mesh['tile'=16,'sub'=8] {'tile','sub'}, dimensions={0} | all-to-all | bytes 262144 | tf_op jit(solution)/shard_map/all_to_all | solution.py:738
  23.0 4.3 %forcing_1.1.force = f32[2048,512]{1,0:T(8,128)S(1)} custom-call(f32[128,2,128]{2,1,0:T(2,128)S(1)} %all_to_all.15.slots), custom_call_target="tpu_custom_call" | custom-call | flops 8000000000 | bytes 4325376 | tf_op jit(solution)/shard_map/forcing_1/pallas_call | solution.py:183
  27.3 3.1 %first_edges.1 = (f32[8192,128]{1,0:T(8,128)S(1)}, f32[10240,128]{1,0:T(8,128)S(1)}, f32[5,32,128]{2,1,0:T(8,128)S(1)}, f32[4,32,128]{2,1,0:T(8,128)S(1)}, f32[4,32,128]{2,1,0:T(8,128)S(1)}) custom-call(s32[16]{0:T(128)S(1)} %copy-done.4, f32[2048,512]{1,0:T(8,128)S(1)} %bitcast.24, f32[2048,512]{1,0:T(8,128)S(1)} %forcing_1.1.force, ...), custom_call_target="tpu_custom_call" | custom-call | flops 30000000 | bytes 10000000 | tf_op jit(solution)/shard_map/first_edges/pallas_call | solution.py:347
  30.4 0.7 collective-permute-start.2
  31.1 2.0 %collective-permute-start.1 = (f32[1,5,32,128]{3,2,1,0:T(8,128)S(1)}, f32[1,5,32,128]{3,2,1,0:T(8,128)S(1)}, u32[]{:S(2)}, u32[]{:S(2)}) collective-permute-start(f32[1,5,32,128]{3,2,1,0:T(8,128)S(1)} %bitcast.31), channel_id=1, source_target_pairs={{0,32},{8,40},{16,48},{24,56},{32,0},{40,8},{48,16},{56,24},{64,96... | collective-permute-start | bytes 245768 | tf_op jit(solution)/shard_map/ppermute | solution.py:423
  33.2 0.1 collective-permute-start
  33.2 4.3 %forcing_0.1.force = f32[2048,512]{1,0:T(8,128)S(1)} custom-call(f32[128,2,128]{2,1,0:T(2,128)S(1)} %all_to_all.15.slots), custom_call_target="tpu_custom_call" | custom-call | flops 8000000000 | bytes 4325376 | tf_op jit(solution)/shard_map/forcing_0/pallas_call | solution.py:183
  37.5 0.0 collective-permute-done.2
  37.6 0.2 collective-permute-done.1
  37.8 1.0 collective-permute-done
  38.9 1.5 %collective-permute-start.3 = (f32[4,5,32,128]{3,2,1,0:T(8,128)S(1)}, f32[4,5,32,128]{3,2,1,0:T(8,128)S(1)}, u32[]{:S(2)}, u32[]{:S(2)}) collective-permute-start(f32[4,5,32,128]{3,2,1,0:T(8,128)S(1)} %pad_maximum_fusion.4), channel_id=1, source_target_pairs={{0,64},{8,72},{16,80},{24,88},{32,96},{40,104},{48,112},{56,120},{... | collective-permute-start | bytes 983048 | tf_op jit(solution)/shard_map/ppermute | solution.py:431
  40.4 2.5 %collective-permute-start.4 = (f32[4,32,128]{2,1,0:T(8,128)S(1)}, f32[4,32,128]{2,1,0:T(8,128)S(1)}, u32[]{:S(2)}, u32[]{:S(2)}) collective-permute-start(f32[4,32,128]{2,1,0:T(8,128)S(1)} %get-tuple-element.65), channel_id=1, source_target_pairs={{0,1},{1,2},{2,3},{3,4},{4,5},{5,6},{6,7},{8,9},{9,10},{10,11},{11... | collective-permute-start | bytes 196616 | tf_op jit(solution)/shard_map/ppermute | solution.py:428
  42.8 1.3 %collective-permute-start.5 = (f32[4,32,128]{2,1,0:T(8,128)S(1)}, f32[4,32,128]{2,1,0:T(8,128)S(1)}, u32[]{:S(2)}, u32[]{:S(2)}) collective-permute-start(f32[4,32,128]{2,1,0:T(8,128)S(1)} %get-tuple-element.66), channel_id=1, source_target_pairs={{1,0},{2,1},{3,2},{4,3},{5,4},{6,5},{7,6},{9,8},{10,9},{11,10},{12... | collective-permute-start | bytes 196616 | tf_op jit(solution)/shard_map/ppermute | solution.py:429
  44.1 1.2 first_inner.1
  45.3 1.8 %second_inner.1 = (f32[8192,128]{1,0:T(8,128)S(1)}, f32[10240,128]{1,0:T(8,128)S(1)}) custom-call(f32[8192,128]{1,0:T(8,128)S(1)} %get-tuple-element.83.solved_in, f32[10240,128]{1,0:T(8,128)S(1)} %get-tuple-element.84.weighted_in, f32[2048,512]{1,0:T(8,128)S(1)} %forcing_0.1.force, f32[960,512]{1,0:T(8,128)S(1)} %bitcast.21, f32[1024,512]{1,0:T(8,128)S(1)} %bitcast.13, ...), custom_call_target="tpu_custom_call" | custom-call | flops 30000000 | bytes 10000000 | tf_op jit(solution)/shard_map/second_inner/pallas_call | solution.py:574
  47.1 3.5 %collective-permute-done.3 = f32[4,5,32,128]{3,2,1,0:T(8,128)S(1)} collective-permute-done((f32[4,5,32,128]{3,2,1,0:T(8,128)S(1)}, f32[4,5,32,128]{3,2,1,0:T(8,128)S(1)}, u32[]{:S(2)}, u32[]{:S(2)}) %collective-permute-start.3) | collective-permute-done | bytes 327712 | tf_op jit(solution)/shard_map/ppermute | solution.py:431
  50.6 0.0 collective-permute-done.4.above
  50.6 0.1 collective-permute-start.6
  50.7 2.1 %collective-permute-done.6 = f32[8,5,32,128]{3,2,1,0:T(8,128)S(1)} collective-permute-done((f32[8,5,32,128]{3,2,1,0:T(8,128)S(1)}, f32[8,5,32,128]{3,2,1,0:T(8,128)S(1)}, u32[]{:S(2)}, u32[]{:S(2)}) %collective-permute-start.6) | collective-permute-done | bytes 655392 | tf_op jit(solution)/shard_map/ppermute | solution.py:438
  52.8 0.1 pad_maximum_fusion.gathered
  52.9 0.7 route.2
  53.6 11.7 %all_to_all.16.got = f32[8,2,32,128]{3,2,1,0:T(8,128)S(1)} all-to-all(f32[8,2,32,128]{3,2,1,0:T(8,128)S(1)} %get-tuple-element.76), channel_id=1, replica_groups=mesh['tile'=16,'sub'=8] {'sub'}, dimensions={0} | all-to-all | bytes 524288 | tf_op jit(solution)/shard_map/all_to_all | solution.py:441
  65.3 3.4 %collective-permute-start.7 = (f32[4,32,128]{2,1,0:T(8,128)S(1)}, f32[4,32,128]{2,1,0:T(8,128)S(1)}, u32[]{:S(2)}, u32[]{:S(2)}) collective-permute-start(f32[4,32,128]{2,1,0:T(8,128)S(1)} %get-tuple-element.80), channel_id=1, source_target_pairs={{0,7},{7,0},{8,15},{15,8},{16,23},{23,16},{24,31},{31,24},{32,39},... | collective-permute-start | bytes 196616 | tf_op jit(solution)/shard_map/ppermute | solution.py:443
  68.7 3.7 %second_sides.1 = (f32[8192,128]{1,0:T(8,128)S(1)}, f32[10240,128]{1,0:T(8,128)S(1)}, f32[128,128]{1,0:T(8,128)S(1)}, f32[128,128]{1,0:T(8,128)S(1)}) custom-call(s32[16]{0:T(128)S(1)} %copy-done.4, f32[8,2,32,128]{3,2,1,0:T(8,128)S(1)} %all_to_all.16.got, ...), custom_call_target="tpu_custom_call", output_to_operand_aliasing={{0}: (8, {}), {1}: (9, {})} | custom-call | flops 30000000 | bytes 10000000 | tf_op jit(solution)/shard_map/second_sides/pallas_call | solution.py:589
  72.3 1.2 %collective-permute-done.7.across = f32[4,32,128]{2,1,0:T(8,128)S(1)} collective-permute-done((f32[4,32,128]{2,1,0:T(8,128)S(1)}, f32[4,32,128]{2,1,0:T(8,128)S(1)}, u32[]{:S(2)}, u32[]{:S(2)}) %collective-permute-start.7) | collective-permute-done | bytes 65568 | tf_op jit(solution)/shard_map/ppermute | solution.py:443
  73.5 2.3 %second_ends.1 = (f32[8192,128]{1,0:T(8,128)S(1)}, f32[10240,128]{1,0:T(8,128)S(1)}, f32[5,32,128]{2,1,0:T(8,128)S(1)}, f32[4,32,128]{2,1,0:T(8,128)S(1)}, f32[4...) custom-call(s32[16]{0:T(128)S(1)} %copy-done.4, ...), custom_call_target="tpu_custom_call", output_to_operand_aliasing={{0}: (14, {}), {1}: (15, {}), {5}: (9, {}), {6}: (7, {})} | custom-call | flops 30000000 | bytes 10000000 | tf_op jit(solution)/shard_map/second_ends/pallas_call | solution.py:602
  75.9 2.0 %collective-permute-start.10 = (f32[1,5,32,128]{3,2,1,0:T(8,128)S(1)}, f32[1,5,32,128]{3,2,1,0:T(8,128)S(1)}, u32[]{:S(2)}, u32[]{:S(2)}) collective-permute-start(f32[1,5,32,128]{3,2,1,0:T(8,128)S(1)} %bitcast.26), channel_id=1, source_target_pairs={{0,48},{8,56},{16,0},{24,8},{32,16},{40,24},{48,32},{56,40},{64,11... | collective-permute-start | bytes 245768 | tf_op jit(solution)/shard_map/ppermute | solution.py:423
  77.8 0.3 collective-permute-start.9
  78.1 1.3 %collective-permute-start.8 = (f32[1,5,32,128]{3,2,1,0:T(8,128)S(1)}, f32[1,5,32,128]{3,2,1,0:T(8,128)S(1)}, u32[]{:S(2)}, u32[]{:S(2)}) collective-permute-start(f32[1,5,32,128]{3,2,1,0:T(8,128)S(1)} %bitcast.28), channel_id=1, source_target_pairs={{0,16},{8,24},{16,32},{24,40},{32,48},{40,56},{48,0},{56,8},{64,80... | collective-permute-start | bytes 245768 | tf_op jit(solution)/shard_map/ppermute | solution.py:423
  79.5 0.9 collective-permute-done.10
  80.3 3.5 %collective-permute-done.9 = f32[1,5,32,128]{3,2,1,0:T(8,128)S(1)} collective-permute-done((f32[1,5,32,128]{3,2,1,0:T(8,128)S(1)}, f32[1,5,32,128]{3,2,1,0:T(8,128)S(1)}, u32[]{:S(2)}, u32[]{:S(2)}) %collective-permute-start.9) | collective-permute-done | bytes 81952 | tf_op jit(solution)/shard_map/ppermute | solution.py:423
  83.9 0.8 collective-permute-done.8
  84.7 2.9 %collective-permute-start.11 = (f32[4,5,32,128]{3,2,1,0:T(8,128)S(1)}, f32[4,5,32,128]{3,2,1,0:T(8,128)S(1)}, u32[]{:S(2)}, u32[]{:S(2)}) collective-permute-start(f32[4,5,32,128]{3,2,1,0:T(8,128)S(1)} %pad_maximum_fusion.5), channel_id=1, source_target_pairs={{0,64},{8,72},{16,80},{24,88},{32,96},{40,104},{48,112},{56,120},{... | collective-permute-start | bytes 983048 | tf_op jit(solution)/shard_map/ppermute | solution.py:431
  87.6 1.3 %collective-permute-start.12 = (f32[4,32,128]{2,1,0:T(8,128)S(1)}, f32[4,32,128]{2,1,0:T(8,128)S(1)}, u32[]{:S(2)}, u32[]{:S(2)}) collective-permute-start(f32[4,32,128]{2,1,0:T(8,128)S(1)} %get-tuple-element.96), channel_id=1, source_target_pairs={{0,1},{1,2},{2,3},{3,4},{4,5},{5,6},{6,7},{8,9},{9,10},{10,11},{11... | collective-permute-start | bytes 196616 | tf_op jit(solution)/shard_map/ppermute | solution.py:428
  88.9 1.3 %collective-permute-start.13 = (f32[4,32,128]{2,1,0:T(8,128)S(1)}, f32[4,32,128]{2,1,0:T(8,128)S(1)}, u32[]{:S(2)}, u32[]{:S(2)}) collective-permute-start(f32[4,32,128]{2,1,0:T(8,128)S(1)} %get-tuple-element.97), channel_id=1, source_target_pairs={{1,0},{2,1},{3,2},{4,3},{5,4},{6,5},{7,6},{9,8},{10,9},{11,10},{12... | collective-permute-start | bytes 196616 | tf_op jit(solution)/shard_map/ppermute | solution.py:429
  90.2 2.5 %last_inner.1._ = f32[32,64,512]{2,1,0:T(8,128)} custom-call(f32[8192,128]{1,0:T(8,128)S(1)} %get-tuple-element.98.solved, f32[10240,128]{1,0:T(8,128)S(1)} %get-tuple-element.99.weighted.weighted_in, f32[1024,512]{1,0:T(8,128)S(1)} %bitcast.16, s32[64,512]{1,0:T(8,128)S(1)} %copy-done.3), custom_call_target="tpu_custom_call" | custom-call | flops 20000000 | bytes 10000000 | tf_op jit(solution)/shard_map/last_inner/pallas_call | solution.py:677
  92.6 1.4 %collective-permute-done.11 = f32[4,5,32,128]{3,2,1,0:T(8,128)S(1)} collective-permute-done((f32[4,5,32,128]{3,2,1,0:T(8,128)S(1)}, f32[4,5,32,128]{3,2,1,0:T(8,128)S(1)}, u32[]{:S(2)}, u32[]{:S(2)}) %collective-permute-start.11) | collective-permute-done | bytes 327712 | tf_op jit(solution)/shard_map/ppermute | solution.py:431
  94.1 0.9 collective-permute-done.13.below
  95.0 0.0 collective-permute-start.14
  95.0 2.1 %collective-permute-done.14 = f32[8,5,32,128]{3,2,1,0:T(8,128)S(1)} collective-permute-done((f32[8,5,32,128]{3,2,1,0:T(8,128)S(1)}, f32[8,5,32,128]{3,2,1,0:T(8,128)S(1)}, u32[]{:S(2)}, u32[]{:S(2)}) %collective-permute-start.14) | collective-permute-done | bytes 655392 | tf_op jit(solution)/shard_map/ppermute | solution.py:438
  97.1 0.1 pad_maximum_fusion.1.gathered
  97.2 0.7 route.3
  97.9 11.6 %all_to_all.17.got = f32[8,2,32,128]{3,2,1,0:T(8,128)S(1)} all-to-all(f32[8,2,32,128]{3,2,1,0:T(8,128)S(1)} %get-tuple-element.102), channel_id=1, replica_groups=mesh['tile'=16,'sub'=8] {'sub'}, dimensions={0} | all-to-all | bytes 524288 | tf_op jit(solution)/shard_map/all_to_all | solution.py:441
  109.5 3.4 %collective-permute-start.15 = (f32[4,32,128]{2,1,0:T(8,128)S(1)}, f32[4,32,128]{2,1,0:T(8,128)S(1)}, u32[]{:S(2)}, u32[]{:S(2)}) collective-permute-start(f32[4,32,128]{2,1,0:T(8,128)S(1)} %get-tuple-element.106), channel_id=1, source_target_pairs={{0,7},{7,0},{8,15},{15,8},{16,23},{23,16},{24,31},{31,24},{32,39},... | collective-permute-start | bytes 196616 | tf_op jit(solution)/shard_map/ppermute | solution.py:443
  112.9 3.7 %last_sides.1 = (f32[32,64,512]{2,1,0:T(8,128)}, f32[128,128]{1,0:T(8,128)S(1)}) custom-call(s32[16]{0:T(128)S(1)} %copy-done.4, f32[8,2,32,128]{3,2,1,0:T(8,128)S(1)} %all_to_all.17.got, f32[8192,128]{1,0:T(8,128)S(1)} %get-tuple-element.98.solved, f32[10240,128]{1,0:T(8,128)S(1)} %get-tuple-element.99.weighted.weighted_in, ...), custom_call_target="tpu_custom_call", output_to_operand_aliasing={{0}: (6, {})} | custom-call | flops 20000000 | bytes 10000000 | tf_op jit(solution)/shard_map/last_sides/pallas_call | solution.py:690
  116.6 1.1 collective-permute-done.15.across
  117.8 2.3 %last_ends.1 = (f32[32,64,512]{2,1,0:T(8,128)}, f32[10240,128]{1,0:T(8,128)S(1)}) custom-call(s32[16]{0:T(128)S(1)} %copy-done.4, f32[8,2,32,128]{3,2,1,0:T(8,128)S(1)} %all_to_all.17.got, f32[4,32,128]{2,1,0:T(8,128)S(1)} %get-tuple-element.105.here, ...), custom_call_target="tpu_custom_call", output_to_operand_aliasing={{0}: (11, {}), {1}: (8, {})} | custom-call | flops 20000000 | bytes 10000000 | tf_op jit(solution)/shard_map/last_ends/pallas_call | solution.py:704
  (16 shorter events, 0.2 us)
Async XLA Ops:
  22.9 4.3 %copy-start = (f32[16,64,512]{2,1,0:T(8,128)S(1)}, f32[16,64,512]{2,1,0:T(8,128)}, u32[]{:S(2)}) copy-start(f32[16,64,512]{2,1,0:T(8,128)} %param.11) | copy-start | bytes 6291460
  22.9 4.3 %copy-start.1 = (f32[15,64,512]{2,1,0:T(8,128)S(1)}, f32[15,64,512]{2,1,0:T(8,128)}, u32[]{:S(2)}) copy-start(f32[15,64,512]{2,1,0:T(8,128)} %param.12) | copy-start | bytes 5898244
  22.9 4.3 %copy-start.2 = (f32[2,16,64,512]{3,2,1,0:T(8,128)S(1)}, f32[2,16,64,512]{3,2,1,0:T(8,128)}, u32[]{:S(2)}) copy-start(f32[2,16,64,512]{3,2,1,0:T(8,128)} %param.10) | copy-start | bytes 12582916
  22.9 4.3 %copy-start.3 = (s32[64,512]{1,0:T(8,128)S(1)}, s32[64,512]{1,0:T(8,128)}, u32[]{:S(2)}) copy-start(s32[64,512]{1,0:T(8,128)} %depth.12) | copy-start | bytes 393220
  23.0 4.4 %copy-start.4 = (s32[16]{0:T(128)S(1)}, s32[16]{0:T(128)}, u32[]{:S(2)}) copy-start(s32[16]{0:T(128)} %get-tuple-element.59.meta) | copy-start | bytes 196
  30.4 7.1 %collective-permute-start.2 = (f32[1,5,32,128]{3,2,1,0:T(8,128)S(1)}, f32[1,5,32,128]{3,2,1,0:T(8,128)S(1)}, u32[]{:S(2)}, u32[]{:S(2)}) collective-permute-start(f32[1,5,32,128]{3,2,1,0:T(8,128)S(1)} %bitcast.30), channel_id=1, source_target_pairs={{0,48},{8,56},{16,0},{24,8},{32,16},{40,24},{48,32},{56,40},{64,11... | collective-permute-start | bytes 245768 | tf_op jit(solution)/shard_map/ppermute | solution.py:423
  31.1 6.7 %collective-permute-start.1 = (f32[1,5,32,128]{3,2,1,0:T(8,128)S(1)}, f32[1,5,32,128]{3,2,1,0:T(8,128)S(1)}, u32[]{:S(2)}, u32[]{:S(2)}) collective-permute-start(f32[1,5,32,128]{3,2,1,0:T(8,128)S(1)} %bitcast.31), channel_id=1, source_target_pairs={{0,32},{8,40},{16,48},{24,56},{32,0},{40,8},{48,16},{56,24},{64,96... | collective-permute-start | bytes 245768 | tf_op jit(solution)/shard_map/ppermute | solution.py:423
  33.2 5.7 %collective-permute-start = (f32[1,5,32,128]{3,2,1,0:T(8,128)S(1)}, f32[1,5,32,128]{3,2,1,0:T(8,128)S(1)}, u32[]{:S(2)}, u32[]{:S(2)}) collective-permute-start(f32[1,5,32,128]{3,2,1,0:T(8,128)S(1)} %bitcast.32), channel_id=1, source_target_pairs={{0,16},{8,24},{16,32},{24,40},{32,48},{40,56},{48,0},{56,8},{64,80... | collective-permute-start | bytes 245768 | tf_op jit(solution)/shard_map/ppermute | solution.py:423
  38.9 11.7 %collective-permute-start.3 = (f32[4,5,32,128]{3,2,1,0:T(8,128)S(1)}, f32[4,5,32,128]{3,2,1,0:T(8,128)S(1)}, u32[]{:S(2)}, u32[]{:S(2)}) collective-permute-start(f32[4,5,32,128]{3,2,1,0:T(8,128)S(1)} %pad_maximum_fusion.4), channel_id=1, source_target_pairs={{0,64},{8,72},{16,80},{24,88},{32,96},{40,104},{48,112},{56,120},{... | collective-permute-start | bytes 983048 | tf_op jit(solution)/shard_map/ppermute | solution.py:431
  40.4 10.2 %collective-permute-start.4 = (f32[4,32,128]{2,1,0:T(8,128)S(1)}, f32[4,32,128]{2,1,0:T(8,128)S(1)}, u32[]{:S(2)}, u32[]{:S(2)}) collective-permute-start(f32[4,32,128]{2,1,0:T(8,128)S(1)} %get-tuple-element.65), channel_id=1, source_target_pairs={{0,1},{1,2},{2,3},{3,4},{4,5},{5,6},{6,7},{8,9},{9,10},{10,11},{11... | collective-permute-start | bytes 196616 | tf_op jit(solution)/shard_map/ppermute | solution.py:428
  42.8 7.8 %collective-permute-start.5 = (f32[4,32,128]{2,1,0:T(8,128)S(1)}, f32[4,32,128]{2,1,0:T(8,128)S(1)}, u32[]{:S(2)}, u32[]{:S(2)}) collective-permute-start(f32[4,32,128]{2,1,0:T(8,128)S(1)} %get-tuple-element.66), channel_id=1, source_target_pairs={{1,0},{2,1},{3,2},{4,3},{5,4},{6,5},{7,6},{9,8},{10,9},{11,10},{12... | collective-permute-start | bytes 196616 | tf_op jit(solution)/shard_map/ppermute | solution.py:429
  50.6 2.2 %collective-permute-start.6 = (f32[8,5,32,128]{3,2,1,0:T(8,128)S(1)}, f32[8,5,32,128]{3,2,1,0:T(8,128)S(1)}, u32[]{:S(2)}, u32[]{:S(2)}) collective-permute-start(f32[8,5,32,128]{3,2,1,0:T(8,128)S(1)} %pad_maximum_fusion.2), channel_id=1, source_target_pairs={{0,8},{8,0},{16,24},{24,16},{32,40},{40,32},{48,56},{56,48},{64,72... | collective-permute-start | bytes 1966088 | tf_op jit(solution)/shard_map/ppermute | solution.py:438
  65.3 8.3 %collective-permute-start.7 = (f32[4,32,128]{2,1,0:T(8,128)S(1)}, f32[4,32,128]{2,1,0:T(8,128)S(1)}, u32[]{:S(2)}, u32[]{:S(2)}) collective-permute-start(f32[4,32,128]{2,1,0:T(8,128)S(1)} %get-tuple-element.80), channel_id=1, source_target_pairs={{0,7},{7,0},{8,15},{15,8},{16,23},{23,16},{24,31},{31,24},{32,39},... | collective-permute-start | bytes 196616 | tf_op jit(solution)/shard_map/ppermute | solution.py:443
  75.9 4.5 %collective-permute-start.10 = (f32[1,5,32,128]{3,2,1,0:T(8,128)S(1)}, f32[1,5,32,128]{3,2,1,0:T(8,128)S(1)}, u32[]{:S(2)}, u32[]{:S(2)}) collective-permute-start(f32[1,5,32,128]{3,2,1,0:T(8,128)S(1)} %bitcast.26), channel_id=1, source_target_pairs={{0,48},{8,56},{16,0},{24,8},{32,16},{40,24},{48,32},{56,40},{64,11... | collective-permute-start | bytes 245768 | tf_op jit(solution)/shard_map/ppermute | solution.py:423
  77.8 6.0 %collective-permute-start.9 = (f32[1,5,32,128]{3,2,1,0:T(8,128)S(1)}, f32[1,5,32,128]{3,2,1,0:T(8,128)S(1)}, u32[]{:S(2)}, u32[]{:S(2)}) collective-permute-start(f32[1,5,32,128]{3,2,1,0:T(8,128)S(1)} %bitcast.27), channel_id=1, source_target_pairs={{0,32},{8,40},{16,48},{24,56},{32,0},{40,8},{48,16},{56,24},{64,96... | collective-permute-start | bytes 245768 | tf_op jit(solution)/shard_map/ppermute | solution.py:423
  78.1 6.5 %collective-permute-start.8 = (f32[1,5,32,128]{3,2,1,0:T(8,128)S(1)}, f32[1,5,32,128]{3,2,1,0:T(8,128)S(1)}, u32[]{:S(2)}, u32[]{:S(2)}) collective-permute-start(f32[1,5,32,128]{3,2,1,0:T(8,128)S(1)} %bitcast.28), channel_id=1, source_target_pairs={{0,16},{8,24},{16,32},{24,40},{32,48},{40,56},{48,0},{56,8},{64,80... | collective-permute-start | bytes 245768 | tf_op jit(solution)/shard_map/ppermute | solution.py:423
  84.7 9.4 %collective-permute-start.11 = (f32[4,5,32,128]{3,2,1,0:T(8,128)S(1)}, f32[4,5,32,128]{3,2,1,0:T(8,128)S(1)}, u32[]{:S(2)}, u32[]{:S(2)}) collective-permute-start(f32[4,5,32,128]{3,2,1,0:T(8,128)S(1)} %pad_maximum_fusion.5), channel_id=1, source_target_pairs={{0,64},{8,72},{16,80},{24,88},{32,96},{40,104},{48,112},{56,120},{... | collective-permute-start | bytes 983048 | tf_op jit(solution)/shard_map/ppermute | solution.py:431
  87.6 6.5 %collective-permute-start.12 = (f32[4,32,128]{2,1,0:T(8,128)S(1)}, f32[4,32,128]{2,1,0:T(8,128)S(1)}, u32[]{:S(2)}, u32[]{:S(2)}) collective-permute-start(f32[4,32,128]{2,1,0:T(8,128)S(1)} %get-tuple-element.96), channel_id=1, source_target_pairs={{0,1},{1,2},{2,3},{3,4},{4,5},{5,6},{6,7},{8,9},{9,10},{10,11},{11... | collective-permute-start | bytes 196616 | tf_op jit(solution)/shard_map/ppermute | solution.py:428
  88.9 6.2 %collective-permute-start.13 = (f32[4,32,128]{2,1,0:T(8,128)S(1)}, f32[4,32,128]{2,1,0:T(8,128)S(1)}, u32[]{:S(2)}, u32[]{:S(2)}) collective-permute-start(f32[4,32,128]{2,1,0:T(8,128)S(1)} %get-tuple-element.97), channel_id=1, source_target_pairs={{1,0},{2,1},{3,2},{4,3},{5,4},{6,5},{7,6},{9,8},{10,9},{11,10},{12... | collective-permute-start | bytes 196616 | tf_op jit(solution)/shard_map/ppermute | solution.py:429
  95.0 2.1 %collective-permute-start.14 = (f32[8,5,32,128]{3,2,1,0:T(8,128)S(1)}, f32[8,5,32,128]{3,2,1,0:T(8,128)S(1)}, u32[]{:S(2)}, u32[]{:S(2)}) collective-permute-start(f32[8,5,32,128]{3,2,1,0:T(8,128)S(1)} %pad_maximum_fusion.3), channel_id=1, source_target_pairs={{0,8},{8,0},{16,24},{24,16},{32,40},{40,32},{48,56},{56,48},{64,72... | collective-permute-start | bytes 1966088 | tf_op jit(solution)/shard_map/ppermute | solution.py:438
  109.5 8.3 %collective-permute-start.15 = (f32[4,32,128]{2,1,0:T(8,128)S(1)}, f32[4,32,128]{2,1,0:T(8,128)S(1)}, u32[]{:S(2)}, u32[]{:S(2)}) collective-permute-start(f32[4,32,128]{2,1,0:T(8,128)S(1)} %get-tuple-element.106), channel_id=1, source_target_pairs={{0,7},{7,0},{8,15},{15,8},{16,23},{23,16},{24,31},{31,24},{32,39},... | collective-permute-start | bytes 196616 | tf_op jit(solution)/shard_map/ppermute | solution.py:443

commit v7 on v5

--- a/solution.py
+++ b/solution.py
@@ -160,7 +160,7 @@
         place[k * DEVICES : (k + 1) * DEVICES, :] = jnp.where(
             iota((DEVICES, COLS), 1) == col, 1.0, 0.0
         ).astype(jnp.bfloat16)
-    group = 4
+    group = 16
 
     def step(g, carry):
         total = None
@@ -189,7 +189,7 @@
             pltpu.VMEM((PARTS, PLANES, CAP * DEVICES), jnp.float32),
             pltpu.VMEM((CAP * DEVICES, COLS), jnp.bfloat16),
         ],
-        compiler_params=params(8),
+        compiler_params=params(16),
         cost_estimate=pl.CostEstimate(flops=8000000000, bytes_accessed=4325376, transcendentals=0),
         name=f"forcing_{moment}",
     )(slots)
@@ -223,7 +223,7 @@
         tile(end * (ROWS // 8 - 1), 2)
         return carry
 
-    lax.fori_loop(0, ROWS // 8, sides, 0)
+    lax.fori_loop(0, ROWS // 8, sides, 0, unroll=4)
     lax.fori_loop(0, 2, ends, 0)
 
 
@@ -364,6 +364,9 @@
     )(*given, solved, weighted)
 
 
+SLOT_ROWS = PLANES + LEVELS
+
+
 def route_kernel(meta, gathered, first_row, last_row, send, here):
     sub = meta[13]
     lane = iota((PLANES, 128), 1)
@@ -377,12 +380,15 @@
         return jnp.where(side == wanted, found, pltpu.roll(found, 64, 1))
 
     for dest in range(N_SUB):
-        send[dest, 0] = jnp.where(lane < 64, half(2, dest, 0), half(3, dest, 1))
-        send[dest, 1] = jnp.zeros((PLANES, 128), jnp.float32)
+        send[dest, :PLANES, :] = jnp.where(lane < 64, half(2, dest, 0), half(3, dest, 1))
+        send[dest, PLANES : PLANES + LEVELS, :] = jnp.zeros((LEVELS, 128), jnp.float32)
     for edge, dest in ((0, 0), (1, N_SUB - 1)):
         found = gathered[meta[3 * edge], 0]
-        send[dest, 1] = jnp.where(
-            meta[3 * edge + 1] == 2, found, pltpu.roll(found, 64, 1)
+        turned = pltpu.roll(found, 64, 1)
+        low = jnp.where(meta[3 * edge + 1] == 2, found, turned)
+        high = jnp.where(meta[3 * edge + 1] == 2, turned, found)
+        send[dest, PLANES : PLANES + LEVELS, :] = jnp.where(
+            lane[:LEVELS] < 64, low[:LEVELS], high[LEVELS:]
         )
     own = jnp.where(sub == N_SUB - 1, 1, 0)
     place_here = meta[3 * own]
@@ -399,13 +405,13 @@
                 row = jnp.where(sub == 0, across, last)
             else:
                 row = jnp.where(sub == dest - 1, last, first)
-            send[dest, 2 + b] = row
+            send[dest, SLOT_ROWS + b * PLANES : SLOT_ROWS + (b + 1) * PLANES, :] = row
 
 
 def route(meta, gathered, first_row, last_row):
     return pl.pallas_call(
         route_kernel,
-        out_shape=(f32(N_SUB, 6, PLANES, 128), f32(4, PLANES, 128)),
+        out_shape=(f32(N_SUB, SLOT_ROWS + 4 * PLANES, 128), f32(4, PLANES, 128)),
         in_specs=[SMEM] + [VMEM] * 3,
         out_specs=(VMEM,) * 2,
         compiler_params=params(8),
@@ -453,7 +459,7 @@
         same = jnp.where(turned == 1, N_SUB - 1 - sub, sub)
         return jnp.where(other_edge == 0, 0, jnp.where(other_edge == 1, N_SUB - 1, same))
 
-    sides = jnp.where(lane < 64, got[source(2), 0], got[source(3), 0])
+    sides = jnp.where(lane < 64, got[source(2), :PLANES, :], got[source(3), :PLANES, :])
     to = iota((128, 128), 0)
     of = iota((128, 128), 1)
     turned = jnp.where(to < 64, meta[8], meta[11])
@@ -468,15 +474,25 @@
     flip = jnp.where(of == jnp.where(turned == 1, 127 - to, to), 1.0, 0.0)
     row = []
     for b in range(4):
-        joined = jnp.where(lane < 64, got[2 * b, 1], pltpu.roll(got[2 * b + 1, 1], 64, 1))
-        joined = jnp.where(other_edge < 2, got[opposite, 2 + b], joined)
+        part = slice(SLOT_ROWS + b * PLANES, SLOT_ROWS + (b + 1) * PLANES)
+        even = got[2 * b, PLANES:SLOT_ROWS, :]
+        odd = got[2 * b + 1, PLANES:SLOT_ROWS, :]
+        joined = jnp.concatenate(
+            [
+                jnp.where(lane[:LEVELS] < 64, even, pltpu.roll(odd, 64, 1)),
+                jnp.where(lane[:LEVELS] < 64, pltpu.roll(even, 64, 1), odd),
+            ],
+            axis=0,
+        )
+        joined = jnp.where(other_edge < 2, got[opposite, part, :], joined)
         row.append(jnp.where(other_edge == own, here[b], joined))
     for b in range(4):
         ordered = jnp.where(turned == 1, row[3 - b], row[b])
         strip = jnp.dot(ordered, flip, precision=HIGHEST, preferred_element_type=jnp.float32)
         at = b * PLANES * PITCH
-        above_row = jnp.where(sub == 0, strip, got[before, 2 + b])
-        below_row = jnp.where(sub == N_SUB - 1, strip, got[after, 2 + b])
+        part = slice(SLOT_ROWS + b * PLANES, SLOT_ROWS + (b + 1) * PLANES)
+        above_row = jnp.where(sub == 0, strip, got[before, part, :])
+        below_row = jnp.where(sub == N_SUB - 1, strip, got[after, part, :])
         weighted[pl.ds(at + 7, PLANES, stride=PITCH), :] = above_row
         weighted[pl.ds(at + ROWS + 8, PLANES, stride=PITCH), :] = below_row
 
@@ -626,7 +642,7 @@
             tile(block, quarter)
             return carry
 
-        lax.fori_loop(0, ROWS // 8, step, 0)
+        lax.fori_loop(0, ROWS // 8, step, 0, unroll=4)
 
     column(0)
     copy(0).start()

time: 116 us -> 111 us (0.957)
  Pallas kernels: 31.5 us -> 27.6 us
  blocking collectives: 52.6 us -> 51.4 us
    pallas_call x2, Pallas kernels: 8.58 us -> 6.6 us  [forcing(): pl.pallas_call(functools.partial(forcing_kernel, moment), out_shape=f32(P...]
    all_to_all x2, blocking collectives: 32 us -> 30.8 us  [exchange(): got = lax.all_to_all(send, 'sub', split_axis=0, concat_axis=0, tiled=True)]
where the time goes in v7:
time: 111 us; the launch traced here: 110 us
  blocking collectives  51.4 us (46%)
  Pallas kernels  27.6 us (25%)
  waiting for transfers between devices  21.2 us (19%)
  starting transfers between devices  9.59 us (9%)
    all_to_all x2, blocking collectives, exchange(): got = lax.all_to_all(send, 'sub', split_axis=0, concat_axis=0, tiled=True)  30.8 us
    all_to_all x1, blocking collectives, body(): lax.all_to_all(slots, ('tile', 'sub'), split_axis=0, concat_axis=0, tiled...  20.6 us
    ppermute x2, waiting for transfers between devices, exchange(): lax.ppermute(all_parts, 'tile', [(i, i ^ 8) for i in range(N_TILE)])  10 us
    ppermute x6, waiting for transfers between devices, exchange(): lax.ppermute(all_parts, 'tile', turn(k))  7.04 us
    pallas_call x2, Pallas kernels, forcing(): pl.pallas_call(functools.partial(forcing_kernel, moment), out_shape=f32(P...  6.6 us
    ppermute x6, starting transfers between devices, exchange(): lax.ppermute(all_parts, 'tile', turn(k))  5.92 us
    pallas_call x1, Pallas kernels, second_edges(): pl.pallas_call(second_edges_kernel, out_shape=BIG + EDGES + BIG[1:], in_s...  5.39 us
    ppermute x2, waiting for transfers between devices, exchange(): lax.ppermute(all_parts, 'tile', [(i, i ^ 1) for i in range(N_TILE)])  4.17 us
  transfers between devices with their start and end apart: 10, of which 9 were waited for; matrix products, arithmetic and copies ran while one was open for 0% of the time, Pallas kernels for 8%

profile of v7, /device:TPU:0, one launch (start us, length us, event | category | flops | bytes accessed | tf_op | source)
XLA Modules:
  0.0 110.4 jit_solution(9337601375677915662)
XLA Ops:
  0.0 2.3 %pack.1 = (f32[128,2,128]{2,1,0:T(2,128)}, s32[16]{0:T(128)}) custom-call(s32[16]{0:T(128)} %owner_in.1, s32[3,4,16]{2,1,0:T(4,128)} %bitcast.32, s32[1,256]{1,0:T(1,128)} %bitcast.33, s32[1,256]{1,0:T(1,128)} %bitcast.34, s32[1,256]{1,0:T(1,128)} %bitcast.35, f32[32,256]{1,0:T(8,128)} %bitcast.31), custom_call_target="tpu_custom_call" | custom-call | tf_op jit(solution)/shard_map/pack/pallas_call | solution.py:126
  2.3 20.6 %all_to_all.15.slots = f32[128,2,128]{2,1,0:T(2,128)S(1)} all-to-all(f32[128,2,128]{2,1,0:T(2,128)} %get-tuple-element.40), channel_id=1, replica_groups=mesh['tile'=16,'sub'=8] {'tile','sub'}, dimensions={0} | all-to-all | bytes 262144 | tf_op jit(solution)/shard_map/all_to_all | solution.py:711
  22.9 0.0 copy-start
  22.9 0.0 copy-start.1
  22.9 0.0 copy-start.2
  22.9 0.0 copy-start.3
  23.0 0.0 copy-start.4
  23.0 3.3 %forcing_1.1.force = f32[2048,512]{1,0:T(8,128)S(1)} custom-call(f32[128,2,128]{2,1,0:T(2,128)S(1)} %all_to_all.15.slots), custom_call_target="tpu_custom_call" | custom-call | flops 8000000000 | bytes 4325376 | tf_op jit(solution)/shard_map/forcing_1/pallas_call | solution.py:183
  26.3 0.0 copy-done
  26.3 0.0 copy-done.1
  26.3 0.1 copy-done.2
  26.4 0.0 copy-done.3
  26.4 0.0 copy-done.4
  26.4 2.5 %first_edges.1 = (f32[8192,128]{1,0:T(8,128)S(1)}, f32[10240,128]{1,0:T(8,128)S(1)}, f32[5,32,128]{2,1,0:T(8,128)S(1)}, f32[4,32,128]{2,1,0:T(8,128)S(1)}, f32[4,32,128]{2,1,0:T(8,128)S(1)}) custom-call(s32[16]{0:T(128)S(1)} %copy-done.4, f32[2048,512]{1,0:T(8,128)S(1)} %bitcast.21, f32[2048,512]{1,0:T(8,128)S(1)} %forcing_1.1.force, ...), custom_call_target="tpu_custom_call" | custom-call | flops 30000000 | bytes 10000000 | tf_op jit(solution)/shard_map/first_edges/pallas_call | solution.py:342
  28.8 0.8 collective-permute-start.2
  29.6 2.0 %collective-permute-start.1 = (f32[1,5,32,128]{3,2,1,0:T(8,128)S(1)}, f32[1,5,32,128]{3,2,1,0:T(8,128)S(1)}, u32[]{:S(2)}, u32[]{:S(2)}) collective-permute-start(f32[1,5,32,128]{3,2,1,0:T(8,128)S(1)} %bitcast.28), channel_id=1, source_target_pairs={{0,32},{8,40},{16,48},{24,56},{32,0},{40,8},{48,16},{56,24},{64,96... | collective-permute-start | bytes 245768 | tf_op jit(solution)/shard_map/ppermute | solution.py:434
  31.6 0.1 collective-permute-start
  31.7 3.3 %forcing_0.1.force = f32[2048,512]{1,0:T(8,128)S(1)} custom-call(f32[128,2,128]{2,1,0:T(2,128)S(1)} %all_to_all.15.slots), custom_call_target="tpu_custom_call" | custom-call | flops 8000000000 | bytes 4325376 | tf_op jit(solution)/shard_map/forcing_0/pallas_call | solution.py:183
  35.0 0.0 collective-permute-done.2
  35.0 1.2 %collective-permute-done.1 = f32[1,5,32,128]{3,2,1,0:T(8,128)S(1)} collective-permute-done((f32[1,5,32,128]{3,2,1,0:T(8,128)S(1)}, f32[1,5,32,128]{3,2,1,0:T(8,128)S(1)}, u32[]{:S(2)}, u32[]{:S(2)}) %collective-permute-start.1) | collective-permute-done | bytes 81952 | tf_op jit(solution)/shard_map/ppermute | solution.py:434
  36.2 1.0 collective-permute-done
  37.3 1.5 %collective-permute-start.3 = (f32[4,5,32,128]{3,2,1,0:T(8,128)S(1)}, f32[4,5,32,128]{3,2,1,0:T(8,128)S(1)}, u32[]{:S(2)}, u32[]{:S(2)}) collective-permute-start(f32[4,5,32,128]{3,2,1,0:T(8,128)S(1)} %pad_maximum_fusion.4), channel_id=1, source_target_pairs={{0,64},{8,72},{16,80},{24,88},{32,96},{40,104},{48,112},{56,120},{... | collective-permute-start | bytes 983048 | tf_op jit(solution)/shard_map/ppermute | solution.py:438
  38.8 1.1 %first_inner.1 = (f32[8192,128]{1,0:T(8,128)S(1)}, f32[10240,128]{1,0:T(8,128)S(1)}) custom-call(f32[2048,512]{1,0:T(8,128)S(1)} %bitcast.22, f32[2048,512]{1,0:T(8,128)S(1)} %forcing_1.1.force, f32[960,512]{1,0:T(8,128)S(1)} %bitcast.18, f32[1024,512]{1,0:T(8,128)S(1)} %bitcast.12, ...), custom_call_target="tpu_custom_call", output_to_operand_aliasing={{0}: (5, {}), {1}: (6, {})} | custom-call | flops 20000000 | bytes 10000000 | tf_op jit(solution)/shard_map/first_inner/pallas_call | solution.py:355
  39.9 1.8 %second_inner.1 = (f32[8192,128]{1,0:T(8,128)S(1)}, f32[10240,128]{1,0:T(8,128)S(1)}) custom-call(f32[8192,128]{1,0:T(8,128)S(1)} %get-tuple-element.56.solved_in, f32[10240,128]{1,0:T(8,128)S(1)} %get-tuple-element.57.weighted_in, f32[2048,512]{1,0:T(8,128)S(1)} %forcing_0.1.force, f32[960,512]{1,0:T(8,128)S(1)} %bitcast.19, f32[1024,512]{1,0:T(8,128)S(1)} %bitcast.13, ...), custom_call_target="tpu_custom_call" | custom-call | flops 30000000 | bytes 10000000 | tf_op jit(solution)/shard_map/second_inner/pallas_call | solution.py:574
  41.7 5.8 %collective-permute-done.3 = f32[4,5,32,128]{3,2,1,0:T(8,128)S(1)} collective-permute-done((f32[4,5,32,128]{3,2,1,0:T(8,128)S(1)}, f32[4,5,32,128]{3,2,1,0:T(8,128)S(1)}, u32[]{:S(2)}, u32[]{:S(2)}) %collective-permute-start.3) | collective-permute-done | bytes 327712 | tf_op jit(solution)/shard_map/ppermute | solution.py:438
  47.6 0.1 collective-permute-start.4
  47.7 2.1 %collective-permute-done.4 = f32[8,5,32,128]{3,2,1,0:T(8,128)S(1)} collective-permute-done((f32[8,5,32,128]{3,2,1,0:T(8,128)S(1)}, f32[8,5,32,128]{3,2,1,0:T(8,128)S(1)}, u32[]{:S(2)}, u32[]{:S(2)}) %collective-permute-start.4) | collective-permute-done | bytes 655392 | tf_op jit(solution)/shard_map/ppermute | solution.py:443
  49.8 0.1 pad_maximum_fusion.gathered
  49.9 0.7 route.2
  50.6 15.2 %all_to_all.16.got = f32[8,176,128]{2,1,0:T(8,128)S(1)} all-to-all(f32[8,176,128]{2,1,0:T(8,128)S(1)} %get-tuple-element.54), channel_id=1, replica_groups=mesh['tile'=16,'sub'=8] {'sub'}, dimensions={0} | all-to-all | bytes 1441792 | tf_op jit(solution)/shard_map/all_to_all | solution.py:446
  65.9 5.4 %second_edges.1 = (f32[8192,128]{1,0:T(8,128)S(1)}, f32[10240,128]{1,0:T(8,128)S(1)}, f32[5,32,128]{2,1,0:T(8,128)S(1)}, f32[4,32,128]{2,1,0:T(8,128)S(1)}, f32[...) custom-call(s32[16]{0:T(128)S(1)} %copy-done.4, ...), custom_call_target="tpu_custom_call", output_to_operand_aliasing={{0}: (9, {}), {1}: (10, {}), {5}: (4, {})} | custom-call | flops 40000000 | bytes 10000000 | tf_op jit(solution)/shard_map/second_edges/pallas_call | solution.py:586
  71.2 0.9 collective-permute-start.7
  72.2 1.1 collective-permute-start.6
  73.3 1.1 collective-permute-start.5
  74.3 1.4 %collective-permute-done.7 = f32[1,5,32,128]{3,2,1,0:T(8,128)S(1)} collective-permute-done((f32[1,5,32,128]{3,2,1,0:T(8,128)S(1)}, f32[1,5,32,128]{3,2,1,0:T(8,128)S(1)}, u32[]{:S(2)}, u32[]{:S(2)}) %collective-permute-start.7) | collective-permute-done | bytes 81952 | tf_op jit(solution)/shard_map/ppermute | solution.py:434
  75.7 2.5 %collective-permute-done.6 = f32[1,5,32,128]{3,2,1,0:T(8,128)S(1)} collective-permute-done((f32[1,5,32,128]{3,2,1,0:T(8,128)S(1)}, f32[1,5,32,128]{3,2,1,0:T(8,128)S(1)}, u32[]{:S(2)}, u32[]{:S(2)}) %collective-permute-start.6) | collective-permute-done | bytes 81952 | tf_op jit(solution)/shard_map/ppermute | solution.py:434
  78.2 0.9 collective-permute-done.5
  79.1 2.0 %collective-permute-start.8 = (f32[4,5,32,128]{3,2,1,0:T(8,128)S(1)}, f32[4,5,32,128]{3,2,1,0:T(8,128)S(1)}, u32[]{:S(2)}, u32[]{:S(2)}) collective-permute-start(f32[4,5,32,128]{3,2,1,0:T(8,128)S(1)} %pad_maximum_fusion.5), channel_id=1, source_target_pairs={{0,64},{8,72},{16,80},{24,88},{32,96},{40,104},{48,112},{56,120},{... | collective-permute-start | bytes 983048 | tf_op jit(solution)/shard_map/ppermute | solution.py:438
  81.1 2.5 %last_inner.1._ = f32[32,64,512]{2,1,0:T(8,128)} custom-call(f32[8192,128]{1,0:T(8,128)S(1)} %get-tuple-element.63.solved, f32[10240,128]{1,0:T(8,128)S(1)} %get-tuple-element.64.weighted.weighted_in, f32[1024,512]{1,0:T(8,128)S(1)} %bitcast.15, s32[64,512]{1,0:T(8,128)S(1)} %copy-done.3), custom_call_target="tpu_custom_call" | custom-call | flops 20000000 | bytes 10000000 | tf_op jit(solution)/shard_map/last_inner/pallas_call | solution.py:664
  83.6 4.2 %collective-permute-done.8 = f32[4,5,32,128]{3,2,1,0:T(8,128)S(1)} collective-permute-done((f32[4,5,32,128]{3,2,1,0:T(8,128)S(1)}, f32[4,5,32,128]{3,2,1,0:T(8,128)S(1)}, u32[]{:S(2)}, u32[]{:S(2)}) %collective-permute-start.8) | collective-permute-done | bytes 327712 | tf_op jit(solution)/shard_map/ppermute | solution.py:438
  87.8 0.1 collective-permute-start.9
  87.9 2.1 %collective-permute-done.9 = f32[8,5,32,128]{3,2,1,0:T(8,128)S(1)} collective-permute-done((f32[8,5,32,128]{3,2,1,0:T(8,128)S(1)}, f32[8,5,32,128]{3,2,1,0:T(8,128)S(1)}, u32[]{:S(2)}, u32[]{:S(2)}) %collective-permute-start.9) | collective-permute-done | bytes 655392 | tf_op jit(solution)/shard_map/ppermute | solution.py:443
  90.0 0.1 pad_maximum_fusion.1.gathered
  90.1 0.7 route.3
  90.8 15.5 %all_to_all.17.got = f32[8,176,128]{2,1,0:T(8,128)S(1)} all-to-all(f32[8,176,128]{2,1,0:T(8,128)S(1)} %get-tuple-element.69), channel_id=1, replica_groups=mesh['tile'=16,'sub'=8] {'sub'}, dimensions={0} | all-to-all | bytes 1441792 | tf_op jit(solution)/shard_map/all_to_all | solution.py:446
  106.3 4.1 %last_edges.1 = (f32[32,64,512]{2,1,0:T(8,128)}, f32[10240,128]{1,0:T(8,128)S(1)}) custom-call(s32[16]{0:T(128)S(1)} %copy-done.4, f32[8,176,128]{2,1,0:T(8,128)S(1)} %all_to_all.17.got, f32[4,32,128]{2,1,0:T(8,128)S(1)} %get-tuple-element.70.here, f32[8192,128]{1,0:T(8,128)S(1)} %get-tuple-element.63.solved, ...), custom_call_target="tpu_custom_call", output_to_operand_aliasing={{0}: (7, {}), {1}: (4, {})} | custom-call | flops 20000000 | bytes 10000000 | tf_op jit(solution)/shard_map/last_edges/pallas_call | solution.py:677
  (4 shorter events, 0.1 us)
Async XLA Ops:
  22.9 3.3 %copy-start = (f32[16,64,512]{2,1,0:T(8,128)S(1)}, f32[16,64,512]{2,1,0:T(8,128)}, u32[]{:S(2)}) copy-start(f32[16,64,512]{2,1,0:T(8,128)} %param.11) | copy-start | bytes 6291460
  22.9 3.3 %copy-start.1 = (f32[15,64,512]{2,1,0:T(8,128)S(1)}, f32[15,64,512]{2,1,0:T(8,128)}, u32[]{:S(2)}) copy-start(f32[15,64,512]{2,1,0:T(8,128)} %param.12) | copy-start | bytes 5898244
  22.9 3.4 %copy-start.2 = (f32[2,16,64,512]{3,2,1,0:T(8,128)S(1)}, f32[2,16,64,512]{3,2,1,0:T(8,128)}, u32[]{:S(2)}) copy-start(f32[2,16,64,512]{3,2,1,0:T(8,128)} %param.10) | copy-start | bytes 12582916
  22.9 3.4 %copy-start.3 = (s32[64,512]{1,0:T(8,128)S(1)}, s32[64,512]{1,0:T(8,128)}, u32[]{:S(2)}) copy-start(s32[64,512]{1,0:T(8,128)} %depth.8) | copy-start | bytes 393220
  23.0 3.4 %copy-start.4 = (s32[16]{0:T(128)S(1)}, s32[16]{0:T(128)}, u32[]{:S(2)}) copy-start(s32[16]{0:T(128)} %get-tuple-element.39.meta) | copy-start | bytes 196
  28.8 6.2 %collective-permute-start.2 = (f32[1,5,32,128]{3,2,1,0:T(8,128)S(1)}, f32[1,5,32,128]{3,2,1,0:T(8,128)S(1)}, u32[]{:S(2)}, u32[]{:S(2)}) collective-permute-start(f32[1,5,32,128]{3,2,1,0:T(8,128)S(1)} %bitcast.27), channel_id=1, source_target_pairs={{0,48},{8,56},{16,0},{24,8},{32,16},{40,24},{48,32},{56,40},{64,11... | collective-permute-start | bytes 245768 | tf_op jit(solution)/shard_map/ppermute | solution.py:434
  29.6 6.7 %collective-permute-start.1 = (f32[1,5,32,128]{3,2,1,0:T(8,128)S(1)}, f32[1,5,32,128]{3,2,1,0:T(8,128)S(1)}, u32[]{:S(2)}, u32[]{:S(2)}) collective-permute-start(f32[1,5,32,128]{3,2,1,0:T(8,128)S(1)} %bitcast.28), channel_id=1, source_target_pairs={{0,32},{8,40},{16,48},{24,56},{32,0},{40,8},{48,16},{56,24},{64,96... | collective-permute-start | bytes 245768 | tf_op jit(solution)/shard_map/ppermute | solution.py:434
  31.6 5.7 %collective-permute-start = (f32[1,5,32,128]{3,2,1,0:T(8,128)S(1)}, f32[1,5,32,128]{3,2,1,0:T(8,128)S(1)}, u32[]{:S(2)}, u32[]{:S(2)}) collective-permute-start(f32[1,5,32,128]{3,2,1,0:T(8,128)S(1)} %bitcast.29), channel_id=1, source_target_pairs={{0,16},{8,24},{16,32},{24,40},{32,48},{40,56},{48,0},{56,8},{64,80... | collective-permute-start | bytes 245768 | tf_op jit(solution)/shard_map/ppermute | solution.py:434
  37.3 10.3 %collective-permute-start.3 = (f32[4,5,32,128]{3,2,1,0:T(8,128)S(1)}, f32[4,5,32,128]{3,2,1,0:T(8,128)S(1)}, u32[]{:S(2)}, u32[]{:S(2)}) collective-permute-start(f32[4,5,32,128]{3,2,1,0:T(8,128)S(1)} %pad_maximum_fusion.4), channel_id=1, source_target_pairs={{0,64},{8,72},{16,80},{24,88},{32,96},{40,104},{48,112},{56,120},{... | collective-permute-start | bytes 983048 | tf_op jit(solution)/shard_map/ppermute | solution.py:438
  47.6 2.2 %collective-permute-start.4 = (f32[8,5,32,128]{3,2,1,0:T(8,128)S(1)}, f32[8,5,32,128]{3,2,1,0:T(8,128)S(1)}, u32[]{:S(2)}, u32[]{:S(2)}) collective-permute-start(f32[8,5,32,128]{3,2,1,0:T(8,128)S(1)} %pad_maximum_fusion.2), channel_id=1, source_target_pairs={{0,8},{8,0},{16,24},{24,16},{32,40},{40,32},{48,56},{56,48},{64,72... | collective-permute-start | bytes 1966088 | tf_op jit(solution)/shard_map/ppermute | solution.py:443
  71.2 4.5 %collective-permute-start.7 = (f32[1,5,32,128]{3,2,1,0:T(8,128)S(1)}, f32[1,5,32,128]{3,2,1,0:T(8,128)S(1)}, u32[]{:S(2)}, u32[]{:S(2)}) collective-permute-start(f32[1,5,32,128]{3,2,1,0:T(8,128)S(1)} %bitcast.23), channel_id=1, source_target_pairs={{0,48},{8,56},{16,0},{24,8},{32,16},{40,24},{48,32},{56,40},{64,11... | collective-permute-start | bytes 245768 | tf_op jit(solution)/shard_map/ppermute | solution.py:434
  72.2 6.0 %collective-permute-start.6 = (f32[1,5,32,128]{3,2,1,0:T(8,128)S(1)}, f32[1,5,32,128]{3,2,1,0:T(8,128)S(1)}, u32[]{:S(2)}, u32[]{:S(2)}) collective-permute-start(f32[1,5,32,128]{3,2,1,0:T(8,128)S(1)} %bitcast.24), channel_id=1, source_target_pairs={{0,32},{8,40},{16,48},{24,56},{32,0},{40,8},{48,16},{56,24},{64,96... | collective-permute-start | bytes 245768 | tf_op jit(solution)/shard_map/ppermute | solution.py:434
  73.3 5.8 %collective-permute-start.5 = (f32[1,5,32,128]{3,2,1,0:T(8,128)S(1)}, f32[1,5,32,128]{3,2,1,0:T(8,128)S(1)}, u32[]{:S(2)}, u32[]{:S(2)}) collective-permute-start(f32[1,5,32,128]{3,2,1,0:T(8,128)S(1)} %bitcast.25), channel_id=1, source_target_pairs={{0,16},{8,24},{16,32},{24,40},{32,48},{40,56},{48,0},{56,8},{64,80... | collective-permute-start | bytes 245768 | tf_op jit(solution)/shard_map/ppermute | solution.py:434
  79.1 8.7 %collective-permute-start.8 = (f32[4,5,32,128]{3,2,1,0:T(8,128)S(1)}, f32[4,5,32,128]{3,2,1,0:T(8,128)S(1)}, u32[]{:S(2)}, u32[]{:S(2)}) collective-permute-start(f32[4,5,32,128]{3,2,1,0:T(8,128)S(1)} %pad_maximum_fusion.5), channel_id=1, source_target_pairs={{0,64},{8,72},{16,80},{24,88},{32,96},{40,104},{48,112},{56,120},{... | collective-permute-start | bytes 983048 | tf_op jit(solution)/shard_map/ppermute | solution.py:438
  87.8 2.2 %collective-permute-start.9 = (f32[8,5,32,128]{3,2,1,0:T(8,128)S(1)}, f32[8,5,32,128]{3,2,1,0:T(8,128)S(1)}, u32[]{:S(2)}, u32[]{:S(2)}) collective-permute-start(f32[8,5,32,128]{3,2,1,0:T(8,128)S(1)} %pad_maximum_fusion.3), channel_id=1, source_target_pairs={{0,8},{8,0},{16,24},{24,16},{32,40},{40,32},{48,56},{56,48},{64,72... | collective-permute-start | bytes 1966088 | tf_op jit(solution)/shard_map/ppermute | solution.py:443

commit v8 on v7

--- a/solution.py
+++ b/solution.py
@@ -73,10 +73,11 @@
     meta[13] = sub
     for edge in range(4):
         other = owner(seam(0, edge, my_face))
+        steps = (((tile >> 1) & 3) + 4 - ((other >> 1) & 3)) & 3
         away = (
             ((other & 1) ^ (tile & 1)) * 8
             + (((other >> 3) & 1) ^ ((tile >> 3) & 1)) * 4
-            + ((((tile >> 1) & 3) + 4 - ((other >> 1) & 3)) & 3)
+            + (steps ^ (steps >> 1))
         )
         meta[3 * edge] = away
         meta[3 * edge + 1] = seam(1, edge, my_face)
@@ -431,7 +432,7 @@
 
     all_parts = payload[None]
     all_parts = jnp.concatenate(
-        [all_parts] + [lax.ppermute(all_parts, "tile", turn(k)) for k in (1, 2, 3)], axis=0
+        [all_parts] + [lax.ppermute(all_parts, "tile", turn(k)) for k in (1, 3, 2)], axis=0
     )
     all_parts, depth, *extra = lax.optimization_barrier((all_parts, depth, *beside_z()))
     all_parts = jnp.concatenate(
@@ -560,13 +561,27 @@
 
 def second_edges_kernel(meta, got, here, solved_in, weighted_in, force, coupling, scale, depth, _,
                         __, solved, weighted, payload, first_row, last_row, weighted_late, sides,
-                        strips):
+                        strips, late):
     place_halo(meta, got, here, weighted_late, strips)
-    edge_tiles(
-        second_tile(
-            solved_in, weighted_late, force, coupling, scale, depth, solved, weighted, strips, sides
-        )
-    )
+
+    def right_side(block, quarter):
+        columns = slice(quarter * 128, (quarter + 1) * 128)
+        value = stepped(solved_in, weighted_late, scale, depth, strips, block, quarter)
+        for level in range(LEVELS):
+            for plane in (level, LEVELS + level):
+                at = (pl.ds(pl.multiple_of(plane * ROWS + block * 8, 8), 8), columns)
+                late[at] = value(plane) + force[at]
+
+    def solve(block, quarter):
+        columns = slice(quarter * 128, (quarter + 1) * 128)
+
+        def value(plane):
+            return late[pl.ds(pl.multiple_of(plane * ROWS + block * 8, 8), 8), columns]
+
+        solve_tile(value, coupling, scale, depth, solved, weighted, sides, block, quarter)
+
+    edge_tiles(right_side)
+    edge_tiles(solve)
     send_edges(meta, weighted, sides, payload, first_row, last_row)
 
 
@@ -589,8 +604,8 @@
         in_specs=[SMEM] + [VMEM] * 10,
         out_specs=(VMEM,) * 6,
         input_output_aliases={9: 0, 10: 1, 4: 5},
-        scratch_shapes=[SIDES] * 2,
-        compiler_params=params(8),
+        scratch_shapes=[SIDES] * 2 + [pltpu.VMEM((PLANES * ROWS, COLS), jnp.float32)],
+        compiler_params=params(12),
         cost_estimate=cost(40000000),
         name="second_edges",
     )(meta, *halos, *given)

time: 111 us -> 111 us (level)
    ppermute x6, starting transfers between devices: 5.92 us -> 7.25 us  [exchange(): lax.ppermute(all_parts, 'tile', turn(k))]
  transfers between devices with their start and end apart: 10 -> 10, of which waited for: 9 -> 7; matrix products, arithmetic and copies ran while one was open for 0% -> 0% of each run, Pallas kernels for 8% -> 8%
where the time goes in v8:
time: 111 us; the launch traced here: 110 us
  blocking collectives  51 us (46%)
  Pallas kernels  27.2 us (25%)
  waiting for transfers between devices  21 us (19%)
  starting transfers between devices  10.5 us (9%)
    all_to_all x2, blocking collectives, exchange(): got = lax.all_to_all(send, 'sub', split_axis=0, concat_axis=0, tiled=True)  30.4 us
    all_to_all x1, blocking collectives, body(): lax.all_to_all(slots, ('tile', 'sub'), split_axis=0, concat_axis=0, tiled...  20.6 us
    ppermute x2, waiting for transfers between devices, exchange(): lax.ppermute(all_parts, 'tile', [(i, i ^ 8) for i in range(N_TILE)])  10.4 us
    ppermute x6, starting transfers between devices, exchange(): lax.ppermute(all_parts, 'tile', turn(k))  7.25 us
    pallas_call x2, Pallas kernels, forcing(): pl.pallas_call(functools.partial(forcing_kernel, moment), out_shape=f32(P...  6.6 us
    ppermute x6, waiting for transfers between devices, exchange(): lax.ppermute(all_parts, 'tile', turn(k))  6.43 us
    pallas_call x1, Pallas kernels, second_edges(): pl.pallas_call(second_edges_kernel, out_shape=BIG + EDGES + BIG[1:], in_s...  4.99 us
    ppermute x2, waiting for transfers between devices, exchange(): lax.ppermute(all_parts, 'tile', [(i, i ^ 1) for i in range(N_TILE)])  4.17 us
  transfers between devices with their start and end apart: 10, of which 7 were waited for; matrix products, arithmetic and copies ran while one was open for 0% of the time, Pallas kernels for 8%

profile of v8, /device:TPU:0, one launch (start us, length us, event | category | flops | bytes accessed | tf_op | source)
XLA Modules:
  0.0 110.4 jit_solution(13789813780300734135)
XLA Ops:
  0.0 2.3 %pack.1 = (f32[128,2,128]{2,1,0:T(2,128)}, s32[16]{0:T(128)}) custom-call(s32[16]{0:T(128)} %owner_in.1, s32[3,4,16]{2,1,0:T(4,128)} %bitcast.32, s32[1,256]{1,0:T(1,128)} %bitcast.33, s32[1,256]{1,0:T(1,128)} %bitcast.34, s32[1,256]{1,0:T(1,128)} %bitcast.35, f32[32,256]{1,0:T(8,128)} %bitcast.31), custom_call_target="tpu_custom_call" | custom-call | tf_op jit(solution)/shard_map/pack/pallas_call | solution.py:127
  2.3 20.6 %all_to_all.15.slots = f32[128,2,128]{2,1,0:T(2,128)S(1)} all-to-all(f32[128,2,128]{2,1,0:T(2,128)} %get-tuple-element.40), channel_id=1, replica_groups=mesh['tile'=16,'sub'=8] {'tile','sub'}, dimensions={0} | all-to-all | bytes 262144 | tf_op jit(solution)/shard_map/all_to_all | solution.py:726
  22.9 0.0 copy-start
  22.9 0.0 copy-start.1
  22.9 0.0 copy-start.2
  22.9 0.0 copy-start.3
  23.0 0.0 copy-start.4
  23.0 3.3 %forcing_1.1.force = f32[2048,512]{1,0:T(8,128)S(1)} custom-call(f32[128,2,128]{2,1,0:T(2,128)S(1)} %all_to_all.15.slots), custom_call_target="tpu_custom_call" | custom-call | flops 8000000000 | bytes 4325376 | tf_op jit(solution)/shard_map/forcing_1/pallas_call | solution.py:184
  26.3 0.0 copy-done
  26.3 0.0 copy-done.1
  26.3 0.1 copy-done.2
  26.4 0.0 copy-done.3
  26.4 0.0 copy-done.4
  26.4 2.5 %first_edges.1 = (f32[8192,128]{1,0:T(8,128)S(1)}, f32[10240,128]{1,0:T(8,128)S(1)}, f32[5,32,128]{2,1,0:T(8,128)S(1)}, f32[4,32,128]{2,1,0:T(8,128)S(1)}, f32[4,32,128]{2,1,0:T(8,128)S(1)}) custom-call(s32[16]{0:T(128)S(1)} %copy-done.4, f32[2048,512]{1,0:T(8,128)S(1)} %bitcast.21, f32[2048,512]{1,0:T(8,128)S(1)} %forcing_1.1.force, ...), custom_call_target="tpu_custom_call" | custom-call | flops 30000000 | bytes 10000000 | tf_op jit(solution)/shard_map/first_edges/pallas_call | solution.py:343
  28.8 1.4 %collective-permute-start.2 = (f32[1,5,32,128]{3,2,1,0:T(8,128)S(1)}, f32[1,5,32,128]{3,2,1,0:T(8,128)S(1)}, u32[]{:S(2)}, u32[]{:S(2)}) collective-permute-start(f32[1,5,32,128]{3,2,1,0:T(8,128)S(1)} %bitcast.27), channel_id=1, source_target_pairs={{0,32},{8,40},{16,48},{24,56},{32,0},{40,8},{48,16},{56,24},{64,96... | collective-permute-start | bytes 245768 | tf_op jit(solution)/shard_map/ppermute | solution.py:435
  30.3 2.0 %collective-permute-start.1 = (f32[1,5,32,128]{3,2,1,0:T(8,128)S(1)}, f32[1,5,32,128]{3,2,1,0:T(8,128)S(1)}, u32[]{:S(2)}, u32[]{:S(2)}) collective-permute-start(f32[1,5,32,128]{3,2,1,0:T(8,128)S(1)} %bitcast.28), channel_id=1, source_target_pairs={{0,48},{8,56},{16,0},{24,8},{32,16},{40,24},{48,32},{56,40},{64,11... | collective-permute-start | bytes 245768 | tf_op jit(solution)/shard_map/ppermute | solution.py:435
  32.2 0.1 collective-permute-start
  32.3 3.3 %forcing_0.1.force = f32[2048,512]{1,0:T(8,128)S(1)} custom-call(f32[128,2,128]{2,1,0:T(2,128)S(1)} %all_to_all.15.slots), custom_call_target="tpu_custom_call" | custom-call | flops 8000000000 | bytes 4325376 | tf_op jit(solution)/shard_map/forcing_0/pallas_call | solution.py:184
  35.6 0.0 collective-permute-done.2
  35.6 0.0 collective-permute-done.1
  35.6 2.3 %collective-permute-done = f32[1,5,32,128]{3,2,1,0:T(8,128)S(1)} collective-permute-done((f32[1,5,32,128]{3,2,1,0:T(8,128)S(1)}, f32[1,5,32,128]{3,2,1,0:T(8,128)S(1)}, u32[]{:S(2)}, u32[]{:S(2)}) %collective-permute-start) | collective-permute-done | bytes 81952 | tf_op jit(solution)/shard_map/ppermute | solution.py:435
  37.9 1.5 %collective-permute-start.3 = (f32[4,5,32,128]{3,2,1,0:T(8,128)S(1)}, f32[4,5,32,128]{3,2,1,0:T(8,128)S(1)}, u32[]{:S(2)}, u32[]{:S(2)}) collective-permute-start(f32[4,5,32,128]{3,2,1,0:T(8,128)S(1)} %pad_maximum_fusion.4), channel_id=1, source_target_pairs={{0,64},{8,72},{16,80},{24,88},{32,96},{40,104},{48,112},{56,120},{... | collective-permute-start | bytes 983048 | tf_op jit(solution)/shard_map/ppermute | solution.py:439
  39.4 1.2 %first_inner.1 = (f32[8192,128]{1,0:T(8,128)S(1)}, f32[10240,128]{1,0:T(8,128)S(1)}) custom-call(f32[2048,512]{1,0:T(8,128)S(1)} %bitcast.22, f32[2048,512]{1,0:T(8,128)S(1)} %forcing_1.1.force, f32[960,512]{1,0:T(8,128)S(1)} %bitcast.18, f32[1024,512]{1,0:T(8,128)S(1)} %bitcast.12, ...), custom_call_target="tpu_custom_call", output_to_operand_aliasing={{0}: (5, {}), {1}: (6, {})} | custom-call | flops 20000000 | bytes 10000000 | tf_op jit(solution)/shard_map/first_inner/pallas_call | solution.py:356
  40.6 1.8 %second_inner.1 = (f32[8192,128]{1,0:T(8,128)S(1)}, f32[10240,128]{1,0:T(8,128)S(1)}) custom-call(f32[8192,128]{1,0:T(8,128)S(1)} %get-tuple-element.56.solved_in, f32[10240,128]{1,0:T(8,128)S(1)} %get-tuple-element.57.weighted_in, f32[2048,512]{1,0:T(8,128)S(1)} %forcing_0.1.force, f32[960,512]{1,0:T(8,128)S(1)} %bitcast.19, f32[1024,512]{1,0:T(8,128)S(1)} %bitcast.13, ...), custom_call_target="tpu_custom_call" | custom-call | flops 30000000 | bytes 10000000 | tf_op jit(solution)/shard_map/second_inner/pallas_call | solution.py:589
  42.4 5.0 %collective-permute-done.3 = f32[4,5,32,128]{3,2,1,0:T(8,128)S(1)} collective-permute-done((f32[4,5,32,128]{3,2,1,0:T(8,128)S(1)}, f32[4,5,32,128]{3,2,1,0:T(8,128)S(1)}, u32[]{:S(2)}, u32[]{:S(2)}) %collective-permute-start.3) | collective-permute-done | bytes 327712 | tf_op jit(solution)/shard_map/ppermute | solution.py:439
  47.4 0.1 collective-permute-start.4
  47.5 2.1 %collective-permute-done.4 = f32[8,5,32,128]{3,2,1,0:T(8,128)S(1)} collective-permute-done((f32[8,5,32,128]{3,2,1,0:T(8,128)S(1)}, f32[8,5,32,128]{3,2,1,0:T(8,128)S(1)}, u32[]{:S(2)}, u32[]{:S(2)}) %collective-permute-start.4) | collective-permute-done | bytes 655392 | tf_op jit(solution)/shard_map/ppermute | solution.py:444
  49.6 0.1 pad_maximum_fusion.gathered
  49.7 0.7 route.2
  50.4 15.2 %all_to_all.16.got = f32[8,176,128]{2,1,0:T(8,128)S(1)} all-to-all(f32[8,176,128]{2,1,0:T(8,128)S(1)} %get-tuple-element.54), channel_id=1, replica_groups=mesh['tile'=16,'sub'=8] {'sub'}, dimensions={0} | all-to-all | bytes 1441792 | tf_op jit(solution)/shard_map/all_to_all | solution.py:447
  65.6 5.0 %second_edges.1 = (f32[8192,128]{1,0:T(8,128)S(1)}, f32[10240,128]{1,0:T(8,128)S(1)}, f32[5,32,128]{2,1,0:T(8,128)S(1)}, f32[4,32,128]{2,1,0:T(8,128)S(1)}, f32[...) custom-call(s32[16]{0:T(128)S(1)} %copy-done.4, ...), custom_call_target="tpu_custom_call", output_to_operand_aliasing={{0}: (9, {}), {1}: (10, {}), {5}: (4, {})} | custom-call | flops 40000000 | bytes 10000000 | tf_op jit(solution)/shard_map/second_edges/pallas_call | solution.py:601
  70.6 1.8 %collective-permute-start.7 = (f32[1,5,32,128]{3,2,1,0:T(8,128)S(1)}, f32[1,5,32,128]{3,2,1,0:T(8,128)S(1)}, u32[]{:S(2)}, u32[]{:S(2)}) collective-permute-start(f32[1,5,32,128]{3,2,1,0:T(8,128)S(1)} %bitcast.23), channel_id=1, source_target_pairs={{0,32},{8,40},{16,48},{24,56},{32,0},{40,8},{48,16},{56,24},{64,96... | collective-permute-start | bytes 245768 | tf_op jit(solution)/shard_map/ppermute | solution.py:435
  72.3 0.5 collective-permute-start.6
  72.9 1.5 %collective-permute-start.5 = (f32[1,5,32,128]{3,2,1,0:T(8,128)S(1)}, f32[1,5,32,128]{3,2,1,0:T(8,128)S(1)}, u32[]{:S(2)}, u32[]{:S(2)}) collective-permute-start(f32[1,5,32,128]{3,2,1,0:T(8,128)S(1)} %bitcast.25), channel_id=1, source_target_pairs={{0,16},{8,24},{16,32},{24,40},{32,48},{40,56},{48,0},{56,8},{64,80... | collective-permute-start | bytes 245768 | tf_op jit(solution)/shard_map/ppermute | solution.py:435
  74.4 2.6 %collective-permute-done.7 = f32[1,5,32,128]{3,2,1,0:T(8,128)S(1)} collective-permute-done((f32[1,5,32,128]{3,2,1,0:T(8,128)S(1)}, f32[1,5,32,128]{3,2,1,0:T(8,128)S(1)}, u32[]{:S(2)}, u32[]{:S(2)}) %collective-permute-start.7) | collective-permute-done | bytes 81952 | tf_op jit(solution)/shard_map/ppermute | solution.py:435
  76.9 0.0 collective-permute-done.6
  76.9 1.6 %collective-permute-done.5 = f32[1,5,32,128]{3,2,1,0:T(8,128)S(1)} collective-permute-done((f32[1,5,32,128]{3,2,1,0:T(8,128)S(1)}, f32[1,5,32,128]{3,2,1,0:T(8,128)S(1)}, u32[]{:S(2)}, u32[]{:S(2)}) %collective-permute-start.5) | collective-permute-done | bytes 81952 | tf_op jit(solution)/shard_map/ppermute | solution.py:435
  78.6 1.6 %collective-permute-start.8 = (f32[4,5,32,128]{3,2,1,0:T(8,128)S(1)}, f32[4,5,32,128]{3,2,1,0:T(8,128)S(1)}, u32[]{:S(2)}, u32[]{:S(2)}) collective-permute-start(f32[4,5,32,128]{3,2,1,0:T(8,128)S(1)} %pad_maximum_fusion.5), channel_id=1, source_target_pairs={{0,64},{8,72},{16,80},{24,88},{32,96},{40,104},{48,112},{56,120},{... | collective-permute-start | bytes 983048 | tf_op jit(solution)/shard_map/ppermute | solution.py:439
  80.2 2.5 %last_inner.1._ = f32[32,64,512]{2,1,0:T(8,128)} custom-call(f32[8192,128]{1,0:T(8,128)S(1)} %get-tuple-element.63.solved, f32[10240,128]{1,0:T(8,128)S(1)} %get-tuple-element.64.weighted.weighted_in, f32[1024,512]{1,0:T(8,128)S(1)} %bitcast.15, s32[64,512]{1,0:T(8,128)S(1)} %copy-done.3), custom_call_target="tpu_custom_call" | custom-call | flops 20000000 | bytes 10000000 | tf_op jit(solution)/shard_map/last_inner/pallas_call | solution.py:679
  82.7 5.4 %collective-permute-done.8 = f32[4,5,32,128]{3,2,1,0:T(8,128)S(1)} collective-permute-done((f32[4,5,32,128]{3,2,1,0:T(8,128)S(1)}, f32[4,5,32,128]{3,2,1,0:T(8,128)S(1)}, u32[]{:S(2)}, u32[]{:S(2)}) %collective-permute-start.8) | collective-permute-done | bytes 327712 | tf_op jit(solution)/shard_map/ppermute | solution.py:439
  88.1 0.1 collective-permute-start.9
  88.2 2.1 %collective-permute-done.9 = f32[8,5,32,128]{3,2,1,0:T(8,128)S(1)} collective-permute-done((f32[8,5,32,128]{3,2,1,0:T(8,128)S(1)}, f32[8,5,32,128]{3,2,1,0:T(8,128)S(1)}, u32[]{:S(2)}, u32[]{:S(2)}) %collective-permute-start.9) | collective-permute-done | bytes 655392 | tf_op jit(solution)/shard_map/ppermute | solution.py:444
  90.3 0.1 pad_maximum_fusion.1.gathered
  90.4 0.7 route.3
  91.1 15.2 %all_to_all.17.got = f32[8,176,128]{2,1,0:T(8,128)S(1)} all-to-all(f32[8,176,128]{2,1,0:T(8,128)S(1)} %get-tuple-element.69), channel_id=1, replica_groups=mesh['tile'=16,'sub'=8] {'sub'}, dimensions={0} | all-to-all | bytes 1441792 | tf_op jit(solution)/shard_map/all_to_all | solution.py:447
  106.3 4.1 %last_edges.1 = (f32[32,64,512]{2,1,0:T(8,128)}, f32[10240,128]{1,0:T(8,128)S(1)}) custom-call(s32[16]{0:T(128)S(1)} %copy-done.4, f32[8,176,128]{2,1,0:T(8,128)S(1)} %all_to_all.17.got, f32[4,32,128]{2,1,0:T(8,128)S(1)} %get-tuple-element.70.here, f32[8192,128]{1,0:T(8,128)S(1)} %get-tuple-element.63.solved, ...), custom_call_target="tpu_custom_call", output_to_operand_aliasing={{0}: (7, {}), {1}: (4, {})} | custom-call | flops 20000000 | bytes 10000000 | tf_op jit(solution)/shard_map/last_edges/pallas_call | solution.py:692
  (4 shorter events, 0.1 us)
Async XLA Ops:
  22.9 3.3 %copy-start = (f32[16,64,512]{2,1,0:T(8,128)S(1)}, f32[16,64,512]{2,1,0:T(8,128)}, u32[]{:S(2)}) copy-start(f32[16,64,512]{2,1,0:T(8,128)} %param.11) | copy-start | bytes 6291460
  22.9 3.3 %copy-start.1 = (f32[15,64,512]{2,1,0:T(8,128)S(1)}, f32[15,64,512]{2,1,0:T(8,128)}, u32[]{:S(2)}) copy-start(f32[15,64,512]{2,1,0:T(8,128)} %param.12) | copy-start | bytes 5898244
  22.9 3.4 %copy-start.2 = (f32[2,16,64,512]{3,2,1,0:T(8,128)S(1)}, f32[2,16,64,512]{3,2,1,0:T(8,128)}, u32[]{:S(2)}) copy-start(f32[2,16,64,512]{3,2,1,0:T(8,128)} %param.10) | copy-start | bytes 12582916
  22.9 3.4 %copy-start.3 = (s32[64,512]{1,0:T(8,128)S(1)}, s32[64,512]{1,0:T(8,128)}, u32[]{:S(2)}) copy-start(s32[64,512]{1,0:T(8,128)} %depth.8) | copy-start | bytes 393220
  23.0 3.4 %copy-start.4 = (s32[16]{0:T(128)S(1)}, s32[16]{0:T(128)}, u32[]{:S(2)}) copy-start(s32[16]{0:T(128)} %get-tuple-element.39.meta) | copy-start | bytes 196
  28.8 6.8 %collective-permute-start.2 = (f32[1,5,32,128]{3,2,1,0:T(8,128)S(1)}, f32[1,5,32,128]{3,2,1,0:T(8,128)S(1)}, u32[]{:S(2)}, u32[]{:S(2)}) collective-permute-start(f32[1,5,32,128]{3,2,1,0:T(8,128)S(1)} %bitcast.27), channel_id=1, source_target_pairs={{0,32},{8,40},{16,48},{24,56},{32,0},{40,8},{48,16},{56,24},{64,96... | collective-permute-start | bytes 245768 | tf_op jit(solution)/shard_map/ppermute | solution.py:435
  30.3 5.3 %collective-permute-start.1 = (f32[1,5,32,128]{3,2,1,0:T(8,128)S(1)}, f32[1,5,32,128]{3,2,1,0:T(8,128)S(1)}, u32[]{:S(2)}, u32[]{:S(2)}) collective-permute-start(f32[1,5,32,128]{3,2,1,0:T(8,128)S(1)} %bitcast.28), channel_id=1, source_target_pairs={{0,48},{8,56},{16,0},{24,8},{32,16},{40,24},{48,32},{56,40},{64,11... | collective-permute-start | bytes 245768 | tf_op jit(solution)/shard_map/ppermute | solution.py:435
  32.2 5.7 %collective-permute-start = (f32[1,5,32,128]{3,2,1,0:T(8,128)S(1)}, f32[1,5,32,128]{3,2,1,0:T(8,128)S(1)}, u32[]{:S(2)}, u32[]{:S(2)}) collective-permute-start(f32[1,5,32,128]{3,2,1,0:T(8,128)S(1)} %bitcast.29), channel_id=1, source_target_pairs={{0,16},{8,24},{16,32},{24,40},{32,48},{40,56},{48,0},{56,8},{64,80... | collective-permute-start | bytes 245768 | tf_op jit(solution)/shard_map/ppermute | solution.py:435
  37.9 9.5 %collective-permute-start.3 = (f32[4,5,32,128]{3,2,1,0:T(8,128)S(1)}, f32[4,5,32,128]{3,2,1,0:T(8,128)S(1)}, u32[]{:S(2)}, u32[]{:S(2)}) collective-permute-start(f32[4,5,32,128]{3,2,1,0:T(8,128)S(1)} %pad_maximum_fusion.4), channel_id=1, source_target_pairs={{0,64},{8,72},{16,80},{24,88},{32,96},{40,104},{48,112},{56,120},{... | collective-permute-start | bytes 983048 | tf_op jit(solution)/shard_map/ppermute | solution.py:439
  47.4 2.2 %collective-permute-start.4 = (f32[8,5,32,128]{3,2,1,0:T(8,128)S(1)}, f32[8,5,32,128]{3,2,1,0:T(8,128)S(1)}, u32[]{:S(2)}, u32[]{:S(2)}) collective-permute-start(f32[8,5,32,128]{3,2,1,0:T(8,128)S(1)} %pad_maximum_fusion.2), channel_id=1, source_target_pairs={{0,8},{8,0},{16,24},{24,16},{32,40},{40,32},{48,56},{56,48},{64,72... | collective-permute-start | bytes 1966088 | tf_op jit(solution)/shard_map/ppermute | solution.py:444
  70.6 6.4 %collective-permute-start.7 = (f32[1,5,32,128]{3,2,1,0:T(8,128)S(1)}, f32[1,5,32,128]{3,2,1,0:T(8,128)S(1)}, u32[]{:S(2)}, u32[]{:S(2)}) collective-permute-start(f32[1,5,32,128]{3,2,1,0:T(8,128)S(1)} %bitcast.23), channel_id=1, source_target_pairs={{0,32},{8,40},{16,48},{24,56},{32,0},{40,8},{48,16},{56,24},{64,96... | collective-permute-start | bytes 245768 | tf_op jit(solution)/shard_map/ppermute | solution.py:435
  72.3 4.6 %collective-permute-start.6 = (f32[1,5,32,128]{3,2,1,0:T(8,128)S(1)}, f32[1,5,32,128]{3,2,1,0:T(8,128)S(1)}, u32[]{:S(2)}, u32[]{:S(2)}) collective-permute-start(f32[1,5,32,128]{3,2,1,0:T(8,128)S(1)} %bitcast.24), channel_id=1, source_target_pairs={{0,48},{8,56},{16,0},{24,8},{32,16},{40,24},{48,32},{56,40},{64,11... | collective-permute-start | bytes 245768 | tf_op jit(solution)/shard_map/ppermute | solution.py:435
  72.9 5.7 %collective-permute-start.5 = (f32[1,5,32,128]{3,2,1,0:T(8,128)S(1)}, f32[1,5,32,128]{3,2,1,0:T(8,128)S(1)}, u32[]{:S(2)}, u32[]{:S(2)}) collective-permute-start(f32[1,5,32,128]{3,2,1,0:T(8,128)S(1)} %bitcast.25), channel_id=1, source_target_pairs={{0,16},{8,24},{16,32},{24,40},{32,48},{40,56},{48,0},{56,8},{64,80... | collective-permute-start | bytes 245768 | tf_op jit(solution)/shard_map/ppermute | solution.py:435
  78.6 9.5 %collective-permute-start.8 = (f32[4,5,32,128]{3,2,1,0:T(8,128)S(1)}, f32[4,5,32,128]{3,2,1,0:T(8,128)S(1)}, u32[]{:S(2)}, u32[]{:S(2)}) collective-permute-start(f32[4,5,32,128]{3,2,1,0:T(8,128)S(1)} %pad_maximum_fusion.5), channel_id=1, source_target_pairs={{0,64},{8,72},{16,80},{24,88},{32,96},{40,104},{48,112},{56,120},{... | collective-permute-start | bytes 983048 | tf_op jit(solution)/shard_map/ppermute | solution.py:439
  88.1 2.2 %collective-permute-start.9 = (f32[8,5,32,128]{3,2,1,0:T(8,128)S(1)}, f32[8,5,32,128]{3,2,1,0:T(8,128)S(1)}, u32[]{:S(2)}, u32[]{:S(2)}) collective-permute-start(f32[8,5,32,128]{3,2,1,0:T(8,128)S(1)} %pad_maximum_fusion.3), channel_id=1, source_target_pairs={{0,8},{8,0},{16,24},{24,16},{32,40},{40,32},{48,56},{56,48},{64,72... | collective-permute-start | bytes 1966088 | tf_op jit(solution)/shard_map/ppermute | solution.py:444

commit v9 on v8

--- a/solution.py
+++ b/solution.py
@@ -225,7 +225,7 @@
         return carry
 
     lax.fori_loop(0, ROWS // 8, sides, 0, unroll=4)
-    lax.fori_loop(0, 2, ends, 0)
+    lax.fori_loop(0, 2, ends, 0, unroll=2)
 
 
 def inner_tiles(tile):
@@ -487,9 +487,15 @@
         )
         joined = jnp.where(other_edge < 2, got[opposite, part, :], joined)
         row.append(jnp.where(other_edge == own, here[b], joined))
+    ordered = [jnp.where(turned == 1, row[3 - b], row[b]) for b in range(4)]
+    strips_in_order = jnp.dot(
+        jnp.concatenate(ordered, axis=0),
+        flip,
+        precision=HIGHEST,
+        preferred_element_type=jnp.float32,
+    )
     for b in range(4):
-        ordered = jnp.where(turned == 1, row[3 - b], row[b])
-        strip = jnp.dot(ordered, flip, precision=HIGHEST, preferred_element_type=jnp.float32)
+        strip = strips_in_order[b * PLANES : (b + 1) * PLANES]
         at = b * PLANES * PITCH
         part = slice(SLOT_ROWS + b * PLANES, SLOT_ROWS + (b + 1) * PLANES)
         above_row = jnp.where(sub == 0, strip, got[before, part, :])

time: 111 us -> 110 us (level)
  no operation moved by 1% of the time
where the time goes in v9:
time: 110 us
  blocking collectives  51 us (46%)
  Pallas kernels  26.6 us (24%)
  waiting for transfers between devices  21 us (19%)
  starting transfers between devices  10.6 us (10%)
    all_to_all x2, blocking collectives, exchange(): got = lax.all_to_all(send, 'sub', split_axis=0, concat_axis=0, tiled=True)  30.4 us
    all_to_all x1, blocking collectives, body(): lax.all_to_all(slots, ('tile', 'sub'), split_axis=0, concat_axis=0, tiled...  20.6 us
    ppermute x2, waiting for transfers between devices, exchange(): lax.ppermute(all_parts, 'tile', [(i, i ^ 8) for i in range(N_TILE)])  10.4 us
    ppermute x6, starting transfers between devices, exchange(): lax.ppermute(all_parts, 'tile', turn(k))  7.27 us
    pallas_call x2, Pallas kernels, forcing(): pl.pallas_call(functools.partial(forcing_kernel, moment), out_shape=f32(P...  6.6 us
    ppermute x6, waiting for transfers between devices, exchange(): lax.ppermute(all_parts, 'tile', turn(k))  6.44 us
    pallas_call x1, Pallas kernels, second_edges(): pl.pallas_call(second_edges_kernel, out_shape=BIG + EDGES + BIG[1:], in_s...  4.64 us
    ppermute x2, waiting for transfers between devices, exchange(): lax.ppermute(all_parts, 'tile', [(i, i ^ 1) for i in range(N_TILE)])  4.17 us
  transfers between devices with their start and end apart: 10, of which 7 were waited for; matrix products, arithmetic and copies ran while one was open for 0% of the time, Pallas kernels for 8%

profile of v9, /device:TPU:0, one launch (start us, length us, event | category | flops | bytes accessed | tf_op | source)
XLA Modules:
  0.0 109.8 jit_solution(7936275051859128189)
XLA Ops:
  0.0 2.3 %pack.1 = (f32[128,2,128]{2,1,0:T(2,128)}, s32[16]{0:T(128)}) custom-call(s32[16]{0:T(128)} %owner_in.1, s32[3,4,16]{2,1,0:T(4,128)} %bitcast.32, s32[1,256]{1,0:T(1,128)} %bitcast.33, s32[1,256]{1,0:T(1,128)} %bitcast.34, s32[1,256]{1,0:T(1,128)} %bitcast.35, f32[32,256]{1,0:T(8,128)} %bitcast.31), custom_call_target="tpu_custom_call" | custom-call | tf_op jit(solution)/shard_map/pack/pallas_call | solution.py:127
  2.3 20.6 %all_to_all.15.slots = f32[128,2,128]{2,1,0:T(2,128)S(1)} all-to-all(f32[128,2,128]{2,1,0:T(2,128)} %get-tuple-element.40), channel_id=1, replica_groups=mesh['tile'=16,'sub'=8] {'tile','sub'}, dimensions={0} | all-to-all | bytes 262144 | tf_op jit(solution)/shard_map/all_to_all | solution.py:732
  22.9 0.0 copy-start
  22.9 0.0 copy-start.1
  22.9 0.0 copy-start.2
  22.9 0.0 copy-start.3
  23.0 0.0 copy-start.4
  23.0 3.3 %forcing_1.1.force = f32[2048,512]{1,0:T(8,128)S(1)} custom-call(f32[128,2,128]{2,1,0:T(2,128)S(1)} %all_to_all.15.slots), custom_call_target="tpu_custom_call" | custom-call | flops 8000000000 | bytes 4325376 | tf_op jit(solution)/shard_map/forcing_1/pallas_call | solution.py:184
  26.3 0.0 copy-done
  26.3 0.0 copy-done.1
  26.3 0.1 copy-done.2
  26.4 0.0 copy-done.3
  26.4 0.0 copy-done.4
  26.4 2.3 %first_edges.1 = (f32[8192,128]{1,0:T(8,128)S(1)}, f32[10240,128]{1,0:T(8,128)S(1)}, f32[5,32,128]{2,1,0:T(8,128)S(1)}, f32[4,32,128]{2,1,0:T(8,128)S(1)}, f32[4,32,128]{2,1,0:T(8,128)S(1)}) custom-call(s32[16]{0:T(128)S(1)} %copy-done.4, f32[2048,512]{1,0:T(8,128)S(1)} %bitcast.21, f32[2048,512]{1,0:T(8,128)S(1)} %forcing_1.1.force, ...), custom_call_target="tpu_custom_call" | custom-call | flops 30000000 | bytes 10000000 | tf_op jit(solution)/shard_map/first_edges/pallas_call | solution.py:343
  28.7 1.4 %collective-permute-start.2 = (f32[1,5,32,128]{3,2,1,0:T(8,128)S(1)}, f32[1,5,32,128]{3,2,1,0:T(8,128)S(1)}, u32[]{:S(2)}, u32[]{:S(2)}) collective-permute-start(f32[1,5,32,128]{3,2,1,0:T(8,128)S(1)} %bitcast.27), channel_id=1, source_target_pairs={{0,32},{8,40},{16,48},{24,56},{32,0},{40,8},{48,16},{56,24},{64,96... | collective-permute-start | bytes 245768 | tf_op jit(solution)/shard_map/ppermute | solution.py:435
  30.1 2.0 %collective-permute-start.1 = (f32[1,5,32,128]{3,2,1,0:T(8,128)S(1)}, f32[1,5,32,128]{3,2,1,0:T(8,128)S(1)}, u32[]{:S(2)}, u32[]{:S(2)}) collective-permute-start(f32[1,5,32,128]{3,2,1,0:T(8,128)S(1)} %bitcast.28), channel_id=1, source_target_pairs={{0,48},{8,56},{16,0},{24,8},{32,16},{40,24},{48,32},{56,40},{64,11... | collective-permute-start | bytes 245768 | tf_op jit(solution)/shard_map/ppermute | solution.py:435
  32.1 0.1 collective-permute-start
  32.2 3.3 %forcing_0.1.force = f32[2048,512]{1,0:T(8,128)S(1)} custom-call(f32[128,2,128]{2,1,0:T(2,128)S(1)} %all_to_all.15.slots), custom_call_target="tpu_custom_call" | custom-call | flops 8000000000 | bytes 4325376 | tf_op jit(solution)/shard_map/forcing_0/pallas_call | solution.py:184
  35.5 0.0 collective-permute-done.2
  35.5 0.0 collective-permute-done.1
  35.5 2.3 %collective-permute-done = f32[1,5,32,128]{3,2,1,0:T(8,128)S(1)} collective-permute-done((f32[1,5,32,128]{3,2,1,0:T(8,128)S(1)}, f32[1,5,32,128]{3,2,1,0:T(8,128)S(1)}, u32[]{:S(2)}, u32[]{:S(2)}) %collective-permute-start) | collective-permute-done | bytes 81952 | tf_op jit(solution)/shard_map/ppermute | solution.py:435
  37.8 1.5 %collective-permute-start.3 = (f32[4,5,32,128]{3,2,1,0:T(8,128)S(1)}, f32[4,5,32,128]{3,2,1,0:T(8,128)S(1)}, u32[]{:S(2)}, u32[]{:S(2)}) collective-permute-start(f32[4,5,32,128]{3,2,1,0:T(8,128)S(1)} %pad_maximum_fusion.4), channel_id=1, source_target_pairs={{0,64},{8,72},{16,80},{24,88},{32,96},{40,104},{48,112},{56,120},{... | collective-permute-start | bytes 983048 | tf_op jit(solution)/shard_map/ppermute | solution.py:439
  39.3 1.2 %first_inner.1 = (f32[8192,128]{1,0:T(8,128)S(1)}, f32[10240,128]{1,0:T(8,128)S(1)}) custom-call(f32[2048,512]{1,0:T(8,128)S(1)} %bitcast.22, f32[2048,512]{1,0:T(8,128)S(1)} %forcing_1.1.force, f32[960,512]{1,0:T(8,128)S(1)} %bitcast.18, f32[1024,512]{1,0:T(8,128)S(1)} %bitcast.12, ...), custom_call_target="tpu_custom_call", output_to_operand_aliasing={{0}: (5, {}), {1}: (6, {})} | custom-call | flops 20000000 | bytes 10000000 | tf_op jit(solution)/shard_map/first_inner/pallas_call | solution.py:356
  40.5 1.8 %second_inner.1 = (f32[8192,128]{1,0:T(8,128)S(1)}, f32[10240,128]{1,0:T(8,128)S(1)}) custom-call(f32[8192,128]{1,0:T(8,128)S(1)} %get-tuple-element.56.solved_in, f32[10240,128]{1,0:T(8,128)S(1)} %get-tuple-element.57.weighted_in, f32[2048,512]{1,0:T(8,128)S(1)} %forcing_0.1.force, f32[960,512]{1,0:T(8,128)S(1)} %bitcast.19, f32[1024,512]{1,0:T(8,128)S(1)} %bitcast.13, ...), custom_call_target="tpu_custom_call" | custom-call | flops 30000000 | bytes 10000000 | tf_op jit(solution)/shard_map/second_inner/pallas_call | solution.py:595
  42.2 5.0 %collective-permute-done.3 = f32[4,5,32,128]{3,2,1,0:T(8,128)S(1)} collective-permute-done((f32[4,5,32,128]{3,2,1,0:T(8,128)S(1)}, f32[4,5,32,128]{3,2,1,0:T(8,128)S(1)}, u32[]{:S(2)}, u32[]{:S(2)}) %collective-permute-start.3) | collective-permute-done | bytes 327712 | tf_op jit(solution)/shard_map/ppermute | solution.py:439
  47.3 0.1 collective-permute-start.4
  47.4 2.1 %collective-permute-done.4 = f32[8,5,32,128]{3,2,1,0:T(8,128)S(1)} collective-permute-done((f32[8,5,32,128]{3,2,1,0:T(8,128)S(1)}, f32[8,5,32,128]{3,2,1,0:T(8,128)S(1)}, u32[]{:S(2)}, u32[]{:S(2)}) %collective-permute-start.4) | collective-permute-done | bytes 655392 | tf_op jit(solution)/shard_map/ppermute | solution.py:444
  49.5 0.1 pad_maximum_fusion.gathered
  49.6 0.7 route.2
  50.3 15.2 %all_to_all.16.got = f32[8,176,128]{2,1,0:T(8,128)S(1)} all-to-all(f32[8,176,128]{2,1,0:T(8,128)S(1)} %get-tuple-element.54), channel_id=1, replica_groups=mesh['tile'=16,'sub'=8] {'sub'}, dimensions={0} | all-to-all | bytes 1441792 | tf_op jit(solution)/shard_map/all_to_all | solution.py:447
  65.4 4.6 %second_edges.1 = (f32[8192,128]{1,0:T(8,128)S(1)}, f32[10240,128]{1,0:T(8,128)S(1)}, f32[5,32,128]{2,1,0:T(8,128)S(1)}, f32[4,32,128]{2,1,0:T(8,128)S(1)}, f32[...) custom-call(s32[16]{0:T(128)S(1)} %copy-done.4, ...), custom_call_target="tpu_custom_call", output_to_operand_aliasing={{0}: (9, {}), {1}: (10, {}), {5}: (4, {})} | custom-call | flops 40000000 | bytes 10000000 | tf_op jit(solution)/shard_map/second_edges/pallas_call | solution.py:607
  70.1 1.8 %collective-permute-start.7 = (f32[1,5,32,128]{3,2,1,0:T(8,128)S(1)}, f32[1,5,32,128]{3,2,1,0:T(8,128)S(1)}, u32[]{:S(2)}, u32[]{:S(2)}) collective-permute-start(f32[1,5,32,128]{3,2,1,0:T(8,128)S(1)} %bitcast.23), channel_id=1, source_target_pairs={{0,32},{8,40},{16,48},{24,56},{32,0},{40,8},{48,16},{56,24},{64,96... | collective-permute-start | bytes 245768 | tf_op jit(solution)/shard_map/ppermute | solution.py:435
  71.9 0.5 collective-permute-start.6
  72.4 1.5 %collective-permute-start.5 = (f32[1,5,32,128]{3,2,1,0:T(8,128)S(1)}, f32[1,5,32,128]{3,2,1,0:T(8,128)S(1)}, u32[]{:S(2)}, u32[]{:S(2)}) collective-permute-start(f32[1,5,32,128]{3,2,1,0:T(8,128)S(1)} %bitcast.25), channel_id=1, source_target_pairs={{0,16},{8,24},{16,32},{24,40},{32,48},{40,56},{48,0},{56,8},{64,80... | collective-permute-start | bytes 245768 | tf_op jit(solution)/shard_map/ppermute | solution.py:435
  73.9 2.6 %collective-permute-done.7 = f32[1,5,32,128]{3,2,1,0:T(8,128)S(1)} collective-permute-done((f32[1,5,32,128]{3,2,1,0:T(8,128)S(1)}, f32[1,5,32,128]{3,2,1,0:T(8,128)S(1)}, u32[]{:S(2)}, u32[]{:S(2)}) %collective-permute-start.7) | collective-permute-done | bytes 81952 | tf_op jit(solution)/shard_map/ppermute | solution.py:435
  76.5 0.0 collective-permute-done.6
  76.5 1.6 %collective-permute-done.5 = f32[1,5,32,128]{3,2,1,0:T(8,128)S(1)} collective-permute-done((f32[1,5,32,128]{3,2,1,0:T(8,128)S(1)}, f32[1,5,32,128]{3,2,1,0:T(8,128)S(1)}, u32[]{:S(2)}, u32[]{:S(2)}) %collective-permute-start.5) | collective-permute-done | bytes 81952 | tf_op jit(solution)/shard_map/ppermute | solution.py:435
  78.1 1.6 %collective-permute-start.8 = (f32[4,5,32,128]{3,2,1,0:T(8,128)S(1)}, f32[4,5,32,128]{3,2,1,0:T(8,128)S(1)}, u32[]{:S(2)}, u32[]{:S(2)}) collective-permute-start(f32[4,5,32,128]{3,2,1,0:T(8,128)S(1)} %pad_maximum_fusion.5), channel_id=1, source_target_pairs={{0,64},{8,72},{16,80},{24,88},{32,96},{40,104},{48,112},{56,120},{... | collective-permute-start | bytes 983048 | tf_op jit(solution)/shard_map/ppermute | solution.py:439
  79.7 2.5 %last_inner.1._ = f32[32,64,512]{2,1,0:T(8,128)} custom-call(f32[8192,128]{1,0:T(8,128)S(1)} %get-tuple-element.63.solved, f32[10240,128]{1,0:T(8,128)S(1)} %get-tuple-element.64.weighted.weighted_in, f32[1024,512]{1,0:T(8,128)S(1)} %bitcast.15, s32[64,512]{1,0:T(8,128)S(1)} %copy-done.3), custom_call_target="tpu_custom_call" | custom-call | flops 20000000 | bytes 10000000 | tf_op jit(solution)/shard_map/last_inner/pallas_call | solution.py:685
  82.2 5.4 %collective-permute-done.8 = f32[4,5,32,128]{3,2,1,0:T(8,128)S(1)} collective-permute-done((f32[4,5,32,128]{3,2,1,0:T(8,128)S(1)}, f32[4,5,32,128]{3,2,1,0:T(8,128)S(1)}, u32[]{:S(2)}, u32[]{:S(2)}) %collective-permute-start.8) | collective-permute-done | bytes 327712 | tf_op jit(solution)/shard_map/ppermute | solution.py:439
  87.7 0.1 collective-permute-start.9
  87.8 2.1 %collective-permute-done.9 = f32[8,5,32,128]{3,2,1,0:T(8,128)S(1)} collective-permute-done((f32[8,5,32,128]{3,2,1,0:T(8,128)S(1)}, f32[8,5,32,128]{3,2,1,0:T(8,128)S(1)}, u32[]{:S(2)}, u32[]{:S(2)}) %collective-permute-start.9) | collective-permute-done | bytes 655392 | tf_op jit(solution)/shard_map/ppermute | solution.py:444
  89.9 0.1 pad_maximum_fusion.1.gathered
  90.0 0.7 route.3
  90.7 15.2 %all_to_all.17.got = f32[8,176,128]{2,1,0:T(8,128)S(1)} all-to-all(f32[8,176,128]{2,1,0:T(8,128)S(1)} %get-tuple-element.69), channel_id=1, replica_groups=mesh['tile'=16,'sub'=8] {'sub'}, dimensions={0} | all-to-all | bytes 1441792 | tf_op jit(solution)/shard_map/all_to_all | solution.py:447
  105.8 4.0 %last_edges.1 = (f32[32,64,512]{2,1,0:T(8,128)}, f32[10240,128]{1,0:T(8,128)S(1)}) custom-call(s32[16]{0:T(128)S(1)} %copy-done.4, f32[8,176,128]{2,1,0:T(8,128)S(1)} %all_to_all.17.got, f32[4,32,128]{2,1,0:T(8,128)S(1)} %get-tuple-element.70.here, f32[8192,128]{1,0:T(8,128)S(1)} %get-tuple-element.63.solved, ...), custom_call_target="tpu_custom_call", output_to_operand_aliasing={{0}: (7, {}), {1}: (4, {})} | custom-call | flops 20000000 | bytes 10000000 | tf_op jit(solution)/shard_map/last_edges/pallas_call | solution.py:698
  (4 shorter events, 0.1 us)
Async XLA Ops:
  22.9 3.3 %copy-start = (f32[16,64,512]{2,1,0:T(8,128)S(1)}, f32[16,64,512]{2,1,0:T(8,128)}, u32[]{:S(2)}) copy-start(f32[16,64,512]{2,1,0:T(8,128)} %param.11) | copy-start | bytes 6291460
  22.9 3.3 %copy-start.1 = (f32[15,64,512]{2,1,0:T(8,128)S(1)}, f32[15,64,512]{2,1,0:T(8,128)}, u32[]{:S(2)}) copy-start(f32[15,64,512]{2,1,0:T(8,128)} %param.12) | copy-start | bytes 5898244
  22.9 3.4 %copy-start.2 = (f32[2,16,64,512]{3,2,1,0:T(8,128)S(1)}, f32[2,16,64,512]{3,2,1,0:T(8,128)}, u32[]{:S(2)}) copy-start(f32[2,16,64,512]{3,2,1,0:T(8,128)} %param.10) | copy-start | bytes 12582916
  22.9 3.4 %copy-start.3 = (s32[64,512]{1,0:T(8,128)S(1)}, s32[64,512]{1,0:T(8,128)}, u32[]{:S(2)}) copy-start(s32[64,512]{1,0:T(8,128)} %depth.8) | copy-start | bytes 393220
  23.0 3.4 %copy-start.4 = (s32[16]{0:T(128)S(1)}, s32[16]{0:T(128)}, u32[]{:S(2)}) copy-start(s32[16]{0:T(128)} %get-tuple-element.39.meta) | copy-start | bytes 196
  28.7 6.8 %collective-permute-start.2 = (f32[1,5,32,128]{3,2,1,0:T(8,128)S(1)}, f32[1,5,32,128]{3,2,1,0:T(8,128)S(1)}, u32[]{:S(2)}, u32[]{:S(2)}) collective-permute-start(f32[1,5,32,128]{3,2,1,0:T(8,128)S(1)} %bitcast.27), channel_id=1, source_target_pairs={{0,32},{8,40},{16,48},{24,56},{32,0},{40,8},{48,16},{56,24},{64,96... | collective-permute-start | bytes 245768 | tf_op jit(solution)/shard_map/ppermute | solution.py:435
  30.1 5.3 %collective-permute-start.1 = (f32[1,5,32,128]{3,2,1,0:T(8,128)S(1)}, f32[1,5,32,128]{3,2,1,0:T(8,128)S(1)}, u32[]{:S(2)}, u32[]{:S(2)}) collective-permute-start(f32[1,5,32,128]{3,2,1,0:T(8,128)S(1)} %bitcast.28), channel_id=1, source_target_pairs={{0,48},{8,56},{16,0},{24,8},{32,16},{40,24},{48,32},{56,40},{64,11... | collective-permute-start | bytes 245768 | tf_op jit(solution)/shard_map/ppermute | solution.py:435
  32.1 5.7 %collective-permute-start = (f32[1,5,32,128]{3,2,1,0:T(8,128)S(1)}, f32[1,5,32,128]{3,2,1,0:T(8,128)S(1)}, u32[]{:S(2)}, u32[]{:S(2)}) collective-permute-start(f32[1,5,32,128]{3,2,1,0:T(8,128)S(1)} %bitcast.29), channel_id=1, source_target_pairs={{0,16},{8,24},{16,32},{24,40},{32,48},{40,56},{48,0},{56,8},{64,80... | collective-permute-start | bytes 245768 | tf_op jit(solution)/shard_map/ppermute | solution.py:435
  37.8 9.5 %collective-permute-start.3 = (f32[4,5,32,128]{3,2,1,0:T(8,128)S(1)}, f32[4,5,32,128]{3,2,1,0:T(8,128)S(1)}, u32[]{:S(2)}, u32[]{:S(2)}) collective-permute-start(f32[4,5,32,128]{3,2,1,0:T(8,128)S(1)} %pad_maximum_fusion.4), channel_id=1, source_target_pairs={{0,64},{8,72},{16,80},{24,88},{32,96},{40,104},{48,112},{56,120},{... | collective-permute-start | bytes 983048 | tf_op jit(solution)/shard_map/ppermute | solution.py:439
  47.3 2.2 %collective-permute-start.4 = (f32[8,5,32,128]{3,2,1,0:T(8,128)S(1)}, f32[8,5,32,128]{3,2,1,0:T(8,128)S(1)}, u32[]{:S(2)}, u32[]{:S(2)}) collective-permute-start(f32[8,5,32,128]{3,2,1,0:T(8,128)S(1)} %pad_maximum_fusion.2), channel_id=1, source_target_pairs={{0,8},{8,0},{16,24},{24,16},{32,40},{40,32},{48,56},{56,48},{64,72... | collective-permute-start | bytes 1966088 | tf_op jit(solution)/shard_map/ppermute | solution.py:444
  70.1 6.4 %collective-permute-start.7 = (f32[1,5,32,128]{3,2,1,0:T(8,128)S(1)}, f32[1,5,32,128]{3,2,1,0:T(8,128)S(1)}, u32[]{:S(2)}, u32[]{:S(2)}) collective-permute-start(f32[1,5,32,128]{3,2,1,0:T(8,128)S(1)} %bitcast.23), channel_id=1, source_target_pairs={{0,32},{8,40},{16,48},{24,56},{32,0},{40,8},{48,16},{56,24},{64,96... | collective-permute-start | bytes 245768 | tf_op jit(solution)/shard_map/ppermute | solution.py:435
  71.9 4.6 %collective-permute-start.6 = (f32[1,5,32,128]{3,2,1,0:T(8,128)S(1)}, f32[1,5,32,128]{3,2,1,0:T(8,128)S(1)}, u32[]{:S(2)}, u32[]{:S(2)}) collective-permute-start(f32[1,5,32,128]{3,2,1,0:T(8,128)S(1)} %bitcast.24), channel_id=1, source_target_pairs={{0,48},{8,56},{16,0},{24,8},{32,16},{40,24},{48,32},{56,40},{64,11... | collective-permute-start | bytes 245768 | tf_op jit(solution)/shard_map/ppermute | solution.py:435
  72.4 5.7 %collective-permute-start.5 = (f32[1,5,32,128]{3,2,1,0:T(8,128)S(1)}, f32[1,5,32,128]{3,2,1,0:T(8,128)S(1)}, u32[]{:S(2)}, u32[]{:S(2)}) collective-permute-start(f32[1,5,32,128]{3,2,1,0:T(8,128)S(1)} %bitcast.25), channel_id=1, source_target_pairs={{0,16},{8,24},{16,32},{24,40},{32,48},{40,56},{48,0},{56,8},{64,80... | collective-permute-start | bytes 245768 | tf_op jit(solution)/shard_map/ppermute | solution.py:435
  78.1 9.5 %collective-permute-start.8 = (f32[4,5,32,128]{3,2,1,0:T(8,128)S(1)}, f32[4,5,32,128]{3,2,1,0:T(8,128)S(1)}, u32[]{:S(2)}, u32[]{:S(2)}) collective-permute-start(f32[4,5,32,128]{3,2,1,0:T(8,128)S(1)} %pad_maximum_fusion.5), channel_id=1, source_target_pairs={{0,64},{8,72},{16,80},{24,88},{32,96},{40,104},{48,112},{56,120},{... | collective-permute-start | bytes 983048 | tf_op jit(solution)/shard_map/ppermute | solution.py:439
  87.7 2.2 %collective-permute-start.9 = (f32[8,5,32,128]{3,2,1,0:T(8,128)S(1)}, f32[8,5,32,128]{3,2,1,0:T(8,128)S(1)}, u32[]{:S(2)}, u32[]{:S(2)}) collective-permute-start(f32[8,5,32,128]{3,2,1,0:T(8,128)S(1)} %pad_maximum_fusion.3), channel_id=1, source_target_pairs={{0,8},{8,0},{16,24},{24,16},{32,40},{40,32},{48,56},{56,48},{64,72... | collective-permute-start | bytes 1966088 | tf_op jit(solution)/shard_map/ppermute | solution.py:444

commit v10 on v9

--- a/solution.py
+++ b/solution.py
@@ -421,7 +421,7 @@
     )(meta, gathered, first_row, last_row)
 
 
-def exchange(meta, depth, beside_z, beside_y, payload, first_row, last_row):
+def exchange(meta, held, beside_z, beside_y, payload, first_row, last_row):
     def turn(k):
         return [
             (y * 8 + z * 2 + c, y * 8 + ((z + k) % 4) * 2 + c)
@@ -434,11 +434,11 @@
     all_parts = jnp.concatenate(
         [all_parts] + [lax.ppermute(all_parts, "tile", turn(k)) for k in (1, 3, 2)], axis=0
     )
-    all_parts, depth, *extra = lax.optimization_barrier((all_parts, depth, *beside_z()))
+    all_parts, held, extra = lax.optimization_barrier((all_parts, held, beside_z()))
     all_parts = jnp.concatenate(
         [all_parts, lax.ppermute(all_parts, "tile", [(i, i ^ 8) for i in range(N_TILE)])], axis=0
     )
-    extra = beside_y(depth, *extra)
+    extra = beside_y(*held, *extra)
     all_parts, *extra = lax.optimization_barrier((all_parts, *extra))
     all_parts = jnp.concatenate(
         [all_parts, lax.ppermute(all_parts, "tile", [(i, i ^ 1) for i in range(N_TILE)])], axis=0
@@ -738,21 +738,21 @@
     solved, weighted, *edges = first_edges(meta, *given)
 
     def beside_z():
-        return (forcing(slots, 0),)
-
-    def beside_y(depth, early):
-        whole = first_inner(solved, weighted, *given[:-1], depth)
-        return *whole, early, *second_inner(*whole, early, coupling, scale, depth)
+        return first_inner(solved, weighted, *given)
+
+    def beside_y(slots, *whole):
+        early = forcing(slots, 0)
+        return *whole, early, *second_inner(*whole, early, coupling, scale, column_depth)
 
     halos, (solved, weighted, early, *begun) = exchange(
-        meta, column_depth, beside_z, beside_y, *edges
+        meta, (slots,), beside_z, beside_y, *edges
     )
     solved, weighted, *edges, _ = second_edges(
         meta, halos, solved, weighted, early, coupling, scale, column_depth, *begun
     )
     halos, begun = exchange(
         meta,
-        column_depth,
+        (column_depth,),
         lambda: (),
         lambda depth: (last_inner(solved, weighted, scale, depth),),
         *edges,

time: 110 us -> 110 us (level)
    ppermute x2, waiting for transfers between devices: 10.4 us -> 8.26 us  [exchange(): lax.ppermute(all_parts, 'tile', [(i, i ^ 8) for i in range(N_TILE)])]
    ppermute x6, waiting for transfers between devices: 6.44 us -> 8.51 us  [exchange(): lax.ppermute(all_parts, 'tile', turn(k))]
  transfers between devices with their start and end apart: 10 -> 10, of which waited for: 7 -> 8; matrix products, arithmetic and copies ran while one was open for 0% -> 0% of each run, Pallas kernels for 8% -> 8%
where the time goes in v10:
time: 110 us
  blocking collectives  51 us (46%)
  Pallas kernels  26.9 us (24%)
  waiting for transfers between devices  20.9 us (19%)
  starting transfers between devices  10.6 us (10%)
    all_to_all x2, blocking collectives, exchange(): got = lax.all_to_all(send, 'sub', split_axis=0, concat_axis=0, tiled=True)  30.4 us
    all_to_all x1, blocking collectives, body(): lax.all_to_all(slots, ('tile', 'sub'), split_axis=0, concat_axis=0, tiled...  20.6 us
    ppermute x6, waiting for transfers between devices, exchange(): lax.ppermute(all_parts, 'tile', turn(k))  8.51 us
    ppermute x2, waiting for transfers between devices, exchange(): lax.ppermute(all_parts, 'tile', [(i, i ^ 8) for i in range(N_TILE)])  8.26 us
    ppermute x6, starting transfers between devices, exchange(): lax.ppermute(all_parts, 'tile', turn(k))  7.27 us
    pallas_call x2, Pallas kernels, forcing(): pl.pallas_call(functools.partial(forcing_kernel, moment), out_shape=f32(P...  6.6 us
    pallas_call x1, Pallas kernels, second_edges(): pl.pallas_call(second_edges_kernel, out_shape=BIG + EDGES + BIG[1:], in_s...  4.75 us
    ppermute x2, waiting for transfers between devices, exchange(): lax.ppermute(all_parts, 'tile', [(i, i ^ 1) for i in range(N_TILE)])  4.17 us
  transfers between devices with their start and end apart: 10, of which 8 were waited for; matrix products, arithmetic and copies ran while one was open for 0% of the time, Pallas kernels for 8%

profile of v10, /device:TPU:0, one launch (start us, length us, event | category | flops | bytes accessed | tf_op | source)
XLA Modules:
  0.0 110.0 jit_solution(18058216266343246097)
XLA Ops:
  0.0 2.3 %pack.1 = (f32[128,2,128]{2,1,0:T(2,128)}, s32[16]{0:T(128)}) custom-call(s32[16]{0:T(128)} %owner_in.1, s32[3,4,16]{2,1,0:T(4,128)} %bitcast.32, s32[1,256]{1,0:T(1,128)} %bitcast.33, s32[1,256]{1,0:T(1,128)} %bitcast.34, s32[1,256]{1,0:T(1,128)} %bitcast.35, f32[32,256]{1,0:T(8,128)} %bitcast.31), custom_call_target="tpu_custom_call" | custom-call | tf_op jit(solution)/shard_map/pack/pallas_call | solution.py:127
  2.3 20.6 %all_to_all.15.slots = f32[128,2,128]{2,1,0:T(2,128)S(1)} all-to-all(f32[128,2,128]{2,1,0:T(2,128)} %get-tuple-element.41), channel_id=1, replica_groups=mesh['tile'=16,'sub'=8] {'tile','sub'}, dimensions={0} | all-to-all | bytes 262144 | tf_op jit(solution)/shard_map/all_to_all | solution.py:732
  22.9 0.0 copy-start
  22.9 0.0 copy-start.1
  22.9 0.0 copy-start.2
  22.9 0.0 copy-start.3
  23.0 0.0 copy-start.4
  23.0 3.3 %forcing_1.1.force = f32[2048,512]{1,0:T(8,128)S(1)} custom-call(f32[128,2,128]{2,1,0:T(2,128)S(1)} %all_to_all.15.slots), custom_call_target="tpu_custom_call" | custom-call | flops 8000000000 | bytes 4325376 | tf_op jit(solution)/shard_map/forcing_1/pallas_call | solution.py:184
  26.3 0.0 copy-done
  26.3 0.0 copy-done.1
  26.3 0.1 copy-done.2
  26.4 0.0 copy-done.3
  26.4 0.0 copy-done.4
  26.4 2.4 %first_edges.1 = (f32[8192,128]{1,0:T(8,128)S(1)}, f32[10240,128]{1,0:T(8,128)S(1)}, f32[5,32,128]{2,1,0:T(8,128)S(1)}, f32[4,32,128]{2,1,0:T(8,128)S(1)}, f32[4,32,128]{2,1,0:T(8,128)S(1)}) custom-call(s32[16]{0:T(128)S(1)} %copy-done.4, f32[2048,512]{1,0:T(8,128)S(1)} %bitcast.21, f32[2048,512]{1,0:T(8,128)S(1)} %forcing_1.1.force, ...), custom_call_target="tpu_custom_call" | custom-call | flops 30000000 | bytes 10000000 | tf_op jit(solution)/shard_map/first_edges/pallas_call | solution.py:343
  28.7 1.4 %collective-permute-start.2 = (f32[1,5,32,128]{3,2,1,0:T(8,128)S(1)}, f32[1,5,32,128]{3,2,1,0:T(8,128)S(1)}, u32[]{:S(2)}, u32[]{:S(2)}) collective-permute-start(f32[1,5,32,128]{3,2,1,0:T(8,128)S(1)} %bitcast.27), channel_id=1, source_target_pairs={{0,32},{8,40},{16,48},{24,56},{32,0},{40,8},{48,16},{56,24},{64,96... | collective-permute-start | bytes 245768 | tf_op jit(solution)/shard_map/ppermute | solution.py:435
  30.2 2.0 %collective-permute-start.1 = (f32[1,5,32,128]{3,2,1,0:T(8,128)S(1)}, f32[1,5,32,128]{3,2,1,0:T(8,128)S(1)}, u32[]{:S(2)}, u32[]{:S(2)}) collective-permute-start(f32[1,5,32,128]{3,2,1,0:T(8,128)S(1)} %bitcast.28), channel_id=1, source_target_pairs={{0,48},{8,56},{16,0},{24,8},{32,16},{40,24},{48,32},{56,40},{64,11... | collective-permute-start | bytes 245768 | tf_op jit(solution)/shard_map/ppermute | solution.py:435
  32.1 0.1 collective-permute-start
  32.2 1.2 %first_inner.1 = (f32[8192,128]{1,0:T(8,128)S(1)}, f32[10240,128]{1,0:T(8,128)S(1)}) custom-call(f32[2048,512]{1,0:T(8,128)S(1)} %bitcast.22, f32[2048,512]{1,0:T(8,128)S(1)} %forcing_1.1.force, f32[960,512]{1,0:T(8,128)S(1)} %bitcast.18, f32[1024,512]{1,0:T(8,128)S(1)} %bitcast.12, ...), custom_call_target="tpu_custom_call", output_to_operand_aliasing={{0}: (5, {}), {1}: (6, {})} | custom-call | flops 20000000 | bytes 10000000 | tf_op jit(solution)/shard_map/first_inner/pallas_call | solution.py:356
  33.4 1.9 %collective-permute-done.2 = f32[1,5,32,128]{3,2,1,0:T(8,128)S(1)} collective-permute-done((f32[1,5,32,128]{3,2,1,0:T(8,128)S(1)}, f32[1,5,32,128]{3,2,1,0:T(8,128)S(1)}, u32[]{:S(2)}, u32[]{:S(2)}) %collective-permute-start.2) | collective-permute-done | bytes 81952 | tf_op jit(solution)/shard_map/ppermute | solution.py:435
  35.4 0.0 collective-permute-done.1
  35.4 2.4 %collective-permute-done = f32[1,5,32,128]{3,2,1,0:T(8,128)S(1)} collective-permute-done((f32[1,5,32,128]{3,2,1,0:T(8,128)S(1)}, f32[1,5,32,128]{3,2,1,0:T(8,128)S(1)}, u32[]{:S(2)}, u32[]{:S(2)}) %collective-permute-start) | collective-permute-done | bytes 81952 | tf_op jit(solution)/shard_map/ppermute | solution.py:435
  37.8 1.5 %collective-permute-start.3 = (f32[4,5,32,128]{3,2,1,0:T(8,128)S(1)}, f32[4,5,32,128]{3,2,1,0:T(8,128)S(1)}, u32[]{:S(2)}, u32[]{:S(2)}) collective-permute-start(f32[4,5,32,128]{3,2,1,0:T(8,128)S(1)} %pad_maximum_fusion.4), channel_id=1, source_target_pairs={{0,64},{8,72},{16,80},{24,88},{32,96},{40,104},{48,112},{56,120},{... | collective-permute-start | bytes 983048 | tf_op jit(solution)/shard_map/ppermute | solution.py:439
  39.3 3.3 %forcing_0.1.force = f32[2048,512]{1,0:T(8,128)S(1)} custom-call(f32[128,2,128]{2,1,0:T(2,128)S(1)} %all_to_all.15.slots), custom_call_target="tpu_custom_call" | custom-call | flops 8000000000 | bytes 4325376 | tf_op jit(solution)/shard_map/forcing_0/pallas_call | solution.py:184
  42.6 1.8 %second_inner.1 = (f32[8192,128]{1,0:T(8,128)S(1)}, f32[10240,128]{1,0:T(8,128)S(1)}) custom-call(f32[8192,128]{1,0:T(8,128)S(1)} %get-tuple-element.58.solved_in, f32[10240,128]{1,0:T(8,128)S(1)} %get-tuple-element.59.weighted_in, f32[2048,512]{1,0:T(8,128)S(1)} %forcing_0.1.force, f32[960,512]{1,0:T(8,128)S(1)} %bitcast.19, f32[1024,512]{1,0:T(8,128)S(1)} %bitcast.13, ...), custom_call_target="tpu_custom_call" | custom-call | flops 30000000 | bytes 10000000 | tf_op jit(solution)/shard_map/second_inner/pallas_call | solution.py:595
  44.4 2.8 %collective-permute-done.3 = f32[4,5,32,128]{3,2,1,0:T(8,128)S(1)} collective-permute-done((f32[4,5,32,128]{3,2,1,0:T(8,128)S(1)}, f32[4,5,32,128]{3,2,1,0:T(8,128)S(1)}, u32[]{:S(2)}, u32[]{:S(2)}) %collective-permute-start.3) | collective-permute-done | bytes 327712 | tf_op jit(solution)/shard_map/ppermute | solution.py:439
  47.3 0.1 collective-permute-start.4
  47.4 2.1 %collective-permute-done.4 = f32[8,5,32,128]{3,2,1,0:T(8,128)S(1)} collective-permute-done((f32[8,5,32,128]{3,2,1,0:T(8,128)S(1)}, f32[8,5,32,128]{3,2,1,0:T(8,128)S(1)}, u32[]{:S(2)}, u32[]{:S(2)}) %collective-permute-start.4) | collective-permute-done | bytes 655392 | tf_op jit(solution)/shard_map/ppermute | solution.py:444
  49.5 0.1 pad_maximum_fusion.gathered
  49.6 0.7 route.2
  50.3 15.2 %all_to_all.16.got = f32[8,176,128]{2,1,0:T(8,128)S(1)} all-to-all(f32[8,176,128]{2,1,0:T(8,128)S(1)} %get-tuple-element.56), channel_id=1, replica_groups=mesh['tile'=16,'sub'=8] {'sub'}, dimensions={0} | all-to-all | bytes 1441792 | tf_op jit(solution)/shard_map/all_to_all | solution.py:447
  65.5 4.8 %second_edges.1 = (f32[8192,128]{1,0:T(8,128)S(1)}, f32[10240,128]{1,0:T(8,128)S(1)}, f32[5,32,128]{2,1,0:T(8,128)S(1)}, f32[4,32,128]{2,1,0:T(8,128)S(1)}, f32[...) custom-call(s32[16]{0:T(128)S(1)} %copy-done.4, ...), custom_call_target="tpu_custom_call", output_to_operand_aliasing={{0}: (9, {}), {1}: (10, {}), {5}: (4, {})} | custom-call | flops 40000000 | bytes 10000000 | tf_op jit(solution)/shard_map/second_edges/pallas_call | solution.py:607
  70.2 1.8 %collective-permute-start.7 = (f32[1,5,32,128]{3,2,1,0:T(8,128)S(1)}, f32[1,5,32,128]{3,2,1,0:T(8,128)S(1)}, u32[]{:S(2)}, u32[]{:S(2)}) collective-permute-start(f32[1,5,32,128]{3,2,1,0:T(8,128)S(1)} %bitcast.23), channel_id=1, source_target_pairs={{0,32},{8,40},{16,48},{24,56},{32,0},{40,8},{48,16},{56,24},{64,96... | collective-permute-start | bytes 245768 | tf_op jit(solution)/shard_map/ppermute | solution.py:435
  72.0 0.5 collective-permute-start.6
  72.6 1.5 %collective-permute-start.5 = (f32[1,5,32,128]{3,2,1,0:T(8,128)S(1)}, f32[1,5,32,128]{3,2,1,0:T(8,128)S(1)}, u32[]{:S(2)}, u32[]{:S(2)}) collective-permute-start(f32[1,5,32,128]{3,2,1,0:T(8,128)S(1)} %bitcast.25), channel_id=1, source_target_pairs={{0,16},{8,24},{16,32},{24,40},{32,48},{40,56},{48,0},{56,8},{64,80... | collective-permute-start | bytes 245768 | tf_op jit(solution)/shard_map/ppermute | solution.py:435
  74.0 2.6 %collective-permute-done.7 = f32[1,5,32,128]{3,2,1,0:T(8,128)S(1)} collective-permute-done((f32[1,5,32,128]{3,2,1,0:T(8,128)S(1)}, f32[1,5,32,128]{3,2,1,0:T(8,128)S(1)}, u32[]{:S(2)}, u32[]{:S(2)}) %collective-permute-start.7) | collective-permute-done | bytes 81952 | tf_op jit(solution)/shard_map/ppermute | solution.py:435
  76.6 0.0 collective-permute-done.6
  76.6 1.6 %collective-permute-done.5 = f32[1,5,32,128]{3,2,1,0:T(8,128)S(1)} collective-permute-done((f32[1,5,32,128]{3,2,1,0:T(8,128)S(1)}, f32[1,5,32,128]{3,2,1,0:T(8,128)S(1)}, u32[]{:S(2)}, u32[]{:S(2)}) %collective-permute-start.5) | collective-permute-done | bytes 81952 | tf_op jit(solution)/shard_map/ppermute | solution.py:435
  78.2 1.6 %collective-permute-start.8 = (f32[4,5,32,128]{3,2,1,0:T(8,128)S(1)}, f32[4,5,32,128]{3,2,1,0:T(8,128)S(1)}, u32[]{:S(2)}, u32[]{:S(2)}) collective-permute-start(f32[4,5,32,128]{3,2,1,0:T(8,128)S(1)} %pad_maximum_fusion.5), channel_id=1, source_target_pairs={{0,64},{8,72},{16,80},{24,88},{32,96},{40,104},{48,112},{56,120},{... | collective-permute-start | bytes 983048 | tf_op jit(solution)/shard_map/ppermute | solution.py:439
  79.9 2.5 %last_inner.1._ = f32[32,64,512]{2,1,0:T(8,128)} custom-call(f32[8192,128]{1,0:T(8,128)S(1)} %get-tuple-element.65.solved, f32[10240,128]{1,0:T(8,128)S(1)} %get-tuple-element.66.weighted.weighted_in, f32[1024,512]{1,0:T(8,128)S(1)} %bitcast.15, s32[64,512]{1,0:T(8,128)S(1)} %copy-done.3), custom_call_target="tpu_custom_call" | custom-call | flops 20000000 | bytes 10000000 | tf_op jit(solution)/shard_map/last_inner/pallas_call | solution.py:685
  82.3 5.4 %collective-permute-done.8 = f32[4,5,32,128]{3,2,1,0:T(8,128)S(1)} collective-permute-done((f32[4,5,32,128]{3,2,1,0:T(8,128)S(1)}, f32[4,5,32,128]{3,2,1,0:T(8,128)S(1)}, u32[]{:S(2)}, u32[]{:S(2)}) %collective-permute-start.8) | collective-permute-done | bytes 327712 | tf_op jit(solution)/shard_map/ppermute | solution.py:439
  87.8 0.1 collective-permute-start.9
  87.9 2.1 %collective-permute-done.9 = f32[8,5,32,128]{3,2,1,0:T(8,128)S(1)} collective-permute-done((f32[8,5,32,128]{3,2,1,0:T(8,128)S(1)}, f32[8,5,32,128]{3,2,1,0:T(8,128)S(1)}, u32[]{:S(2)}, u32[]{:S(2)}) %collective-permute-start.9) | collective-permute-done | bytes 655392 | tf_op jit(solution)/shard_map/ppermute | solution.py:444
  90.0 0.1 pad_maximum_fusion.1.gathered
  90.1 0.7 route.3
  90.8 15.2 %all_to_all.17.got = f32[8,176,128]{2,1,0:T(8,128)S(1)} all-to-all(f32[8,176,128]{2,1,0:T(8,128)S(1)} %get-tuple-element.71), channel_id=1, replica_groups=mesh['tile'=16,'sub'=8] {'sub'}, dimensions={0} | all-to-all | bytes 1441792 | tf_op jit(solution)/shard_map/all_to_all | solution.py:447
  106.0 4.0 %last_edges.1 = (f32[32,64,512]{2,1,0:T(8,128)}, f32[10240,128]{1,0:T(8,128)S(1)}) custom-call(s32[16]{0:T(128)S(1)} %copy-done.4, f32[8,176,128]{2,1,0:T(8,128)S(1)} %all_to_all.17.got, f32[4,32,128]{2,1,0:T(8,128)S(1)} %get-tuple-element.72.here, f32[8192,128]{1,0:T(8,128)S(1)} %get-tuple-element.65.solved, ...), custom_call_target="tpu_custom_call", output_to_operand_aliasing={{0}: (7, {}), {1}: (4, {})} | custom-call | flops 20000000 | bytes 10000000 | tf_op jit(solution)/shard_map/last_edges/pallas_call | solution.py:698
  (4 shorter events, 0.1 us)
Async XLA Ops:
  22.9 3.3 %copy-start = (f32[16,64,512]{2,1,0:T(8,128)S(1)}, f32[16,64,512]{2,1,0:T(8,128)}, u32[]{:S(2)}) copy-start(f32[16,64,512]{2,1,0:T(8,128)} %param.11) | copy-start | bytes 6291460
  22.9 3.3 %copy-start.1 = (f32[15,64,512]{2,1,0:T(8,128)S(1)}, f32[15,64,512]{2,1,0:T(8,128)}, u32[]{:S(2)}) copy-start(f32[15,64,512]{2,1,0:T(8,128)} %param.12) | copy-start | bytes 5898244
  22.9 3.4 %copy-start.2 = (f32[2,16,64,512]{3,2,1,0:T(8,128)S(1)}, f32[2,16,64,512]{3,2,1,0:T(8,128)}, u32[]{:S(2)}) copy-start(f32[2,16,64,512]{3,2,1,0:T(8,128)} %param.10) | copy-start | bytes 12582916
  22.9 3.4 %copy-start.3 = (s32[64,512]{1,0:T(8,128)S(1)}, s32[64,512]{1,0:T(8,128)}, u32[]{:S(2)}) copy-start(s32[64,512]{1,0:T(8,128)} %depth.10) | copy-start | bytes 393220
  23.0 3.4 %copy-start.4 = (s32[16]{0:T(128)S(1)}, s32[16]{0:T(128)}, u32[]{:S(2)}) copy-start(s32[16]{0:T(128)} %get-tuple-element.40.meta) | copy-start | bytes 196
  28.7 6.6 %collective-permute-start.2 = (f32[1,5,32,128]{3,2,1,0:T(8,128)S(1)}, f32[1,5,32,128]{3,2,1,0:T(8,128)S(1)}, u32[]{:S(2)}, u32[]{:S(2)}) collective-permute-start(f32[1,5,32,128]{3,2,1,0:T(8,128)S(1)} %bitcast.27), channel_id=1, source_target_pairs={{0,32},{8,40},{16,48},{24,56},{32,0},{40,8},{48,16},{56,24},{64,96... | collective-permute-start | bytes 245768 | tf_op jit(solution)/shard_map/ppermute | solution.py:435
  30.2 5.2 %collective-permute-start.1 = (f32[1,5,32,128]{3,2,1,0:T(8,128)S(1)}, f32[1,5,32,128]{3,2,1,0:T(8,128)S(1)}, u32[]{:S(2)}, u32[]{:S(2)}) collective-permute-start(f32[1,5,32,128]{3,2,1,0:T(8,128)S(1)} %bitcast.28), channel_id=1, source_target_pairs={{0,48},{8,56},{16,0},{24,8},{32,16},{40,24},{48,32},{56,40},{64,11... | collective-permute-start | bytes 245768 | tf_op jit(solution)/shard_map/ppermute | solution.py:435
  32.1 5.7 %collective-permute-start = (f32[1,5,32,128]{3,2,1,0:T(8,128)S(1)}, f32[1,5,32,128]{3,2,1,0:T(8,128)S(1)}, u32[]{:S(2)}, u32[]{:S(2)}) collective-permute-start(f32[1,5,32,128]{3,2,1,0:T(8,128)S(1)} %bitcast.29), channel_id=1, source_target_pairs={{0,16},{8,24},{16,32},{24,40},{32,48},{40,56},{48,0},{56,8},{64,80... | collective-permute-start | bytes 245768 | tf_op jit(solution)/shard_map/ppermute | solution.py:435
  37.8 9.5 %collective-permute-start.3 = (f32[4,5,32,128]{3,2,1,0:T(8,128)S(1)}, f32[4,5,32,128]{3,2,1,0:T(8,128)S(1)}, u32[]{:S(2)}, u32[]{:S(2)}) collective-permute-start(f32[4,5,32,128]{3,2,1,0:T(8,128)S(1)} %pad_maximum_fusion.4), channel_id=1, source_target_pairs={{0,64},{8,72},{16,80},{24,88},{32,96},{40,104},{48,112},{56,120},{... | collective-permute-start | bytes 983048 | tf_op jit(solution)/shard_map/ppermute | solution.py:439
  47.3 2.2 %collective-permute-start.4 = (f32[8,5,32,128]{3,2,1,0:T(8,128)S(1)}, f32[8,5,32,128]{3,2,1,0:T(8,128)S(1)}, u32[]{:S(2)}, u32[]{:S(2)}) collective-permute-start(f32[8,5,32,128]{3,2,1,0:T(8,128)S(1)} %pad_maximum_fusion.2), channel_id=1, source_target_pairs={{0,8},{8,0},{16,24},{24,16},{32,40},{40,32},{48,56},{56,48},{64,72... | collective-permute-start | bytes 1966088 | tf_op jit(solution)/shard_map/ppermute | solution.py:444
  70.2 6.4 %collective-permute-start.7 = (f32[1,5,32,128]{3,2,1,0:T(8,128)S(1)}, f32[1,5,32,128]{3,2,1,0:T(8,128)S(1)}, u32[]{:S(2)}, u32[]{:S(2)}) collective-permute-start(f32[1,5,32,128]{3,2,1,0:T(8,128)S(1)} %bitcast.23), channel_id=1, source_target_pairs={{0,32},{8,40},{16,48},{24,56},{32,0},{40,8},{48,16},{56,24},{64,96... | collective-permute-start | bytes 245768 | tf_op jit(solution)/shard_map/ppermute | solution.py:435
  72.0 4.6 %collective-permute-start.6 = (f32[1,5,32,128]{3,2,1,0:T(8,128)S(1)}, f32[1,5,32,128]{3,2,1,0:T(8,128)S(1)}, u32[]{:S(2)}, u32[]{:S(2)}) collective-permute-start(f32[1,5,32,128]{3,2,1,0:T(8,128)S(1)} %bitcast.24), channel_id=1, source_target_pairs={{0,48},{8,56},{16,0},{24,8},{32,16},{40,24},{48,32},{56,40},{64,11... | collective-permute-start | bytes 245768 | tf_op jit(solution)/shard_map/ppermute | solution.py:435
  72.6 5.7 %collective-permute-start.5 = (f32[1,5,32,128]{3,2,1,0:T(8,128)S(1)}, f32[1,5,32,128]{3,2,1,0:T(8,128)S(1)}, u32[]{:S(2)}, u32[]{:S(2)}) collective-permute-start(f32[1,5,32,128]{3,2,1,0:T(8,128)S(1)} %bitcast.25), channel_id=1, source_target_pairs={{0,16},{8,24},{16,32},{24,40},{32,48},{40,56},{48,0},{56,8},{64,80... | collective-permute-start | bytes 245768 | tf_op jit(solution)/shard_map/ppermute | solution.py:435
  78.2 9.5 %collective-permute-start.8 = (f32[4,5,32,128]{3,2,1,0:T(8,128)S(1)}, f32[4,5,32,128]{3,2,1,0:T(8,128)S(1)}, u32[]{:S(2)}, u32[]{:S(2)}) collective-permute-start(f32[4,5,32,128]{3,2,1,0:T(8,128)S(1)} %pad_maximum_fusion.5), channel_id=1, source_target_pairs={{0,64},{8,72},{16,80},{24,88},{32,96},{40,104},{48,112},{56,120},{... | collective-permute-start | bytes 983048 | tf_op jit(solution)/shard_map/ppermute | solution.py:439
  87.8 2.2 %collective-permute-start.9 = (f32[8,5,32,128]{3,2,1,0:T(8,128)S(1)}, f32[8,5,32,128]{3,2,1,0:T(8,128)S(1)}, u32[]{:S(2)}, u32[]{:S(2)}) collective-permute-start(f32[8,5,32,128]{3,2,1,0:T(8,128)S(1)} %pad_maximum_fusion.3), channel_id=1, source_target_pairs={{0,8},{8,0},{16,24},{24,16},{32,40},{40,32},{48,56},{56,48},{64,72... | collective-permute-start | bytes 1966088 | tf_op jit(solution)/shard_map/ppermute | solution.py:444

commit v11 on v9

--- a/solution.py
+++ b/solution.py
@@ -114,10 +114,13 @@
             pieces.append(jnp.zeros((PLANES * (CAP - 1 - k), rows), jnp.float32))
         pieces.append(jnp.where(dest == k, tag, 0.0))
         stacked = jnp.concatenate(pieces, axis=0)
-        total = total + lax.dot_general(
-            hit, stacked, (((1,), (1,)), ((), ())), precision=HIGHEST,
-            preferred_element_type=jnp.float32,
-        )
+        hit = hit.astype(jnp.bfloat16)
+        for _ in range(3):
+            piece = stacked.astype(jnp.bfloat16)
+            stacked = stacked - piece.astype(jnp.float32)
+            total = total + lax.dot_general(
+                hit, piece, (((1,), (1,)), ((), ())), preferred_element_type=jnp.float32
+            )
     out[:, 0, :] = total[:, :DEVICES]
     out[:, 1, :] = total[:, DEVICES:] - 1.0
 
@@ -161,7 +164,7 @@
         place[k * DEVICES : (k + 1) * DEVICES, :] = jnp.where(
             iota((DEVICES, COLS), 1) == col, 1.0, 0.0
         ).astype(jnp.bfloat16)
-    group = 16
+    group = 32
 
     def step(g, carry):
         total = None

time: 110 us -> 110 us (level)
  Pallas kernels: 26.6 us -> 25.5 us
  transfers between devices with their start and end apart: 10 -> 10, of which waited for: 7 -> 8; matrix products, arithmetic and copies ran while one was open for 0% -> 0% of each run, Pallas kernels for 8% -> 7%
where the time goes in v11:
time: 110 us
  blocking collectives  51 us (46%)
  Pallas kernels  25.5 us (23%)
  waiting for transfers between devices  21.6 us (20%)
  starting transfers between devices  10.7 us (10%)
    all_to_all x2, blocking collectives, exchange(): got = lax.all_to_all(send, 'sub', split_axis=0, concat_axis=0, tiled=True)  30.4 us
    all_to_all x1, blocking collectives, body(): lax.all_to_all(slots, ('tile', 'sub'), split_axis=0, concat_axis=0, tiled...  20.6 us
    ppermute x2, waiting for transfers between devices, exchange(): lax.ppermute(all_parts, 'tile', [(i, i ^ 8) for i in range(N_TILE)])  10.5 us
    ppermute x6, starting transfers between devices, exchange(): lax.ppermute(all_parts, 'tile', turn(k))  7.45 us
    ppermute x6, waiting for transfers between devices, exchange(): lax.ppermute(all_parts, 'tile', turn(k))  6.98 us
    pallas_call x2, Pallas kernels, forcing(): pl.pallas_call(functools.partial(forcing_kernel, moment), out_shape=f32(P...  5.54 us
    pallas_call x1, Pallas kernels, second_edges(): pl.pallas_call(second_edges_kernel, out_shape=BIG + EDGES + BIG[1:], in_s...  4.64 us
    ppermute x2, waiting for transfers between devices, exchange(): lax.ppermute(all_parts, 'tile', [(i, i ^ 1) for i in range(N_TILE)])  4.17 us
  transfers between devices with their start and end apart: 10, of which 8 were waited for; matrix products, arithmetic and copies ran while one was open for 0% of the time, Pallas kernels for 7%

profile of v11, /device:TPU:0, one launch (start us, length us, event | category | flops | bytes accessed | tf_op | source)
XLA Modules:
  0.0 110.1 jit_solution(4419984952158747387)
XLA Ops:
  0.0 2.2 %pack.1 = (f32[128,2,128]{2,1,0:T(2,128)}, s32[16]{0:T(128)}) custom-call(s32[16]{0:T(128)} %owner_in.1, s32[3,4,16]{2,1,0:T(4,128)} %bitcast.32, s32[1,256]{1,0:T(1,128)} %bitcast.33, s32[1,256]{1,0:T(1,128)} %bitcast.34, s32[1,256]{1,0:T(1,128)} %bitcast.35, f32[32,256]{1,0:T(8,128)} %bitcast.31), custom_call_target="tpu_custom_call" | custom-call | tf_op jit(solution)/shard_map/pack/pallas_call | solution.py:130
  2.2 20.6 %all_to_all.15.slots = f32[128,2,128]{2,1,0:T(2,128)S(1)} all-to-all(f32[128,2,128]{2,1,0:T(2,128)} %get-tuple-element.40), channel_id=1, replica_groups=mesh['tile'=16,'sub'=8] {'tile','sub'}, dimensions={0} | all-to-all | bytes 262144 | tf_op jit(solution)/shard_map/all_to_all | solution.py:735
  22.9 0.0 copy-start
  22.9 0.0 copy-start.1
  22.9 0.0 copy-start.2
  22.9 0.0 copy-start.3
  22.9 0.0 copy-start.4
  22.9 2.8 %forcing_1.1.force = f32[2048,512]{1,0:T(8,128)S(1)} custom-call(f32[128,2,128]{2,1,0:T(2,128)S(1)} %all_to_all.15.slots), custom_call_target="tpu_custom_call" | custom-call | flops 8000000000 | bytes 4325376 | tf_op jit(solution)/shard_map/forcing_1/pallas_call | solution.py:187
  25.7 0.0 copy-done
  25.7 0.0 copy-done.1
  25.7 0.6 copy-done.2
  26.3 0.0 copy-done.3
  26.3 0.0 copy-done.4
  26.3 2.3 %first_edges.1 = (f32[8192,128]{1,0:T(8,128)S(1)}, f32[10240,128]{1,0:T(8,128)S(1)}, f32[5,32,128]{2,1,0:T(8,128)S(1)}, f32[4,32,128]{2,1,0:T(8,128)S(1)}, f32[4,32,128]{2,1,0:T(8,128)S(1)}) custom-call(s32[16]{0:T(128)S(1)} %copy-done.4, f32[2048,512]{1,0:T(8,128)S(1)} %bitcast.21, f32[2048,512]{1,0:T(8,128)S(1)} %forcing_1.1.force, ...), custom_call_target="tpu_custom_call" | custom-call | flops 30000000 | bytes 10000000 | tf_op jit(solution)/shard_map/first_edges/pallas_call | solution.py:346
  28.6 1.4 %collective-permute-start.2 = (f32[1,5,32,128]{3,2,1,0:T(8,128)S(1)}, f32[1,5,32,128]{3,2,1,0:T(8,128)S(1)}, u32[]{:S(2)}, u32[]{:S(2)}) collective-permute-start(f32[1,5,32,128]{3,2,1,0:T(8,128)S(1)} %bitcast.27), channel_id=1, source_target_pairs={{0,32},{8,40},{16,48},{24,56},{32,0},{40,8},{48,16},{56,24},{64,96... | collective-permute-start | bytes 245768 | tf_op jit(solution)/shard_map/ppermute | solution.py:438
  30.0 2.0 %collective-permute-start.1 = (f32[1,5,32,128]{3,2,1,0:T(8,128)S(1)}, f32[1,5,32,128]{3,2,1,0:T(8,128)S(1)}, u32[]{:S(2)}, u32[]{:S(2)}) collective-permute-start(f32[1,5,32,128]{3,2,1,0:T(8,128)S(1)} %bitcast.28), channel_id=1, source_target_pairs={{0,48},{8,56},{16,0},{24,8},{32,16},{40,24},{48,32},{56,40},{64,11... | collective-permute-start | bytes 245768 | tf_op jit(solution)/shard_map/ppermute | solution.py:438
  32.0 0.1 collective-permute-start
  32.1 2.8 %forcing_0.1.force = f32[2048,512]{1,0:T(8,128)S(1)} custom-call(f32[128,2,128]{2,1,0:T(2,128)S(1)} %all_to_all.15.slots), custom_call_target="tpu_custom_call" | custom-call | flops 8000000000 | bytes 4325376 | tf_op jit(solution)/shard_map/forcing_0/pallas_call | solution.py:187
  34.8 0.4 collective-permute-done.2
  35.2 0.0 collective-permute-done.1
  35.2 2.4 %collective-permute-done = f32[1,5,32,128]{3,2,1,0:T(8,128)S(1)} collective-permute-done((f32[1,5,32,128]{3,2,1,0:T(8,128)S(1)}, f32[1,5,32,128]{3,2,1,0:T(8,128)S(1)}, u32[]{:S(2)}, u32[]{:S(2)}) %collective-permute-start) | collective-permute-done | bytes 81952 | tf_op jit(solution)/shard_map/ppermute | solution.py:438
  37.7 1.5 %collective-permute-start.3 = (f32[4,5,32,128]{3,2,1,0:T(8,128)S(1)}, f32[4,5,32,128]{3,2,1,0:T(8,128)S(1)}, u32[]{:S(2)}, u32[]{:S(2)}) collective-permute-start(f32[4,5,32,128]{3,2,1,0:T(8,128)S(1)} %pad_maximum_fusion.4), channel_id=1, source_target_pairs={{0,64},{8,72},{16,80},{24,88},{32,96},{40,104},{48,112},{56,120},{... | collective-permute-start | bytes 983048 | tf_op jit(solution)/shard_map/ppermute | solution.py:442
  39.2 1.2 %first_inner.1 = (f32[8192,128]{1,0:T(8,128)S(1)}, f32[10240,128]{1,0:T(8,128)S(1)}) custom-call(f32[2048,512]{1,0:T(8,128)S(1)} %bitcast.22, f32[2048,512]{1,0:T(8,128)S(1)} %forcing_1.1.force, f32[960,512]{1,0:T(8,128)S(1)} %bitcast.18, f32[1024,512]{1,0:T(8,128)S(1)} %bitcast.12, ...), custom_call_target="tpu_custom_call", output_to_operand_aliasing={{0}: (5, {}), {1}: (6, {})} | custom-call | flops 20000000 | bytes 10000000 | tf_op jit(solution)/shard_map/first_inner/pallas_call | solution.py:359
  40.4 1.8 %second_inner.1 = (f32[8192,128]{1,0:T(8,128)S(1)}, f32[10240,128]{1,0:T(8,128)S(1)}) custom-call(f32[8192,128]{1,0:T(8,128)S(1)} %get-tuple-element.56.solved_in, f32[10240,128]{1,0:T(8,128)S(1)} %get-tuple-element.57.weighted_in, f32[2048,512]{1,0:T(8,128)S(1)} %forcing_0.1.force, f32[960,512]{1,0:T(8,128)S(1)} %bitcast.19, f32[1024,512]{1,0:T(8,128)S(1)} %bitcast.13, ...), custom_call_target="tpu_custom_call" | custom-call | flops 30000000 | bytes 10000000 | tf_op jit(solution)/shard_map/second_inner/pallas_call | solution.py:598
  42.2 5.0 %collective-permute-done.3 = f32[4,5,32,128]{3,2,1,0:T(8,128)S(1)} collective-permute-done((f32[4,5,32,128]{3,2,1,0:T(8,128)S(1)}, f32[4,5,32,128]{3,2,1,0:T(8,128)S(1)}, u32[]{:S(2)}, u32[]{:S(2)}) %collective-permute-start.3) | collective-permute-done | bytes 327712 | tf_op jit(solution)/shard_map/ppermute | solution.py:442
  47.2 0.1 collective-permute-start.4
  47.3 2.1 %collective-permute-done.4 = f32[8,5,32,128]{3,2,1,0:T(8,128)S(1)} collective-permute-done((f32[8,5,32,128]{3,2,1,0:T(8,128)S(1)}, f32[8,5,32,128]{3,2,1,0:T(8,128)S(1)}, u32[]{:S(2)}, u32[]{:S(2)}) %collective-permute-start.4) | collective-permute-done | bytes 655392 | tf_op jit(solution)/shard_map/ppermute | solution.py:447
  49.4 0.1 pad_maximum_fusion.gathered
  49.5 0.7 route.2
  50.2 15.2 %all_to_all.16.got = f32[8,176,128]{2,1,0:T(8,128)S(1)} all-to-all(f32[8,176,128]{2,1,0:T(8,128)S(1)} %get-tuple-element.54), channel_id=1, replica_groups=mesh['tile'=16,'sub'=8] {'sub'}, dimensions={0} | all-to-all | bytes 1441792 | tf_op jit(solution)/shard_map/all_to_all | solution.py:450
  65.4 4.6 %second_edges.1 = (f32[8192,128]{1,0:T(8,128)S(1)}, f32[10240,128]{1,0:T(8,128)S(1)}, f32[5,32,128]{2,1,0:T(8,128)S(1)}, f32[4,32,128]{2,1,0:T(8,128)S(1)}, f32[...) custom-call(s32[16]{0:T(128)S(1)} %copy-done.4, ...), custom_call_target="tpu_custom_call", output_to_operand_aliasing={{0}: (9, {}), {1}: (10, {}), {5}: (4, {})} | custom-call | flops 40000000 | bytes 10000000 | tf_op jit(solution)/shard_map/second_edges/pallas_call | solution.py:610
  70.0 2.0 %collective-permute-start.7 = (f32[1,5,32,128]{3,2,1,0:T(8,128)S(1)}, f32[1,5,32,128]{3,2,1,0:T(8,128)S(1)}, u32[]{:S(2)}, u32[]{:S(2)}) collective-permute-start(f32[1,5,32,128]{3,2,1,0:T(8,128)S(1)} %bitcast.23), channel_id=1, source_target_pairs={{0,32},{8,40},{16,48},{24,56},{32,0},{40,8},{48,16},{56,24},{64,96... | collective-permute-start | bytes 245768 | tf_op jit(solution)/shard_map/ppermute | solution.py:438
  72.0 0.5 collective-permute-start.6
  72.5 1.5 %collective-permute-start.5 = (f32[1,5,32,128]{3,2,1,0:T(8,128)S(1)}, f32[1,5,32,128]{3,2,1,0:T(8,128)S(1)}, u32[]{:S(2)}, u32[]{:S(2)}) collective-permute-start(f32[1,5,32,128]{3,2,1,0:T(8,128)S(1)} %bitcast.25), channel_id=1, source_target_pairs={{0,16},{8,24},{16,32},{24,40},{32,48},{40,56},{48,0},{56,8},{64,80... | collective-permute-start | bytes 245768 | tf_op jit(solution)/shard_map/ppermute | solution.py:438
  74.0 2.6 %collective-permute-done.7 = f32[1,5,32,128]{3,2,1,0:T(8,128)S(1)} collective-permute-done((f32[1,5,32,128]{3,2,1,0:T(8,128)S(1)}, f32[1,5,32,128]{3,2,1,0:T(8,128)S(1)}, u32[]{:S(2)}, u32[]{:S(2)}) %collective-permute-start.7) | collective-permute-done | bytes 81952 | tf_op jit(solution)/shard_map/ppermute | solution.py:438
  76.6 0.0 collective-permute-done.6
  76.6 1.6 %collective-permute-done.5 = f32[1,5,32,128]{3,2,1,0:T(8,128)S(1)} collective-permute-done((f32[1,5,32,128]{3,2,1,0:T(8,128)S(1)}, f32[1,5,32,128]{3,2,1,0:T(8,128)S(1)}, u32[]{:S(2)}, u32[]{:S(2)}) %collective-permute-start.5) | collective-permute-done | bytes 81952 | tf_op jit(solution)/shard_map/ppermute | solution.py:438
  78.2 1.6 %collective-permute-start.8 = (f32[4,5,32,128]{3,2,1,0:T(8,128)S(1)}, f32[4,5,32,128]{3,2,1,0:T(8,128)S(1)}, u32[]{:S(2)}, u32[]{:S(2)}) collective-permute-start(f32[4,5,32,128]{3,2,1,0:T(8,128)S(1)} %pad_maximum_fusion.5), channel_id=1, source_target_pairs={{0,64},{8,72},{16,80},{24,88},{32,96},{40,104},{48,112},{56,120},{... | collective-permute-start | bytes 983048 | tf_op jit(solution)/shard_map/ppermute | solution.py:442
  79.8 2.5 %last_inner.1._ = f32[32,64,512]{2,1,0:T(8,128)} custom-call(f32[8192,128]{1,0:T(8,128)S(1)} %get-tuple-element.63.solved, f32[10240,128]{1,0:T(8,128)S(1)} %get-tuple-element.64.weighted.weighted_in, f32[1024,512]{1,0:T(8,128)S(1)} %bitcast.15, s32[64,512]{1,0:T(8,128)S(1)} %copy-done.3), custom_call_target="tpu_custom_call" | custom-call | flops 20000000 | bytes 10000000 | tf_op jit(solution)/shard_map/last_inner/pallas_call | solution.py:688
  82.3 5.5 %collective-permute-done.8 = f32[4,5,32,128]{3,2,1,0:T(8,128)S(1)} collective-permute-done((f32[4,5,32,128]{3,2,1,0:T(8,128)S(1)}, f32[4,5,32,128]{3,2,1,0:T(8,128)S(1)}, u32[]{:S(2)}, u32[]{:S(2)}) %collective-permute-start.8) | collective-permute-done | bytes 327712 | tf_op jit(solution)/shard_map/ppermute | solution.py:442
  87.8 0.1 collective-permute-start.9
  87.9 2.1 %collective-permute-done.9 = f32[8,5,32,128]{3,2,1,0:T(8,128)S(1)} collective-permute-done((f32[8,5,32,128]{3,2,1,0:T(8,128)S(1)}, f32[8,5,32,128]{3,2,1,0:T(8,128)S(1)}, u32[]{:S(2)}, u32[]{:S(2)}) %collective-permute-start.9) | collective-permute-done | bytes 655392 | tf_op jit(solution)/shard_map/ppermute | solution.py:447
  90.0 0.1 pad_maximum_fusion.1.gathered
  90.1 0.7 route.3
  90.8 15.2 %all_to_all.17.got = f32[8,176,128]{2,1,0:T(8,128)S(1)} all-to-all(f32[8,176,128]{2,1,0:T(8,128)S(1)} %get-tuple-element.69), channel_id=1, replica_groups=mesh['tile'=16,'sub'=8] {'sub'}, dimensions={0} | all-to-all | bytes 1441792 | tf_op jit(solution)/shard_map/all_to_all | solution.py:450
  106.0 4.0 %last_edges.1 = (f32[32,64,512]{2,1,0:T(8,128)}, f32[10240,128]{1,0:T(8,128)S(1)}) custom-call(s32[16]{0:T(128)S(1)} %copy-done.4, f32[8,176,128]{2,1,0:T(8,128)S(1)} %all_to_all.17.got, f32[4,32,128]{2,1,0:T(8,128)S(1)} %get-tuple-element.70.here, f32[8192,128]{1,0:T(8,128)S(1)} %get-tuple-element.63.solved, ...), custom_call_target="tpu_custom_call", output_to_operand_aliasing={{0}: (7, {}), {1}: (4, {})} | custom-call | flops 20000000 | bytes 10000000 | tf_op jit(solution)/shard_map/last_edges/pallas_call | solution.py:701
  (4 shorter events, 0.1 us)
Async XLA Ops:
  22.9 2.8 %copy-start = (f32[16,64,512]{2,1,0:T(8,128)S(1)}, f32[16,64,512]{2,1,0:T(8,128)}, u32[]{:S(2)}) copy-start(f32[16,64,512]{2,1,0:T(8,128)} %param.11) | copy-start | bytes 6291460
  22.9 2.8 %copy-start.1 = (f32[15,64,512]{2,1,0:T(8,128)S(1)}, f32[15,64,512]{2,1,0:T(8,128)}, u32[]{:S(2)}) copy-start(f32[15,64,512]{2,1,0:T(8,128)} %param.12) | copy-start | bytes 5898244
  22.9 3.4 %copy-start.2 = (f32[2,16,64,512]{3,2,1,0:T(8,128)S(1)}, f32[2,16,64,512]{3,2,1,0:T(8,128)}, u32[]{:S(2)}) copy-start(f32[2,16,64,512]{3,2,1,0:T(8,128)} %param.10) | copy-start | bytes 12582916
  22.9 3.4 %copy-start.3 = (s32[64,512]{1,0:T(8,128)S(1)}, s32[64,512]{1,0:T(8,128)}, u32[]{:S(2)}) copy-start(s32[64,512]{1,0:T(8,128)} %depth.8) | copy-start | bytes 393220
  22.9 3.4 %copy-start.4 = (s32[16]{0:T(128)S(1)}, s32[16]{0:T(128)}, u32[]{:S(2)}) copy-start(s32[16]{0:T(128)} %get-tuple-element.39.meta) | copy-start | bytes 196
  28.6 6.6 %collective-permute-start.2 = (f32[1,5,32,128]{3,2,1,0:T(8,128)S(1)}, f32[1,5,32,128]{3,2,1,0:T(8,128)S(1)}, u32[]{:S(2)}, u32[]{:S(2)}) collective-permute-start(f32[1,5,32,128]{3,2,1,0:T(8,128)S(1)} %bitcast.27), channel_id=1, source_target_pairs={{0,32},{8,40},{16,48},{24,56},{32,0},{40,8},{48,16},{56,24},{64,96... | collective-permute-start | bytes 245768 | tf_op jit(solution)/shard_map/ppermute | solution.py:438
  30.0 5.2 %collective-permute-start.1 = (f32[1,5,32,128]{3,2,1,0:T(8,128)S(1)}, f32[1,5,32,128]{3,2,1,0:T(8,128)S(1)}, u32[]{:S(2)}, u32[]{:S(2)}) collective-permute-start(f32[1,5,32,128]{3,2,1,0:T(8,128)S(1)} %bitcast.28), channel_id=1, source_target_pairs={{0,48},{8,56},{16,0},{24,8},{32,16},{40,24},{48,32},{56,40},{64,11... | collective-permute-start | bytes 245768 | tf_op jit(solution)/shard_map/ppermute | solution.py:438
  32.0 5.7 %collective-permute-start = (f32[1,5,32,128]{3,2,1,0:T(8,128)S(1)}, f32[1,5,32,128]{3,2,1,0:T(8,128)S(1)}, u32[]{:S(2)}, u32[]{:S(2)}) collective-permute-start(f32[1,5,32,128]{3,2,1,0:T(8,128)S(1)} %bitcast.29), channel_id=1, source_target_pairs={{0,16},{8,24},{16,32},{24,40},{32,48},{40,56},{48,0},{56,8},{64,80... | collective-permute-start | bytes 245768 | tf_op jit(solution)/shard_map/ppermute | solution.py:438
  37.7 9.5 %collective-permute-start.3 = (f32[4,5,32,128]{3,2,1,0:T(8,128)S(1)}, f32[4,5,32,128]{3,2,1,0:T(8,128)S(1)}, u32[]{:S(2)}, u32[]{:S(2)}) collective-permute-start(f32[4,5,32,128]{3,2,1,0:T(8,128)S(1)} %pad_maximum_fusion.4), channel_id=1, source_target_pairs={{0,64},{8,72},{16,80},{24,88},{32,96},{40,104},{48,112},{56,120},{... | collective-permute-start | bytes 983048 | tf_op jit(solution)/shard_map/ppermute | solution.py:442
  47.2 2.2 %collective-permute-start.4 = (f32[8,5,32,128]{3,2,1,0:T(8,128)S(1)}, f32[8,5,32,128]{3,2,1,0:T(8,128)S(1)}, u32[]{:S(2)}, u32[]{:S(2)}) collective-permute-start(f32[8,5,32,128]{3,2,1,0:T(8,128)S(1)} %pad_maximum_fusion.2), channel_id=1, source_target_pairs={{0,8},{8,0},{16,24},{24,16},{32,40},{40,32},{48,56},{56,48},{64,72... | collective-permute-start | bytes 1966088 | tf_op jit(solution)/shard_map/ppermute | solution.py:447
  70.0 6.6 %collective-permute-start.7 = (f32[1,5,32,128]{3,2,1,0:T(8,128)S(1)}, f32[1,5,32,128]{3,2,1,0:T(8,128)S(1)}, u32[]{:S(2)}, u32[]{:S(2)}) collective-permute-start(f32[1,5,32,128]{3,2,1,0:T(8,128)S(1)} %bitcast.23), channel_id=1, source_target_pairs={{0,32},{8,40},{16,48},{24,56},{32,0},{40,8},{48,16},{56,24},{64,96... | collective-permute-start | bytes 245768 | tf_op jit(solution)/shard_map/ppermute | solution.py:438
  72.0 4.6 %collective-permute-start.6 = (f32[1,5,32,128]{3,2,1,0:T(8,128)S(1)}, f32[1,5,32,128]{3,2,1,0:T(8,128)S(1)}, u32[]{:S(2)}, u32[]{:S(2)}) collective-permute-start(f32[1,5,32,128]{3,2,1,0:T(8,128)S(1)} %bitcast.24), channel_id=1, source_target_pairs={{0,48},{8,56},{16,0},{24,8},{32,16},{40,24},{48,32},{56,40},{64,11... | collective-permute-start | bytes 245768 | tf_op jit(solution)/shard_map/ppermute | solution.py:438
  72.5 5.7 %collective-permute-start.5 = (f32[1,5,32,128]{3,2,1,0:T(8,128)S(1)}, f32[1,5,32,128]{3,2,1,0:T(8,128)S(1)}, u32[]{:S(2)}, u32[]{:S(2)}) collective-permute-start(f32[1,5,32,128]{3,2,1,0:T(8,128)S(1)} %bitcast.25), channel_id=1, source_target_pairs={{0,16},{8,24},{16,32},{24,40},{32,48},{40,56},{48,0},{56,8},{64,80... | collective-permute-start | bytes 245768 | tf_op jit(solution)/shard_map/ppermute | solution.py:438
  78.2 9.6 %collective-permute-start.8 = (f32[4,5,32,128]{3,2,1,0:T(8,128)S(1)}, f32[4,5,32,128]{3,2,1,0:T(8,128)S(1)}, u32[]{:S(2)}, u32[]{:S(2)}) collective-permute-start(f32[4,5,32,128]{3,2,1,0:T(8,128)S(1)} %pad_maximum_fusion.5), channel_id=1, source_target_pairs={{0,64},{8,72},{16,80},{24,88},{32,96},{40,104},{48,112},{56,120},{... | collective-permute-start | bytes 983048 | tf_op jit(solution)/shard_map/ppermute | solution.py:442
  87.8 2.2 %collective-permute-start.9 = (f32[8,5,32,128]{3,2,1,0:T(8,128)S(1)}, f32[8,5,32,128]{3,2,1,0:T(8,128)S(1)}, u32[]{:S(2)}, u32[]{:S(2)}) collective-permute-start(f32[8,5,32,128]{3,2,1,0:T(8,128)S(1)} %pad_maximum_fusion.3), channel_id=1, source_target_pairs={{0,8},{8,0},{16,24},{24,16},{32,40},{40,32},{48,56},{56,48},{64,72... | collective-permute-start | bytes 1966088 | tf_op jit(solution)/shard_map/ppermute | solution.py:447

commit v12 on v9

--- a/solution.py
+++ b/solution.py
@@ -224,7 +224,7 @@
         tile(end * (ROWS // 8 - 1), 2)
         return carry
 
-    lax.fori_loop(0, ROWS // 8, sides, 0, unroll=4)
+    lax.fori_loop(0, ROWS // 8, sides, 0, unroll=8)
     lax.fori_loop(0, 2, ends, 0, unroll=2)
 
 
@@ -663,7 +663,7 @@
             tile(block, quarter)
             return carry
 
-        lax.fori_loop(0, ROWS // 8, step, 0, unroll=4)
+        lax.fori_loop(0, ROWS // 8, step, 0, unroll=8)
 
     column(0)
     copy(0).start()

time: 110 us -> 109 us (level)
  no operation moved by 1% of the time
where the time goes in v12:
time: 109 us
  blocking collectives  51 us (47%)
  Pallas kernels  25.6 us (23%)
  waiting for transfers between devices  21 us (19%)
  starting transfers between devices  10.5 us (10%)
    all_to_all x2, blocking collectives, exchange(): got = lax.all_to_all(send, 'sub', split_axis=0, concat_axis=0, tiled=True)  30.4 us
    all_to_all x1, blocking collectives, body(): lax.all_to_all(slots, ('tile', 'sub'), split_axis=0, concat_axis=0, tiled...  20.6 us
    ppermute x2, waiting for transfers between devices, exchange(): lax.ppermute(all_parts, 'tile', [(i, i ^ 8) for i in range(N_TILE)])  10.4 us
    ppermute x6, starting transfers between devices, exchange(): lax.ppermute(all_parts, 'tile', turn(k))  7.21 us
    pallas_call x2, Pallas kernels, forcing(): pl.pallas_call(functools.partial(forcing_kernel, moment), out_shape=f32(P...  6.6 us
    ppermute x6, waiting for transfers between devices, exchange(): lax.ppermute(all_parts, 'tile', turn(k))  6.44 us
    pallas_call x1, Pallas kernels, second_edges(): pl.pallas_call(second_edges_kernel, out_shape=BIG + EDGES + BIG[1:], in_s...  4.29 us
    ppermute x2, waiting for transfers between devices, exchange(): lax.ppermute(all_parts, 'tile', [(i, i ^ 1) for i in range(N_TILE)])  4.17 us
  transfers between devices with their start and end apart: 10, of which 7 were waited for; matrix products, arithmetic and copies ran while one was open for 0% of the time, Pallas kernels for 8%

profile of v12, /device:TPU:0, one launch (start us, length us, event | category | flops | bytes accessed | tf_op | source)
XLA Modules:
  0.0 108.9 jit_solution(3802412609897594004)
XLA Ops:
  0.0 2.3 %pack.1 = (f32[128,2,128]{2,1,0:T(2,128)}, s32[16]{0:T(128)}) custom-call(s32[16]{0:T(128)} %owner_in.1, s32[3,4,16]{2,1,0:T(4,128)} %bitcast.32, s32[1,256]{1,0:T(1,128)} %bitcast.33, s32[1,256]{1,0:T(1,128)} %bitcast.34, s32[1,256]{1,0:T(1,128)} %bitcast.35, f32[32,256]{1,0:T(8,128)} %bitcast.31), custom_call_target="tpu_custom_call" | custom-call | tf_op jit(solution)/shard_map/pack/pallas_call | solution.py:127
  2.3 20.6 %all_to_all.15.slots = f32[128,2,128]{2,1,0:T(2,128)S(1)} all-to-all(f32[128,2,128]{2,1,0:T(2,128)} %get-tuple-element.40), channel_id=1, replica_groups=mesh['tile'=16,'sub'=8] {'tile','sub'}, dimensions={0} | all-to-all | bytes 262144 | tf_op jit(solution)/shard_map/all_to_all | solution.py:732
  22.9 0.0 copy-start
  22.9 0.0 copy-start.1
  22.9 0.0 copy-start.2
  22.9 0.0 copy-start.3
  22.9 0.0 copy-start.4
  23.0 3.3 %forcing_1.1.force = f32[2048,512]{1,0:T(8,128)S(1)} custom-call(f32[128,2,128]{2,1,0:T(2,128)S(1)} %all_to_all.15.slots), custom_call_target="tpu_custom_call" | custom-call | flops 8000000000 | bytes 4325376 | tf_op jit(solution)/shard_map/forcing_1/pallas_call | solution.py:184
  26.3 0.0 copy-done
  26.3 0.0 copy-done.1
  26.3 0.1 copy-done.2
  26.4 0.0 copy-done.3
  26.4 0.0 copy-done.4
  26.4 2.0 %first_edges.1 = (f32[8192,128]{1,0:T(8,128)S(1)}, f32[10240,128]{1,0:T(8,128)S(1)}, f32[5,32,128]{2,1,0:T(8,128)S(1)}, f32[4,32,128]{2,1,0:T(8,128)S(1)}, f32[4,32,128]{2,1,0:T(8,128)S(1)}) custom-call(s32[16]{0:T(128)S(1)} %copy-done.4, f32[2048,512]{1,0:T(8,128)S(1)} %bitcast.21, f32[2048,512]{1,0:T(8,128)S(1)} %forcing_1.1.force, ...), custom_call_target="tpu_custom_call" | custom-call | flops 30000000 | bytes 10000000 | tf_op jit(solution)/shard_map/first_edges/pallas_call | solution.py:343
  28.4 1.4 %collective-permute-start.2 = (f32[1,5,32,128]{3,2,1,0:T(8,128)S(1)}, f32[1,5,32,128]{3,2,1,0:T(8,128)S(1)}, u32[]{:S(2)}, u32[]{:S(2)}) collective-permute-start(f32[1,5,32,128]{3,2,1,0:T(8,128)S(1)} %bitcast.27), channel_id=1, source_target_pairs={{0,32},{8,40},{16,48},{24,56},{32,0},{40,8},{48,16},{56,24},{64,96... | collective-permute-start | bytes 245768 | tf_op jit(solution)/shard_map/ppermute | solution.py:435
  29.8 2.0 %collective-permute-start.1 = (f32[1,5,32,128]{3,2,1,0:T(8,128)S(1)}, f32[1,5,32,128]{3,2,1,0:T(8,128)S(1)}, u32[]{:S(2)}, u32[]{:S(2)}) collective-permute-start(f32[1,5,32,128]{3,2,1,0:T(8,128)S(1)} %bitcast.28), channel_id=1, source_target_pairs={{0,48},{8,56},{16,0},{24,8},{32,16},{40,24},{48,32},{56,40},{64,11... | collective-permute-start | bytes 245768 | tf_op jit(solution)/shard_map/ppermute | solution.py:435
  31.8 0.1 collective-permute-start
  31.9 3.3 %forcing_0.1.force = f32[2048,512]{1,0:T(8,128)S(1)} custom-call(f32[128,2,128]{2,1,0:T(2,128)S(1)} %all_to_all.15.slots), custom_call_target="tpu_custom_call" | custom-call | flops 8000000000 | bytes 4325376 | tf_op jit(solution)/shard_map/forcing_0/pallas_call | solution.py:184
  35.2 0.0 collective-permute-done.2
  35.2 0.0 collective-permute-done.1
  35.2 2.3 %collective-permute-done = f32[1,5,32,128]{3,2,1,0:T(8,128)S(1)} collective-permute-done((f32[1,5,32,128]{3,2,1,0:T(8,128)S(1)}, f32[1,5,32,128]{3,2,1,0:T(8,128)S(1)}, u32[]{:S(2)}, u32[]{:S(2)}) %collective-permute-start) | collective-permute-done | bytes 81952 | tf_op jit(solution)/shard_map/ppermute | solution.py:435
  37.5 1.5 %collective-permute-start.3 = (f32[4,5,32,128]{3,2,1,0:T(8,128)S(1)}, f32[4,5,32,128]{3,2,1,0:T(8,128)S(1)}, u32[]{:S(2)}, u32[]{:S(2)}) collective-permute-start(f32[4,5,32,128]{3,2,1,0:T(8,128)S(1)} %pad_maximum_fusion.4), channel_id=1, source_target_pairs={{0,64},{8,72},{16,80},{24,88},{32,96},{40,104},{48,112},{56,120},{... | collective-permute-start | bytes 983048 | tf_op jit(solution)/shard_map/ppermute | solution.py:439
  39.0 1.2 %first_inner.1 = (f32[8192,128]{1,0:T(8,128)S(1)}, f32[10240,128]{1,0:T(8,128)S(1)}) custom-call(f32[2048,512]{1,0:T(8,128)S(1)} %bitcast.22, f32[2048,512]{1,0:T(8,128)S(1)} %forcing_1.1.force, f32[960,512]{1,0:T(8,128)S(1)} %bitcast.18, f32[1024,512]{1,0:T(8,128)S(1)} %bitcast.12, ...), custom_call_target="tpu_custom_call", output_to_operand_aliasing={{0}: (5, {}), {1}: (6, {})} | custom-call | flops 20000000 | bytes 10000000 | tf_op jit(solution)/shard_map/first_inner/pallas_call | solution.py:356
  40.1 1.8 %second_inner.1 = (f32[8192,128]{1,0:T(8,128)S(1)}, f32[10240,128]{1,0:T(8,128)S(1)}) custom-call(f32[8192,128]{1,0:T(8,128)S(1)} %get-tuple-element.56.solved_in, f32[10240,128]{1,0:T(8,128)S(1)} %get-tuple-element.57.weighted_in, f32[2048,512]{1,0:T(8,128)S(1)} %forcing_0.1.force, f32[960,512]{1,0:T(8,128)S(1)} %bitcast.19, f32[1024,512]{1,0:T(8,128)S(1)} %bitcast.13, ...), custom_call_target="tpu_custom_call" | custom-call | flops 30000000 | bytes 10000000 | tf_op jit(solution)/shard_map/second_inner/pallas_call | solution.py:595
  41.9 5.0 %collective-permute-done.3 = f32[4,5,32,128]{3,2,1,0:T(8,128)S(1)} collective-permute-done((f32[4,5,32,128]{3,2,1,0:T(8,128)S(1)}, f32[4,5,32,128]{3,2,1,0:T(8,128)S(1)}, u32[]{:S(2)}, u32[]{:S(2)}) %collective-permute-start.3) | collective-permute-done | bytes 327712 | tf_op jit(solution)/shard_map/ppermute | solution.py:439
  47.0 0.1 collective-permute-start.4
  47.1 2.1 %collective-permute-done.4 = f32[8,5,32,128]{3,2,1,0:T(8,128)S(1)} collective-permute-done((f32[8,5,32,128]{3,2,1,0:T(8,128)S(1)}, f32[8,5,32,128]{3,2,1,0:T(8,128)S(1)}, u32[]{:S(2)}, u32[]{:S(2)}) %collective-permute-start.4) | collective-permute-done | bytes 655392 | tf_op jit(solution)/shard_map/ppermute | solution.py:444
  49.1 0.1 pad_maximum_fusion.gathered
  49.3 0.7 route.2
  50.0 15.2 %all_to_all.16.got = f32[8,176,128]{2,1,0:T(8,128)S(1)} all-to-all(f32[8,176,128]{2,1,0:T(8,128)S(1)} %get-tuple-element.54), channel_id=1, replica_groups=mesh['tile'=16,'sub'=8] {'sub'}, dimensions={0} | all-to-all | bytes 1441792 | tf_op jit(solution)/shard_map/all_to_all | solution.py:447
  65.1 4.3 %second_edges.1 = (f32[8192,128]{1,0:T(8,128)S(1)}, f32[10240,128]{1,0:T(8,128)S(1)}, f32[5,32,128]{2,1,0:T(8,128)S(1)}, f32[4,32,128]{2,1,0:T(8,128)S(1)}, f32[...) custom-call(s32[16]{0:T(128)S(1)} %copy-done.4, ...), custom_call_target="tpu_custom_call", output_to_operand_aliasing={{0}: (9, {}), {1}: (10, {}), {5}: (4, {})} | custom-call | flops 40000000 | bytes 10000000 | tf_op jit(solution)/shard_map/second_edges/pallas_call | solution.py:607
  69.4 1.7 %collective-permute-start.7 = (f32[1,5,32,128]{3,2,1,0:T(8,128)S(1)}, f32[1,5,32,128]{3,2,1,0:T(8,128)S(1)}, u32[]{:S(2)}, u32[]{:S(2)}) collective-permute-start(f32[1,5,32,128]{3,2,1,0:T(8,128)S(1)} %bitcast.23), channel_id=1, source_target_pairs={{0,32},{8,40},{16,48},{24,56},{32,0},{40,8},{48,16},{56,24},{64,96... | collective-permute-start | bytes 245768 | tf_op jit(solution)/shard_map/ppermute | solution.py:435
  71.2 0.5 collective-permute-start.6
  71.7 1.5 %collective-permute-start.5 = (f32[1,5,32,128]{3,2,1,0:T(8,128)S(1)}, f32[1,5,32,128]{3,2,1,0:T(8,128)S(1)}, u32[]{:S(2)}, u32[]{:S(2)}) collective-permute-start(f32[1,5,32,128]{3,2,1,0:T(8,128)S(1)} %bitcast.25), channel_id=1, source_target_pairs={{0,16},{8,24},{16,32},{24,40},{32,48},{40,56},{48,0},{56,8},{64,80... | collective-permute-start | bytes 245768 | tf_op jit(solution)/shard_map/ppermute | solution.py:435
  73.2 2.6 %collective-permute-done.7 = f32[1,5,32,128]{3,2,1,0:T(8,128)S(1)} collective-permute-done((f32[1,5,32,128]{3,2,1,0:T(8,128)S(1)}, f32[1,5,32,128]{3,2,1,0:T(8,128)S(1)}, u32[]{:S(2)}, u32[]{:S(2)}) %collective-permute-start.7) | collective-permute-done | bytes 81952 | tf_op jit(solution)/shard_map/ppermute | solution.py:435
  75.8 0.0 collective-permute-done.6
  75.8 1.6 %collective-permute-done.5 = f32[1,5,32,128]{3,2,1,0:T(8,128)S(1)} collective-permute-done((f32[1,5,32,128]{3,2,1,0:T(8,128)S(1)}, f32[1,5,32,128]{3,2,1,0:T(8,128)S(1)}, u32[]{:S(2)}, u32[]{:S(2)}) %collective-permute-start.5) | collective-permute-done | bytes 81952 | tf_op jit(solution)/shard_map/ppermute | solution.py:435
  77.4 1.6 %collective-permute-start.8 = (f32[4,5,32,128]{3,2,1,0:T(8,128)S(1)}, f32[4,5,32,128]{3,2,1,0:T(8,128)S(1)}, u32[]{:S(2)}, u32[]{:S(2)}) collective-permute-start(f32[4,5,32,128]{3,2,1,0:T(8,128)S(1)} %pad_maximum_fusion.5), channel_id=1, source_target_pairs={{0,64},{8,72},{16,80},{24,88},{32,96},{40,104},{48,112},{56,120},{... | collective-permute-start | bytes 983048 | tf_op jit(solution)/shard_map/ppermute | solution.py:439
  79.0 2.5 %last_inner.1._ = f32[32,64,512]{2,1,0:T(8,128)} custom-call(f32[8192,128]{1,0:T(8,128)S(1)} %get-tuple-element.63.solved, f32[10240,128]{1,0:T(8,128)S(1)} %get-tuple-element.64.weighted.weighted_in, f32[1024,512]{1,0:T(8,128)S(1)} %bitcast.15, s32[64,512]{1,0:T(8,128)S(1)} %copy-done.3), custom_call_target="tpu_custom_call" | custom-call | flops 20000000 | bytes 10000000 | tf_op jit(solution)/shard_map/last_inner/pallas_call | solution.py:685
  81.5 5.4 %collective-permute-done.8 = f32[4,5,32,128]{3,2,1,0:T(8,128)S(1)} collective-permute-done((f32[4,5,32,128]{3,2,1,0:T(8,128)S(1)}, f32[4,5,32,128]{3,2,1,0:T(8,128)S(1)}, u32[]{:S(2)}, u32[]{:S(2)}) %collective-permute-start.8) | collective-permute-done | bytes 327712 | tf_op jit(solution)/shard_map/ppermute | solution.py:439
  87.0 0.1 collective-permute-start.9
  87.1 2.1 %collective-permute-done.9 = f32[8,5,32,128]{3,2,1,0:T(8,128)S(1)} collective-permute-done((f32[8,5,32,128]{3,2,1,0:T(8,128)S(1)}, f32[8,5,32,128]{3,2,1,0:T(8,128)S(1)}, u32[]{:S(2)}, u32[]{:S(2)}) %collective-permute-start.9) | collective-permute-done | bytes 655392 | tf_op jit(solution)/shard_map/ppermute | solution.py:444
  89.2 0.1 pad_maximum_fusion.1.gathered
  89.3 0.7 route.3
  90.0 15.2 %all_to_all.17.got = f32[8,176,128]{2,1,0:T(8,128)S(1)} all-to-all(f32[8,176,128]{2,1,0:T(8,128)S(1)} %get-tuple-element.69), channel_id=1, replica_groups=mesh['tile'=16,'sub'=8] {'sub'}, dimensions={0} | all-to-all | bytes 1441792 | tf_op jit(solution)/shard_map/all_to_all | solution.py:447
  105.2 3.6 %last_edges.1 = (f32[32,64,512]{2,1,0:T(8,128)}, f32[10240,128]{1,0:T(8,128)S(1)}) custom-call(s32[16]{0:T(128)S(1)} %copy-done.4, f32[8,176,128]{2,1,0:T(8,128)S(1)} %all_to_all.17.got, f32[4,32,128]{2,1,0:T(8,128)S(1)} %get-tuple-element.70.here, f32[8192,128]{1,0:T(8,128)S(1)} %get-tuple-element.63.solved, ...), custom_call_target="tpu_custom_call", output_to_operand_aliasing={{0}: (7, {}), {1}: (4, {})} | custom-call | flops 20000000 | bytes 10000000 | tf_op jit(solution)/shard_map/last_edges/pallas_call | solution.py:698
  (4 shorter events, 0.1 us)
Async XLA Ops:
  22.9 3.3 %copy-start = (f32[16,64,512]{2,1,0:T(8,128)S(1)}, f32[16,64,512]{2,1,0:T(8,128)}, u32[]{:S(2)}) copy-start(f32[16,64,512]{2,1,0:T(8,128)} %param.11) | copy-start | bytes 6291460
  22.9 3.3 %copy-start.1 = (f32[15,64,512]{2,1,0:T(8,128)S(1)}, f32[15,64,512]{2,1,0:T(8,128)}, u32[]{:S(2)}) copy-start(f32[15,64,512]{2,1,0:T(8,128)} %param.12) | copy-start | bytes 5898244
  22.9 3.4 %copy-start.2 = (f32[2,16,64,512]{3,2,1,0:T(8,128)S(1)}, f32[2,16,64,512]{3,2,1,0:T(8,128)}, u32[]{:S(2)}) copy-start(f32[2,16,64,512]{3,2,1,0:T(8,128)} %param.10) | copy-start | bytes 12582916
  22.9 3.4 %copy-start.3 = (s32[64,512]{1,0:T(8,128)S(1)}, s32[64,512]{1,0:T(8,128)}, u32[]{:S(2)}) copy-start(s32[64,512]{1,0:T(8,128)} %depth.8) | copy-start | bytes 393220
  22.9 3.4 %copy-start.4 = (s32[16]{0:T(128)S(1)}, s32[16]{0:T(128)}, u32[]{:S(2)}) copy-start(s32[16]{0:T(128)} %get-tuple-element.39.meta) | copy-start | bytes 196
  28.4 6.7 %collective-permute-start.2 = (f32[1,5,32,128]{3,2,1,0:T(8,128)S(1)}, f32[1,5,32,128]{3,2,1,0:T(8,128)S(1)}, u32[]{:S(2)}, u32[]{:S(2)}) collective-permute-start(f32[1,5,32,128]{3,2,1,0:T(8,128)S(1)} %bitcast.27), channel_id=1, source_target_pairs={{0,32},{8,40},{16,48},{24,56},{32,0},{40,8},{48,16},{56,24},{64,96... | collective-permute-start | bytes 245768 | tf_op jit(solution)/shard_map/ppermute | solution.py:435
  29.8 5.3 %collective-permute-start.1 = (f32[1,5,32,128]{3,2,1,0:T(8,128)S(1)}, f32[1,5,32,128]{3,2,1,0:T(8,128)S(1)}, u32[]{:S(2)}, u32[]{:S(2)}) collective-permute-start(f32[1,5,32,128]{3,2,1,0:T(8,128)S(1)} %bitcast.28), channel_id=1, source_target_pairs={{0,48},{8,56},{16,0},{24,8},{32,16},{40,24},{48,32},{56,40},{64,11... | collective-permute-start | bytes 245768 | tf_op jit(solution)/shard_map/ppermute | solution.py:435
  31.8 5.7 %collective-permute-start = (f32[1,5,32,128]{3,2,1,0:T(8,128)S(1)}, f32[1,5,32,128]{3,2,1,0:T(8,128)S(1)}, u32[]{:S(2)}, u32[]{:S(2)}) collective-permute-start(f32[1,5,32,128]{3,2,1,0:T(8,128)S(1)} %bitcast.29), channel_id=1, source_target_pairs={{0,16},{8,24},{16,32},{24,40},{32,48},{40,56},{48,0},{56,8},{64,80... | collective-permute-start | bytes 245768 | tf_op jit(solution)/shard_map/ppermute | solution.py:435
  37.5 9.5 %collective-permute-start.3 = (f32[4,5,32,128]{3,2,1,0:T(8,128)S(1)}, f32[4,5,32,128]{3,2,1,0:T(8,128)S(1)}, u32[]{:S(2)}, u32[]{:S(2)}) collective-permute-start(f32[4,5,32,128]{3,2,1,0:T(8,128)S(1)} %pad_maximum_fusion.4), channel_id=1, source_target_pairs={{0,64},{8,72},{16,80},{24,88},{32,96},{40,104},{48,112},{56,120},{... | collective-permute-start | bytes 983048 | tf_op jit(solution)/shard_map/ppermute | solution.py:439
  47.0 2.2 %collective-permute-start.4 = (f32[8,5,32,128]{3,2,1,0:T(8,128)S(1)}, f32[8,5,32,128]{3,2,1,0:T(8,128)S(1)}, u32[]{:S(2)}, u32[]{:S(2)}) collective-permute-start(f32[8,5,32,128]{3,2,1,0:T(8,128)S(1)} %pad_maximum_fusion.2), channel_id=1, source_target_pairs={{0,8},{8,0},{16,24},{24,16},{32,40},{40,32},{48,56},{56,48},{64,72... | collective-permute-start | bytes 1966088 | tf_op jit(solution)/shard_map/ppermute | solution.py:444
  69.4 6.3 %collective-permute-start.7 = (f32[1,5,32,128]{3,2,1,0:T(8,128)S(1)}, f32[1,5,32,128]{3,2,1,0:T(8,128)S(1)}, u32[]{:S(2)}, u32[]{:S(2)}) collective-permute-start(f32[1,5,32,128]{3,2,1,0:T(8,128)S(1)} %bitcast.23), channel_id=1, source_target_pairs={{0,32},{8,40},{16,48},{24,56},{32,0},{40,8},{48,16},{56,24},{64,96... | collective-permute-start | bytes 245768 | tf_op jit(solution)/shard_map/ppermute | solution.py:435
  71.2 4.6 %collective-permute-start.6 = (f32[1,5,32,128]{3,2,1,0:T(8,128)S(1)}, f32[1,5,32,128]{3,2,1,0:T(8,128)S(1)}, u32[]{:S(2)}, u32[]{:S(2)}) collective-permute-start(f32[1,5,32,128]{3,2,1,0:T(8,128)S(1)} %bitcast.24), channel_id=1, source_target_pairs={{0,48},{8,56},{16,0},{24,8},{32,16},{40,24},{48,32},{56,40},{64,11... | collective-permute-start | bytes 245768 | tf_op jit(solution)/shard_map/ppermute | solution.py:435
  71.7 5.7 %collective-permute-start.5 = (f32[1,5,32,128]{3,2,1,0:T(8,128)S(1)}, f32[1,5,32,128]{3,2,1,0:T(8,128)S(1)}, u32[]{:S(2)}, u32[]{:S(2)}) collective-permute-start(f32[1,5,32,128]{3,2,1,0:T(8,128)S(1)} %bitcast.25), channel_id=1, source_target_pairs={{0,16},{8,24},{16,32},{24,40},{32,48},{40,56},{48,0},{56,8},{64,80... | collective-permute-start | bytes 245768 | tf_op jit(solution)/shard_map/ppermute | solution.py:435
  77.4 9.5 %collective-permute-start.8 = (f32[4,5,32,128]{3,2,1,0:T(8,128)S(1)}, f32[4,5,32,128]{3,2,1,0:T(8,128)S(1)}, u32[]{:S(2)}, u32[]{:S(2)}) collective-permute-start(f32[4,5,32,128]{3,2,1,0:T(8,128)S(1)} %pad_maximum_fusion.5), channel_id=1, source_target_pairs={{0,64},{8,72},{16,80},{24,88},{32,96},{40,104},{48,112},{56,120},{... | collective-permute-start | bytes 983048 | tf_op jit(solution)/shard_map/ppermute | solution.py:439
  87.0 2.2 %collective-permute-start.9 = (f32[8,5,32,128]{3,2,1,0:T(8,128)S(1)}, f32[8,5,32,128]{3,2,1,0:T(8,128)S(1)}, u32[]{:S(2)}, u32[]{:S(2)}) collective-permute-start(f32[8,5,32,128]{3,2,1,0:T(8,128)S(1)} %pad_maximum_fusion.3), channel_id=1, source_target_pairs={{0,8},{8,0},{16,24},{24,16},{32,40},{40,32},{48,56},{56,48},{64,72... | collective-permute-start | bytes 1966088 | tf_op jit(solution)/shard_map/ppermute | solution.py:444
